TPU v7x, 32 devices: a whole 2x2x4 slice. The times are simulated.
32 devices in a mesh: dp: 8 (over y, x, core), tensor: 4 (over z).
Axes of the slice: x: 2, y: 2, z: 4, core: 2. Of those that a mesh axis runs over, the one named last changes fastest.
Arguments:
- tokens: bfloat16 [32768, 768], P(('dp', 'tensor')), may hold values from -6 to 6
- norm1_gain: float32 [768], replicated, may hold values from 0.5 to 1.5
- qkv_weight: bfloat16 [768, 3, 768], P('dp', None, 'tensor'), may hold values from -0.21875 to 0.21875
- attn_proj: bfloat16 [768, 768], P('tensor', 'dp'), may hold values from -3 to 3
- norm2_gain: float32 [768], replicated, may hold values from 0.5 to 1.5
- router_proj: float32 [768, 16], replicated, may hold values from -0.21875 to 0.21875
- expert_embed: float32 [4, 16], replicated, may hold values from -6 to 6
- expert_in: bfloat16 [768, 12288], P(None, 'dp'), may hold values from -0.21875 to 0.21875
- expert_out: bfloat16 [12288, 768], P('dp'), may hold values from -0.4375 to 0.4375
- routes: int32 [32768, 1], P(('dp', 'tensor')), may hold values from 0 to 3
- orders: int32 [32, 1024], P(('dp', 'tensor')), may hold values from 0 to 1023, each once within a row
- leaf_parent: int32 [8, 8], P('dp'), may hold values from 1 to 4, as said below
- cotangent: bfloat16 [32768, 768], P(('dp', 'tensor')), may hold values from -6 to 6
Outputs:
- output: bfloat16 [32768, 768], P(('dp', 'tensor'))
- grad_tokens: float32 [32768, 768], P(('dp', 'tensor'))
- grad_norm1: float32 [768], replicated
- grad_qkv: float32 [768, 3, 768], P('dp', None, 'tensor')
- grad_attn_proj: float32 [768, 768], P('tensor', 'dp')
- grad_norm2: float32 [768], replicated
- grad_router: float32 [768, 16], replicated
- grad_embed: float32 [4, 16], replicated
- grad_expert_in: float32 [768, 12288], P(None, ('dp', 'tensor'))
- grad_expert_out: float32 [12288, 768], P(('dp', 'tensor'))
Inputs may be any that keep to these rules, and one draw needn't show every extreme that they name: `leaf_parent`: in each tree, each branch segment 1 to 4 is the parent of exactly two of the 8 leaves.
All inputs are finite; a program needn't handle non-finite values.
Results may differ from a plain program's by a relative error of at most 0.014.
Values may be sent and summed in bfloat16 or wider, within the bound.
A program may use at most 256 MiB of HBM per device.

v0:
```python
import jax
import jax.numpy as jnp
from jax import lax
from jax.sharding import PartitionSpec as P

HEAD_DIM = 64
TRUNK = 1024
BRANCH = 256
BRANCHES = 4
QBLOCK = 512
LEAVES = 8


norm_eps = 1e-05
route_scale = 3.0
masked_score = -1e30
highest = lax.Precision.HIGHEST


def layer_norm(values, norm_gain):
    centred = values - jnp.mean(values, axis=-1, keepdims=True)
    spread = jnp.mean(centred * centred, axis=-1, keepdims=True)
    return centred * lax.rsqrt(spread + norm_eps) * norm_gain


def unit_rows(values):
    return values * lax.rsqrt(jnp.sum(values * values, axis=-1, keepdims=True) + 1.0)


def router_gate(normed, router_proj, expert_embed, picked):
    routed = jnp.dot(normed, router_proj, precision=highest)
    logits = route_scale * jnp.dot(unit_rows(routed), unit_rows(expert_embed).T, precision=highest)
    return jnp.sum(jax.nn.softmax(logits, axis=-1) * picked, axis=-1)


def gelu_exact(values):
    return jax.nn.gelu(values, approximate=False)


def segment_of(positions):
    past_trunk = positions - TRUNK
    past_branches = past_trunk - BRANCHES * BRANCH
    inner = jnp.where(
        past_branches < 0, 1 + past_trunk // BRANCH, 1 + BRANCHES + past_branches // BRANCH
    )
    return jnp.where(positions < TRUNK, 0, inner)


def parent_of(segments, leaf_parents):
    leaf_index = segments - 1 - BRANCHES
    matches = leaf_index[:, None] == jnp.arange(LEAVES)[None, :]
    return jnp.sum(jnp.where(matches, leaf_parents[None, :], 0), axis=1)


def visible(query_pos, key_pos, leaf_parents):
    query_seg = segment_of(query_pos)
    query_parent = parent_of(query_seg, leaf_parents)
    key_seg = segment_of(key_pos)[None, :]
    related = (key_seg == 0) | (key_seg == query_seg[:, None]) | (key_seg == query_parent[:, None])
    return related & (key_pos[None, :] <= query_pos[:, None])


def slot_table(route_ids, order_ids, capacity):
    same_expert = route_ids[:, None] == route_ids[None, :]
    earlier = order_ids[None, :] < order_ids[:, None]
    ranking = jnp.sum(jnp.where(same_expert & earlier, 1, 0), axis=1).astype(jnp.int32)
    kept_mask = ranking < capacity
    column = route_ids * capacity + jnp.minimum(ranking, capacity - 1)
    return (column, kept_mask)


def shards(
    tokens,
    norm1_gain,
    qkv_weight,
    attn_proj,
    norm2_gain,
    router_proj,
    expert_embed,
    expert_in,
    expert_out,
    routes,
    orders,
    leaf_parent,
    cotangent,
):
    rows_here = tokens.shape[0]
    model_width = tokens.shape[1]
    experts = expert_embed.shape[0]
    capacity = rows_here // experts
    dp_size = lax.axis_size("dp")
    score_scale = HEAD_DIM ** (-0.5)
    leaf_parents = leaf_parent[0]

    def whole_tree(local_rows):
        return lax.all_gather(local_rows, "tensor", axis=0, tiled=True)

    def own_rows(term_of):
        return lax.psum_scatter(
            term_of(jnp.int32(0), rows_here * lax.axis_size("tensor")),
            "tensor",
            scatter_dimension=0,
            tiled=True,
        )

    def dispatch(slot_input):
        doubled = jnp.broadcast_to(
            slot_input.reshape(experts, 1, capacity, model_width),
            (experts, 2, capacity, model_width),
        )
        arrived = lax.all_to_all(
            doubled.reshape(dp_size, capacity, model_width),
            "dp",
            split_axis=0,
            concat_axis=0,
            tiled=True,
        )
        return arrived.reshape(dp_size * capacity, model_width)

    def combine(partial_rows):
        returned = lax.all_to_all(
            partial_rows.reshape(dp_size, capacity, model_width),
            "dp",
            split_axis=0,
            concat_axis=0,
            tiled=True,
        )
        summed = jnp.sum(returned.reshape(experts, 2, capacity, model_width), axis=1)
        return summed.reshape(experts * capacity, model_width)

    hidden = tokens.astype(jnp.float32)
    normed_in, norm1_back = jax.vjp(layer_norm, hidden, norm1_gain)
    tree_in = whole_tree(normed_in.astype(jnp.bfloat16))
    tree_len = tree_in.shape[0]
    qkv_full, proj_full = (
        lax.all_gather(qkv_weight, "dp", axis=0, tiled=True),
        lax.all_gather(attn_proj, "dp", axis=1, tiled=True),
    )
    heads_here = qkv_full.shape[2] // HEAD_DIM
    projected = jnp.einsum(
        "sd,dkc->skc", tree_in, qkv_full, preferred_element_type=jnp.float32
    ).astype(jnp.bfloat16)
    query_rows = projected[:, 0].reshape(tree_len, heads_here, HEAD_DIM)
    key_rows = projected[:, 1].reshape(tree_len, heads_here, HEAD_DIM)
    value_rows = projected[:, 2].reshape(tree_len, heads_here, HEAD_DIM)
    positions = jnp.arange(tree_len)
    block_count = tree_len // QBLOCK

    def block_scores(block_id):
        first_row = block_id * QBLOCK
        block_queries = lax.dynamic_slice_in_dim(query_rows, first_row, QBLOCK, 0)
        allowed = visible(first_row + jnp.arange(QBLOCK), positions, leaf_parents)
        scores = (
            jnp.einsum("qhc,khc->hqk", block_queries, key_rows, preferred_element_type=jnp.float32)
            * score_scale
        )
        return (jnp.where(allowed[None], scores, masked_score), block_queries, first_row)

    def forward_block(block_id):
        scores = block_scores(block_id)[0]
        row_max = jnp.max(scores, axis=-1, keepdims=True)
        weights = jnp.exp(scores - row_max)
        row_total = jnp.sum(weights, axis=-1, keepdims=True)
        attn_probs = (weights / row_total).astype(jnp.bfloat16)
        outputs = jnp.einsum(
            "hqk,khc->qhc", attn_probs, value_rows, preferred_element_type=jnp.float32
        )
        return (outputs.astype(jnp.bfloat16), (row_max + jnp.log(row_total))[..., 0])

    attended_blocks, log_totals = lax.map(forward_block, jnp.arange(block_count))
    attended = attended_blocks.reshape(tree_len, heads_here * HEAD_DIM)

    def branch_term(first_row, row_count):
        return jnp.dot(attended, proj_full, preferred_element_type=jnp.float32)

    branch_out = own_rows(branch_term)
    mid_stream = hidden + branch_out
    normed_mid, norm2_back = jax.vjp(layer_norm, mid_stream, norm2_gain)
    moe_in = normed_mid.astype(jnp.bfloat16)
    route_ids = routes[:, 0]
    column, kept_mask = slot_table(route_ids, orders[0], capacity)
    picked = (route_ids[:, None] == jnp.arange(experts)[None, :]).astype(jnp.float32)
    gate_value, gate_back = jax.vjp(
        lambda normed_rows, route_proj, embed_rows: router_gate(
            normed_rows, route_proj, embed_rows, picked
        ),
        moe_in.astype(jnp.float32),
        router_proj,
        expert_embed,
    )
    select = (
        (column[:, None] == jnp.arange(experts * capacity)[None, :]) & kept_mask[:, None]
    ).astype(jnp.bfloat16)
    kept_float = kept_mask[:, None].astype(jnp.float32)

    def to_slots(token_rows):
        return jnp.einsum(
            "ts,td->sd", select, token_rows, preferred_element_type=jnp.float32
        ).astype(jnp.bfloat16)

    def from_slots(slot_rows):
        return jnp.take(slot_rows, column, axis=0) * kept_float

    expert_rows = dispatch(to_slots(moe_in))
    up_values = jnp.dot(expert_rows, expert_in, preferred_element_type=jnp.float32)
    active_full, gelu_back = jax.vjp(gelu_exact, up_values)
    active = active_full.astype(jnp.bfloat16)
    expert_result = from_slots(
        combine(jnp.dot(active, expert_out, preferred_element_type=jnp.float32))
    )
    output = (mid_stream + gate_value[:, None] * expert_result).astype(jnp.bfloat16)
    upstream = cotangent.astype(jnp.float32)
    arrived_grad = dispatch(to_slots((gate_value[:, None] * upstream).astype(jnp.bfloat16)))
    out_weight_grad = jnp.einsum(
        "rf,rd->fd", active, arrived_grad, preferred_element_type=jnp.float32
    )
    active_grad = jnp.einsum(
        "rd,fd->rf", arrived_grad, expert_out, preferred_element_type=jnp.float32
    )
    up_grad = gelu_back(active_grad)[0].astype(jnp.bfloat16)
    in_weight_grad = jnp.einsum(
        "rd,rf->df", expert_rows, up_grad, preferred_element_type=jnp.float32
    )
    moe_grad = from_slots(
        combine(jnp.einsum("rf,df->rd", up_grad, expert_in, preferred_element_type=jnp.float32))
    )
    gate_grad = jnp.sum(upstream * expert_result, axis=-1)
    router_part, proj_grad, embed_grad = gate_back(gate_grad)
    mid_part, gain2_grad = norm2_back(moe_grad + router_part)
    mid_grad = upstream + mid_part
    expert_in_grad, expert_out_grad = (
        lax.psum_scatter(
            in_weight_grad.astype(jnp.bfloat16), "tensor", scatter_dimension=1, tiled=True
        ).astype(jnp.float32),
        lax.psum_scatter(
            out_weight_grad.astype(jnp.bfloat16), "tensor", scatter_dimension=0, tiled=True
        ).astype(jnp.float32),
    )
    branch_grad = whole_tree(mid_grad.astype(jnp.bfloat16))
    proj_grad_full = jnp.einsum(
        "sc,sd->cd", attended, branch_grad, preferred_element_type=jnp.float32
    )
    attended_grad = (
        jnp.einsum("sd,cd->sc", branch_grad, proj_full, preferred_element_type=jnp.float32)
        .astype(jnp.bfloat16)
        .reshape(tree_len, heads_here, HEAD_DIM)
    )

    def backward_block(running, block_id):
        key_grad, value_grad = running
        scores, block_queries, first_row = block_scores(block_id)
        block_grads = lax.dynamic_slice_in_dim(attended_grad, first_row, QBLOCK, 0)
        attn_probs = jnp.exp(scores - log_totals[block_id][..., None])
        low_probs = attn_probs.astype(jnp.bfloat16)
        value_grad = value_grad + jnp.einsum(
            "hqk,qhc->khc", low_probs, block_grads, preferred_element_type=jnp.float32
        )
        prob_grad = jnp.einsum(
            "qhc,khc->hqk", block_grads, value_rows, preferred_element_type=jnp.float32
        )
        centre = jnp.sum(attn_probs * prob_grad, axis=-1, keepdims=True)
        score_grad = (attn_probs * (prob_grad - centre)).astype(jnp.bfloat16)
        query_grad = (
            jnp.einsum("hqk,khc->qhc", score_grad, key_rows, preferred_element_type=jnp.float32)
            * score_scale
        )
        key_grad = (
            key_grad
            + jnp.einsum(
                "hqk,qhc->khc", score_grad, block_queries, preferred_element_type=jnp.float32
            )
            * score_scale
        )
        return ((key_grad, value_grad), query_grad)

    empty_grads = jnp.zeros((tree_len, heads_here, HEAD_DIM), jnp.float32)
    (key_total, value_total), query_blocks = lax.scan(
        backward_block, (empty_grads, empty_grads), jnp.arange(block_count)
    )
    projected_grad = jnp.stack(
        [query_blocks.reshape(tree_len, heads_here, HEAD_DIM), key_total, value_total], axis=1
    )
    projected_grad = projected_grad.reshape(tree_len, 3, heads_here * HEAD_DIM).astype(jnp.bfloat16)
    qkv_grad_full = jnp.einsum(
        "sd,skc->dkc", tree_in, projected_grad, preferred_element_type=jnp.float32
    )
    qkv_grad, attn_proj_grad = (
        lax.psum_scatter(qkv_grad_full, "dp", scatter_dimension=0, tiled=True),
        lax.psum_scatter(proj_grad_full, "dp", scatter_dimension=1, tiled=True),
    )

    def input_term(first_row, row_count):
        return jnp.einsum(
            "skc,dkc->sd", projected_grad, qkv_full, preferred_element_type=jnp.float32
        )

    input_grad = own_rows(input_term)
    token_part, gain1_grad = norm1_back(input_grad)
    token_grad = mid_grad + token_part
    gain1_sum, gain2_sum, router_sum, embed_sum = lax.psum(
        (gain1_grad, gain2_grad, proj_grad, embed_grad), ("dp", "tensor")
    )
    return (
        output,
        token_grad,
        gain1_sum,
        qkv_grad,
        attn_proj_grad,
        gain2_sum,
        router_sum,
        embed_sum,
        expert_in_grad,
        expert_out_grad,
    )


def solution(mesh):
    in_specs = (
        P(("dp", "tensor"), None),
        P(),
        P("dp", None, "tensor"),
        P("tensor", "dp"),
        P(),
        P(),
        P(),
        P(None, "dp"),
        P("dp", None),
        P(("dp", "tensor"), None),
        P(("dp", "tensor"), None),
        P("dp", None),
        P(("dp", "tensor"), None),
    )
    out_specs = (
        P(("dp", "tensor"), None),
        P(("dp", "tensor"), None),
        P(),
        P("dp", None, "tensor"),
        P("tensor", "dp"),
        P(),
        P(),
        P(),
        P(None, ("dp", "tensor")),
        P(("dp", "tensor"), None),
    )
    return jax.shard_map(shards, mesh=mesh, in_specs=in_specs, out_specs=out_specs, check_vma=False)
```

profile of v0, /device:TPU:0, one launch (start us, length us, event | category | flops | bytes accessed | tf_op | source)
XLA Modules:
  0.0 2240.5 jit_solution(14569765892642481141)
XLA Ops:
  14.4 15.5 all_gather.13
  42.2 90.1 %all-gather.3.cloned.1.call-done = bf16[4096,768]{1,0:T(8,128)(2,1)} async-done(((bf16[1024,768]{1,0:T(8,128)(2,1)}), bf16[4096,768]{1,0:T(8,128)(2,1)}) %all-gather.3.cloned.1.call-update) | async-done | bytes 6291472 | tf_op jit(solution)/shard_map/all_gather | solution.py:96
  141.4 340.5 %while.40 = (s32[]{:T(128)}, bf16[8,512,3,64]{1,3,2,0:T(8,128)(2,1)}, f32[8,3,512]{2,1,0:T(4,128)}, s32[8]{0:T(128)S(1)}, s32[1,8]{1,0:T(1,128)S(1)}, /*index=5*...) while((s32[]{:T(128)}, ...), condition=%wide.region_6.7_spmd.clone.clone, body=%wide.region_2.6_spmd.clone.clone.sunk | while | flops 1699148288 | bytes 93825288 | solution.py:170
  494.3 208.5 %reduce-scatter.11.cloned.1.call-done = f32[1024,768]{1,0:T(8,128)} async-done(((f32[4096,768]{1,0:T(8,128)}), f32[1024,768]{1,0:T(8,128)}) %reduce-scatter.11.cloned.1.call-update) | async-done | bytes 3145744 | tf_op jit(solution)/shard_map/reduce_scatter | solution.py:99
  709.9 41.3 %all_to_all.20 = bf16[8,256,768]{2,1,0:T(8,128)(2,1)S(1)} all-to-all(bf16[8,256,768]{2,1,0:T(8,128)(2,1)S(1)} %bitcast.144), channel_id=1, replica_groups=mesh['dp'=8,'tensor'=4] {'dp'}, dimensions={0} | all-to-all | bytes 6291456 | tf_op jit(solution)/shard_map/all_to_all | solution.py:111
  751.2 35.4 %multiply_convert_fusion.1 = (bf16[2048,1536]{1,0:T(8,128)(2,1)S(1)}, f32[2048,1536]{1,0:T(8,128)}, f32[2048,1536]{1,0:T(8,128)}) fusion(bf16[2048,768]{1,0:T(8,128)(2,1)S(1)} %bitcast.155, bf16[768,1536]{1,0:T(8,128)(2,1)S(1)} %copy-done), kind=kOutput, calls=%fused_computation.171 | convolution fusion | flops 5036310528 | bytes 36962304 | tf_op jit(solution)/shard_map/dot_general | solution.py:205
  802.4 67.9 %all-to-all-done.1 = f32[8,256,768]{2,1,0:T(8,128)} async-done(((f32[8,256,768]{2,1,0:T(8,128)}), f32[8,256,768]{2,1,0:T(8,128)}, u32[]{:S(2)}, u32[]{:S(2)}) %all-to-all-start.1) | async-done | bytes 6291488 | tf_op jit(solution)/shard_map/all_to_all | solution.py:121
  889.3 40.4 %all_to_all.21 = bf16[8,256,768]{2,1,0:T(8,128)(2,1)S(1)} all-to-all(bf16[8,256,768]{2,1,0:T(8,128)(2,1)S(1)} %bitcast.145), channel_id=1, replica_groups=mesh['dp'=8,'tensor'=4] {'dp'}, dimensions={0} | all-to-all | bytes 6291456 | tf_op jit(solution)/shard_map/all_to_all | solution.py:111
  929.7 16.7 add_convert_fusion
  961.4 71.1 %all-to-all-done.3 = f32[8,256,768]{2,1,0:T(8,128)} async-done(((f32[8,256,768]{2,1,0:T(8,128)}), f32[8,256,768]{2,1,0:T(8,128)}, u32[]{:S(2)}, u32[]{:S(2)}) %all-to-all-start.3) | async-done | bytes 6291488 | tf_op jit(solution)/shard_map/all_to_all | solution.py:121
  1079.5 94.5 %all-gather.5.cloned.1.call-done = bf16[4096,768]{1,0:T(8,128)(2,1)} async-done(((bf16[1024,768]{1,0:T(8,128)(2,1)}), bf16[4096,768]{1,0:T(8,128)(2,1)}) %all-gather.5.cloned.1.call-update) | async-done | bytes 6291472 | tf_op jit(solution)/shard_map/all_gather | solution.py:96
  1180.1 734.9 %while.41 = (s32[]{:T(128)}, f32[4096,3,64]{0,2,1:T(8,128)}, f32[4096,3,64]{0,2,1:T(8,128)}, bf16[8,512,3,64]{1,3,2,0:T(8,128)(2,1)}, s32[8]{0:T(128)S(1)}, /*in...) while((s32[]{:T(128)}, f32[4096,3,64]{0,2,1:T(8,128)}, ...), condition=%wide.region_26.28_spmd.clone.clone, body=%wide.region_23.27_spmd.clone.clone.sunk | while | flops 4137873920 | bytes 222005600 | solution.py:277
  1212.6 18.2 multiply_reduce_fusion.9
  1230.8 21.8 multiply_convert_fusion.4
  1290.0 13.9 fusion.266
  1304.0 18.2 multiply_reduce_fusion.9
  1322.2 21.7 multiply_convert_fusion.4
  1395.9 18.2 multiply_reduce_fusion.9
  1414.1 21.7 multiply_convert_fusion.4
  1487.9 18.2 multiply_reduce_fusion.9
  1506.1 21.7 multiply_convert_fusion.4
  1579.9 18.2 multiply_reduce_fusion.9
  1598.1 21.7 multiply_convert_fusion.4
  1671.9 18.2 multiply_reduce_fusion.9
  1690.0 21.7 multiply_convert_fusion.4
  1749.9 13.9 fusion.266
  1763.8 18.2 multiply_reduce_fusion.9
  1782.0 21.7 multiply_convert_fusion.4
  1855.8 18.2 multiply_reduce_fusion.9
  1874.0 21.7 multiply_convert_fusion.4
  1967.8 212.6 %reduce-scatter.13.cloned.1.call-done = f32[1024,768]{1,0:T(8,128)} async-done(((f32[4096,768]{1,0:T(8,128)}), f32[1024,768]{1,0:T(8,128)}) %reduce-scatter.13.cloned.1.call-update) | async-done | bytes 3145744 | tf_op jit(solution)/shard_map/reduce_scatter | solution.py:99
  2185.1 42.4 %all-reduce = (f32[768]{0:T(1024)}, f32[768]{0:T(1024)}, f32[768,16]{0,1:T(8,128)}, f32[4,16]{1,0:T(4,128)}) all-reduce(f32[768]{0:T(1024)S(1)} %get-tuple-element.664, f32[768]{0:T(1024)S(1)} %copy-done.64, f32[768,16]{0,1:T(8,128)S(1)} %fusion.163, f32[4,16]{1,0:T(4,128)S(1)} %add_add_fusion.6), channel_id=1, replica_groups=mesh['dp'=8,'tensor'=4] {'dp','tensor'}, use_global_device_ids=true, to_apply=%region_31.33 | all-reduce | flops 13888 | bytes 111104 | tf_op jit(solution)/shard_map/psum | solution.py:300
  (468 shorter events, 913.6 us)
Async XLA Ops:
  7.2 744.0 %copy-start = (bf16[768,1536]{1,0:T(8,128)(2,1)S(1)}, bf16[768,1536]{1,0:T(8,128)(2,1)}, u32[]{:S(2)}) copy-start(bf16[768,1536]{1,0:T(8,128)(2,1)} %param.26) | copy-start | bytes 7077892
  7.2 125.1 %all-gather.3.cloned.1.call-start = ((), (), s32[]{:S(2)}) async-start(), calls=%async_computation.10 | async-start | bytes 7864320 | tf_op jit(solution)/shard_map/all_gather | solution.py:96
  14.1 688.7 %reduce-scatter.11.cloned.1.call-start = ((), (), s32[]{:S(2)}) async-start(), calls=%async_computation.11 | async-start | bytes 15728640 | tf_op jit(solution)/shard_map/reduce_scatter | solution.py:99
  32.5 106.0 %copy-start.23 = (bf16[768,3,192]{0,2,1:T(8,128)(2,1)}, bf16[768,3,192]{0,2,1:T(8,128)(2,1)S(1)}, u32[]{:S(2)}) copy-start(bf16[768,3,192]{0,2,1:T(8,128)(2,1)S(1)} %copy.43) | copy-start | bytes 2654212
  751.2 35.4 %copy-start.74 = (bf16[1536,768]{1,0:T(8,128)(2,1)S(1)}, bf16[1536,768]{1,0:T(8,128)(2,1)}, u32[]{:S(2)}) copy-start(bf16[1536,768]{1,0:T(8,128)(2,1)} %param.27) | copy-start | bytes 7077892
  793.5 76.7 %all-to-all-start.1 = ((f32[8,256,768]{2,1,0:T(8,128)}), f32[8,256,768]{2,1,0:T(8,128)}, u32[]{:S(2)}, u32[]{:S(2)}) async-start(f32[8,256,768]{2,1,0:T(8,128)} %bitcast.152), calls=%async_computation.2 | async-start | bytes 12582912 | tf_op jit(solution)/shard_map/all_to_all | solution.py:121
  799.2 161.7 %copy-start.70 = (f32[4]{0:T(128)}, f32[4]{0:T(128)S(1)}, u32[]{:S(2)}) copy-start(f32[4]{0:T(128)S(1)} %add_rsqrt_fusion.1) | copy-start | bytes 52
  802.0 243.9 %copy-start.21 = (f32[1024,16]{0,1:T(8,128)}, f32[1024,16]{0,1:T(8,128)S(1)}, u32[]{:S(2)}) copy-start(f32[1024,16]{0,1:T(8,128)S(1)} %get-tuple-element.735) | copy-start | bytes 196612
  802.0 243.9 %copy-start.37 = (f32[1024]{0:T(1024)}, f32[1024]{0:T(1024)S(1)}, u32[]{:S(2)}) copy-start(f32[1024]{0:T(1024)S(1)} %add_rsqrt_fusion) | copy-start | bytes 12292
  802.3 158.7 %copy-start.31 = (f32[1024,4]{0,1:T(4,128)}, f32[1024,4]{0,1:T(4,128)S(1)}, u32[]{:S(2)}) copy-start(f32[1024,4]{0,1:T(4,128)S(1)} %get-tuple-element.737) | copy-start | bytes 49156
  802.3 158.7 %copy-start.56 = (f32[1024]{0:T(1024)}, f32[1024]{0:T(1024)S(1)}, u32[]{:S(2)}) copy-start(f32[1024]{0:T(1024)S(1)} %get-tuple-element.736) | copy-start | bytes 12292
  802.3 158.6 %copy-start.58 = (f32[1024]{0:T(1024)}, f32[1024]{0:T(1024)S(1)}, u32[]{:S(2)}) copy-start(f32[1024]{0:T(1024)S(1)} %fusion.173) | copy-start | bytes 12292
  886.4 74.6 %copy-start.66 = (f32[1024]{0:T(1024)}, f32[1024]{0:T(1024)S(1)}, u32[]{:S(2)}) copy-start(f32[1024]{0:T(1024)S(1)} %fusion.137) | copy-start | bytes 12292
  889.3 40.4 %copy-start.75 = (bf16[1536,768]{1,0:T(8,128)(2,1)S(1)}, bf16[1536,768]{1,0:T(8,128)(2,1)}, u32[]{:S(2)}) copy-start(bf16[1536,768]{1,0:T(8,128)(2,1)} %param.27) | copy-start | bytes 7077892
  956.1 76.4 %all-to-all-start.3 = ((f32[8,256,768]{2,1,0:T(8,128)}), f32[8,256,768]{2,1,0:T(8,128)}, u32[]{:S(2)}, u32[]{:S(2)}) async-start(f32[8,256,768]{2,1,0:T(8,128)} %bitcast.153), calls=%async_computation.4 | async-start | bytes 12582912 | tf_op jit(solution)/shard_map/all_to_all | solution.py:121
  960.9 213.1 %all-gather.5.cloned.1.call-start = ((), (), s32[]{:S(2)}) async-start(), calls=%async_computation.12 | async-start | bytes 7864320 | tf_op jit(solution)/shard_map/all_gather | solution.py:96
  961.0 76.7 %copy-start.68 = (f32[1024]{0:T(1024)}, f32[1024]{0:T(1024)S(1)}, u32[]{:S(2)}) copy-start(f32[1024]{0:T(1024)S(1)} %neg.21) | copy-start | bytes 12292
  961.3 84.5 %copy-start.25 = (f32[1024,16]{0,1:T(8,128)}, f32[1024,16]{0,1:T(8,128)S(1)}, u32[]{:S(2)}) copy-start(f32[1024,16]{0,1:T(8,128)S(1)} %get-tuple-element.739) | copy-start | bytes 196612
  961.4 84.5 %copy-start.48 = (f32[1024]{0:T(1024)}, f32[1024]{0:T(1024)S(1)}, u32[]{:S(2)}) copy-start(f32[1024]{0:T(1024)S(1)} %multiply_multiply_fusion.7) | copy-start | bytes 12292
  1059.2 897.3 %reduce-scatter.21.cloned.1.call-start = ((), (), s32[]{:S(2)}) async-start(), calls=%async_computation.17 | async-start | bytes 2949120
  1070.0 889.0 %reduce-scatter.17.cloned.1.call-start = ((), (), s32[]{:S(2)}) async-start(), calls=%async_computation.15 | async-start | bytes 2949120 | tf_op jit(solution)/shard_map/reduce_scatter | solution.py:235
  1070.1 103.9 %copy-start.17 = (bf16[192,768]{0,1:T(8,128)(2,1)S(1)}, bf16[192,768]{0,1:T(8,128)(2,1)}, u32[]{:S(2)}) copy-start(bf16[192,768]{0,1:T(8,128)(2,1)} %all_gather.14) | copy-start | bytes 884740
  1079.4 100.7 %copy-start.46 = (s32[1,8]{1,0:T(1,128)S(1)}, s32[1,8]{1,0:T(1,128)}, u32[]{:S(2)}) copy-start(s32[1,8]{1,0:T(1,128)} %param.30) | copy-start | bytes 100
  1079.5 886.7 %reduce-scatter.19.cloned.1.call-start = ((), (), s32[]{:S(2)}) async-start(), calls=%async_computation.16 | async-start | bytes 884736
  1932.4 248.1 %reduce-scatter.13.cloned.1.call-start = ((), (), s32[]{:S(2)}) async-start(), calls=%async_computation.13 | async-start | bytes 15728640 | tf_op jit(solution)/shard_map/reduce_scatter | solution.py:99
  1942.2 291.1 %reduce-scatter.15.cloned.1.call-start = ((), (), s32[]{:S(2)}) async-start(), calls=%async_computation.14 | async-start | bytes 2654208 | tf_op jit(solution)/shard_map/reduce_scatter | solution.py:288
  1954.2 226.3 %copy-start.6 = (bf16[1024,768]{1,0:T(8,128)(2,1)S(1)}, bf16[1024,768]{1,0:T(8,128)(2,1)}, u32[]{:S(2)}) copy-start(bf16[1024,768]{1,0:T(8,128)(2,1)} %param.19) | copy-start | bytes 4718596
  1954.2 226.3 %copy-start.34 = (f32[1024]{0:T(1024)S(1)}, f32[1024]{0:T(1024)}, u32[]{:S(2)}) copy-start(f32[1024]{0:T(1024)} %copy-done.33) | copy-start | bytes 12292
  1954.2 226.3 %copy-start.44 = (f32[768]{0:T(1024)S(1)}, f32[768]{0:T(1024)}, u32[]{:S(2)}) copy-start(f32[768]{0:T(1024)} %param.20) | copy-start | bytes 9220
  1959.0 224.3 %copy-start.53 = (f32[1024]{0:T(1024)S(1)}, f32[1024]{0:T(1024)}, u32[]{:S(2)}) copy-start(f32[1024]{0:T(1024)} %copy-done.52) | copy-start | bytes 12292
  1959.0 224.3 %copy-start.42 = (f32[1024]{0:T(1024)S(1)}, f32[1024]{0:T(1024)}, u32[]{:S(2)}) copy-start(f32[1024]{0:T(1024)} %copy-done.41) | copy-start | bytes 12292
  2183.3 44.2 %copy-start.61 = (f32[1024]{0:T(1024)S(1)}, f32[1024]{0:T(1024)}, u32[]{:S(2)}) copy-start(f32[1024]{0:T(1024)} %copy-done.60) | copy-start | bytes 12292
  (69 other events, 483.1 us)
Sparse Core Ops, SparseCore 0:
  14.2 118.0 all-gather.2
  492.6 210.0 reduce-scatter.10
  1059.3 114.6 all-gather.4
  1176.1 46.2 reduce-scatter.20
  1224.6 47.5 reduce-scatter.16
  1932.5 33.6 reduce-scatter.18
  1968.6 211.8 reduce-scatter.12
  2184.4 43.9 reduce-scatter.14
where the time goes:
time: 2250 us; the launch traced here: 2240 us
  matrix products  844 us (38%)
  waiting for transfers between devices  750 us (33%)
  other arithmetic  387 us (17%)
  blocking collectives  149 us (7%)
  local copies, waits for them, and re-layouts  57.3 us (3%)
  loops' own time  27.4 us (1%)
    reduce_scatter x2, waiting for transfers between devices, own_rows(): lax.psum_scatter(term_of(jnp.int32(0), rows_here * lax.axis_size('tensor'...  421 us
    dot_general x16, matrix products, block_scores(): jnp.einsum('qhc,khc->hqk', block_queries, key_rows, preferred_element_typ...  185 us
    all_gather x2, waiting for transfers between devices, whole_tree(): return lax.all_gather(local_rows, 'tensor', axis=0, tiled=True)  185 us
    convert_element_type x8, other arithmetic, backward_block(): score_grad = (attn_probs * (prob_grad - centre)).astype(jnp.bfloat16)  174 us
    dot_general x8, matrix products, backward_block(): jnp.einsum('qhc,khc->hqk', block_grads, value_rows, preferred_element_typ...  146 us
    all_to_all x2, waiting for transfers between devices, combine(): lax.all_to_all(partial_rows.reshape(dp_size, capacity, model_width), 'dp'...  139 us
    dot_general x8, matrix products, backward_block(): jnp.einsum('hqk,qhc->khc', low_probs, block_grads, preferred_element_type...  110 us
    dot_general x8, matrix products, forward_block(): jnp.einsum('hqk,khc->qhc', attn_probs, value_rows, preferred_element_type...  101 us
  transfers between devices with their start and end apart: 10, of which 7 were waited for; matrix products, arithmetic and copies ran while one was open for 36% of the time, Pallas kernels for 0%

commit v1 on v0

v1 whole, which is shorter than its diff:
```python
import math

import jax
import jax.numpy as jnp
from jax import lax
from jax.experimental import pallas as pl
from jax.experimental.pallas import tpu as pltpu
from jax.sharding import PartitionSpec as P

HEAD_DIM = 64
TRUNK = 1024
BRANCH = 256
MASKED = -1e30
LOG2E = math.log2(math.e)
EXP_SCALE = HEAD_DIM ** (-0.5) * LOG2E

NT = (((1,), (1,)), ((), ()))
NN = (((1,), (0,)), ((), ()))


def dot_nt(a, b):
    return lax.dot_general(a, b, NT, preferred_element_type=jnp.float32)


def dot_nn(a, b):
    return lax.dot_general(a, b, NN, preferred_element_type=jnp.float32)


def head_lanes(shape, dim, head):
    return lax.broadcasted_iota(jnp.int32, shape, dim) // HEAD_DIM == head


def fwd_kernel(meta_ref, q_ref, k_ref, v_ref, o_ref, lse_ref, vt_ref):
    block = pl.program_id(1)
    place = meta_ref[0]
    parent_row = pl.multiple_of(TRUNK + meta_ref[1 + block] * BRANCH, BRANCH)
    own_row = pl.multiple_of(2 * TRUNK + block * BRANCH, BRANCH)
    width = k_ref.shape[1]

    @pl.when(block == 0)
    def _():
        flipped = v_ref[...].T
        for head in range(2):
            vt_ref[head] = jnp.where(
                head_lanes(flipped.shape, 0, head), flipped, jnp.ones_like(flipped)
            )

    queries = q_ref[...]

    def finish(outs):
        rows = []
        for head, (acc, top) in enumerate(outs):
            mine, other = head * HEAD_DIM, (1 - head) * HEAD_DIM
            total = acc[other : other + 1]
            rows.append(acc[mine : mine + HEAD_DIM] / total)
            lse_ref[0, head : head + 1, :] = top * EXP_SCALE + jnp.log2(total)
        o_ref[...] = jnp.concatenate(rows, axis=0).T.astype(o_ref.dtype)

    def probs(scores, top):
        return jnp.exp2(scores * EXP_SCALE - top * EXP_SCALE).astype(jnp.bfloat16)

    def masked_queries(head):
        return jnp.where(head_lanes(queries.shape, 1, head), queries, jnp.zeros_like(queries))

    @pl.when(place == 0)
    def _():
        outs = []
        for head in range(2):
            scores = dot_nt(k_ref[0:TRUNK], masked_queries(head))
            keys = lax.broadcasted_iota(jnp.int32, scores.shape, 0)
            rows = lax.broadcasted_iota(jnp.int32, scores.shape, 1) + block * BRANCH
            scores = jnp.where(keys <= rows, scores, MASKED)
            top = jnp.max(scores, axis=0, keepdims=True)
            outs.append((dot_nn(vt_ref[head, :, 0:TRUNK], probs(scores, top)), top))
        finish(outs)

    @pl.when(place > 0)
    def _():
        outs = []
        for head in range(2):
            qm = masked_queries(head)
            trunk = dot_nt(k_ref[0:TRUNK], qm)
            parent = dot_nt(k_ref[pl.ds(parent_row, BRANCH)], qm)
            parent = jnp.where(place > 1, parent, MASKED)
            own = dot_nt(k_ref[pl.ds(own_row, BRANCH)], qm)
            keys = lax.broadcasted_iota(jnp.int32, own.shape, 0)
            rows = lax.broadcasted_iota(jnp.int32, own.shape, 1)
            own = jnp.where(keys <= rows, own, MASKED)
            top = jnp.maximum(
                jnp.maximum(
                    jnp.max(trunk, axis=0, keepdims=True), jnp.max(parent, axis=0, keepdims=True)
                ),
                jnp.max(own, axis=0, keepdims=True),
            )
            acc = dot_nn(vt_ref[head, :, 0:TRUNK], probs(trunk, top))
            acc = acc + dot_nn(vt_ref[head, :, pl.ds(parent_row, BRANCH)], probs(parent, top))
            acc = acc + dot_nn(vt_ref[head, :, pl.ds(own_row, BRANCH)], probs(own, top))
            outs.append((acc, top))
        finish(outs)


def attend(meta, q, k, v):
    rows, width = q.shape
    keys = k.shape[0]
    pairs = width // 128
    blocks = rows // BRANCH
    return pl.pallas_call(
        fwd_kernel,
        out_shape=(
            jax.ShapeDtypeStruct((rows, width), jnp.bfloat16),
            jax.ShapeDtypeStruct((pairs, 2, rows), jnp.float32),
        ),
        grid_spec=pltpu.PrefetchScalarGridSpec(
            num_scalar_prefetch=1,
            grid=(pairs, blocks),
            in_specs=[
                pl.BlockSpec((BRANCH, 128), lambda p, i, m: (i, p)),
                pl.BlockSpec((keys, 128), lambda p, i, m: (0, p)),
                pl.BlockSpec((keys, 128), lambda p, i, m: (0, p)),
            ],
            out_specs=[
                pl.BlockSpec((BRANCH, 128), lambda p, i, m: (i, p)),
                pl.BlockSpec((1, 2, BRANCH), lambda p, i, m: (p, 0, i)),
            ],
            scratch_shapes=[pltpu.VMEM((2, 128, keys), jnp.bfloat16)],
        ),
        compiler_params=pltpu.CompilerParams(vmem_limit_bytes=40 << 20),
        name="attend_forward",
    )(meta, q, k, v)


def bwd_kernel(meta_ref, q_ref, k_ref, v_ref, o_ref, g_ref, lse_ref,
               dq_ref, dk_ref, dv_ref, kt_ref, qm_ref, gm_ref, delta_ref, dqt_ref, dkp_ref, dvp_ref):
    place = meta_ref[0]
    scale = HEAD_DIM ** (-0.5)
    rows = q_ref.shape[0]
    blocks = rows // BRANCH
    kt_ref[...] = k_ref[...].T
    queries, grads = q_ref[...], g_ref[...]
    for head in range(2):
        lanes = head_lanes(queries.shape, 1, head)
        qm_ref[head] = jnp.where(lanes, queries, jnp.zeros_like(queries))
        gm_ref[head] = jnp.where(lanes, grads, jnp.zeros_like(grads))
    product = (grads.astype(jnp.float32) * o_ref[...].astype(jnp.float32)).T
    for head in range(2):
        delta_ref[head : head + 1, :] = jnp.sum(
            product[head * HEAD_DIM : (head + 1) * HEAD_DIM], axis=0, keepdims=True
        )
    dqt_ref[...] = jnp.zeros_like(dqt_ref)

    def step(key_row, query_row, count, mask_of=None):
        kb = k_ref[pl.ds(key_row, BRANCH)]
        vb = v_ref[pl.ds(key_row, BRANCH)]
        dk = dv = None
        for head in range(2):
            at = pl.ds(query_row, count)
            qm, gm = qm_ref[head, at], gm_ref[head, at]
            scores = dot_nt(kb, qm)
            probs = jnp.exp2(scores * EXP_SCALE - lse_ref[0, head : head + 1, at])
            if mask_of is not None:
                probs = mask_of(probs)
            prob_grad = dot_nt(vb, gm)
            score_grad = (probs * (prob_grad - delta_ref[head : head + 1, at])).astype(jnp.bfloat16)
            dv_part = dot_nn(probs.astype(jnp.bfloat16), gm)
            dk_part = dot_nn(score_grad, qm)
            dv = dv_part if dv is None else dv + dv_part
            dk = dk_part if dk is None else dk + dk_part
            mine = slice(head * HEAD_DIM, (head + 1) * HEAD_DIM)
            dqt_ref[mine, at] += dot_nn(kt_ref[mine, pl.ds(key_row, BRANCH)], score_grad)
        return dk * scale, dv

    def causal(offset):
        def mask_of(probs):
            keys = lax.broadcasted_iota(jnp.int32, probs.shape, 0) + offset
            at = lax.broadcasted_iota(jnp.int32, probs.shape, 1)
            return jnp.where(keys <= at, probs, 0.0)
        return mask_of

    @pl.when(place == 0)
    def _():
        @pl.loop(0, TRUNK // BRANCH)
        def _(b):
            row = pl.multiple_of(b * BRANCH, BRANCH)
            dk, dv = step(row, 0, rows, causal(row))
            dk_ref[pl.ds(row, BRANCH)] = dk.astype(dk_ref.dtype)
            dv_ref[pl.ds(row, BRANCH)] = dv.astype(dv_ref.dtype)
        rest = (dk_ref.shape[0] - TRUNK, dk_ref.shape[1])
        dk_ref[TRUNK:] = jnp.zeros(rest, dk_ref.dtype)
        dv_ref[TRUNK:] = jnp.zeros(rest, dv_ref.dtype)

    @pl.when(place > 0)
    def _():
        @pl.loop(0, TRUNK // BRANCH)
        def _(b):
            row = pl.multiple_of(b * BRANCH, BRANCH)
            dk, dv = step(row, 0, rows)
            dk_ref[pl.ds(row, BRANCH)] = dk.astype(dk_ref.dtype)
            dv_ref[pl.ds(row, BRANCH)] = dv.astype(dv_ref.dtype)

        dkp_ref[...] = jnp.zeros_like(dkp_ref)
        dvp_ref[...] = jnp.zeros_like(dvp_ref)

        @pl.loop(0, blocks)
        def _(b):
            at = pl.multiple_of(b * BRANCH, BRANCH)
            parent = pl.multiple_of(meta_ref[1 + b] * BRANCH, BRANCH)
            dk, dv = step(TRUNK + parent, at, BRANCH, lambda probs: jnp.where(place > 1, probs, 0.0))
            dkp_ref[pl.ds(parent, BRANCH)] += dk
            dvp_ref[pl.ds(parent, BRANCH)] += dv
            own = pl.multiple_of(2 * TRUNK + at, BRANCH)
            dk, dv = step(own, at, BRANCH, causal(0))
            dk_ref[pl.ds(own, BRANCH)] = dk.astype(dk_ref.dtype)
            dv_ref[pl.ds(own, BRANCH)] = dv.astype(dv_ref.dtype)

        dk_ref[TRUNK : 2 * TRUNK] = dkp_ref[...].astype(dk_ref.dtype)
        dv_ref[TRUNK : 2 * TRUNK] = dvp_ref[...].astype(dv_ref.dtype)

    dq_ref[...] = (dqt_ref[...] * scale).T.astype(dq_ref.dtype)


def attend_back(meta, q, k, v, o, grad, lse):
    rows, width = q.shape
    keys = k.shape[0]
    pairs = width // 128
    here = pl.BlockSpec((rows, 128), lambda p, m: (0, p))
    wide = pl.BlockSpec((keys, 128), lambda p, m: (0, p))
    return pl.pallas_call(
        bwd_kernel,
        out_shape=(
            jax.ShapeDtypeStruct((rows, width), jnp.bfloat16),
            jax.ShapeDtypeStruct((keys, width), jnp.bfloat16),
            jax.ShapeDtypeStruct((keys, width), jnp.bfloat16),
        ),
        grid_spec=pltpu.PrefetchScalarGridSpec(
            num_scalar_prefetch=1,
            grid=(pairs,),
            in_specs=[here, wide, wide, here, here, pl.BlockSpec((1, 2, rows), lambda p, m: (p, 0, 0))],
            out_specs=[here, wide, wide],
            scratch_shapes=[
                pltpu.VMEM((128, keys), jnp.bfloat16),
                pltpu.VMEM((2, rows, 128), jnp.bfloat16),
                pltpu.VMEM((2, rows, 128), jnp.bfloat16),
                pltpu.VMEM((2, rows), jnp.float32),
                pltpu.VMEM((128, rows), jnp.float32),
                pltpu.VMEM((TRUNK, 128), jnp.float32),
                pltpu.VMEM((TRUNK, 128), jnp.float32),
            ],
        ),
        compiler_params=pltpu.CompilerParams(vmem_limit_bytes=48 << 20),
        name="attend_backward",
    )(meta, q, k, v, o, grad, lse)


norm_eps = 1e-05
route_scale = 3.0
masked_score = -1e30
highest = lax.Precision.HIGHEST


def layer_norm(values, norm_gain):
    centred = values - jnp.mean(values, axis=-1, keepdims=True)
    spread = jnp.mean(centred * centred, axis=-1, keepdims=True)
    return centred * lax.rsqrt(spread + norm_eps) * norm_gain


def unit_rows(values):
    return values * lax.rsqrt(jnp.sum(values * values, axis=-1, keepdims=True) + 1.0)


def router_gate(normed, router_proj, expert_embed, picked):
    routed = jnp.dot(normed, router_proj, precision=highest)
    logits = route_scale * jnp.dot(unit_rows(routed), unit_rows(expert_embed).T, precision=highest)
    return jnp.sum(jax.nn.softmax(logits, axis=-1) * picked, axis=-1)


def gelu_exact(values):
    return jax.nn.gelu(values, approximate=False)


def slot_table(route_ids, order_ids, capacity):
    same_expert = route_ids[:, None] == route_ids[None, :]
    earlier = order_ids[None, :] < order_ids[:, None]
    ranking = jnp.sum(jnp.where(same_expert & earlier, 1, 0), axis=1).astype(jnp.int32)
    kept_mask = ranking < capacity
    column = route_ids * capacity + jnp.minimum(ranking, capacity - 1)
    return (column, kept_mask)


def low_dot(rows, weight):
    return jnp.dot(rows, weight, preferred_element_type=jnp.float32).astype(jnp.bfloat16)


def shards(
    tokens,
    norm1_gain,
    qkv_weight,
    attn_proj,
    norm2_gain,
    router_proj,
    expert_embed,
    expert_in,
    expert_out,
    routes,
    orders,
    leaf_parent,
    cotangent,
):
    rows_here = tokens.shape[0]
    model_width = tokens.shape[1]
    experts = expert_embed.shape[0]
    capacity = rows_here // experts
    dp_size = lax.axis_size("dp")
    leaf_parents = leaf_parent[0]

    def whole_tree(local_rows):
        return lax.all_gather(local_rows, "tensor", axis=0, tiled=True)

    def dispatch(slot_input):
        doubled = jnp.broadcast_to(
            slot_input.reshape(experts, 1, capacity, model_width),
            (experts, 2, capacity, model_width),
        )
        arrived = lax.all_to_all(
            doubled.reshape(dp_size, capacity, model_width),
            "dp",
            split_axis=0,
            concat_axis=0,
            tiled=True,
        )
        return arrived.reshape(dp_size * capacity, model_width)

    def combine(partial_rows):
        returned = lax.all_to_all(
            partial_rows.reshape(dp_size, capacity, model_width),
            "dp",
            split_axis=0,
            concat_axis=0,
            tiled=True,
        )
        summed = jnp.sum(returned.reshape(experts, 2, capacity, model_width), axis=1)
        return summed.reshape(experts * capacity, model_width)

    hidden = tokens.astype(jnp.float32)
    normed_in, norm1_back = jax.vjp(layer_norm, hidden, norm1_gain)
    own_in = normed_in.astype(jnp.bfloat16)
    shared_in = whole_tree(own_in)[: 2 * TRUNK]
    seen_in = jnp.concatenate([shared_in, own_in], axis=0)
    qkv_cols = lax.all_gather(qkv_weight, "tensor", axis=2, tiled=True)
    qkv_full = lax.all_gather(qkv_cols, "dp", axis=0, tiled=True)
    proj_rows = lax.all_gather(attn_proj, "tensor", axis=0, tiled=True)
    proj_full = lax.all_gather(proj_rows, "dp", axis=1, tiled=True)
    query_weight, key_weight, value_weight = (qkv_full[:, part] for part in range(3))
    query_rows = low_dot(own_in, query_weight)
    key_rows = low_dot(seen_in, key_weight)
    value_rows = low_dot(seen_in, value_weight)
    place = lax.axis_index("tensor")
    leaf_blocks = rows_here // BRANCH
    first_leaf = jnp.maximum(place - 2, 0) * leaf_blocks
    parents = lax.dynamic_slice_in_dim(leaf_parents, first_leaf, leaf_blocks, 0) - 1
    meta = jnp.concatenate([place[None], parents]).astype(jnp.int32)
    attended, log_totals = attend(meta, query_rows, key_rows, value_rows)
    branch_out = jnp.dot(attended, proj_full, preferred_element_type=jnp.float32)
    mid_stream = hidden + branch_out
    normed_mid, norm2_back = jax.vjp(layer_norm, mid_stream, norm2_gain)
    moe_in = normed_mid.astype(jnp.bfloat16)
    route_ids = routes[:, 0]
    column, kept_mask = slot_table(route_ids, orders[0], capacity)
    picked = (route_ids[:, None] == jnp.arange(experts)[None, :]).astype(jnp.float32)
    gate_value, gate_back = jax.vjp(
        lambda normed_rows, route_proj, embed_rows: router_gate(
            normed_rows, route_proj, embed_rows, picked
        ),
        moe_in.astype(jnp.float32),
        router_proj,
        expert_embed,
    )
    select = (
        (column[:, None] == jnp.arange(experts * capacity)[None, :]) & kept_mask[:, None]
    ).astype(jnp.bfloat16)
    kept_float = kept_mask[:, None].astype(jnp.float32)

    def to_slots(token_rows):
        return jnp.einsum(
            "ts,td->sd", select, token_rows, preferred_element_type=jnp.float32
        ).astype(jnp.bfloat16)

    def from_slots(slot_rows):
        return jnp.take(slot_rows, column, axis=0) * kept_float

    expert_rows = dispatch(to_slots(moe_in))
    up_values = jnp.dot(expert_rows, expert_in, preferred_element_type=jnp.float32)
    active_full, gelu_back = jax.vjp(gelu_exact, up_values)
    active = active_full.astype(jnp.bfloat16)
    expert_result = from_slots(
        combine(jnp.dot(active, expert_out, preferred_element_type=jnp.float32))
    )
    output = (mid_stream + gate_value[:, None] * expert_result).astype(jnp.bfloat16)
    upstream = cotangent.astype(jnp.float32)
    arrived_grad = dispatch(to_slots((gate_value[:, None] * upstream).astype(jnp.bfloat16)))
    out_weight_grad = jnp.einsum(
        "rf,rd->fd", active, arrived_grad, preferred_element_type=jnp.float32
    )
    active_grad = jnp.einsum(
        "rd,fd->rf", arrived_grad, expert_out, preferred_element_type=jnp.float32
    )
    up_grad = gelu_back(active_grad)[0].astype(jnp.bfloat16)
    in_weight_grad = jnp.einsum(
        "rd,rf->df", expert_rows, up_grad, preferred_element_type=jnp.float32
    )
    moe_grad = from_slots(
        combine(jnp.einsum("rf,df->rd", up_grad, expert_in, preferred_element_type=jnp.float32))
    )
    gate_grad = jnp.sum(upstream * expert_result, axis=-1)
    router_part, proj_grad, embed_grad = gate_back(gate_grad)
    mid_part, gain2_grad = norm2_back(moe_grad + router_part)
    mid_grad = upstream + mid_part
    expert_in_grad, expert_out_grad = (
        lax.psum_scatter(
            in_weight_grad.astype(jnp.bfloat16), "tensor", scatter_dimension=1, tiled=True
        ).astype(jnp.float32),
        lax.psum_scatter(
            out_weight_grad.astype(jnp.bfloat16), "tensor", scatter_dimension=0, tiled=True
        ).astype(jnp.float32),
    )
    branch_grad = mid_grad.astype(jnp.bfloat16)
    proj_grad_full = jnp.einsum(
        "sc,sd->cd", attended, branch_grad, preferred_element_type=jnp.float32
    )
    attn_proj_grad = lax.psum_scatter(
        lax.psum_scatter(proj_grad_full, "dp", scatter_dimension=1, tiled=True),
        "tensor",
        scatter_dimension=0,
        tiled=True,
    )
    attended_grad = jnp.einsum(
        "sd,cd->sc", branch_grad, proj_full, preferred_element_type=jnp.float32
    ).astype(jnp.bfloat16)
    query_grad, key_grad, value_grad = attend_back(
        meta, query_rows, key_rows, value_rows, attended, attended_grad, log_totals
    )

    def weight_grad(rows, row_grads):
        return jnp.einsum("sd,sc->dc", rows, row_grads, preferred_element_type=jnp.float32)

    def row_grad(row_grads, weight):
        return jnp.einsum("sc,dc->sd", row_grads, weight, preferred_element_type=jnp.float32)

    qkv_grad_full = jnp.stack(
        [
            weight_grad(own_in, query_grad),
            weight_grad(seen_in, key_grad),
            weight_grad(seen_in, value_grad),
        ],
        axis=1,
    )
    qkv_grad = lax.psum_scatter(
        lax.psum_scatter(qkv_grad_full, "dp", scatter_dimension=0, tiled=True),
        "tensor",
        scatter_dimension=2,
        tiled=True,
    )
    seen_grad = row_grad(key_grad, key_weight) + row_grad(value_grad, value_weight)
    own_grad = seen_grad[2 * TRUNK :] + row_grad(query_grad, query_weight)
    shared_grad = jnp.concatenate(
        [seen_grad[: 2 * TRUNK], jnp.zeros_like(seen_grad[: 2 * TRUNK])], axis=0
    ).astype(jnp.bfloat16)
    input_grad = own_grad + lax.psum_scatter(
        shared_grad, "tensor", scatter_dimension=0, tiled=True
    ).astype(jnp.float32)
    token_part, gain1_grad = norm1_back(input_grad)
    token_grad = mid_grad + token_part
    gain1_sum, gain2_sum, router_sum, embed_sum = lax.psum(
        (gain1_grad, gain2_grad, proj_grad, embed_grad), ("dp", "tensor")
    )
    return (
        output,
        token_grad,
        gain1_sum,
        qkv_grad,
        attn_proj_grad,
        gain2_sum,
        router_sum,
        embed_sum,
        expert_in_grad,
        expert_out_grad,
    )


def solution(mesh):
    in_specs = (
        P(("dp", "tensor"), None),
        P(),
        P("dp", None, "tensor"),
        P("tensor", "dp"),
        P(),
        P(),
        P(),
        P(None, "dp"),
        P("dp", None),
        P(("dp", "tensor"), None),
        P(("dp", "tensor"), None),
        P("dp", None),
        P(("dp", "tensor"), None),
    )
    out_specs = (
        P(("dp", "tensor"), None),
        P(("dp", "tensor"), None),
        P(),
        P("dp", None, "tensor"),
        P("tensor", "dp"),
        P(),
        P(),
        P(),
        P(None, ("dp", "tensor")),
        P(("dp", "tensor"), None),
    )
    return jax.shard_map(shards, mesh=mesh, in_specs=in_specs, out_specs=out_specs, check_vma=False)
```

time: 2250 us -> 1120 us (0.50)
  matrix products: 844 us -> 158 us
  other arithmetic: 387 us -> 36.8 us
  waiting for transfers between devices: 750 us -> 570 us
  Pallas kernels: 0 us -> 96 us
  loops' own time: 27.4 us -> 0 us
    dot_general x59 -> x11, matrix products: 721 us -> 51.6 us  [the longest x3 17.6 us: row_grad(): jnp.einsum('sc,dc->sd', row_grads, weight, preferred_element_type=jnp.flo...]
    reduce_scatter x2, waiting for transfers between devices: 421 us -> 150 us  [the longest x1 110 us: shards(): lax.psum_scatter(shared_grad, 'tensor', scatter_dimension=0, tiled=True)]
    convert_element_type x11 -> x2, other arithmetic: 178 us -> 2.2 us  [the longest x1 1.62 us: shards(): own_in = normed_in.astype(jnp.bfloat16)]
    reduce_sum x24 -> x0, other arithmetic: 96.9 us -> none  [the longest x8 95.5 us: forward_block(): row_total = jnp.sum(weights, axis=-1, keepdims=True)]
    pallas_call x0 -> x2, Pallas kernels: none -> 96 us  [the longest x1 51.8 us: attend_back(): pl.pallas_call(bwd_kernel, out_shape=(jax.ShapeDtypeStruct((rows, width),...]
    all_gather x2 -> x1, waiting for transfers between devices: 185 us -> 113 us  [whole_tree(): return lax.all_gather(local_rows, 'tensor', axis=0, tiled=True)]
    reduce_scatter x1, waiting for transfers between devices: 0.01 us -> 63 us  [shards(): lax.psum_scatter(qkv_grad_full, 'dp', scatter_dimension=0, tiled=True)]
    and x16 -> x0, other arithmetic: 60.8 us -> none  [visible(): return related & (key_pos[None, :] <= query_pos[:, None])]
  transfers between devices with their start and end apart: 10 -> 12, of which waited for: 7 -> 10; matrix products, arithmetic and copies ran while one was open for 36% -> 10% of each run, Pallas kernels for 0% -> 4%
where the time goes in v1:
time: 1120 us
  waiting for transfers between devices  570 us (51%)
  blocking collectives  159 us (14%)
  matrix products  158 us (14%)
  Pallas kernels  96 us (9%)
  local copies, waits for them, and re-layouts  71.7 us (6%)
  other arithmetic  36.8 us (3%)
  between operations  15.3 us (1%)
    all_to_all x2, waiting for transfers between devices, combine(): lax.all_to_all(partial_rows.reshape(dp_size, capacity, model_width), 'dp'...  138 us
    all_gather x1, waiting for transfers between devices, whole_tree(): return lax.all_gather(local_rows, 'tensor', axis=0, tiled=True)  113 us
    reduce_scatter x1, waiting for transfers between devices, shards(): lax.psum_scatter(shared_grad, 'tensor', scatter_dimension=0, tiled=True)  110 us
    all_to_all x2, blocking collectives, dispatch(): lax.all_to_all(doubled.reshape(dp_size, capacity, model_width), 'dp', spl...  81.7 us
    reduce_scatter x1, waiting for transfers between devices, shards(): lax.psum_scatter(qkv_grad_full, 'dp', scatter_dimension=0, tiled=True)  63 us
    pallas_call x1, Pallas kernels, attend_back(): pl.pallas_call(bwd_kernel, out_shape=(jax.ShapeDtypeStruct((rows, width),...  51.8 us
    unnamed x13, waiting for transfers between devices  51.7 us
    reduce_scatter x1, waiting for transfers between devices, shards(): lax.psum_scatter(out_weight_grad.astype(jnp.bfloat16), 'tensor', scatter_...  47.4 us
  transfers between devices with their start and end apart: 12, of which 10 were waited for; matrix products, arithmetic and copies ran while one was open for 10% of the time, Pallas kernels for 4%

profile of v1, /device:TPU:0, one launch (start us, length us, event | category | flops | bytes accessed | tf_op | source)
XLA Modules:
  0.0 1117.6 jit_solution(8716283660565871271)
XLA Ops:
  8.5 21.3 %all_gather.15 = bf16[96,3,768]{0,1,2:T(4,128)(2,1)S(1)} all-gather(bf16[96,3,192]{0,1,2:T(4,128)(2,1)S(1)} %copy.60), channel_id=1, replica_groups=mesh['dp'=8,'tensor'=4] {'tensor'}, dimensions={2}, use_global_device_ids=true | all-gather | bytes 552960 | tf_op jit(solution)/shard_map/all_gather | solution.py:348
  39.7 14.5 %all_gather.18 = bf16[768,96]{1,0:T(8,128)(2,1)S(1)} all-gather(bf16[192,96]{1,0:T(8,128)(2,1)S(1)} %copy-done.39), channel_id=1, replica_groups=mesh['dp'=8,'tensor'=4] {'tensor'}, dimensions={0}, use_global_device_ids=true | all-gather | bytes 184320 | tf_op jit(solution)/shard_map/all_gather | solution.py:350
  57.4 7.0 all-gather.4.cloned.1.call-done
  68.7 113.2 %all-gather.6.cloned.1.call-done = bf16[4096,768]{0,1:T(8,128)(2,1)} async-done(((bf16[1024,768]{0,1:T(8,128)(2,1)}), bf16[4096,768]{0,1:T(8,128)(2,1)}) %all-gather.6.cloned.1.call-update) | async-done | bytes 6291472 | tf_op jit(solution)/shard_map/all_gather | solution.py:316
  194.9 44.2 %attend_forward.1 = (bf16[1024,768]{1,0:T(8,128)(2,1)S(1)}, f32[6,2,1024]{2,1,0:T(2,128)S(1)}) custom-call(s32[5]{0:T(128)S(1)} %pad_add_fusion.meta_ref, bf16[1024,768]{1,0:T(8,128)(2,1)S(1)} %copy-done.3, bf16[3072,768]{1,0:T(8,128)(2,1)S(1)} %convolution_convert_fusion.1.k_ref, bf16[3072,768]{1,0:T(8,128)(2,1)S(1)} %convolution_convert_fusion.v_ref), custom_call_target="tpu_custom_call" | custom-call | tf_op jit(solution)/shard_map/attend_forward/pallas_call | solution.py:107
  250.4 41.3 %all_to_all.20 = bf16[8,256,768]{2,1,0:T(8,128)(2,1)S(1)} all-to-all(bf16[8,256,768]{2,1,0:T(8,128)(2,1)S(1)} %bitcast.80), channel_id=1, replica_groups=mesh['dp'=8,'tensor'=4] {'dp'}, dimensions={0} | all-to-all | bytes 6291456 | tf_op jit(solution)/shard_map/all_to_all | solution.py:323
  291.7 35.4 %multiply_convert_fusion = (bf16[2048,1536]{1,0:T(8,128)(2,1)S(1)}, f32[2048,1536]{1,0:T(8,128)}, f32[2048,1536]{1,0:T(8,128)}) fusion(bf16[2048,768]{1,0:T(8,128)(2,1)S(1)} %bitcast.86, bf16[768,1536]{1,0:T(8,128)(2,1)S(1)} %copy-done), kind=kOutput, calls=%fused_computation.5 | convolution fusion | flops 5036310528 | bytes 36962304 | tf_op jit(solution)/shard_map/dot_general | solution.py:391
  327.1 6.9 fusion.68
  344.2 66.4 %all-to-all-done.1 = f32[8,256,768]{2,1,0:T(8,128)} async-done(((f32[8,256,768]{2,1,0:T(8,128)}), f32[8,256,768]{2,1,0:T(8,128)}, u32[]{:S(2)}, u32[]{:S(2)}) %all-to-all-start.1) | async-done | bytes 6291488 | tf_op jit(solution)/shard_map/all_to_all | solution.py:333
  410.5 5.2 bitcast_reduce_fusion.1
  415.7 7.8 gather_fusion
  432.8 40.4 %all_to_all.21 = bf16[8,256,768]{2,1,0:T(8,128)(2,1)S(1)} all-to-all(bf16[8,256,768]{2,1,0:T(8,128)(2,1)S(1)} %bitcast.81), channel_id=1, replica_groups=mesh['dp'=8,'tensor'=4] {'dp'}, dimensions={0} | all-to-all | bytes 6291456 | tf_op jit(solution)/shard_map/all_to_all | solution.py:323
  473.2 16.7 %add_convert_fusion = bf16[2048,1536]{1,0:T(8,128)(2,1)} fusion(f32[2048,1536]{1,0:T(8,128)} %get-tuple-element.86, f32[2048,1536]{1,0:T(8,128)} %get-tuple-element.93, bf16[2048,768]{1,0:T(8,128)(2,1)S(1)} %bitcast.88, bf16[1536,768]{1,0:T(8,128)(2,1)S(1)} %copy-done.57), kind=kOutput, calls=%fused_computation.4 | convolution fusion | flops 4875878400 | bytes 36962304 | tf_op jit(solution)/shard_map/rd,fd->rf/dot_general | solution.py:403
  490.0 9.7 fusion.69
  504.8 71.2 %all-to-all-done.3 = f32[8,256,768]{2,1,0:T(8,128)} async-done(((f32[8,256,768]{2,1,0:T(8,128)}), f32[8,256,768]{2,1,0:T(8,128)}, u32[]{:S(2)}, u32[]{:S(2)}) %all-to-all-start.3) | async-done | bytes 6291488 | tf_op jit(solution)/shard_map/all_to_all | solution.py:333
  576.0 5.2 bitcast_reduce_fusion
  581.2 8.1 gather_fusion.1
  593.0 6.0 multiply_reduce_fusion
  606.8 51.8 %attend_backward.1 = (bf16[1024,768]{1,0:T(8,128)(2,1)S(1)}, bf16[3072,768]{1,0:T(8,128)(2,1)}, bf16[3072,768]{1,0:T(8,128)(2,1)}) custom-call(s32[5]{0:T(128)S(1)} %pad_add_fusion.meta_ref, bf16[1024,768]{1,0:T(8,128)(2,1)S(1)} %copy-done.4, bf16[3072,768]{1,0:T(8,128)(2,1)} %copy-done.2, bf16[3072,768]{1,0:T(8,128)(2,1)} %copy-done.1, ...), custom_call_target="tpu_custom_call" | custom-call | tf_op jit(solution)/shard_map/attend_backward/pallas_call | solution.py:227
  658.7 6.7 convolution_bitcast_fusion
  674.1 9.3 convolution_convert_fusion.3
  687.8 9.5 convolution_convert_fusion.2
  702.1 63.0 %reduce-scatter.16.cloned.1.call-done = f32[96,3,768]{2,0,1:T(8,128)} async-done(((f32[768,3,768]{2,0,1:T(8,128)}), f32[96,3,768]{2,0,1:T(8,128)}) %reduce-scatter.16.cloned.1.call-update) | async-done | bytes 884752 | tf_op jit(solution)/shard_map/reduce_scatter | solution.py:457
  770.5 6.1 fusion.39
  776.6 6.1 convolution_add_fusion
  793.4 22.0 %reduce-scatter.26.cloned.1.call-done = bf16[384,768]{1,0:T(8,128)(2,1)} async-done(((bf16[1536,768]{1,0:T(8,128)(2,1)}), bf16[384,768]{1,0:T(8,128)(2,1)}) %reduce-scatter.26.cloned.1.call-update) | async-done | bytes 589840
  817.8 47.4 %reduce-scatter.20.cloned.1.call-done = bf16[384,768]{1,0:T(8,128)(2,1)} async-done(((bf16[1536,768]{1,0:T(8,128)(2,1)}), bf16[384,768]{1,0:T(8,128)(2,1)}) %reduce-scatter.20.cloned.1.call-update) | async-done | bytes 589840 | tf_op jit(solution)/shard_map/reduce_scatter | solution.py:421
  870.1 40.7 %reduce-scatter.18.cloned.1.call-done = f32[768,96]{0,1:T(8,128)} async-done(((f32[768,768]{0,1:T(8,128)}), f32[768,96]{0,1:T(8,128)}) %reduce-scatter.18.cloned.1.call-update) | async-done | bytes 294928 | tf_op jit(solution)/shard_map/reduce_scatter | solution.py:430
  912.8 29.6 %reduce-scatter.22.cloned.1.call-done = f32[192,288]{1,0:T(8,128)} async-done(((f32[768,288]{1,0:T(8,128)}), f32[192,288]{1,0:T(8,128)}) %reduce-scatter.22.cloned.1.call-update) | async-done | bytes 221200
  944.5 109.7 %reduce-scatter.14.cloned.1.call-done = bf16[1024,768]{0,1:T(8,128)(2,1)} async-done(((bf16[4096,768]{0,1:T(8,128)(2,1)}), bf16[1024,768]{0,1:T(8,128)(2,1)}) %reduce-scatter.14.cloned.1.call-update) | async-done | bytes 1572880 | tf_op jit(solution)/shard_map/reduce_scatter | solution.py:467
  1054.2 5.5 fusion.17
  1068.7 41.8 %all-reduce.1 = (f32[768]{0:T(1024)}, f32[768]{0:T(1024)}, f32[768,16]{0,1:T(8,128)}, f32[4,16]{1,0:T(4,128)}) all-reduce(f32[768]{0:T(1024)S(1)} %get-tuple-element.73, f32[768]{0:T(1024)S(1)} %get-tuple-element.71, f32[768,16]{0,1:T(8,128)S(1)} %fusion.52, ...), channel_id=1, replica_groups=mesh['dp'=8,'tensor'=4] {'dp','tensor'}, use_global_device_ids=true, to_apply=%region_21.23 | all-reduce | flops 13888 | bytes 111104 | tf_op jit(solution)/shard_map/psum | solution.py:472
  (219 shorter events, 132.8 us)
Async XLA Ops:
  7.2 284.5 %copy-start = (bf16[768,1536]{1,0:T(8,128)(2,1)S(1)}, bf16[768,1536]{1,0:T(8,128)(2,1)}, u32[]{:S(2)}) copy-start(bf16[768,1536]{1,0:T(8,128)(2,1)} %param.22) | copy-start | bytes 7077892
  7.2 57.2 %all-gather.4.cloned.1.call-start = ((), (), s32[]{:S(2)}) async-start(), calls=%async_computation.11 | async-start | bytes 3981312 | tf_op jit(solution)/shard_map/all_gather | solution.py:349
  30.9 7.1 copy-start.42
  31.0 151.0 %all-gather.6.cloned.1.call-start = ((), (), s32[]{:S(2)}) async-start(), calls=%async_computation.12 | async-start | bytes 7864320 | tf_op jit(solution)/shard_map/all_gather | solution.py:316
  35.4 19.6 %copy-start.28 = (s32[1024,1]{0,1:T(1,128)S(1)}, s32[1024,1]{0,1:T(1,128)}, u32[]{:S(2)}) copy-start(s32[1024,1]{0,1:T(1,128)} %param.24) | copy-start | bytes 12292
  35.5 19.6 %copy-start.50 = (s32[1,1024]{1,0:T(1,128)S(1)}, s32[1,1024]{1,0:T(1,128)}, u32[]{:S(2)}) copy-start(s32[1,1024]{1,0:T(1,128)} %param.25) | copy-start | bytes 12292
  37.4 19.9 %copy-start.59 = (s32[1,8]{1,0:T(1,128)S(1)}, s32[1,8]{1,0:T(1,128)}, u32[]{:S(2)}) copy-start(s32[1,8]{1,0:T(1,128)} %param.26) | copy-start | bytes 100
  39.7 202.9 %all-gather.8.cloned.1.call-start = ((), (), s32[]{:S(2)}) async-start(), calls=%async_computation.13 | async-start | bytes 1327104 | tf_op jit(solution)/shard_map/all_gather | solution.py:351
  291.7 35.4 %copy-start.23 = (bf16[8,256,768]{2,1,0:T(8,128)(2,1)}, bf16[8,256,768]{2,1,0:T(8,128)(2,1)S(1)}, u32[]{:S(2)}) copy-start(bf16[8,256,768]{2,1,0:T(8,128)(2,1)S(1)} %all_to_all.20) | copy-start | bytes 9437188
  291.7 35.4 %copy-start.56 = (bf16[1536,768]{1,0:T(8,128)(2,1)S(1)}, bf16[1536,768]{1,0:T(8,128)(2,1)}, u32[]{:S(2)}) copy-start(bf16[1536,768]{1,0:T(8,128)(2,1)} %param.23) | copy-start | bytes 7077892
  327.1 6.9 copy-start.60
  334.0 76.6 %all-to-all-start.1 = ((f32[8,256,768]{2,1,0:T(8,128)}), f32[8,256,768]{2,1,0:T(8,128)}, u32[]{:S(2)}, u32[]{:S(2)}) async-start(f32[8,256,768]{2,1,0:T(8,128)} %bitcast.83), calls=%async_computation.1 | async-start | bytes 12582912 | tf_op jit(solution)/shard_map/all_to_all | solution.py:333
  341.7 74.1 %copy-start.52 = (f32[4]{0:T(128)}, f32[4]{0:T(128)S(1)}, u32[]{:S(2)}) copy-start(f32[4]{0:T(128)S(1)} %multiply_reduce_fusion.6) | copy-start | bytes 52
  344.2 71.6 %copy-start.48 = (s32[1024]{0:T(1024)S(1)}, s32[1024]{0:T(1024)}, u32[]{:S(2)}) copy-start(s32[1024]{0:T(1024)} %get-tuple-element.89) | copy-start | bytes 12292
  432.8 40.4 %copy-start.57 = (bf16[1536,768]{1,0:T(8,128)(2,1)S(1)}, bf16[1536,768]{1,0:T(8,128)(2,1)}, u32[]{:S(2)}) copy-start(bf16[1536,768]{1,0:T(8,128)(2,1)} %param.23) | copy-start | bytes 7077892
  473.2 16.7 %copy-start.24 = (bf16[8,256,768]{2,1,0:T(8,128)(2,1)}, bf16[8,256,768]{2,1,0:T(8,128)(2,1)S(1)}, u32[]{:S(2)}) copy-start(bf16[8,256,768]{2,1,0:T(8,128)(2,1)S(1)} %all_to_all.21) | copy-start | bytes 9437188
  499.7 76.4 %all-to-all-start.3 = ((f32[8,256,768]{2,1,0:T(8,128)}), f32[8,256,768]{2,1,0:T(8,128)}, u32[]{:S(2)}, u32[]{:S(2)}) async-start(f32[8,256,768]{2,1,0:T(8,128)} %bitcast.84), calls=%async_computation.3 | async-start | bytes 12582912 | tf_op jit(solution)/shard_map/all_to_all | solution.py:333
  504.4 260.6 %reduce-scatter.16.cloned.1.call-start = ((), (), s32[]{:S(2)}) async-start(), calls=%async_computation.15 | async-start | bytes 7962624 | tf_op jit(solution)/shard_map/reduce_scatter | solution.py:457
  606.8 51.8 %copy-start.20 = (bf16[1024,768]{0,1:T(8,128)(2,1)S(1)}, bf16[1024,768]{0,1:T(8,128)(2,1)}, u32[]{:S(2)}) copy-start(bf16[1024,768]{0,1:T(8,128)(2,1)} %fusion.14) | copy-start | bytes 4718596
  606.8 51.8 %copy-start.22 = (bf16[2048,768]{0,1:T(8,128)(2,1)S(1)}, bf16[2048,768]{0,1:T(8,128)(2,1)}, u32[]{:S(2)}) copy-start(bf16[2048,768]{0,1:T(8,128)(2,1)} %copy-done.21) | copy-start | bytes 9437188
  658.6 10.6 copy-start.7
  658.7 6.8 copy-start.54
  674.0 141.3 %reduce-scatter.26.cloned.1.call-start = ((), (), s32[]{:S(2)}) async-start(), calls=%async_computation.20 | async-start | bytes 2949120
  687.7 177.4 %reduce-scatter.20.cloned.1.call-start = ((), (), s32[]{:S(2)}) async-start(), calls=%async_computation.17 | async-start | bytes 2949120 | tf_op jit(solution)/shard_map/reduce_scatter | solution.py:421
  697.3 213.6 %reduce-scatter.18.cloned.1.call-start = ((), (), s32[]{:S(2)}) async-start(), calls=%async_computation.16 | async-start | bytes 2654208 | tf_op jit(solution)/shard_map/reduce_scatter | solution.py:430
  702.0 240.4 %reduce-scatter.22.cloned.1.call-start = ((), (), s32[]{:S(2)}) async-start(), calls=%async_computation.18 | async-start | bytes 1474560
  770.5 283.7 %reduce-scatter.14.cloned.1.call-start = ((), (), s32[]{:S(2)}) async-start(), calls=%async_computation.14 | async-start | bytes 7864320 | tf_op jit(solution)/shard_map/reduce_scatter | solution.py:467
  789.9 320.6 %reduce-scatter.24.cloned.1.call-start = ((), (), s32[]{:S(2)}) async-start(), calls=%async_computation.19 | async-start | bytes 491520
  867.3 186.9 %copy-start.33 = (f32[1024]{0:T(1024)S(1)}, f32[1024]{0:T(1024)}, u32[]{:S(2)}) copy-start(f32[1024]{0:T(1024)} %copy-done.32) | copy-start | bytes 12292
  867.3 186.9 %copy-start.43 = (f32[768]{0:T(1024)S(1)}, f32[768]{0:T(1024)}, u32[]{:S(2)}) copy-start(f32[768]{0:T(1024)} %param.16) | copy-start | bytes 9220
  944.5 115.2 %copy-start.45 = (f32[1024]{0:T(1024)S(1)}, f32[1024]{0:T(1024)}, u32[]{:S(2)}) copy-start(f32[1024]{0:T(1024)} %copy-done.44) | copy-start | bytes 12292
  944.5 115.2 %copy-start.38 = (f32[1024]{0:T(1024)S(1)}, f32[1024]{0:T(1024)}, u32[]{:S(2)}) copy-start(f32[1024]{0:T(1024)} %copy-done.37) | copy-start | bytes 12292
  (41 other events, 123.6 us)
Sparse Core Ops, SparseCore 0:
  31.1 33.3 all-gather.3
  66.6 115.3 all-gather.5
  184.4 22.2 all-gather.7
  674.2 90.8 reduce-scatter.15
  767.3 48.0 reduce-scatter.25
  817.6 47.5 reduce-scatter.19
  868.9 41.9 reduce-scatter.17
  913.2 29.1 reduce-scatter.21
  944.7 109.4 reduce-scatter.13
  1056.9 21.1 reduce-scatter.23

commit v2 on v1

--- a/solution.py
+++ b/solution.py
@@ -251,6 +251,212 @@
     )(meta, q, k, v, o, grad, lse)
 
 
+ROWS = 256
+HALF_ROOT = math.sqrt(0.5)
+PDF_SCALE = 1.0 / math.sqrt(2.0 * math.pi)
+CHUNK = 512
+
+
+def expert_fwd_kernel(x_ref, in_ref, out_ref, active_ref, slope_ref, keep_ref, send_ref):
+    step = pl.program_id(0)
+    half = pl.num_programs(0) // 2
+    rows = x_ref[...]
+    total = None
+    for first in range(0, in_ref.shape[1], CHUNK):
+        cols = slice(first, first + CHUNK)
+        up = dot_nn(rows, in_ref[:, cols])
+        below = 0.5 * (1.0 + lax.erf(up * HALF_ROOT))
+        active = (up * below).astype(jnp.bfloat16)
+        slope = below + up * (jnp.exp(-0.5 * up * up) * PDF_SCALE)
+        active_ref[:, cols] = active
+        slope_ref[:, cols] = slope.astype(jnp.bfloat16)
+        part = dot_nn(active, out_ref[cols])
+        total = part if total is None else total + part
+
+    @pl.when(step < half)
+    def _():
+        keep_ref[...] = total
+
+    @pl.when(step >= half)
+    def _():
+        send_ref[...] = total.astype(send_ref.dtype)
+
+
+def expert_bwd_kernel(grad_ref, slope_ref, in_ref, out_ref, upgrad_ref, keep_ref, send_ref):
+    step = pl.program_id(0)
+    half = pl.num_programs(0) // 2
+    grads = grad_ref[...]
+    total = None
+    for first in range(0, in_ref.shape[1], CHUNK):
+        cols = slice(first, first + CHUNK)
+        active_grad = dot_nt(grads, out_ref[cols])
+        up_grad = (active_grad * slope_ref[:, cols].astype(jnp.float32)).astype(jnp.bfloat16)
+        upgrad_ref[:, cols] = up_grad
+        part = dot_nt(up_grad, in_ref[:, cols])
+        total = part if total is None else total + part
+
+    @pl.when(step < half)
+    def _():
+        keep_ref[...] = total
+
+    @pl.when(step >= half)
+    def _():
+        send_ref[...] = total.astype(send_ref.dtype)
+
+
+def split_specs(count, width):
+    half = count // 2
+    return [
+        pl.BlockSpec((ROWS, width), lambda i: (jnp.minimum(i, half - 1), 0)),
+        pl.BlockSpec((ROWS, width), lambda i: (jnp.maximum(i - half, 0), 0)),
+    ]
+
+
+def expert_forward(x, w_in, w_out):
+    rows, width = x.shape
+    hidden = w_in.shape[1]
+    count = rows // ROWS
+    def wide(cols):
+        return pl.BlockSpec((ROWS, cols), lambda i: (i, 0))
+    def whole(shape):
+        return pl.BlockSpec(shape, lambda i: (0, 0), pipeline_mode=pl.Buffered(1))
+    return pl.pallas_call(
+        expert_fwd_kernel,
+        grid=(count,),
+        in_specs=[wide(width), whole(w_in.shape), whole(w_out.shape)],
+        out_specs=[wide(hidden), wide(hidden)] + split_specs(count, width),
+        out_shape=(
+            jax.ShapeDtypeStruct((rows, hidden), jnp.bfloat16),
+            jax.ShapeDtypeStruct((rows, hidden), jnp.bfloat16),
+            jax.ShapeDtypeStruct((rows // 2, width), jnp.float32),
+            jax.ShapeDtypeStruct((rows // 2, width), jnp.bfloat16),
+        ),
+        cost_estimate=pl.CostEstimate(flops=4 * rows * width * hidden, bytes_accessed=24 << 20, transcendentals=2 * rows * hidden),
+        compiler_params=pltpu.CompilerParams(vmem_limit_bytes=40 << 20),
+        name="expert_forward",
+    )(x, w_in, w_out)
+
+
+def expert_back(grads, slope, w_in, w_out):
+    rows, width = grads.shape
+    hidden = w_in.shape[1]
+    count = rows // ROWS
+    def wide(cols):
+        return pl.BlockSpec((ROWS, cols), lambda i: (i, 0))
+    def whole(shape):
+        return pl.BlockSpec(shape, lambda i: (0, 0), pipeline_mode=pl.Buffered(1))
+    return pl.pallas_call(
+        expert_bwd_kernel,
+        grid=(count,),
+        in_specs=[wide(width), wide(hidden), whole(w_in.shape), whole(w_out.shape)],
+        out_specs=[wide(hidden)] + split_specs(count, width),
+        out_shape=(
+            jax.ShapeDtypeStruct((rows, hidden), jnp.bfloat16),
+            jax.ShapeDtypeStruct((rows // 2, width), jnp.float32),
+            jax.ShapeDtypeStruct((rows // 2, width), jnp.bfloat16),
+        ),
+        cost_estimate=pl.CostEstimate(flops=4 * rows * width * hidden, bytes_accessed=24 << 20, transcendentals=0),
+        compiler_params=pltpu.CompilerParams(vmem_limit_bytes=40 << 20),
+        name="expert_backward",
+    )(grads, slope, w_in, w_out)
+
+
+MESH = pl.DeviceIdType.MESH
+
+
+def total_kernel(ways, tensor, part_ref, out_ref, land_ref, send1, recv1, send2, recv2):
+    me = lax.axis_index("dp") * tensor + lax.axis_index("tensor")
+
+    def other(step):
+        peer = lax.rem(me + step, ways)
+        return peer, (peer // tensor, lax.rem(peer, tensor))
+
+    barrier = pltpu.get_barrier_semaphore()
+
+    @pl.loop(1, ways)
+    def _(step):
+        pl.semaphore_signal(barrier, inc=1, device_id=other(step)[1], device_id_type=MESH)
+
+    pl.semaphore_wait(barrier, ways - 1)
+
+    def scatter(step):
+        peer, where = other(step)
+        return pltpu.make_async_remote_copy(
+            src_ref=part_ref.at[peer], dst_ref=land_ref.at[me],
+            send_sem=send1.at[step], recv_sem=recv1.at[me],
+            device_id=where, device_id_type=MESH,
+        )
+
+    def arrival(step):
+        source = lax.rem(me - step + ways, ways)
+        return pltpu.make_async_remote_copy(
+            src_ref=part_ref.at[source], dst_ref=land_ref.at[source],
+            send_sem=send1.at[step], recv_sem=recv1.at[source],
+            device_id=other(step)[1], device_id_type=MESH,
+        )
+
+    def spread(step):
+        return pltpu.make_async_remote_copy(
+            src_ref=out_ref.at[me], dst_ref=out_ref.at[me],
+            send_sem=send2.at[step], recv_sem=recv2.at[me],
+            device_id=other(step)[1], device_id_type=MESH,
+        )
+
+    def landing(step):
+        source = lax.rem(me - step + ways, ways)
+        return pltpu.make_async_remote_copy(
+            src_ref=out_ref.at[source], dst_ref=out_ref.at[source],
+            send_sem=send2.at[step], recv_sem=recv2.at[source],
+            device_id=other(step)[1], device_id_type=MESH,
+        )
+
+    @pl.loop(1, ways)
+    def _(step):
+        scatter(step).start()
+
+    def add(step, total):
+        arrival(step).wait_recv()
+        return total + land_ref[lax.rem(me - step + ways, ways)]
+
+    out_ref[me] = lax.fori_loop(1, ways, add, part_ref[me])
+
+    @pl.loop(1, ways)
+    def _(step):
+        spread(step).start()
+
+    @pl.loop(1, ways)
+    def _(step):
+        landing(step).wait_recv()
+
+    @pl.loop(1, ways)
+    def _(step):
+        scatter(step).wait_send()
+        spread(step).wait_send()
+
+
+def total_over_devices(parts):
+    tensor = lax.axis_size("tensor")
+    ways = lax.axis_size("dp") * tensor
+    flat = jnp.concatenate([part.reshape(-1) for part in parts])
+    lanes = -(-flat.shape[0] // (ways * 8 * 128)) * 128
+    padded = jnp.pad(flat, (0, ways * 8 * lanes - flat.shape[0])).reshape(ways, 8, lanes)
+    summed = pl.pallas_call(
+        lambda *refs: total_kernel(ways, tensor, *refs),
+        out_shape=jax.ShapeDtypeStruct(padded.shape, jnp.float32),
+        in_specs=[pl.BlockSpec(memory_space=pltpu.VMEM)],
+        out_specs=pl.BlockSpec(memory_space=pltpu.VMEM),
+        scratch_shapes=[pltpu.VMEM(padded.shape, jnp.float32)]
+        + [pltpu.SemaphoreType.DMA((ways,))] * 4,
+        compiler_params=pltpu.CompilerParams(collective_id=1, has_side_effects=True),
+        name="total_over_devices",
+    )(padded).reshape(-1)
+    results, first = [], 0
+    for part in parts:
+        results.append(summed[first : first + part.size].reshape(part.shape))
+        first += part.size
+    return results
+
+
 norm_eps = 1e-05
 route_scale = 3.0
 masked_score = -1e30
@@ -315,30 +521,25 @@
     def whole_tree(local_rows):
         return lax.all_gather(local_rows, "tensor", axis=0, tiled=True)
 
+    def hop(rows, chip_step, core_step):
+        route = []
+        for source in range(dp_size):
+            chip, core = source // 2, source % 2
+            route.append((source, (chip ^ chip_step) * 2 + (core ^ core_step)))
+        return lax.ppermute(rows, "dp", route)
+
+    def across_chips(rows):
+        blocks = rows.reshape(experts, capacity, model_width)
+        moved = [blocks[0]] + [hop(blocks[step], step, 0) for step in range(1, experts)]
+        return jnp.concatenate(moved, axis=0)
+
     def dispatch(slot_input):
-        doubled = jnp.broadcast_to(
-            slot_input.reshape(experts, 1, capacity, model_width),
-            (experts, 2, capacity, model_width),
-        )
-        arrived = lax.all_to_all(
-            doubled.reshape(dp_size, capacity, model_width),
-            "dp",
-            split_axis=0,
-            concat_axis=0,
-            tiled=True,
-        )
-        return arrived.reshape(dp_size * capacity, model_width)
-
-    def combine(partial_rows):
-        returned = lax.all_to_all(
-            partial_rows.reshape(dp_size, capacity, model_width),
-            "dp",
-            split_axis=0,
-            concat_axis=0,
-            tiled=True,
-        )
-        summed = jnp.sum(returned.reshape(experts, 2, capacity, model_width), axis=1)
-        return summed.reshape(experts * capacity, model_width)
+        arrived = across_chips(slot_input)
+        return jnp.concatenate([arrived, hop(arrived, 0, 1)], axis=0)
+
+    def combine(kept_rows, sent_rows):
+        paired = (kept_rows + hop(sent_rows, 0, 1).astype(jnp.float32)).astype(jnp.bfloat16)
+        return across_chips(paired)
 
     hidden = tokens.astype(jnp.float32)
     normed_in, norm1_back = jax.vjp(layer_norm, hidden, norm1_gain)
@@ -364,7 +565,8 @@
     normed_mid, norm2_back = jax.vjp(layer_norm, mid_stream, norm2_gain)
     moe_in = normed_mid.astype(jnp.bfloat16)
     route_ids = routes[:, 0]
-    column, kept_mask = slot_table(route_ids, orders[0], capacity)
+    near_route = route_ids ^ (lax.axis_index("dp") // 2)
+    column, kept_mask = slot_table(near_route, orders[0], capacity)
     picked = (route_ids[:, None] == jnp.arange(experts)[None, :]).astype(jnp.float32)
     gate_value, gate_back = jax.vjp(
         lambda normed_rows, route_proj, embed_rows: router_gate(
@@ -377,50 +579,42 @@
     select = (
         (column[:, None] == jnp.arange(experts * capacity)[None, :]) & kept_mask[:, None]
     ).astype(jnp.bfloat16)
-    kept_float = kept_mask[:, None].astype(jnp.float32)
-
     def to_slots(token_rows):
         return jnp.einsum(
             "ts,td->sd", select, token_rows, preferred_element_type=jnp.float32
         ).astype(jnp.bfloat16)
 
     def from_slots(slot_rows):
-        return jnp.take(slot_rows, column, axis=0) * kept_float
-
+        return jnp.dot(select, slot_rows, preferred_element_type=jnp.float32)
+
+    upstream = cotangent.astype(jnp.float32)
     expert_rows = dispatch(to_slots(moe_in))
-    up_values = jnp.dot(expert_rows, expert_in, preferred_element_type=jnp.float32)
-    active_full, gelu_back = jax.vjp(gelu_exact, up_values)
-    active = active_full.astype(jnp.bfloat16)
-    expert_result = from_slots(
-        combine(jnp.dot(active, expert_out, preferred_element_type=jnp.float32))
-    )
+    arrived_grad = dispatch(to_slots((gate_value[:, None] * upstream).astype(jnp.bfloat16)))
+    active, slope, kept_result, sent_result = expert_forward(expert_rows, expert_in, expert_out)
+    expert_result = from_slots(combine(kept_result, sent_result))
     output = (mid_stream + gate_value[:, None] * expert_result).astype(jnp.bfloat16)
-    upstream = cotangent.astype(jnp.float32)
-    arrived_grad = dispatch(to_slots((gate_value[:, None] * upstream).astype(jnp.bfloat16)))
     out_weight_grad = jnp.einsum(
         "rf,rd->fd", active, arrived_grad, preferred_element_type=jnp.float32
-    )
-    active_grad = jnp.einsum(
-        "rd,fd->rf", arrived_grad, expert_out, preferred_element_type=jnp.float32
-    )
-    up_grad = gelu_back(active_grad)[0].astype(jnp.bfloat16)
+    ).astype(jnp.bfloat16)
+    up_grad, kept_grad, sent_grad = expert_back(arrived_grad, slope, expert_in, expert_out)
     in_weight_grad = jnp.einsum(
         "rd,rf->df", expert_rows, up_grad, preferred_element_type=jnp.float32
-    )
-    moe_grad = from_slots(
-        combine(jnp.einsum("rf,df->rd", up_grad, expert_in, preferred_element_type=jnp.float32))
-    )
+    ).astype(jnp.bfloat16)
+    moe_grad = from_slots(combine(kept_grad, sent_grad))
     gate_grad = jnp.sum(upstream * expert_result, axis=-1)
     router_part, proj_grad, embed_grad = gate_back(gate_grad)
     mid_part, gain2_grad = norm2_back(moe_grad + router_part)
     mid_grad = upstream + mid_part
+    mid_grad, in_weight_grad, out_weight_grad = lax.optimization_barrier(
+        (mid_grad, in_weight_grad, out_weight_grad)
+    )
     expert_in_grad, expert_out_grad = (
-        lax.psum_scatter(
-            in_weight_grad.astype(jnp.bfloat16), "tensor", scatter_dimension=1, tiled=True
-        ).astype(jnp.float32),
-        lax.psum_scatter(
-            out_weight_grad.astype(jnp.bfloat16), "tensor", scatter_dimension=0, tiled=True
-        ).astype(jnp.float32),
+        lax.psum_scatter(in_weight_grad, "tensor", scatter_dimension=1, tiled=True).astype(
+            jnp.float32
+        ),
+        lax.psum_scatter(out_weight_grad, "tensor", scatter_dimension=0, tiled=True).astype(
+            jnp.float32
+        ),
     )
     branch_grad = mid_grad.astype(jnp.bfloat16)
     proj_grad_full = jnp.einsum(
@@ -452,13 +646,13 @@
             weight_grad(seen_in, value_grad),
         ],
         axis=1,
-    )
+    ).astype(jnp.bfloat16)
     qkv_grad = lax.psum_scatter(
         lax.psum_scatter(qkv_grad_full, "dp", scatter_dimension=0, tiled=True),
         "tensor",
         scatter_dimension=2,
         tiled=True,
-    )
+    ).astype(jnp.float32)
     seen_grad = row_grad(key_grad, key_weight) + row_grad(value_grad, value_weight)
     own_grad = seen_grad[2 * TRUNK :] + row_grad(query_grad, query_weight)
     shared_grad = jnp.concatenate(
@@ -469,8 +663,8 @@
     ).astype(jnp.float32)
     token_part, gain1_grad = norm1_back(input_grad)
     token_grad = mid_grad + token_part
-    gain1_sum, gain2_sum, router_sum, embed_sum = lax.psum(
-        (gain1_grad, gain2_grad, proj_grad, embed_grad), ("dp", "tensor")
+    gain1_sum, gain2_sum, router_sum, embed_sum = total_over_devices(
+        (gain1_grad, gain2_grad, proj_grad, embed_grad)
     )
     return (
         output,

time: 1120 us -> 891 us (0.80)
  blocking collectives: 159 us -> 35.2 us
  waiting for transfers between devices: 570 us -> 494 us
  matrix products: 158 us -> 105 us
  Pallas kernels: 96 us -> 148 us
  local copies, waits for them, and re-layouts: 71.7 us -> 51.6 us
    all_to_all x2 -> x0, waiting for transfers between devices: 138 us -> none  [combine(): lax.all_to_all(partial_rows.reshape(dp_size, capacity, model_width), 'dp'...]
    all_to_all x2 -> x0, blocking collectives: 81.7 us -> none  [dispatch(): lax.all_to_all(doubled.reshape(dp_size, capacity, model_width), 'dp', spl...]
    ppermute x0 -> x16, waiting for transfers between devices: none -> 66.9 us  [hop(): return lax.ppermute(rows, 'dp', route)]
    dot_general x4 -> x2, matrix products: 68.7 us -> 6.65 us  [from_slots(): return jnp.dot(select, slot_rows, preferred_element_type=jnp.float32)]
    pallas_call x0 -> x3, Pallas kernels: none -> 52.1 us  [the longest x1 20.4 us: total_over_devices(): pl.pallas_call(lambda *refs: total_kernel(ways, tensor, *refs), out_shape...]
    psum x1 -> x0, blocking collectives: 41.8 us -> none  [shards(): lax.psum((gain1_grad, gain2_grad, proj_grad, embed_grad), ('dp', 'tensor'))]
    gather x4 -> x0, local copies, waits for them, and re-layouts: 23.1 us -> none  [from_slots(): return jnp.take(slot_rows, column, axis=0) * kept_float]
    reduce_scatter x1, waiting for transfers between devices: 40.7 us -> 19.4 us  [shards(): lax.psum_scatter(proj_grad_full, 'dp', scatter_dimension=1, tiled=True)]
  transfers between devices with their start and end apart: 12 -> 26, of which waited for: 10 -> 20; matrix products, arithmetic and copies ran while one was open for 10% -> 14% of each run, Pallas kernels for 4% -> 7%
where the time goes in v2:
time: 891 us; the launch traced here: 894 us
  waiting for transfers between devices  494 us (55%)
  Pallas kernels  148 us (17%)
  matrix products  105 us (12%)
  local copies, waits for them, and re-layouts  51.6 us (6%)
  blocking collectives  35.2 us (4%)
  other arithmetic  29.2 us (3%)
  starting transfers between devices  15.4 us (2%)
  between operations  15.3 us (2%)
    all_gather x1, waiting for transfers between devices, whole_tree(): return lax.all_gather(local_rows, 'tensor', axis=0, tiled=True)  114 us
    reduce_scatter x1, waiting for transfers between devices, shards(): lax.psum_scatter(shared_grad, 'tensor', scatter_dimension=0, tiled=True)  110 us
    unnamed x13, waiting for transfers between devices  71 us
    ppermute x16, waiting for transfers between devices, hop(): return lax.ppermute(rows, 'dp', route)  66.9 us
    reduce_scatter x1, waiting for transfers between devices, shards(): lax.psum_scatter(qkv_grad_full, 'dp', scatter_dimension=0, tiled=True)  54.4 us
    pallas_call x1, Pallas kernels, attend_back(): pl.pallas_call(bwd_kernel, out_shape=(jax.ShapeDtypeStruct((rows, width),...  52.1 us
    reduce_scatter x1, waiting for transfers between devices, shards(): lax.psum_scatter(out_weight_grad, 'tensor', scatter_dimension=0, tiled=True)  45.7 us
    pallas_call x1, Pallas kernels, attend(): pl.pallas_call(fwd_kernel, out_shape=(jax.ShapeDtypeStruct((rows, width),...  44.3 us
  transfers between devices with their start and end apart: 26, of which 20 were waited for; matrix products, arithmetic and copies ran while one was open for 14% of the time, Pallas kernels for 7%

profile of v2, /device:TPU:0, one launch (start us, length us, event | category | flops | bytes accessed | tf_op | source)
XLA Modules:
  0.0 893.7 jit_solution(191328518118969846)
XLA Ops:
  8.4 21.3 %all_gather.15 = bf16[96,3,768]{0,1,2:T(4,128)(2,1)S(1)} all-gather(bf16[96,3,192]{0,1,2:T(4,128)(2,1)S(1)} %copy.66), channel_id=1, replica_groups=mesh['dp'=8,'tensor'=4] {'tensor'}, dimensions={2}, use_global_device_ids=true | all-gather | bytes 552960 | tf_op jit(solution)/shard_map/all_gather | solution.py:549
  35.2 13.9 %all_gather.18 = bf16[768,96]{1,0:T(8,128)(2,1)S(1)} all-gather(bf16[192,96]{1,0:T(8,128)(2,1)S(1)} %copy-done.39), channel_id=1, replica_groups=mesh['dp'=8,'tensor'=4] {'tensor'}, dimensions={0}, use_global_device_ids=true | all-gather | bytes 184320 | tf_op jit(solution)/shard_map/all_gather | solution.py:551
  51.4 12.9 %all-gather.4.cloned.1.call-done = bf16[768,3,768]{2,0,1:T(8,128)(2,1)} async-done(((bf16[96,3,768]{2,0,1:T(8,128)(2,1)}), bf16[768,3,768]{2,0,1:T(8,128)(2,1)}) %all-gather.4.cloned.1.call-update) | async-done | bytes 3538960 | tf_op jit(solution)/shard_map/all_gather | solution.py:550
  67.6 113.8 %all-gather.6.cloned.1.call-done = bf16[4096,768]{0,1:T(8,128)(2,1)} async-done(((bf16[1024,768]{0,1:T(8,128)(2,1)}), bf16[4096,768]{0,1:T(8,128)(2,1)}) %all-gather.6.cloned.1.call-update) | async-done | bytes 6291472 | tf_op jit(solution)/shard_map/all_gather | solution.py:522
  184.3 4.7 convolution_convert_fusion.v_ref
  189.0 4.7 convolution_convert_fusion.1.k_ref
  193.8 44.3 %attend_forward.1 = (bf16[1024,768]{1,0:T(8,128)(2,1)S(1)}, f32[6,2,1024]{2,1,0:T(2,128)S(1)}) custom-call(s32[5]{0:T(128)S(1)} %pad_add_fusion.meta_ref, bf16[1024,768]{1,0:T(8,128)(2,1)S(1)} %convolution_convert_fusion.5.q_ref, bf16[3072,768]{1,0:T(8,128)(2,1)S(1)} %convolution_convert_fusion.1.k_ref, bf16[3072,768]{1,0:T(8,128)(2,1)S(1)} %convolution_convert_fusion.v_ref), custom_call_target="tpu_custom_call" | custom-call | tf_op jit(solution)/shard_map/attend_forward/pallas_call | solution.py:107
  251.1 8.5 collective-permute-done
  259.6 8.7 collective-permute-done.1
  272.1 16.0 %expert_forward.1 = (bf16[2048,1536]{1,0:T(8,128)(2,1)}, bf16[2048,1536]{1,0:T(8,128)(2,1)}, f32[1024,768]{1,0:T(8,128)S(1)}, bf16[1024,768]{1,0:T(8,128)(2,1)}) custom-call(bf16[2048,768]{1,0:T(8,128)(2,1)S(1)} %constant_dynamic-update-slice_fusion.x_ref, bf16[768,1536]{1,0:T(8,128)(2,1)S(1)} %copy-done.8, bf16[1536,768]{1,0:T(8,128)(2,1)S(1)} %copy-done.10), custom_call_target="tpu_custom_call" | custom-call | flops 9663676416 | bytes 25165824 | tf_op jit(solution)/shard_map/expert_forward/pallas_call | solution.py:323
  301.7 8.2 collective-permute-done.5
  309.8 7.2 collective-permute-done.6
  328.5 9.5 %collective-permute-done.10 = bf16[256,768]{1,0:T(8,128)(2,1)S(1)} collective-permute-done((bf16[256,768]{1,0:T(8,128)(2,1)S(1)}, bf16[256,768]{1,0:T(8,128)(2,1)S(1)}, u32[]{:S(2)}, u32[]{:S(2)}) %collective-permute-start.10) | collective-permute-done | bytes 393248 | tf_op jit(solution)/shard_map/ppermute | solution.py:529
  338.0 6.1 collective-permute-done.8
  348.7 15.8 %expert_backward.1 = (bf16[2048,1536]{1,0:T(8,128)(2,1)}, f32[1024,768]{1,0:T(8,128)S(1)}, bf16[1024,768]{1,0:T(8,128)(2,1)}) custom-call(bf16[2048,768]{1,0:T(8,128)(2,1)S(1)} %constant_dynamic-update-slice_fusion.5.grad_ref, bf16[2048,1536]{1,0:T(8,128)(2,1)} %get-tuple-element.28.slope_ref, bf16[768,1536]{1,0:T(8,128)(2,1)S(1)} %copy-done.9, ...), custom_call_target="tpu_custom_call" | custom-call | flops 9663676416 | bytes 25165824 | tf_op jit(solution)/shard_map/expert_backward/pallas_call | solution.py:348
  370.7 18.5 %convolution_convert_fusion.2 = bf16[1536,768]{1,0:T(8,128)(2,1)} fusion(bf16[2048,1536]{1,0:T(8,128)(2,1)S(1)} %bitcast.75, bf16[2048,768]{1,0:T(8,128)(2,1)S(1)} %constant_dynamic-update-slice_fusion.5.grad_ref), kind=kOutput, calls=%fused_computation.26 | convolution fusion | flops 4833017856 | bytes 11796480 | tf_op jit(solution)/shard_map/rf,rd->fd/dot_general | solution.py:596
  395.8 6.5 convolution_convert_fusion.3
  404.2 8.2 collective-permute-done.14
  423.2 52.1 %attend_backward.1 = (bf16[1024,768]{1,0:T(8,128)(2,1)S(1)}, bf16[3072,768]{1,0:T(8,128)(2,1)}, bf16[3072,768]{1,0:T(8,128)(2,1)}) custom-call(s32[5]{0:T(128)S(1)} %pad_add_fusion.meta_ref, bf16[1024,768]{1,0:T(8,128)(2,1)S(1)} %convolution_convert_fusion.5.q_ref, bf16[3072,768]{1,0:T(8,128)(2,1)} %copy-done.3, bf16[3072,768]{1,0:T(8,128)(2,1)} %copy-done.2, ...), custom_call_target="tpu_custom_call" | custom-call | tf_op jit(solution)/shard_map/attend_backward/pallas_call | solution.py:227
  475.3 6.7 fusion.57
  489.4 4.7 fusion.60
  499.2 10.2 %fusion.59 = f32[3072,768]{0,1:T(8,128)} fusion(bf16[3072,768]{1,0:T(8,128)(2,1)} %get-tuple-element.35, bf16[768,3,768]{2,0,1:T(8,128)(2,1)} %all-gather.4.cloned.1.call-done), kind=kOutput, calls=%fused_computation.86 | convolution fusion | flops 3623878656 | bytes 15335424 | tf_op jit(solution)/shard_map/sc,dc->sd/dot_general | solution.py:640
  509.4 54.4 %reduce-scatter.16.cloned.1.call-done = bf16[96,3,768]{2,0,1:T(8,128)(2,1)} async-done(((bf16[768,3,768]{2,0,1:T(8,128)(2,1)}), bf16[96,3,768]{2,0,1:T(8,128)(2,1)}) %reduce-scatter.16.cloned.1.call-update) | async-done | bytes 442384 | tf_op jit(solution)/shard_map/reduce_scatter | solution.py:651
  566.7 9.3 %convolution_add_fusion = f32[3072,768]{0,1:T(8,128)S(1)} fusion(f32[3072,768]{0,1:T(8,128)} %fusion.59, bf16[3072,768]{1,0:T(8,128)(2,1)} %get-tuple-element.36, bf16[768,3,768]{2,0,1:T(8,128)(2,1)} %all-gather.4.cloned.1.call-done), kind=kOutput, calls=%fused_computation.1 | convolution fusion | flops 3626237952 | bytes 24772608 | tf_op jit(solution)/shard_map/sc,dc->sd/dot_general | solution.py:640
  590.1 19.4 %reduce-scatter.18.cloned.1.call-done = f32[768,96]{0,1:T(8,128)} async-done(((f32[768,768]{0,1:T(8,128)}), f32[768,96]{0,1:T(8,128)}) %reduce-scatter.18.cloned.1.call-update) | async-done | bytes 294928 | tf_op jit(solution)/shard_map/reduce_scatter | solution.py:624
  611.4 48.4 %reduce-scatter.26.cloned.1.call-done = bf16[384,768]{1,0:T(8,128)(2,1)} async-done(((bf16[1536,768]{1,0:T(8,128)(2,1)}), bf16[384,768]{1,0:T(8,128)(2,1)}) %reduce-scatter.26.cloned.1.call-update) | async-done | bytes 589840
  664.1 45.7 %reduce-scatter.20.cloned.1.call-done = bf16[384,768]{1,0:T(8,128)(2,1)} async-done(((bf16[1536,768]{1,0:T(8,128)(2,1)}), bf16[384,768]{1,0:T(8,128)(2,1)}) %reduce-scatter.20.cloned.1.call-update) | async-done | bytes 589840 | tf_op jit(solution)/shard_map/reduce_scatter | solution.py:615
  711.9 21.8 %reduce-scatter.22.cloned.1.call-done = bf16[192,288]{1,0:T(8,128)(2,1)} async-done(((bf16[768,288]{1,0:T(8,128)(2,1)}), bf16[192,288]{1,0:T(8,128)(2,1)}) %reduce-scatter.22.cloned.1.call-update) | async-done | bytes 110608
  735.6 109.6 %reduce-scatter.14.cloned.1.call-done = bf16[1024,768]{0,1:T(8,128)(2,1)} async-done(((bf16[4096,768]{0,1:T(8,128)(2,1)}), bf16[1024,768]{0,1:T(8,128)(2,1)}) %reduce-scatter.14.cloned.1.call-update) | async-done | bytes 1572880 | tf_op jit(solution)/shard_map/reduce_scatter | solution.py:661
  845.2 4.4 fusion.15
  853.3 20.4 %total_over_devices.1 = f32[32,8,128]{2,1,0:T(8,128)} custom-call(f32[32,8,128]{2,1,0:T(8,128)} %fusion.64.refs_0_), custom_call_target="tpu_custom_call" | custom-call | tf_op jit(solution)/shard_map/total_over_devices/pallas_call | solution.py:443
  876.3 5.5 add_add_fusion.2
  (250 shorter events, 137.1 us)
Async XLA Ops:
  7.2 285.7 %copy-start = (f32[768,16]{0,1:T(8,128)S(1)}, f32[768,16]{0,1:T(8,128)}, u32[]{:S(2)}) copy-start(f32[768,16]{0,1:T(8,128)} %param.18) | copy-start | bytes 147460
  7.2 57.2 %all-gather.4.cloned.1.call-start = ((), (), s32[]{:S(2)}) async-start(), calls=%async_computation.7 | async-start | bytes 3981312 | tf_op jit(solution)/shard_map/all_gather | solution.py:550
  30.9 150.4 %all-gather.6.cloned.1.call-start = ((), (), s32[]{:S(2)}) async-start(), calls=%async_computation.8 | async-start | bytes 7864320 | tf_op jit(solution)/shard_map/all_gather | solution.py:522
  35.1 205.1 %all-gather.8.cloned.1.call-start = ((), (), s32[]{:S(2)}) async-start(), calls=%async_computation.9 | async-start | bytes 1327104 | tf_op jit(solution)/shard_map/all_gather | solution.py:552
  49.9 513.8 %reduce-scatter.16.cloned.1.call-start = ((), (), s32[]{:S(2)}) async-start(), calls=%async_computation.11 | async-start | bytes 3981312 | tf_op jit(solution)/shard_map/reduce_scatter | solution.py:651
  67.6 116.2 %copy-start.22 = (bf16[1024,768]{0,1:T(8,128)(2,1)S(1)}, bf16[1024,768]{0,1:T(8,128)(2,1)}, u32[]{:S(2)}) copy-start(bf16[1024,768]{0,1:T(8,128)(2,1)} %fusion.12) | copy-start | bytes 4718596
  247.6 12.0 %collective-permute-start = (bf16[256,768]{1,0:T(8,128)(2,1)S(1)}, bf16[256,768]{1,0:T(8,128)(2,1)S(1)}, u32[]{:S(2)}, u32[]{:S(2)}) collective-permute-start(bf16[256,768]{1,0:T(8,128)(2,1)S(1)} %get-tuple-element.125), channel_id=1, source_target_pairs={{0,8},{4,12},{8,0},{12,4},{16,24},{20,28},{24,16},{28,20},{1,9},{5... | collective-permute-start | bytes 1179656 | tf_op jit(solution)/shard_map/ppermute | solution.py:529
  249.1 19.2 %collective-permute-start.1 = (bf16[256,768]{1,0:T(8,128)(2,1)S(1)}, bf16[256,768]{1,0:T(8,128)(2,1)S(1)}, u32[]{:S(2)}, u32[]{:S(2)}) collective-permute-start(bf16[256,768]{1,0:T(8,128)(2,1)S(1)} %get-tuple-element.124), channel_id=1, source_target_pairs={{0,16},{4,20},{8,24},{12,28},{16,0},{20,4},{24,8},{28,12},{1,17},{... | collective-permute-start | bytes 1179656 | tf_op jit(solution)/shard_map/ppermute | solution.py:529
  250.6 17.7 %collective-permute-start.2 = (bf16[256,768]{1,0:T(8,128)(2,1)S(1)}, bf16[256,768]{1,0:T(8,128)(2,1)S(1)}, u32[]{:S(2)}, u32[]{:S(2)}) collective-permute-start(bf16[256,768]{1,0:T(8,128)(2,1)S(1)} %get-tuple-element.123), channel_id=1, source_target_pairs={{0,24},{4,28},{8,16},{12,20},{16,8},{20,12},{24,0},{28,4},{1,25},{... | collective-permute-start | bytes 1179656 | tf_op jit(solution)/shard_map/ppermute | solution.py:529
  268.4 3.5 collective-permute-start.3
  289.7 5.3 collective-permute-start.4
  297.8 12.0 %collective-permute-start.5 = (bf16[256,768]{1,0:T(8,128)(2,1)S(1)}, bf16[256,768]{1,0:T(8,128)(2,1)S(1)}, u32[]{:S(2)}, u32[]{:S(2)}) collective-permute-start(bf16[256,768]{1,0:T(8,128)(2,1)S(1)} %get-tuple-element.120), channel_id=1, source_target_pairs={{0,8},{4,12},{8,0},{12,4},{16,24},{20,28},{24,16},{28,20},{1,9},{5... | collective-permute-start | bytes 1179656 | tf_op jit(solution)/shard_map/ppermute | solution.py:529
  299.1 17.9 %collective-permute-start.6 = (bf16[256,768]{1,0:T(8,128)(2,1)S(1)}, bf16[256,768]{1,0:T(8,128)(2,1)S(1)}, u32[]{:S(2)}, u32[]{:S(2)}) collective-permute-start(bf16[256,768]{1,0:T(8,128)(2,1)S(1)} %get-tuple-element.119), channel_id=1, source_target_pairs={{0,16},{4,20},{8,24},{12,28},{16,0},{20,4},{24,8},{28,12},{1,17},{... | collective-permute-start | bytes 1179656 | tf_op jit(solution)/shard_map/ppermute | solution.py:529
  299.9 18.7 %collective-permute-start.7 = (bf16[256,768]{1,0:T(8,128)(2,1)S(1)}, bf16[256,768]{1,0:T(8,128)(2,1)S(1)}, u32[]{:S(2)}, u32[]{:S(2)}) collective-permute-start(bf16[256,768]{1,0:T(8,128)(2,1)S(1)} %get-tuple-element.118), channel_id=1, source_target_pairs={{0,24},{4,28},{8,16},{12,20},{16,8},{20,12},{24,0},{28,4},{1,25},{... | collective-permute-start | bytes 1179656 | tf_op jit(solution)/shard_map/ppermute | solution.py:529
  325.0 13.1 %collective-permute-start.10 = (bf16[256,768]{1,0:T(8,128)(2,1)S(1)}, bf16[256,768]{1,0:T(8,128)(2,1)S(1)}, u32[]{:S(2)}, u32[]{:S(2)}) collective-permute-start(bf16[256,768]{1,0:T(8,128)(2,1)S(1)} %get-tuple-element.114), channel_id=1, source_target_pairs={{0,24},{4,28},{8,16},{12,20},{16,8},{20,12},{24,0},{28,4},{1,25},{... | collective-permute-start | bytes 1179656 | tf_op jit(solution)/shard_map/ppermute | solution.py:529
  326.8 17.3 %collective-permute-start.8 = (bf16[256,768]{1,0:T(8,128)(2,1)S(1)}, bf16[256,768]{1,0:T(8,128)(2,1)S(1)}, u32[]{:S(2)}, u32[]{:S(2)}) collective-permute-start(bf16[256,768]{1,0:T(8,128)(2,1)S(1)} %get-tuple-element.116), channel_id=1, source_target_pairs={{0,8},{4,12},{8,0},{12,4},{16,24},{20,28},{24,16},{28,20},{1,9},{5... | collective-permute-start | bytes 1179656 | tf_op jit(solution)/shard_map/ppermute | solution.py:529
  327.4 17.6 %collective-permute-start.9 = (bf16[256,768]{1,0:T(8,128)(2,1)S(1)}, bf16[256,768]{1,0:T(8,128)(2,1)S(1)}, u32[]{:S(2)}, u32[]{:S(2)}) collective-permute-start(bf16[256,768]{1,0:T(8,128)(2,1)S(1)} %get-tuple-element.115), channel_id=1, source_target_pairs={{0,16},{4,20},{8,24},{12,28},{16,0},{20,4},{24,8},{28,12},{1,17},{... | collective-permute-start | bytes 1179656 | tf_op jit(solution)/shard_map/ppermute | solution.py:529
  345.1 3.5 collective-permute-start.11
  366.2 23.0 %collective-permute-start.12 = (bf16[1024,768]{1,0:T(8,128)(2,1)}, bf16[1024,768]{1,0:T(8,128)(2,1)}, u32[]{:S(2)}, u32[]{:S(2)}) collective-permute-start(bf16[1024,768]{1,0:T(8,128)(2,1)} %get-tuple-element.30), channel_id=1, source_target_pairs={{0,4},{4,0},{8,12},{12,8},{16,20},{20,16},{24,28},{28,24},{1,5},{5... | collective-permute-start | bytes 4718600 | tf_op jit(solution)/shard_map/ppermute | solution.py:529
  392.2 12.0 %collective-permute-start.13 = (bf16[256,768]{1,0:T(8,128)(2,1)S(1)}, bf16[256,768]{1,0:T(8,128)(2,1)S(1)}, u32[]{:S(2)}, u32[]{:S(2)}) collective-permute-start(bf16[256,768]{1,0:T(8,128)(2,1)S(1)} %get-tuple-element.111), channel_id=1, source_target_pairs={{0,8},{4,12},{8,0},{12,4},{16,24},{20,28},{24,16},{28,20},{1,9},{5... | collective-permute-start | bytes 1179656 | tf_op jit(solution)/shard_map/ppermute | solution.py:529
  392.9 19.5 %collective-permute-start.14 = (bf16[256,768]{1,0:T(8,128)(2,1)S(1)}, bf16[256,768]{1,0:T(8,128)(2,1)S(1)}, u32[]{:S(2)}, u32[]{:S(2)}) collective-permute-start(bf16[256,768]{1,0:T(8,128)(2,1)S(1)} %get-tuple-element.110), channel_id=1, source_target_pairs={{0,16},{4,20},{8,24},{12,28},{16,0},{20,4},{24,8},{28,12},{1,17},{... | collective-permute-start | bytes 1179656 | tf_op jit(solution)/shard_map/ppermute | solution.py:529
  394.1 18.3 %collective-permute-start.15 = (bf16[256,768]{1,0:T(8,128)(2,1)S(1)}, bf16[256,768]{1,0:T(8,128)(2,1)S(1)}, u32[]{:S(2)}, u32[]{:S(2)}) collective-permute-start(bf16[256,768]{1,0:T(8,128)(2,1)S(1)} %get-tuple-element.109), channel_id=1, source_target_pairs={{0,24},{4,28},{8,16},{12,20},{16,8},{20,12},{24,0},{28,4},{1,25},{... | collective-permute-start | bytes 1179656 | tf_op jit(solution)/shard_map/ppermute | solution.py:529
  489.4 120.1 %reduce-scatter.18.cloned.1.call-start = ((), (), s32[]{:S(2)}) async-start(), calls=%async_computation.12 | async-start | bytes 2654208 | tf_op jit(solution)/shard_map/reduce_scatter | solution.py:624
  494.2 165.6 %reduce-scatter.26.cloned.1.call-start = ((), (), s32[]{:S(2)}) async-start(), calls=%async_computation.16 | async-start | bytes 2949120
  498.4 211.4 %reduce-scatter.20.cloned.1.call-start = ((), (), s32[]{:S(2)}) async-start(), calls=%async_computation.13 | async-start | bytes 2949120 | tf_op jit(solution)/shard_map/reduce_scatter | solution.py:615
  499.1 234.5 %reduce-scatter.22.cloned.1.call-start = ((), (), s32[]{:S(2)}) async-start(), calls=%async_computation.14 | async-start | bytes 737280
  566.5 278.7 %reduce-scatter.14.cloned.1.call-start = ((), (), s32[]{:S(2)}) async-start(), calls=%async_computation.10 | async-start | bytes 7864320 | tf_op jit(solution)/shard_map/reduce_scatter | solution.py:661
  583.4 303.3 %reduce-scatter.24.cloned.1.call-start = ((), (), s32[]{:S(2)}) async-start(), calls=%async_computation.15 | async-start | bytes 491520
  611.3 233.9 %copy-start.13 = (bf16[1024,768]{1,0:T(8,128)(2,1)S(1)}, bf16[1024,768]{1,0:T(8,128)(2,1)}, u32[]{:S(2)}) copy-start(bf16[1024,768]{1,0:T(8,128)(2,1)} %copy-done.12) | copy-start | bytes 4718596
  611.3 233.9 %copy-start.15 = (bf16[1024,768]{0,1:T(8,128)(2,1)S(1)}, bf16[1024,768]{0,1:T(8,128)(2,1)}, u32[]{:S(2)}) copy-start(bf16[1024,768]{0,1:T(8,128)(2,1)} %copy-done.14) | copy-start | bytes 4718596
  611.3 233.9 %copy-start.35 = (f32[1024]{0:T(1024)S(1)}, f32[1024]{0:T(1024)}, u32[]{:S(2)}) copy-start(f32[1024]{0:T(1024)} %copy-done.34) | copy-start | bytes 12292
  611.3 233.9 %copy-start.41 = (f32[768]{0:T(1024)S(1)}, f32[768]{0:T(1024)}, u32[]{:S(2)}) copy-start(f32[768]{0:T(1024)} %param.14) | copy-start | bytes 9220
  (48 other events, 672.3 us)
Sparse Core Ops, SparseCore 0:
  31.0 33.3 all-gather.3
  66.0 115.3 all-gather.5
  183.8 22.2 all-gather.7
  489.5 74.1 reduce-scatter.15
  566.9 42.4 reduce-scatter.17
  611.7 48.0 reduce-scatter.25
  662.2 47.5 reduce-scatter.19
  712.1 21.4 reduce-scatter.21
  736.1 109.0 reduce-scatter.13
  848.0 22.8 reduce-scatter.23

commit v3 on v2

--- a/solution.py
+++ b/solution.py
@@ -457,6 +457,395 @@
     return results
 
 
+PIECE = 64
+
+
+def greet(peers):
+    barrier = pltpu.get_barrier_semaphore()
+    for peer in peers:
+        pl.semaphore_signal(barrier, inc=1, device_id=peer, device_id_type=MESH)
+    pl.semaphore_wait(barrier, len(peers))
+
+
+def share_kernel(dp, tensor, own_ref, block_ref, seen_ref, weights_ref,
+                 row_send, row_recv, copy_sem, block_sem,
+                 line_send, line_recv, chip_send, chip_recv, pair_send, pair_recv):
+    spot, place = lax.axis_index("dp"), lax.axis_index("tensor")
+    chip, core = spot // 2, lax.rem(spot, 2)
+    chips = dp // 2
+    rows = own_ref.shape[0]
+    pieces = rows // PIECE
+    partner = (chip * 2 + 1 - core, place)
+
+    def along(step):
+        return lax.rem(place + step, tensor)
+
+    def chip_at(step):
+        return lax.rem(chip + step, chips)
+
+    greet(
+        [(spot, along(step)) for step in range(1, tensor)]
+        + [(chip_at(step) * 2 + core, place) for step in range(1, chips)]
+        + [partner]
+    )
+
+    def keep(part):
+        return pltpu.make_async_copy(
+            own_ref, seen_ref.at[pl.ds(part * rows, rows)], copy_sem.at[part]
+        )
+
+    def keep_block():
+        return pltpu.make_async_copy(block_ref, weights_ref.at[place, spot], block_sem)
+
+    def pass_on(part, piece, fresh):
+        at = pl.ds(part * rows + piece * PIECE, PIECE)
+        source = own_ref.at[pl.ds(piece * PIECE, PIECE)] if fresh else seen_ref.at[at]
+        return pltpu.make_async_remote_copy(
+            src_ref=source, dst_ref=seen_ref.at[at],
+            send_sem=row_send.at[part, piece], recv_sem=row_recv.at[part, piece],
+            device_id=(spot, lax.rem(place + 1, tensor)), device_id_type=MESH,
+        )
+
+    def line(step):
+        return pltpu.make_async_remote_copy(
+            src_ref=block_ref, dst_ref=weights_ref.at[place, spot],
+            send_sem=line_send.at[step], recv_sem=line_recv.at[place],
+            device_id=(spot, along(step)), device_id_type=MESH,
+        )
+
+    def line_in(step):
+        source = along(tensor - step)
+        return pltpu.make_async_remote_copy(
+            src_ref=block_ref, dst_ref=weights_ref.at[source, spot],
+            send_sem=line_send.at[step], recv_sem=line_recv.at[source],
+            device_id=(spot, along(step)), device_id_type=MESH,
+        )
+
+    def plane(part, step):
+        block = weights_ref.at[part, spot]
+        return pltpu.make_async_remote_copy(
+            src_ref=block, dst_ref=block,
+            send_sem=chip_send.at[part, step], recv_sem=chip_recv.at[part, chip],
+            device_id=(chip_at(step) * 2 + core, place), device_id_type=MESH,
+        )
+
+    def plane_in(part, step):
+        source = chip_at(chips - step)
+        block = weights_ref.at[part, source * 2 + core]
+        return pltpu.make_async_remote_copy(
+            src_ref=block, dst_ref=block,
+            send_sem=chip_send.at[part, step], recv_sem=chip_recv.at[part, source],
+            device_id=(chip_at(step) * 2 + core, place), device_id_type=MESH,
+        )
+
+    def across(part, source, source_core):
+        block = weights_ref.at[part, source * 2 + source_core]
+        return pltpu.make_async_remote_copy(
+            src_ref=block, dst_ref=block,
+            send_sem=pair_send.at[part, source], recv_sem=pair_recv.at[part, source],
+            device_id=partner, device_id_type=MESH,
+        )
+
+    keep_block().start()
+    keep(2).start()
+
+    @pl.when(place < 2)
+    def _():
+        keep(1).start()
+
+    @pl.when(place == 0)
+    def _():
+        keep(0).start()
+
+    for step in range(1, tensor):
+        line(step).start()
+
+    def row_steps(first, last):
+        @pl.loop(first, last)
+        def _(piece):
+            @pl.when(place == 0)
+            def _():
+                pass_on(0, piece, True).start()
+
+            @pl.when(place > 0)
+            def _():
+                pass_on(0, piece, False).wait_recv()
+
+            @pl.when((place > 0) & (place < tensor - 1))
+            def _():
+                pass_on(0, piece, False).start()
+
+            @pl.when(place == 1)
+            def _():
+                pass_on(1, piece, True).start()
+
+            @pl.when(place > 1)
+            def _():
+                pass_on(1, piece, False).wait_recv()
+
+            @pl.when((place > 1) & (place < tensor - 1))
+            def _():
+                pass_on(1, piece, False).start()
+
+    row_steps(0, pieces // 4)
+    keep_block().wait()
+    for step in range(tensor):
+        part = along(tensor - step)
+        if step:
+            line_in(step).wait_recv()
+
+        @pl.loop(1, chips)
+        def _(hop):
+            plane(part, hop).start()
+
+        across(part, chip, core).start()
+    row_steps(pieces // 4, (pieces * 5) // 8)
+    for step in range(tensor):
+        part = along(tensor - step)
+
+        @pl.loop(1, chips)
+        def _(hop):
+            plane_in(part, hop).wait_recv()
+            across(part, chip_at(chips - hop), core).start()
+
+    row_steps((pieces * 5) // 8, pieces)
+    for part in range(tensor):
+
+        @pl.loop(0, chips)
+        def _(source):
+            across(part, source, 1 - core).wait_recv()
+            across(part, source, core).wait_send()
+
+        @pl.loop(1, chips)
+        def _(hop):
+            plane(part, hop).wait_send()
+
+    for step in range(1, tensor):
+        line(step).wait_send()
+
+    @pl.when(place < tensor - 1)
+    def _():
+        @pl.loop(0, pieces)
+        def _(piece):
+            pass_on(0, piece, False).wait_send()
+
+    @pl.when((place > 0) & (place < tensor - 1))
+    def _():
+        @pl.loop(0, pieces)
+        def _(piece):
+            pass_on(1, piece, False).wait_send()
+
+    keep(2).wait()
+
+    @pl.when(place < 2)
+    def _():
+        keep(1).wait()
+
+    @pl.when(place == 0)
+    def _():
+        keep(0).wait()
+
+
+def share_rows_and_weights(own, block):
+    dp, tensor = lax.axis_size("dp"), lax.axis_size("tensor")
+    rows, width = own.shape
+    pieces, chips = rows // PIECE, dp // 2
+    dma = pltpu.SemaphoreType.DMA
+    anywhere = pl.BlockSpec(memory_space=pl.ANY)
+    return pl.pallas_call(
+        lambda *refs: share_kernel(dp, tensor, *refs),
+        out_shape=(
+            jax.ShapeDtypeStruct((3 * rows, width), own.dtype),
+            jax.ShapeDtypeStruct((tensor, dp) + block.shape, block.dtype),
+        ),
+        in_specs=[anywhere, anywhere],
+        out_specs=[anywhere, anywhere],
+        scratch_shapes=[
+            dma((2, pieces)), dma((2, pieces)), dma((3,)), dma,
+            dma((tensor,)), dma((tensor,)),
+            dma((tensor, chips)), dma((tensor, chips)),
+            dma((tensor, chips)), dma((tensor, chips)),
+        ],
+        compiler_params=pltpu.CompilerParams(collective_id=2, has_side_effects=True),
+        name="share_rows_and_weights",
+    )(own, block)
+
+
+def gather_grads_kernel(dp, tensor, rows_ref, grads_ref, out_ref, sum_ref,
+                        land_ref, pass_ref, grad_land, grad_sum, line_out, line_land,
+                        row_send, row_recv, grad_send, grad_recv, line_send, line_recv):
+    spot, place = lax.axis_index("dp"), lax.axis_index("tensor")
+    rows = out_ref.shape[0]
+    pieces = rows // PIECE
+    parts = grads_ref.shape[2] // (tensor * sum_ref.shape[1] // 4)
+    share = sum_ref.shape[1] // parts
+
+    def along(step):
+        return lax.rem(place + step, tensor)
+
+    def peer(step):
+        return lax.rem(spot + step, dp)
+
+    greet(
+        [(spot, along(step)) for step in range(1, tensor)]
+        + [(peer(step), place) for step in range(1, dp)]
+    )
+
+    def pass_down(piece, fresh):
+        at = pl.ds(piece * PIECE, PIECE)
+        source = rows_ref if fresh else pass_ref
+        return pltpu.make_async_remote_copy(
+            src_ref=source.at[at], dst_ref=land_ref.at[at],
+            send_sem=row_send.at[piece], recv_sem=row_recv.at[piece],
+            device_id=(spot, lax.rem(place + tensor - 1, tensor)), device_id_type=MESH,
+        )
+
+    def give(step):
+        return pltpu.make_async_remote_copy(
+            src_ref=grads_ref.at[peer(step)], dst_ref=grad_land.at[spot],
+            send_sem=grad_send.at[step], recv_sem=grad_recv.at[spot],
+            device_id=(peer(step), place), device_id_type=MESH,
+        )
+
+    def take(step):
+        source = peer(dp - step)
+        return pltpu.make_async_remote_copy(
+            src_ref=grads_ref.at[source], dst_ref=grad_land.at[source],
+            send_sem=grad_send.at[step], recv_sem=grad_recv.at[source],
+            device_id=(peer(step), place), device_id_type=MESH,
+        )
+
+    def line(step):
+        return pltpu.make_async_remote_copy(
+            src_ref=line_out.at[along(step)], dst_ref=line_land.at[place],
+            send_sem=line_send.at[step], recv_sem=line_recv.at[place],
+            device_id=(spot, along(step)), device_id_type=MESH,
+        )
+
+    def line_in(step):
+        source = along(tensor - step)
+        return pltpu.make_async_remote_copy(
+            src_ref=line_out.at[source], dst_ref=line_land.at[source],
+            send_sem=line_send.at[step], recv_sem=line_recv.at[source],
+            device_id=(spot, along(step)), device_id_type=MESH,
+        )
+
+    @pl.when(place == tensor - 1)
+    def _():
+        @pl.loop(0, 2 * pieces)
+        def _(piece):
+            pass_down(piece, True).start()
+
+    @pl.loop(1, dp)
+    def _(step):
+        give(step).start()
+
+    @pl.when(place > 1)
+    def _():
+        out_ref[...] = jnp.zeros_like(out_ref)
+
+    def row_steps(first, last):
+        @pl.loop(first, last)
+        def _(piece):
+            trunk = piece < pieces
+            at = pl.ds(pl.multiple_of(piece * PIECE, PIECE), PIECE)
+            takes = (place < tensor - 1) & ((place > 0) | trunk)
+            sends = takes & (place > 0) & ((place > 1) | trunk)
+
+            @pl.when(takes)
+            def _():
+                pass_down(piece, False).wait_recv()
+
+            @pl.when(sends)
+            def _():
+                total = rows_ref[at].astype(jnp.float32) + land_ref[at].astype(jnp.float32)
+                pass_ref[at] = total.astype(pass_ref.dtype)
+                pass_down(piece, False).start()
+
+            @pl.when(takes & jnp.logical_not(sends))
+            def _():
+                total = rows_ref[at].astype(jnp.float32) + land_ref[at].astype(jnp.float32)
+                here = lax.rem(piece, pieces) * PIECE
+                out_ref[pl.ds(pl.multiple_of(here, PIECE), PIECE)] = total
+
+    row_steps(0, pieces + pieces // 2)
+    grad_sum[...] = grads_ref[spot].astype(jnp.float32)
+
+    @pl.loop(1, dp)
+    def _(step):
+        take(step).wait_recv()
+        grad_sum[...] += grad_land[peer(dp - step)].astype(jnp.float32)
+
+    for target in range(tensor):
+        mine = jnp.concatenate(
+            [
+                grad_sum[:, (part * tensor + target) * share : (part * tensor + target + 1) * share]
+                for part in range(parts)
+            ],
+            axis=1,
+        )
+        line_out[target] = mine.astype(line_out.dtype)
+
+        @pl.when(place == target)
+        def _():
+            sum_ref[...] = mine
+
+    for step in range(1, tensor):
+        line(step).start()
+    row_steps(pieces + pieces // 2, 2 * pieces)
+    for step in range(1, tensor):
+        line_in(step).wait_recv()
+        sum_ref[...] += line_land[along(tensor - step)].astype(jnp.float32)
+    for step in range(1, tensor):
+        line(step).wait_send()
+
+    @pl.loop(1, dp)
+    def _(step):
+        give(step).wait_send()
+
+    @pl.loop(0, 2 * pieces)
+    def _(piece):
+        sends = (place > 0) & ((place > 1) | (piece < pieces))
+
+        @pl.when(sends)
+        def _():
+            pass_down(piece, True).wait_send()
+
+
+def collect_grads(rows, grads):
+    dp, tensor = lax.axis_size("dp"), lax.axis_size("tensor")
+    count, width = rows.shape[0] // 2, rows.shape[1]
+    depth = grads.shape[0] // dp
+    grads = grads.reshape(dp, depth, grads.shape[1])
+    slab = grads.shape[2] // tensor
+    pieces = count // PIECE
+    dma = pltpu.SemaphoreType.DMA
+    here = pl.BlockSpec(memory_space=pltpu.VMEM)
+    return pl.pallas_call(
+        lambda *refs: gather_grads_kernel(dp, tensor, *refs),
+        out_shape=(
+            jax.ShapeDtypeStruct((count, width), jnp.float32),
+            jax.ShapeDtypeStruct((depth, slab), jnp.float32),
+        ),
+        in_specs=[here, here],
+        out_specs=[here, here],
+        scratch_shapes=[
+            pltpu.VMEM(rows.shape, rows.dtype),
+            pltpu.VMEM(rows.shape, rows.dtype),
+            pltpu.VMEM(grads.shape, grads.dtype),
+            pltpu.VMEM(grads.shape[1:], jnp.float32),
+            pltpu.VMEM((tensor, depth, slab), grads.dtype),
+            pltpu.VMEM((tensor, depth, slab), grads.dtype),
+            dma((2 * pieces,)), dma((2 * pieces,)),
+            dma((dp,)), dma((dp,)), dma((tensor,)), dma((tensor,)),
+        ],
+        compiler_params=pltpu.CompilerParams(
+            collective_id=3, has_side_effects=True, vmem_limit_bytes=56 << 20
+        ),
+        name="collect_grads",
+    )(rows, grads)
+
+
 norm_eps = 1e-05
 route_scale = 3.0
 masked_score = -1e30
@@ -515,11 +904,8 @@
     model_width = tokens.shape[1]
     experts = expert_embed.shape[0]
     capacity = rows_here // experts
-    dp_size = lax.axis_size("dp")
+    dp_size, tensor_size = lax.axis_size("dp"), lax.axis_size("tensor")
     leaf_parents = leaf_parent[0]
-
-    def whole_tree(local_rows):
-        return lax.all_gather(local_rows, "tensor", axis=0, tiled=True)
 
     def hop(rows, chip_step, core_step):
         route = []
@@ -544,13 +930,13 @@
     hidden = tokens.astype(jnp.float32)
     normed_in, norm1_back = jax.vjp(layer_norm, hidden, norm1_gain)
     own_in = normed_in.astype(jnp.bfloat16)
-    shared_in = whole_tree(own_in)[: 2 * TRUNK]
-    seen_in = jnp.concatenate([shared_in, own_in], axis=0)
-    qkv_cols = lax.all_gather(qkv_weight, "tensor", axis=2, tiled=True)
-    qkv_full = lax.all_gather(qkv_cols, "dp", axis=0, tiled=True)
-    proj_rows = lax.all_gather(attn_proj, "tensor", axis=0, tiled=True)
-    proj_full = lax.all_gather(proj_rows, "dp", axis=1, tiled=True)
-    query_weight, key_weight, value_weight = (qkv_full[:, part] for part in range(3))
+    flat_qkv = qkv_weight.reshape(qkv_weight.shape[0], -1)
+    seen_in, weights = share_rows_and_weights(
+        own_in, jnp.concatenate([flat_qkv, attn_proj.T], axis=1)
+    )
+    weights = weights.reshape(tensor_size, model_width, 4, model_width // tensor_size)
+    weights = weights.transpose(2, 1, 0, 3).reshape(4, model_width, model_width)
+    query_weight, key_weight, value_weight, proj_back = weights
     query_rows = low_dot(own_in, query_weight)
     key_rows = low_dot(seen_in, key_weight)
     value_rows = low_dot(seen_in, value_weight)
@@ -560,7 +946,9 @@
     parents = lax.dynamic_slice_in_dim(leaf_parents, first_leaf, leaf_blocks, 0) - 1
     meta = jnp.concatenate([place[None], parents]).astype(jnp.int32)
     attended, log_totals = attend(meta, query_rows, key_rows, value_rows)
-    branch_out = jnp.dot(attended, proj_full, preferred_element_type=jnp.float32)
+    branch_out = jnp.einsum(
+        "sc,dc->sd", attended, proj_back, preferred_element_type=jnp.float32
+    )
     mid_stream = hidden + branch_out
     normed_mid, norm2_back = jax.vjp(layer_norm, mid_stream, norm2_gain)
     moe_in = normed_mid.astype(jnp.bfloat16)
@@ -588,8 +976,14 @@
         return jnp.dot(select, slot_rows, preferred_element_type=jnp.float32)
 
     upstream = cotangent.astype(jnp.float32)
-    expert_rows = dispatch(to_slots(moe_in))
-    arrived_grad = dispatch(to_slots((gate_value[:, None] * upstream).astype(jnp.bfloat16)))
+    slot_rows, slot_grads = lax.optimization_barrier(
+        (
+            to_slots(moe_in),
+            to_slots((gate_value[:, None] * upstream).astype(jnp.bfloat16)),
+        )
+    )
+    expert_rows = dispatch(slot_rows)
+    arrived_grad = dispatch(slot_grads)
     active, slope, kept_result, sent_result = expert_forward(expert_rows, expert_in, expert_out)
     expert_result = from_slots(combine(kept_result, sent_result))
     output = (mid_stream + gate_value[:, None] * expert_result).astype(jnp.bfloat16)
@@ -617,17 +1011,8 @@
         ),
     )
     branch_grad = mid_grad.astype(jnp.bfloat16)
-    proj_grad_full = jnp.einsum(
-        "sc,sd->cd", attended, branch_grad, preferred_element_type=jnp.float32
-    )
-    attn_proj_grad = lax.psum_scatter(
-        lax.psum_scatter(proj_grad_full, "dp", scatter_dimension=1, tiled=True),
-        "tensor",
-        scatter_dimension=0,
-        tiled=True,
-    )
     attended_grad = jnp.einsum(
-        "sd,cd->sc", branch_grad, proj_full, preferred_element_type=jnp.float32
+        "sd,dc->sc", branch_grad, proj_back, preferred_element_type=jnp.float32
     ).astype(jnp.bfloat16)
     query_grad, key_grad, value_grad = attend_back(
         meta, query_rows, key_rows, value_rows, attended, attended_grad, log_totals
@@ -639,28 +1024,23 @@
     def row_grad(row_grads, weight):
         return jnp.einsum("sc,dc->sd", row_grads, weight, preferred_element_type=jnp.float32)
 
-    qkv_grad_full = jnp.stack(
+    weight_grads = jnp.concatenate(
         [
             weight_grad(own_in, query_grad),
             weight_grad(seen_in, key_grad),
             weight_grad(seen_in, value_grad),
+            weight_grad(branch_grad, attended),
         ],
         axis=1,
     ).astype(jnp.bfloat16)
-    qkv_grad = lax.psum_scatter(
-        lax.psum_scatter(qkv_grad_full, "dp", scatter_dimension=0, tiled=True),
-        "tensor",
-        scatter_dimension=2,
-        tiled=True,
-    ).astype(jnp.float32)
     seen_grad = row_grad(key_grad, key_weight) + row_grad(value_grad, value_weight)
     own_grad = seen_grad[2 * TRUNK :] + row_grad(query_grad, query_weight)
-    shared_grad = jnp.concatenate(
-        [seen_grad[: 2 * TRUNK], jnp.zeros_like(seen_grad[: 2 * TRUNK])], axis=0
-    ).astype(jnp.bfloat16)
-    input_grad = own_grad + lax.psum_scatter(
-        shared_grad, "tensor", scatter_dimension=0, tiled=True
-    ).astype(jnp.float32)
+    arrived_rows, grad_block = collect_grads(
+        seen_grad[: 2 * TRUNK].astype(jnp.bfloat16), weight_grads
+    )
+    input_grad = own_grad + arrived_rows
+    qkv_grad = grad_block[:, : flat_qkv.shape[1]].reshape(qkv_weight.shape)
+    attn_proj_grad = grad_block[:, flat_qkv.shape[1] :].T
     token_part, gain1_grad = norm1_back(input_grad)
     token_grad = mid_grad + token_part
     gain1_sum, gain2_sum, router_sum, embed_sum = total_over_devices(

time: 891 us -> 691 us (0.78); the launches traced: 894 us -> 682 us
  waiting for transfers between devices: 494 us -> 57.7 us
  Pallas kernels: 148 us -> 398 us
  blocking collectives: 35.2 us -> 0 us
  local copies, waits for them, and re-layouts: 51.6 us -> 66.2 us
    pallas_call x0 -> x2, Pallas kernels: none -> 243 us  [the longest x1 155 us: share_rows_and_weights(): pl.pallas_call(lambda *refs: share_kernel(dp, tensor, *refs), out_shape=(...]
    reduce_scatter x3 -> x0, waiting for transfers between devices: 183 us -> none  [the longest x1 110 us: shards(): lax.psum_scatter(shared_grad, 'tensor', scatter_dimension=0, tiled=True)]
    all_gather x3 -> x0, waiting for transfers between devices: 127 us -> none  [the longest x1 114 us: whole_tree(): return lax.all_gather(local_rows, 'tensor', axis=0, tiled=True)]
    unnamed x13 -> x3, waiting for transfers between devices: 71 us -> 0.03 us
    reduce_scatter x1, waiting for transfers between devices: 45.7 us -> 0.01 us  [shards(): lax.psum_scatter(out_weight_grad, 'tensor', scatter_dimension=0, tiled=True)]
    all_gather x2 -> x0, blocking collectives: 35.2 us -> none  [the longest x1 21.3 us: shards(): qkv_cols = lax.all_gather(qkv_weight, 'tensor', axis=2, tiled=True)]
    reshape x0 -> x3, local copies, waits for them, and re-layouts: none -> 23.4 us  [the longest x2 23.3 us: shards(): weights.reshape(tensor_size, model_width, 4, model_width // tensor_size)]
    unnamed x127 -> x139, local copies, waits for them, and re-layouts: 38.4 us -> 28.2 us
  transfers between devices with their start and end apart: 26 -> 18, of which waited for: 20 -> 9; matrix products, arithmetic and copies ran while one was open for 14% -> 15% of each run, Pallas kernels for 7% -> 29%
where the time goes in v3:
time: 691 us; the launch traced here: 682 us
  Pallas kernels  398 us (58%)
  matrix products  96.1 us (14%)
  local copies, waits for them, and re-layouts  66.2 us (10%)
  waiting for transfers between devices  57.7 us (8%)
  other arithmetic  32.3 us (5%)
  starting transfers between devices  15.9 us (2%)
  between operations  15.2 us (2%)
    pallas_call x1, Pallas kernels, share_rows_and_weights(): pl.pallas_call(lambda *refs: share_kernel(dp, tensor, *refs), out_shape=(...  155 us
    pallas_call x1, Pallas kernels, collect_grads(): pl.pallas_call(lambda *refs: gather_grads_kernel(dp, tensor, *refs), out_...  87.7 us
    ppermute x16, waiting for transfers between devices, hop(): return lax.ppermute(rows, 'dp', route)  57.7 us
    pallas_call x1, Pallas kernels, attend_back(): pl.pallas_call(bwd_kernel, out_shape=(jax.ShapeDtypeStruct((rows, width),...  51.7 us
    pallas_call x1, Pallas kernels, attend(): pl.pallas_call(fwd_kernel, out_shape=(jax.ShapeDtypeStruct((rows, width),...  44.2 us
    pallas_call x1, Pallas kernels, total_over_devices(): pl.pallas_call(lambda *refs: total_kernel(ways, tensor, *refs), out_shape...  28.6 us
    unnamed x139, local copies, waits for them, and re-layouts  28.2 us
    dot_general x3, matrix products, row_grad(): jnp.einsum('sc,dc->sd', row_grads, weight, preferred_element_type=jnp.flo...  27.7 us
  transfers between devices with their start and end apart: 18, of which 9 were waited for; matrix products, arithmetic and copies ran while one was open for 15% of the time, Pallas kernels for 29%

profile of v3, /device:TPU:0, one launch (start us, length us, event | category | flops | bytes accessed | tf_op | source)
XLA Modules:
  0.0 681.8 jit_solution(15278553841328358997)
XLA Ops:
  19.6 154.8 %share_rows_and_weights.1 = (bf16[3072,768]{1,0:T(8,128)(2,1)}, bf16[4,8,96,768]{3,2,1,0:T(8,128)(2,1)}) custom-call(bf16[1024,768]{1,0:T(8,128)(2,1)} %fusion.15.refs_0_, bf16[96,768]{1,0:T(8,128)(2,1)} %pad_maximum_fusion.3.refs_1_), custom_call_target="tpu_custom_call" | custom-call | tf_op jit(solution)/shard_map/share_rows_and_weights/pallas_call | solution.py:655
  174.4 12.9 %reshape.224 = bf16[4,768,4,192]{3,2,1,0:T(4,128)(2,1)} reshape(bf16[4,8,96,768]{3,2,1,0:T(8,128)(2,1)} %get-tuple-element.31) | data formatting | bytes 9437184 | tf_op jit(solution)/shard_map/reshape | solution.py:937
  187.3 10.3 %copy.95 = bf16[4,768,4,192]{1,3,2,0:T(8,128)(2,1)} copy(bf16[4,768,4,192]{3,2,1,0:T(4,128)(2,1)} %reshape.224) | data formatting | bytes 9437184 | tf_op jit(solution)/shard_map/reshape | solution.py:937
  197.6 3.8 fusion.85
  203.0 5.6 convolution_convert_fusion.v_ref
  208.7 5.5 convolution_convert_fusion.1.k_ref
  219.0 44.2 %attend_forward.1 = (bf16[1024,768]{1,0:T(8,128)(2,1)S(1)}, f32[6,2,1024]{2,1,0:T(2,128)S(1)}) custom-call(s32[5]{0:T(128)S(1)} %pad_add_fusion.meta_ref, bf16[1024,768]{1,0:T(8,128)(2,1)S(1)} %convolution_convert_fusion.5.q_ref, bf16[3072,768]{1,0:T(8,128)(2,1)S(1)} %copy-done.3, bf16[3072,768]{1,0:T(8,128)(2,1)S(1)} %copy-done.2), custom_call_target="tpu_custom_call" | custom-call | tf_op jit(solution)/shard_map/attend_forward/pallas_call | solution.py:107
  277.0 9.5 %collective-permute-done.2 = bf16[256,768]{1,0:T(8,128)(2,1)S(1)} collective-permute-done((bf16[256,768]{1,0:T(8,128)(2,1)S(1)}, bf16[256,768]{1,0:T(8,128)(2,1)S(1)}, u32[]{:S(2)}, u32[]{:S(2)}) %collective-permute-start.2) | collective-permute-done | bytes 393248 | tf_op jit(solution)/shard_map/ppermute | solution.py:915
  286.5 6.9 %collective-permute-done.1 = bf16[256,768]{1,0:T(8,128)(2,1)S(1)} collective-permute-done((bf16[256,768]{1,0:T(8,128)(2,1)S(1)}, bf16[256,768]{1,0:T(8,128)(2,1)S(1)}, u32[]{:S(2)}, u32[]{:S(2)}) %collective-permute-start.1) | collective-permute-done | bytes 393248 | tf_op jit(solution)/shard_map/ppermute | solution.py:915
  297.4 9.4 %collective-permute-done.10 = bf16[256,768]{1,0:T(8,128)(2,1)S(1)} collective-permute-done((bf16[256,768]{1,0:T(8,128)(2,1)S(1)}, bf16[256,768]{1,0:T(8,128)(2,1)S(1)}, u32[]{:S(2)}, u32[]{:S(2)}) %collective-permute-start.10) | collective-permute-done | bytes 393248 | tf_op jit(solution)/shard_map/ppermute | solution.py:915
  306.8 8.0 %collective-permute-done.9 = bf16[256,768]{1,0:T(8,128)(2,1)S(1)} collective-permute-done((bf16[256,768]{1,0:T(8,128)(2,1)S(1)}, bf16[256,768]{1,0:T(8,128)(2,1)S(1)}, u32[]{:S(2)}, u32[]{:S(2)}) %collective-permute-start.9) | collective-permute-done | bytes 393248 | tf_op jit(solution)/shard_map/ppermute | solution.py:915
  317.4 15.9 %expert_forward.1 = (bf16[2048,1536]{1,0:T(8,128)(2,1)}, bf16[2048,1536]{1,0:T(8,128)(2,1)}, f32[1024,768]{1,0:T(8,128)S(1)}, bf16[1024,768]{1,0:T(8,128)(2,1)}) custom-call(bf16[2048,768]{1,0:T(8,128)(2,1)S(1)} %constant_dynamic-update-slice_fusion.x_ref, bf16[768,1536]{1,0:T(8,128)(2,1)S(1)} %copy-done.12, bf16[1536,768]{1,0:T(8,128)(2,1)S(1)} %copy-done.14), custom_call_target="tpu_custom_call" | custom-call | flops 9663676416 | bytes 25165824 | tf_op jit(solution)/shard_map/expert_forward/pallas_call | solution.py:323
  335.5 9.3 %convolution_convert_fusion.2 = bf16[1536,768]{1,0:T(8,128)(2,1)} fusion(bf16[2048,1536]{1,0:T(8,128)(2,1)} %get-tuple-element.42, bf16[2048,768]{1,0:T(8,128)(2,1)S(1)} %constant_dynamic-update-slice_fusion.5.grad_ref), kind=kOutput, calls=%fused_computation.26 | convolution fusion | flops 4833017856 | bytes 11796480 | tf_op jit(solution)/shard_map/rf,rd->fd/dot_general | solution.py:990
  351.7 15.5 %expert_backward.1 = (bf16[2048,1536]{1,0:T(8,128)(2,1)}, f32[1024,768]{1,0:T(8,128)S(1)}, bf16[1024,768]{1,0:T(8,128)(2,1)S(1)}) custom-call(bf16[2048,768]{1,0:T(8,128)(2,1)S(1)} %copy-done.11, bf16[2048,1536]{1,0:T(8,128)(2,1)} %get-tuple-element.38.slope_ref, bf16[768,1536]{1,0:T(8,128)(2,1)S(1)} %copy-done.13, bf16[1536,768]{1,0:T(8,128)(2,1)S(1)} %copy-done.15), custom_call_target="tpu_custom_call" | custom-call | flops 9663676416 | bytes 25165824 | tf_op jit(solution)/shard_map/expert_backward/pallas_call | solution.py:348
  367.2 9.4 %convolution_convert_fusion.3 = bf16[768,1536]{1,0:T(8,128)(2,1)} fusion(bf16[2048,768]{1,0:T(8,128)(2,1)S(1)} %copy-done.9, bf16[2048,1536]{1,0:T(8,128)(2,1)} %get-tuple-element.41), kind=kOutput, calls=%fused_computation.27 | convolution fusion | flops 4833017856 | bytes 11796480 | tf_op jit(solution)/shard_map/rd,rf->df/dot_general | solution.py:994
  385.6 5.9 collective-permute-done.7
  392.9 7.0 %collective-permute-done.6 = bf16[256,768]{1,0:T(8,128)(2,1)S(1)} collective-permute-done((bf16[256,768]{1,0:T(8,128)(2,1)S(1)}, bf16[256,768]{1,0:T(8,128)(2,1)S(1)}, u32[]{:S(2)}, u32[]{:S(2)}) %collective-permute-start.6) | collective-permute-done | bytes 393248 | tf_op jit(solution)/shard_map/ppermute | solution.py:915
  402.6 2.8 fusion.70
  405.4 3.0 collective-permute-done.15
  408.3 7.9 %collective-permute-done.14 = bf16[256,768]{1,0:T(8,128)(2,1)S(1)} collective-permute-done((bf16[256,768]{1,0:T(8,128)(2,1)S(1)}, bf16[256,768]{1,0:T(8,128)(2,1)S(1)}, u32[]{:S(2)}, u32[]{:S(2)}) %collective-permute-start.14) | collective-permute-done | bytes 393248 | tf_op jit(solution)/shard_map/ppermute | solution.py:915
  423.8 4.3 copy.96
  429.2 4.8 convolution_convert_fusion.4.g_ref
  434.0 51.7 %attend_backward.1 = (bf16[1024,768]{1,0:T(8,128)(2,1)S(1)}, bf16[3072,768]{1,0:T(8,128)(2,1)}, bf16[3072,768]{1,0:T(8,128)(2,1)}) custom-call(s32[5]{0:T(128)S(1)} %pad_add_fusion.meta_ref, bf16[1024,768]{1,0:T(8,128)(2,1)S(1)} %convolution_convert_fusion.5.q_ref, bf16[3072,768]{1,0:T(8,128)(2,1)} %convolution_convert_fusion.1.k_ref, ...), custom_call_target="tpu_custom_call" | custom-call | tf_op jit(solution)/shard_map/attend_backward/pallas_call | solution.py:227
  488.2 9.6 %fusion.93 = f32[3072,768]{1,0:T(8,128)} fusion(bf16[3072,768]{1,0:T(8,128)(2,1)} %get-tuple-element.45, bf16[768,768]{0,1:T(8,128)(2,1)S(1)} %bitcast.67), kind=kOutput, calls=%fused_computation.162 | convolution fusion | flops 3623878656 | bytes 15335424 | tf_op jit(solution)/shard_map/sc,dc->sd/dot_general | solution.py:1025
  497.9 4.9 convolution_convert_fusion.8
  502.8 13.5 %convolution_add_fusion = f32[3072,768]{1,0:T(8,128)} fusion(f32[3072,768]{1,0:T(8,128)} %fusion.93, bf16[3072,768]{1,0:T(8,128)(2,1)} %get-tuple-element.46, bf16[768,768]{0,1:T(8,128)(2,1)} %bitcast.65), kind=kOutput, calls=%fused_computation.1 | convolution fusion | flops 3626237952 | bytes 24772608 | tf_op jit(solution)/shard_map/sc,dc->sd/dot_general | solution.py:1025
  520.0 4.9 slice.143.refs_0_
  527.8 4.3 convolution_convert_fusion.7
  534.7 87.7 %collect_grads.1 = (f32[1024,768]{1,0:T(8,128)}, f32[96,768]{1,0:T(8,128)}) custom-call(bf16[2048,768]{1,0:T(8,128)(2,1)} %slice.143.refs_0_, bf16[8,96,3072]{2,1,0:T(8,128)(2,1)} %pad_maximum_fusion.refs_1_), custom_call_target="tpu_custom_call" | custom-call | tf_op jit(solution)/shard_map/collect_grads/pallas_call | solution.py:824
  622.5 4.6 fusion.18
  631.1 28.6 %total_over_devices.1 = f32[32,8,128]{2,1,0:T(8,128)} custom-call(f32[32,8,128]{2,1,0:T(8,128)} %fusion.57.refs_0_), custom_call_target="tpu_custom_call" | custom-call | tf_op jit(solution)/shard_map/total_over_devices/pallas_call | solution.py:443
  665.5 4.6 add_add_fusion.2
  (246 shorter events, 95.5 us)
Async XLA Ops:
  7.2 259.3 %copy-start = (f32[768,16]{0,1:T(8,128)S(1)}, f32[768,16]{0,1:T(8,128)}, u32[]{:S(2)}) copy-start(f32[768,16]{0,1:T(8,128)} %param.18) | copy-start | bytes 147460
  7.2 662.9 %reduce-scatter.7.cloned.1.call-start = ((), (), s32[]{:S(2)}) async-start(), calls=%async_computation.3 | async-start | bytes 2949120
  14.0 160.3 %copy-start.38 = (f32[1024]{0:T(1024)}, f32[1024]{0:T(1024)S(1)}, u32[]{:S(2)}) copy-start(f32[1024]{0:T(1024)S(1)} %broadcast_multiply_fusion.1) | copy-start | bytes 12292
  16.7 170.6 %copy-start.44 = (f32[1024]{0:T(1024)}, f32[1024]{0:T(1024)S(1)}, u32[]{:S(2)}) copy-start(f32[1024]{0:T(1024)S(1)} %fusion.71) | copy-start | bytes 12292
  219.0 44.3 %copy-start.17 = (bf16[1024,768]{1,0:T(8,128)(2,1)S(1)}, bf16[1024,768]{1,0:T(8,128)(2,1)}, u32[]{:S(2)}) copy-start(bf16[1024,768]{1,0:T(8,128)(2,1)} %param.13) | copy-start | bytes 4718596
  219.0 44.3 %copy-start.34 = (bf16[1,768,4,192]{1,3,0,2:T(8,128)(2,1)S(1)}, bf16[1,768,4,192]{1,3,0,2:T(8,128)(2,1)}, u32[]{:S(2)}) copy-start(bf16[1,768,4,192]{1,3,0,2:T(8,128)(2,1)} %get-tuple-element.98) | copy-start | bytes 3538948
  273.5 13.0 %collective-permute-start.2 = (bf16[256,768]{1,0:T(8,128)(2,1)S(1)}, bf16[256,768]{1,0:T(8,128)(2,1)S(1)}, u32[]{:S(2)}, u32[]{:S(2)}) collective-permute-start(bf16[256,768]{1,0:T(8,128)(2,1)S(1)} %get-tuple-element.118), channel_id=1, source_target_pairs={{0,24},{4,28},{8,16},{12,20},{16,8},{20,12},{24,0},{28,4},{1,25},{... | collective-permute-start | bytes 1179656 | tf_op jit(solution)/shard_map/ppermute | solution.py:915
  276.0 17.5 %collective-permute-start.1 = (bf16[256,768]{1,0:T(8,128)(2,1)S(1)}, bf16[256,768]{1,0:T(8,128)(2,1)S(1)}, u32[]{:S(2)}, u32[]{:S(2)}) collective-permute-start(bf16[256,768]{1,0:T(8,128)(2,1)S(1)} %get-tuple-element.119), channel_id=1, source_target_pairs={{0,16},{4,20},{8,24},{12,28},{16,0},{20,4},{24,8},{28,12},{1,17},{... | collective-permute-start | bytes 1179656 | tf_op jit(solution)/shard_map/ppermute | solution.py:915
  276.5 17.0 %collective-permute-start = (bf16[256,768]{1,0:T(8,128)(2,1)S(1)}, bf16[256,768]{1,0:T(8,128)(2,1)S(1)}, u32[]{:S(2)}, u32[]{:S(2)}) collective-permute-start(bf16[256,768]{1,0:T(8,128)(2,1)S(1)} %get-tuple-element.120), channel_id=1, source_target_pairs={{0,8},{4,12},{8,0},{12,4},{16,24},{20,28},{24,16},{28,20},{1,9},{5... | collective-permute-start | bytes 1179656 | tf_op jit(solution)/shard_map/ppermute | solution.py:915
  293.7 21.6 %collective-permute-start.3 = (bf16[1024,768]{1,0:T(8,128)(2,1)S(1)}, bf16[1024,768]{1,0:T(8,128)(2,1)S(1)}, u32[]{:S(2)}, u32[]{:S(2)}) collective-permute-start(bf16[1024,768]{1,0:T(8,128)(2,1)S(1)} %pad_maximum_fusion.1), channel_id=1, source_target_pairs={{0,4},{4,0},{8,12},{12,8},{16,20},{20,16},{24,28},{28,24},{1,5},{5... | collective-permute-start | bytes 4718600 | tf_op jit(solution)/shard_map/ppermute | solution.py:915
  293.9 12.9 %collective-permute-start.10 = (bf16[256,768]{1,0:T(8,128)(2,1)S(1)}, bf16[256,768]{1,0:T(8,128)(2,1)S(1)}, u32[]{:S(2)}, u32[]{:S(2)}) collective-permute-start(bf16[256,768]{1,0:T(8,128)(2,1)S(1)} %get-tuple-element.109), channel_id=1, source_target_pairs={{0,24},{4,28},{8,16},{12,20},{16,8},{20,12},{24,0},{28,4},{1,25},{... | collective-permute-start | bytes 1179656 | tf_op jit(solution)/shard_map/ppermute | solution.py:915
  295.6 19.2 %collective-permute-start.9 = (bf16[256,768]{1,0:T(8,128)(2,1)S(1)}, bf16[256,768]{1,0:T(8,128)(2,1)S(1)}, u32[]{:S(2)}, u32[]{:S(2)}) collective-permute-start(bf16[256,768]{1,0:T(8,128)(2,1)S(1)} %get-tuple-element.110), channel_id=1, source_target_pairs={{0,16},{4,20},{8,24},{12,28},{16,0},{20,4},{24,8},{28,12},{1,17},{... | collective-permute-start | bytes 1179656 | tf_op jit(solution)/shard_map/ppermute | solution.py:915
  296.9 17.9 %collective-permute-start.8 = (bf16[256,768]{1,0:T(8,128)(2,1)S(1)}, bf16[256,768]{1,0:T(8,128)(2,1)S(1)}, u32[]{:S(2)}, u32[]{:S(2)}) collective-permute-start(bf16[256,768]{1,0:T(8,128)(2,1)S(1)} %get-tuple-element.111), channel_id=1, source_target_pairs={{0,8},{4,12},{8,0},{12,4},{16,24},{20,28},{24,16},{28,20},{1,9},{5... | collective-permute-start | bytes 1179656 | tf_op jit(solution)/shard_map/ppermute | solution.py:915
  314.9 20.5 %collective-permute-start.11 = (bf16[1024,768]{1,0:T(8,128)(2,1)S(1)}, bf16[1024,768]{1,0:T(8,128)(2,1)S(1)}, u32[]{:S(2)}, u32[]{:S(2)}) collective-permute-start(bf16[1024,768]{1,0:T(8,128)(2,1)S(1)} %pad_maximum_fusion.2), channel_id=1, source_target_pairs={{0,4},{4,0},{8,12},{12,8},{16,20},{20,16},{24,28},{28,24},{1,5},{5... | collective-permute-start | bytes 4718600 | tf_op jit(solution)/shard_map/ppermute | solution.py:915
  317.4 15.9 %copy-start.8 = (bf16[2048,768]{1,0:T(8,128)(2,1)}, bf16[2048,768]{1,0:T(8,128)(2,1)S(1)}, u32[]{:S(2)}) copy-start(bf16[2048,768]{1,0:T(8,128)(2,1)S(1)} %constant_dynamic-update-slice_fusion.x_ref) | copy-start | bytes 9437188
  334.9 41.7 %collective-permute-start.4 = (bf16[1024,768]{1,0:T(8,128)(2,1)}, bf16[1024,768]{1,0:T(8,128)(2,1)}, u32[]{:S(2)}, u32[]{:S(2)}) collective-permute-start(bf16[1024,768]{1,0:T(8,128)(2,1)} %get-tuple-element.36), channel_id=1, source_target_pairs={{0,4},{4,0},{8,12},{12,8},{16,20},{20,16},{24,28},{28,24},{1,5},{5... | collective-permute-start | bytes 4718600 | tf_op jit(solution)/shard_map/ppermute | solution.py:915
  367.1 14.9 %collective-permute-start.12 = (bf16[1024,768]{1,0:T(8,128)(2,1)S(1)}, bf16[1024,768]{1,0:T(8,128)(2,1)S(1)}, u32[]{:S(2)}, u32[]{:S(2)}) collective-permute-start(bf16[1024,768]{1,0:T(8,128)(2,1)S(1)} %get-tuple-element.40), channel_id=1, source_target_pairs={{0,4},{4,0},{8,12},{12,8},{16,20},{20,16},{24,28},{28,24},{1,5},{5... | collective-permute-start | bytes 4718600 | tf_op jit(solution)/shard_map/ppermute | solution.py:915
  378.5 12.9 %collective-permute-start.7 = (bf16[256,768]{1,0:T(8,128)(2,1)S(1)}, bf16[256,768]{1,0:T(8,128)(2,1)S(1)}, u32[]{:S(2)}, u32[]{:S(2)}) collective-permute-start(bf16[256,768]{1,0:T(8,128)(2,1)S(1)} %get-tuple-element.113), channel_id=1, source_target_pairs={{0,24},{4,28},{8,16},{12,20},{16,8},{20,12},{24,0},{28,4},{1,25},{... | collective-permute-start | bytes 1179656 | tf_op jit(solution)/shard_map/ppermute | solution.py:915
  380.2 19.7 %collective-permute-start.6 = (bf16[256,768]{1,0:T(8,128)(2,1)S(1)}, bf16[256,768]{1,0:T(8,128)(2,1)S(1)}, u32[]{:S(2)}, u32[]{:S(2)}) collective-permute-start(bf16[256,768]{1,0:T(8,128)(2,1)S(1)} %get-tuple-element.114), channel_id=1, source_target_pairs={{0,16},{4,20},{8,24},{12,28},{16,0},{20,4},{24,8},{28,12},{1,17},{... | collective-permute-start | bytes 1179656 | tf_op jit(solution)/shard_map/ppermute | solution.py:915
  381.5 18.4 %collective-permute-start.5 = (bf16[256,768]{1,0:T(8,128)(2,1)S(1)}, bf16[256,768]{1,0:T(8,128)(2,1)S(1)}, u32[]{:S(2)}, u32[]{:S(2)}) collective-permute-start(bf16[256,768]{1,0:T(8,128)(2,1)S(1)} %get-tuple-element.115), channel_id=1, source_target_pairs={{0,8},{4,12},{8,0},{12,4},{16,24},{20,28},{24,16},{28,20},{1,9},{5... | collective-permute-start | bytes 1179656 | tf_op jit(solution)/shard_map/ppermute | solution.py:915
  382.4 17.5 %copy-start.30 = (bf16[1024,768]{1,0:T(8,128)(2,1)S(1)}, bf16[1024,768]{1,0:T(8,128)(2,1)}, u32[]{:S(2)}) copy-start(bf16[1024,768]{1,0:T(8,128)(2,1)} %param.25) | copy-start | bytes 4718596
  382.6 25.8 %collective-permute-start.15 = (bf16[256,768]{1,0:T(8,128)(2,1)S(1)}, bf16[256,768]{1,0:T(8,128)(2,1)S(1)}, u32[]{:S(2)}, u32[]{:S(2)}) collective-permute-start(bf16[256,768]{1,0:T(8,128)(2,1)S(1)} %get-tuple-element.104), channel_id=1, source_target_pairs={{0,24},{4,28},{8,16},{12,20},{16,8},{20,12},{24,0},{28,4},{1,25},{... | collective-permute-start | bytes 1179656 | tf_op jit(solution)/shard_map/ppermute | solution.py:915
  384.3 32.0 %collective-permute-start.14 = (bf16[256,768]{1,0:T(8,128)(2,1)S(1)}, bf16[256,768]{1,0:T(8,128)(2,1)S(1)}, u32[]{:S(2)}, u32[]{:S(2)}) collective-permute-start(bf16[256,768]{1,0:T(8,128)(2,1)S(1)} %get-tuple-element.105), channel_id=1, source_target_pairs={{0,16},{4,20},{8,24},{12,28},{16,0},{20,4},{24,8},{28,12},{1,17},{... | collective-permute-start | bytes 1179656 | tf_op jit(solution)/shard_map/ppermute | solution.py:915
  391.5 24.8 %collective-permute-start.13 = (bf16[256,768]{1,0:T(8,128)(2,1)S(1)}, bf16[256,768]{1,0:T(8,128)(2,1)S(1)}, u32[]{:S(2)}, u32[]{:S(2)}) collective-permute-start(bf16[256,768]{1,0:T(8,128)(2,1)S(1)} %get-tuple-element.106), channel_id=1, source_target_pairs={{0,8},{4,12},{8,0},{12,4},{16,24},{20,28},{24,16},{28,20},{1,9},{5... | collective-permute-start | bytes 1179656 | tf_op jit(solution)/shard_map/ppermute | solution.py:915
  428.1 244.4 %reduce-scatter.5.cloned.1.call-start = ((), (), s32[]{:S(2)}) async-start(), calls=%async_computation.2 | async-start | bytes 2949120 | tf_op jit(solution)/shard_map/reduce_scatter | solution.py:1009
  434.0 51.7 %copy-start.26 = (bf16[1024,768]{1,0:T(8,128)(2,1)S(1)}, bf16[1024,768]{1,0:T(8,128)(2,1)}, u32[]{:S(2)}) copy-start(bf16[1024,768]{1,0:T(8,128)(2,1)} %fusion.15.refs_0_) | copy-start | bytes 4718596
  534.6 87.8 %copy-start.7 = (bf16[1024,768]{1,0:T(8,128)(2,1)S(1)}, bf16[1024,768]{1,0:T(8,128)(2,1)}, u32[]{:S(2)}) copy-start(bf16[1024,768]{1,0:T(8,128)(2,1)} %copy-done.6) | copy-start | bytes 4718596
  534.6 87.8 %copy-start.18 = (bf16[1024,768]{1,0:T(8,128)(2,1)S(1)}, bf16[1024,768]{1,0:T(8,128)(2,1)}, u32[]{:S(2)}) copy-start(bf16[1024,768]{1,0:T(8,128)(2,1)} %param.13) | copy-start | bytes 4718596
  534.6 87.8 %copy-start.28 = (bf16[1,768,4,192]{1,3,0,2:T(8,128)(2,1)S(1)}, bf16[1,768,4,192]{1,3,0,2:T(8,128)(2,1)}, u32[]{:S(2)}) copy-start(bf16[1,768,4,192]{1,3,0,2:T(8,128)(2,1)} %copy-done.27) | copy-start | bytes 3538948
  534.7 87.8 %copy-start.39 = (f32[1024]{0:T(1024)S(1)}, f32[1024]{0:T(1024)}, u32[]{:S(2)}) copy-start(f32[1024]{0:T(1024)} %copy-done.38) | copy-start | bytes 12292
  534.7 87.8 %copy-start.43 = (f32[768]{0:T(1024)S(1)}, f32[768]{0:T(1024)}, u32[]{:S(2)}) copy-start(f32[768]{0:T(1024)} %param.14) | copy-start | bytes 9220
  628.8 32.8 %copy-start.37 = (f32[96,768]{1,0:T(8,128)S(1)}, f32[96,768]{1,0:T(8,128)}, u32[]{:S(2)}) copy-start(f32[96,768]{1,0:T(8,128)} %get-tuple-element.49) | copy-start | bytes 884740
  (49 other events, 257.7 us)
Sparse Core Ops, SparseCore 0:
  428.3 45.4 reduce-scatter.6
  502.9 49.5 reduce-scatter.4

commit v4 on v3

--- a/solution.py
+++ b/solution.py
@@ -467,14 +467,15 @@
     pl.semaphore_wait(barrier, len(peers))
 
 
-def share_kernel(dp, tensor, own_ref, block_ref, seen_ref, weights_ref,
-                 row_send, row_recv, copy_sem, block_sem,
+def share_kernel(dp, tensor, own_ref, block_ref, seen_ref, out_ref, weights_ref,
+                 row_send, row_recv,
                  line_send, line_recv, chip_send, chip_recv, pair_send, pair_recv):
     spot, place = lax.axis_index("dp"), lax.axis_index("tensor")
     chip, core = spot // 2, lax.rem(spot, 2)
     chips = dp // 2
     rows = own_ref.shape[0]
     pieces = rows // PIECE
+    part_width = out_ref.shape[2] // tensor
     partner = (chip * 2 + 1 - core, place)
 
     def along(step):
@@ -489,14 +490,6 @@
         + [partner]
     )
 
-    def keep(part):
-        return pltpu.make_async_copy(
-            own_ref, seen_ref.at[pl.ds(part * rows, rows)], copy_sem.at[part]
-        )
-
-    def keep_block():
-        return pltpu.make_async_copy(block_ref, weights_ref.at[place, spot], block_sem)
-
     def pass_on(part, piece, fresh):
         at = pl.ds(part * rows + piece * PIECE, PIECE)
         source = own_ref.at[pl.ds(piece * PIECE, PIECE)] if fresh else seen_ref.at[at]
@@ -545,17 +538,6 @@
             send_sem=pair_send.at[part, source], recv_sem=pair_recv.at[part, source],
             device_id=partner, device_id_type=MESH,
         )
-
-    keep_block().start()
-    keep(2).start()
-
-    @pl.when(place < 2)
-    def _():
-        keep(1).start()
-
-    @pl.when(place == 0)
-    def _():
-        keep(0).start()
 
     for step in range(1, tensor):
         line(step).start()
@@ -587,8 +569,18 @@
             def _():
                 pass_on(1, piece, False).start()
 
+    weights_ref[place, spot] = block_ref[...]
+    seen_ref[2 * rows :] = own_ref[...]
+
+    @pl.when(place < 2)
+    def _():
+        seen_ref[rows : 2 * rows] = own_ref[...]
+
+    @pl.when(place == 0)
+    def _():
+        seen_ref[0:rows] = own_ref[...]
+
     row_steps(0, pieces // 4)
-    keep_block().wait()
     for step in range(tensor):
         part = along(tensor - step)
         if step:
@@ -635,40 +627,49 @@
         def _(piece):
             pass_on(1, piece, False).wait_send()
 
-    keep(2).wait()
-
-    @pl.when(place < 2)
-    def _():
-        keep(1).wait()
-
-    @pl.when(place == 0)
-    def _():
-        keep(0).wait()
+    @pl.loop(0, dp)
+    def _(source):
+        depth = block_ref.shape[0]
+        at = pl.ds(pl.multiple_of(source * depth, depth), depth)
+        for kind in range(out_ref.shape[0]):
+            cols = slice(kind * part_width, (kind + 1) * part_width)
+            out_ref[kind, at] = jnp.concatenate(
+                [weights_ref[part, source][:, cols] for part in range(tensor)], axis=1
+            )
 
 
 def share_rows_and_weights(own, block):
     dp, tensor = lax.axis_size("dp"), lax.axis_size("tensor")
     rows, width = own.shape
+    depth, cols = block.shape
     pieces, chips = rows // PIECE, dp // 2
+    kinds = cols * tensor // width
+    padded = -(-depth // 16) * 16
+    block = jnp.pad(block, ((0, padded - depth), (0, 0)))
     dma = pltpu.SemaphoreType.DMA
-    anywhere = pl.BlockSpec(memory_space=pl.ANY)
-    return pl.pallas_call(
+    here = pl.BlockSpec(memory_space=pltpu.VMEM)
+    seen, weights = pl.pallas_call(
         lambda *refs: share_kernel(dp, tensor, *refs),
         out_shape=(
             jax.ShapeDtypeStruct((3 * rows, width), own.dtype),
-            jax.ShapeDtypeStruct((tensor, dp) + block.shape, block.dtype),
-        ),
-        in_specs=[anywhere, anywhere],
-        out_specs=[anywhere, anywhere],
+            jax.ShapeDtypeStruct((kinds, dp * padded, width), block.dtype),
+        ),
+        in_specs=[here, here],
+        out_specs=[here, here],
         scratch_shapes=[
-            dma((2, pieces)), dma((2, pieces)), dma((3,)), dma,
+            pltpu.VMEM((tensor, dp, padded, cols), block.dtype),
+            dma((2, pieces)), dma((2, pieces)),
             dma((tensor,)), dma((tensor,)),
             dma((tensor, chips)), dma((tensor, chips)),
             dma((tensor, chips)), dma((tensor, chips)),
         ],
-        compiler_params=pltpu.CompilerParams(collective_id=2, has_side_effects=True),
+        compiler_params=pltpu.CompilerParams(
+            collective_id=2, has_side_effects=True, vmem_limit_bytes=48 << 20
+        ),
         name="share_rows_and_weights",
     )(own, block)
+    weights = weights.reshape(kinds, dp, padded, width)[:, :, :depth]
+    return seen, weights.reshape(kinds, dp * depth, width)
 
 
 def gather_grads_kernel(dp, tensor, rows_ref, grads_ref, out_ref, sum_ref,
@@ -914,18 +915,19 @@
             route.append((source, (chip ^ chip_step) * 2 + (core ^ core_step)))
         return lax.ppermute(rows, "dp", route)
 
+    def chip_blocks(rows):
+        blocks = rows.reshape(experts, capacity, model_width)
+        return [blocks[0]] + [hop(blocks[step], step, 0) for step in range(1, experts)]
+
     def across_chips(rows):
-        blocks = rows.reshape(experts, capacity, model_width)
-        moved = [blocks[0]] + [hop(blocks[step], step, 0) for step in range(1, experts)]
-        return jnp.concatenate(moved, axis=0)
-
-    def dispatch(slot_input):
-        arrived = across_chips(slot_input)
+        return jnp.concatenate(chip_blocks(rows), axis=0)
+
+    def with_partner(blocks):
+        arrived = jnp.concatenate(blocks, axis=0)
         return jnp.concatenate([arrived, hop(arrived, 0, 1)], axis=0)
 
-    def combine(kept_rows, sent_rows):
-        paired = (kept_rows + hop(sent_rows, 0, 1).astype(jnp.float32)).astype(jnp.bfloat16)
-        return across_chips(paired)
+    def pair_sum(kept_rows, sent_rows):
+        return (kept_rows + hop(sent_rows, 0, 1).astype(jnp.float32)).astype(jnp.bfloat16)
 
     hidden = tokens.astype(jnp.float32)
     normed_in, norm1_back = jax.vjp(layer_norm, hidden, norm1_gain)
@@ -934,8 +936,6 @@
     seen_in, weights = share_rows_and_weights(
         own_in, jnp.concatenate([flat_qkv, attn_proj.T], axis=1)
     )
-    weights = weights.reshape(tensor_size, model_width, 4, model_width // tensor_size)
-    weights = weights.transpose(2, 1, 0, 3).reshape(4, model_width, model_width)
     query_weight, key_weight, value_weight, proj_back = weights
     query_rows = low_dot(own_in, query_weight)
     key_rows = low_dot(seen_in, key_weight)
@@ -976,25 +976,30 @@
         return jnp.dot(select, slot_rows, preferred_element_type=jnp.float32)
 
     upstream = cotangent.astype(jnp.float32)
-    slot_rows, slot_grads = lax.optimization_barrier(
-        (
-            to_slots(moe_in),
-            to_slots((gate_value[:, None] * upstream).astype(jnp.bfloat16)),
-        )
-    )
-    expert_rows = dispatch(slot_rows)
-    arrived_grad = dispatch(slot_grads)
+    slot_grads = to_slots((gate_value[:, None] * upstream).astype(jnp.bfloat16))
+    row_blocks, slot_grads = lax.optimization_barrier(
+        (chip_blocks(to_slots(moe_in)), slot_grads)
+    )
+    grad_blocks = chip_blocks(slot_grads)
+    expert_rows = with_partner(row_blocks)
     active, slope, kept_result, sent_result = expert_forward(expert_rows, expert_in, expert_out)
-    expert_result = from_slots(combine(kept_result, sent_result))
+    grad_blocks, kept_result, sent_result = lax.optimization_barrier(
+        (grad_blocks, kept_result, sent_result)
+    )
+    arrived_grad = with_partner(grad_blocks)
+    result_rows, late_grad = lax.optimization_barrier(
+        (pair_sum(kept_result, sent_result), arrived_grad)
+    )
+    expert_result = from_slots(across_chips(result_rows))
     output = (mid_stream + gate_value[:, None] * expert_result).astype(jnp.bfloat16)
     out_weight_grad = jnp.einsum(
         "rf,rd->fd", active, arrived_grad, preferred_element_type=jnp.float32
     ).astype(jnp.bfloat16)
-    up_grad, kept_grad, sent_grad = expert_back(arrived_grad, slope, expert_in, expert_out)
+    up_grad, kept_grad, sent_grad = expert_back(late_grad, slope, expert_in, expert_out)
     in_weight_grad = jnp.einsum(
         "rd,rf->df", expert_rows, up_grad, preferred_element_type=jnp.float32
     ).astype(jnp.bfloat16)
-    moe_grad = from_slots(combine(kept_grad, sent_grad))
+    moe_grad = from_slots(across_chips(pair_sum(kept_grad, sent_grad)))
     gate_grad = jnp.sum(upstream * expert_result, axis=-1)
     router_part, proj_grad, embed_grad = gate_back(gate_grad)
     mid_part, gain2_grad = norm2_back(moe_grad + router_part)

time: 691 us -> 607 us (0.88)
  local copies, waits for them, and re-layouts: 66.2 us -> 34.8 us
  waiting for transfers between devices: 57.7 us -> 31.6 us
  Pallas kernels: 398 us -> 385 us
  other arithmetic: 32.3 us -> 25.2 us
    pallas_call x1, Pallas kernels: 155 us -> 54.4 us  [share_rows_and_weights(): pl.pallas_call(lambda *refs: share_kernel(dp, tensor, *refs), out_shape=(...]
    pallas_call x1, Pallas kernels: 87.7 us -> 173 us  [collect_grads(): pl.pallas_call(lambda *refs: gather_grads_kernel(dp, tensor, *refs), out_...]
    ppermute x16, waiting for transfers between devices: 57.7 us -> 31.6 us  [hop(): return lax.ppermute(rows, 'dp', route)]
    reshape x2 -> x0, local copies, waits for them, and re-layouts: 23.3 us -> none  [shards(): weights.reshape(tensor_size, model_width, 4, model_width // tensor_size)]
    unnamed x139 -> x127, local copies, waits for them, and re-layouts: 28.2 us -> 22.3 us
  transfers between devices with their start and end apart: 18 -> 18, of which waited for: 9 -> 7; matrix products, arithmetic and copies ran while one was open for 15% -> 16% of each run, Pallas kernels for 29% -> 47%
where the time goes in v4:
time: 607 us; the launch traced here: 604 us
  Pallas kernels  385 us (63%)
  matrix products  97.9 us (16%)
  local copies, waits for them, and re-layouts  34.8 us (6%)
  waiting for transfers between devices  31.6 us (5%)
  other arithmetic  25.2 us (4%)
  between operations  15.2 us (3%)
  starting transfers between devices  14.9 us (2%)
    pallas_call x1, Pallas kernels, collect_grads(): pl.pallas_call(lambda *refs: gather_grads_kernel(dp, tensor, *refs), out_...  173 us
    pallas_call x1, Pallas kernels, share_rows_and_weights(): pl.pallas_call(lambda *refs: share_kernel(dp, tensor, *refs), out_shape=(...  54.4 us
    pallas_call x1, Pallas kernels, attend_back(): pl.pallas_call(bwd_kernel, out_shape=(jax.ShapeDtypeStruct((rows, width),...  52.2 us
    pallas_call x1, Pallas kernels, attend(): pl.pallas_call(fwd_kernel, out_shape=(jax.ShapeDtypeStruct((rows, width),...  44.5 us
    ppermute x16, waiting for transfers between devices, hop(): return lax.ppermute(rows, 'dp', route)  31.6 us
    pallas_call x1, Pallas kernels, total_over_devices(): pl.pallas_call(lambda *refs: total_kernel(ways, tensor, *refs), out_shape...  28.8 us
    dot_general x3, matrix products, row_grad(): jnp.einsum('sc,dc->sd', row_grads, weight, preferred_element_type=jnp.flo...  23.4 us
    unnamed x127, local copies, waits for them, and re-layouts  22.3 us
  transfers between devices with their start and end apart: 18, of which 7 were waited for; matrix products, arithmetic and copies ran while one was open for 16% of the time, Pallas kernels for 47%

profile of v4, /device:TPU:0, one launch (start us, length us, event | category | flops | bytes accessed | tf_op | source)
XLA Modules:
  0.0 604.1 jit_solution(9560010694848782012)
XLA Ops:
  12.6 54.4 %share_rows_and_weights.1 = (bf16[3072,768]{1,0:T(8,128)(2,1)}, bf16[4,768,768]{2,1,0:T(8,128)(2,1)}) custom-call(bf16[1024,768]{1,0:T(8,128)(2,1)S(1)} %fusion.15.refs_0_, bf16[96,768]{1,0:T(8,128)(2,1)S(1)} %pad_maximum_fusion.3.refs_1_), custom_call_target="tpu_custom_call" | custom-call | tf_op jit(solution)/shard_map/share_rows_and_weights/pallas_call | solution.py:651
  67.0 8.9 %convolution_convert_fusion.v_ref = bf16[3072,768]{1,0:T(8,128)(2,1)} fusion(bf16[3072,768]{1,0:T(8,128)(2,1)} %get-tuple-element.43, bf16[4,768,768]{2,1,0:T(8,128)(2,1)} %get-tuple-element.42), kind=kOutput, calls=%fused_computation.2 | convolution fusion | flops 3626237952 | bytes 10616832 | tf_op jit(solution)/shard_map/dot_general | solution.py:886
  75.9 5.5 convolution_convert_fusion.1.k_ref
  88.8 44.5 %attend_forward.1 = (bf16[1024,768]{1,0:T(8,128)(2,1)S(1)}, f32[6,2,1024]{2,1,0:T(2,128)S(1)}) custom-call(s32[5]{0:T(128)S(1)} %pad_add_fusion.meta_ref, bf16[1024,768]{1,0:T(8,128)(2,1)S(1)} %convolution_convert_fusion.5.q_ref, bf16[3072,768]{1,0:T(8,128)(2,1)S(1)} %copy-done.3, bf16[3072,768]{1,0:T(8,128)(2,1)S(1)} %copy-done.2), custom_call_target="tpu_custom_call" | custom-call | tf_op jit(solution)/shard_map/attend_forward/pallas_call | solution.py:107
  133.3 3.4 fusion.107
  146.5 2.6 fusion.36
  149.1 4.1 collective-permute-done
  153.2 7.6 %collective-permute-done.1 = bf16[256,768]{1,0:T(8,128)(2,1)S(1)} collective-permute-done((bf16[256,768]{1,0:T(8,128)(2,1)S(1)}, bf16[256,768]{1,0:T(8,128)(2,1)S(1)}, u32[]{:S(2)}, u32[]{:S(2)}) %collective-permute-start.1) | collective-permute-done | bytes 393248 | tf_op jit(solution)/shard_map/ppermute | solution.py:916
  165.6 16.0 %expert_forward.1 = (bf16[2048,1536]{1,0:T(8,128)(2,1)}, bf16[2048,1536]{1,0:T(8,128)(2,1)}, f32[1024,768]{1,0:T(8,128)S(1)}, bf16[1024,768]{1,0:T(8,128)(2,1)S(1)}) custom-call(bf16[2048,768]{1,0:T(8,128)(2,1)S(1)} %constant_dynamic-update-slice_fusion.x_ref, bf16[768,1536]{1,0:T(8,128)(2,1)S(1)} %copy-done.13, bf16[1536,768]{1,0:T(8,128)(2,1)S(1)} %copy-done.15), custom_call_target="tpu_custom_call" | custom-call | flops 9663676416 | bytes 25165824 | tf_op jit(solution)/shard_map/expert_forward/pallas_call | solution.py:323
  182.8 2.8 collective-permute-done.8
  192.9 6.7 %convolution_convert_fusion.2 = bf16[1536,768]{1,0:T(8,128)(2,1)} fusion(bf16[2048,1536]{1,0:T(8,128)(2,1)S(1)} %bitcast.98, bf16[2048,768]{1,0:T(8,128)(2,1)S(1)} %constant_dynamic-update-slice_fusion.5.grad_ref), kind=kOutput, calls=%fused_computation.26 | convolution fusion | flops 4833017856 | bytes 11796480 | tf_op jit(solution)/shard_map/rf,rd->fd/dot_general | solution.py:995
  204.9 15.6 %expert_backward.1 = (bf16[2048,1536]{1,0:T(8,128)(2,1)}, f32[1024,768]{1,0:T(8,128)S(1)}, bf16[1024,768]{1,0:T(8,128)(2,1)S(1)}) custom-call(bf16[2048,768]{1,0:T(8,128)(2,1)S(1)} %copy-done.12, bf16[2048,1536]{1,0:T(8,128)(2,1)} %get-tuple-element.60.slope_ref, bf16[768,1536]{1,0:T(8,128)(2,1)S(1)} %copy-done.14, bf16[1536,768]{1,0:T(8,128)(2,1)S(1)} %copy-done.16), custom_call_target="tpu_custom_call" | custom-call | flops 9663676416 | bytes 25165824 | tf_op jit(solution)/shard_map/expert_backward/pallas_call | solution.py:348
  220.5 9.3 %convolution_convert_fusion.3 = bf16[768,1536]{1,0:T(8,128)(2,1)} fusion(bf16[2048,768]{1,0:T(8,128)(2,1)S(1)} %copy-done.10, bf16[2048,1536]{1,0:T(8,128)(2,1)} %get-tuple-element.63), kind=kOutput, calls=%fused_computation.27 | convolution fusion | flops 4833017856 | bytes 11796480 | tf_op jit(solution)/shard_map/rd,rf->df/dot_general | solution.py:999
  229.8 3.4 fusion.20
  237.7 2.7 fusion.87
  240.4 5.7 collective-permute-done.13
  246.2 8.8 %collective-permute-done.14 = bf16[256,768]{1,0:T(8,128)(2,1)S(1)} collective-permute-done((bf16[256,768]{1,0:T(8,128)(2,1)S(1)}, bf16[256,768]{1,0:T(8,128)(2,1)S(1)}, u32[]{:S(2)}, u32[]{:S(2)}) %collective-permute-start.14) | collective-permute-done | bytes 393248 | tf_op jit(solution)/shard_map/ppermute | solution.py:916
  255.0 2.5 multiply_reduce_fusion
  257.5 2.5 fusion.101
  262.1 4.3 copy.92
  266.5 3.9 fusion.86
  273.2 5.0 convolution_convert_fusion.4.g_ref
  278.1 52.2 %attend_backward.1 = (bf16[1024,768]{1,0:T(8,128)(2,1)S(1)}, bf16[3072,768]{1,0:T(8,128)(2,1)}, bf16[3072,768]{1,0:T(8,128)(2,1)}) custom-call(s32[5]{0:T(128)S(1)} %pad_add_fusion.meta_ref, bf16[1024,768]{1,0:T(8,128)(2,1)S(1)} %convolution_convert_fusion.5.q_ref, bf16[3072,768]{1,0:T(8,128)(2,1)} %convolution_convert_fusion.1.k_ref, ...), custom_call_target="tpu_custom_call" | custom-call | tf_op jit(solution)/shard_map/attend_backward/pallas_call | solution.py:227
  330.3 9.4 %fusion.59 = f32[3072,768]{1,0:T(8,128)} fusion(bf16[3072,768]{1,0:T(8,128)(2,1)} %get-tuple-element.67, bf16[4,768,768]{2,1,0:T(8,128)(2,1)S(1)} %bitcast.79), kind=kOutput, calls=%fused_computation.82 | convolution fusion | flops 3623878656 | bytes 15335424 | tf_op jit(solution)/shard_map/sc,dc->sd/dot_general | solution.py:1030
  339.8 5.1 convolution_convert_fusion.8
  344.8 9.1 %convolution_add_fusion = f32[3072,768]{1,0:T(8,128)} fusion(f32[3072,768]{1,0:T(8,128)} %fusion.59, bf16[3072,768]{1,0:T(8,128)(2,1)S(1)} %copy-done.45, bf16[4,768,768]{2,1,0:T(8,128)(2,1)S(1)} %bitcast.79), kind=kOutput, calls=%fused_computation.1 | convolution fusion | flops 3626237952 | bytes 24772608 | tf_op jit(solution)/shard_map/sc,dc->sd/dot_general | solution.py:1030
  355.4 4.9 slice.137.refs_0_
  362.1 6.4 %convolution_convert_fusion.7 = bf16[768,768]{1,0:T(8,128)(2,1)S(1)} fusion(bf16[3072,768]{1,0:T(8,128)(2,1)S(1)} %bitcast.96, bf16[3072,768]{1,0:T(8,128)(2,1)} %get-tuple-element.68), kind=kOutput, calls=%fused_computation.75 | convolution fusion | flops 3624468480 | bytes 10616832 | tf_op jit(solution)/shard_map/sd,sc->dc/dot_general | solution.py:1027
  371.0 173.1 %collect_grads.1 = (f32[1024,768]{1,0:T(8,128)}, f32[96,768]{1,0:T(8,128)}) custom-call(bf16[2048,768]{1,0:T(8,128)(2,1)} %slice.137.refs_0_, bf16[8,96,3072]{2,1,0:T(8,128)(2,1)} %pad_maximum_fusion.refs_1_), custom_call_target="tpu_custom_call" | custom-call | tf_op jit(solution)/shard_map/collect_grads/pallas_call | solution.py:825
  544.2 5.0 fusion.18
  553.2 28.8 %total_over_devices.1 = f32[32,8,128]{2,1,0:T(8,128)} custom-call(f32[32,8,128]{2,1,0:T(8,128)} %fusion.74.refs_0_), custom_call_target="tpu_custom_call" | custom-call | tf_op jit(solution)/shard_map/total_over_devices/pallas_call | solution.py:443
  587.8 4.6 add_add_fusion.2
  (230 shorter events, 70.2 us)
Async XLA Ops:
  7.2 137.5 %copy-start = (f32[768,16]{0,1:T(8,128)S(1)}, f32[768,16]{0,1:T(8,128)}, u32[]{:S(2)}) copy-start(f32[768,16]{0,1:T(8,128)} %param.18) | copy-start | bytes 147460
  7.2 585.2 %reduce-scatter.7.cloned.1.call-start = ((), (), s32[]{:S(2)}) async-start(), calls=%async_computation.3 | async-start | bytes 2949120
  11.1 64.8 %copy-start.35 = (f32[1024]{0:T(1024)}, f32[1024]{0:T(1024)S(1)}, u32[]{:S(2)}) copy-start(f32[1024]{0:T(1024)S(1)} %fusion.88) | copy-start | bytes 12292
  88.8 44.5 %copy-start.18 = (bf16[1024,768]{1,0:T(8,128)(2,1)S(1)}, bf16[1024,768]{1,0:T(8,128)(2,1)}, u32[]{:S(2)}) copy-start(bf16[1024,768]{1,0:T(8,128)(2,1)} %param.13) | copy-start | bytes 4718596
  141.1 12.1 %collective-permute-start = (bf16[256,768]{1,0:T(8,128)(2,1)S(1)}, bf16[256,768]{1,0:T(8,128)(2,1)S(1)}, u32[]{:S(2)}, u32[]{:S(2)}) collective-permute-start(bf16[256,768]{1,0:T(8,128)(2,1)S(1)} %get-tuple-element.135), channel_id=1, source_target_pairs={{0,8},{4,12},{8,0},{12,4},{16,24},{20,28},{24,16},{28,20},{1,9},{5... | collective-permute-start | bytes 1179656 | tf_op jit(solution)/shard_map/ppermute | solution.py:916
  142.6 18.1 %collective-permute-start.1 = (bf16[256,768]{1,0:T(8,128)(2,1)S(1)}, bf16[256,768]{1,0:T(8,128)(2,1)S(1)}, u32[]{:S(2)}, u32[]{:S(2)}) collective-permute-start(bf16[256,768]{1,0:T(8,128)(2,1)S(1)} %get-tuple-element.134), channel_id=1, source_target_pairs={{0,16},{4,20},{8,24},{12,28},{16,0},{20,4},{24,8},{28,12},{1,17},{... | collective-permute-start | bytes 1179656 | tf_op jit(solution)/shard_map/ppermute | solution.py:916
  144.2 16.6 %collective-permute-start.2 = (bf16[256,768]{1,0:T(8,128)(2,1)S(1)}, bf16[256,768]{1,0:T(8,128)(2,1)S(1)}, u32[]{:S(2)}, u32[]{:S(2)}) collective-permute-start(bf16[256,768]{1,0:T(8,128)(2,1)S(1)} %get-tuple-element.133), channel_id=1, source_target_pairs={{0,24},{4,28},{8,16},{12,20},{16,8},{20,12},{24,0},{28,4},{1,25},{... | collective-permute-start | bytes 1179656 | tf_op jit(solution)/shard_map/ppermute | solution.py:916
  160.9 3.9 collective-permute-start.6
  161.1 20.5 %collective-permute-start.3 = (bf16[256,768]{1,0:T(8,128)(2,1)S(1)}, bf16[256,768]{1,0:T(8,128)(2,1)S(1)}, u32[]{:S(2)}, u32[]{:S(2)}) collective-permute-start(bf16[256,768]{1,0:T(8,128)(2,1)S(1)} %get-tuple-element.131), channel_id=1, source_target_pairs={{0,8},{4,12},{8,0},{12,4},{16,24},{20,28},{24,16},{28,20},{1,9},{5... | collective-permute-start | bytes 1179656 | tf_op jit(solution)/shard_map/ppermute | solution.py:916
  162.4 19.2 %collective-permute-start.4 = (bf16[256,768]{1,0:T(8,128)(2,1)S(1)}, bf16[256,768]{1,0:T(8,128)(2,1)S(1)}, u32[]{:S(2)}, u32[]{:S(2)}) collective-permute-start(bf16[256,768]{1,0:T(8,128)(2,1)S(1)} %get-tuple-element.130), channel_id=1, source_target_pairs={{0,16},{4,20},{8,24},{12,28},{16,0},{20,4},{24,8},{28,12},{1,17},{... | collective-permute-start | bytes 1179656 | tf_op jit(solution)/shard_map/ppermute | solution.py:916
  163.2 18.8 %collective-permute-start.5 = (bf16[256,768]{1,0:T(8,128)(2,1)S(1)}, bf16[256,768]{1,0:T(8,128)(2,1)S(1)}, u32[]{:S(2)}, u32[]{:S(2)}) collective-permute-start(bf16[256,768]{1,0:T(8,128)(2,1)S(1)} %get-tuple-element.129), channel_id=1, source_target_pairs={{0,24},{4,28},{8,16},{12,20},{16,8},{20,12},{24,0},{28,4},{1,25},{... | collective-permute-start | bytes 1179656 | tf_op jit(solution)/shard_map/ppermute | solution.py:916
  165.6 16.0 %copy-start.9 = (bf16[2048,768]{1,0:T(8,128)(2,1)}, bf16[2048,768]{1,0:T(8,128)(2,1)S(1)}, u32[]{:S(2)}) copy-start(bf16[2048,768]{1,0:T(8,128)(2,1)S(1)} %constant_dynamic-update-slice_fusion.x_ref) | copy-start | bytes 9437188
  182.1 3.5 collective-permute-start.8
  182.2 5.6 collective-permute-start.7
  189.4 40.4 %collective-permute-start.10 = (bf16[256,768]{1,0:T(8,128)(2,1)}, bf16[256,768]{1,0:T(8,128)(2,1)}, u32[]{:S(2)}, u32[]{:S(2)}) collective-permute-start(bf16[256,768]{1,0:T(8,128)(2,1)} %get-tuple-element.127), channel_id=1, source_target_pairs={{0,16},{4,20},{8,24},{12,28},{16,0},{20,4},{24,8},{28,12},{1,17},{... | collective-permute-start | bytes 1179656 | tf_op jit(solution)/shard_map/ppermute | solution.py:916
  190.2 39.6 %collective-permute-start.11 = (bf16[256,768]{1,0:T(8,128)(2,1)}, bf16[256,768]{1,0:T(8,128)(2,1)}, u32[]{:S(2)}, u32[]{:S(2)}) collective-permute-start(bf16[256,768]{1,0:T(8,128)(2,1)} %get-tuple-element.126), channel_id=1, source_target_pairs={{0,24},{4,28},{8,16},{12,20},{16,8},{20,12},{24,0},{28,4},{1,25},{... | collective-permute-start | bytes 1179656 | tf_op jit(solution)/shard_map/ppermute | solution.py:916
  191.9 37.9 %collective-permute-start.9 = (bf16[256,768]{1,0:T(8,128)(2,1)}, bf16[256,768]{1,0:T(8,128)(2,1)}, u32[]{:S(2)}, u32[]{:S(2)}) collective-permute-start(bf16[256,768]{1,0:T(8,128)(2,1)} %get-tuple-element.128), channel_id=1, source_target_pairs={{0,8},{4,12},{8,0},{12,4},{16,24},{20,28},{24,16},{28,20},{1,9},{5... | collective-permute-start | bytes 1179656 | tf_op jit(solution)/shard_map/ppermute | solution.py:916
  204.9 15.6 %copy-start.10 = (bf16[2048,768]{1,0:T(8,128)(2,1)S(1)}, bf16[2048,768]{1,0:T(8,128)(2,1)}, u32[]{:S(2)}) copy-start(bf16[2048,768]{1,0:T(8,128)(2,1)} %copy-done.9) | copy-start | bytes 9437188
  220.4 13.2 %collective-permute-start.12 = (bf16[1024,768]{1,0:T(8,128)(2,1)S(1)}, bf16[1024,768]{1,0:T(8,128)(2,1)S(1)}, u32[]{:S(2)}, u32[]{:S(2)}) collective-permute-start(bf16[1024,768]{1,0:T(8,128)(2,1)S(1)} %get-tuple-element.62), channel_id=1, source_target_pairs={{0,4},{4,0},{8,12},{12,8},{16,20},{20,16},{24,28},{28,24},{1,5},{5... | collective-permute-start | bytes 4718600 | tf_op jit(solution)/shard_map/ppermute | solution.py:916
  234.1 20.9 %copy-start.22 = (f32[1024,768]{1,0:T(8,128)S(1)}, f32[1024,768]{1,0:T(8,128)}, u32[]{:S(2)}) copy-start(f32[1024,768]{1,0:T(8,128)} %copy-done.21) | copy-start | bytes 9437188
  234.2 12.0 %collective-permute-start.13 = (bf16[256,768]{1,0:T(8,128)(2,1)S(1)}, bf16[256,768]{1,0:T(8,128)(2,1)S(1)}, u32[]{:S(2)}, u32[]{:S(2)}) collective-permute-start(bf16[256,768]{1,0:T(8,128)(2,1)S(1)} %get-tuple-element.124), channel_id=1, source_target_pairs={{0,8},{4,12},{8,0},{12,4},{16,24},{20,28},{24,16},{28,20},{1,9},{5... | collective-permute-start | bytes 1179656 | tf_op jit(solution)/shard_map/ppermute | solution.py:916
  235.3 19.7 %collective-permute-start.14 = (bf16[256,768]{1,0:T(8,128)(2,1)S(1)}, bf16[256,768]{1,0:T(8,128)(2,1)S(1)}, u32[]{:S(2)}, u32[]{:S(2)}) collective-permute-start(bf16[256,768]{1,0:T(8,128)(2,1)S(1)} %get-tuple-element.123), channel_id=1, source_target_pairs={{0,16},{4,20},{8,24},{12,28},{16,0},{20,4},{24,8},{28,12},{1,17},{... | collective-permute-start | bytes 1179656 | tf_op jit(solution)/shard_map/ppermute | solution.py:916
  236.6 18.4 %collective-permute-start.15 = (bf16[256,768]{1,0:T(8,128)(2,1)S(1)}, bf16[256,768]{1,0:T(8,128)(2,1)S(1)}, u32[]{:S(2)}, u32[]{:S(2)}) collective-permute-start(bf16[256,768]{1,0:T(8,128)(2,1)S(1)} %get-tuple-element.122), channel_id=1, source_target_pairs={{0,24},{4,28},{8,16},{12,20},{16,8},{20,12},{24,0},{28,4},{1,25},{... | collective-permute-start | bytes 1179656 | tf_op jit(solution)/shard_map/ppermute | solution.py:916
  266.4 328.5 %reduce-scatter.5.cloned.1.call-start = ((), (), s32[]{:S(2)}) async-start(), calls=%async_computation.2 | async-start | bytes 2949120 | tf_op jit(solution)/shard_map/reduce_scatter | solution.py:1014
  273.2 57.1 %slice-start = ((s8[4718592]{0:T(1024)(128)(4,1)}), s8[4194304]{0:T(1024)(128)(4,1)S(1)}, s32[]{:S(2)}) async-start(s8[4718592]{0:T(1024)(128)(4,1)} %bitcast.78), calls=%async_computation.4 | async-start | bytes 8388608
  278.1 52.2 %slice-start.1 = ((s8[4718592]{0:T(1024)(128)(4,1)}), s8[524288]{0:T(1024)(128)(4,1)S(1)}, s32[]{:S(2)}) async-start(s8[4718592]{0:T(1024)(128)(4,1)} %bitcast.78), calls=%async_computation.5 | async-start | bytes 1048576
  278.1 61.6 %slice-start.2 = ((s8[4718592]{0:T(1024)(128)(4,1)}), s8[4194304]{0:T(1024)(128)(4,1)S(1)}, s32[]{:S(2)}) async-start(s8[4718592]{0:T(1024)(128)(4,1)} %bitcast.93), calls=%async_computation.6 | async-start | bytes 8388608
  330.3 9.4 %copy-start.7 = (bf16[1024,768]{1,0:T(8,128)(2,1)}, bf16[1024,768]{1,0:T(8,128)(2,1)S(1)}, u32[]{:S(2)}) copy-start(bf16[1024,768]{1,0:T(8,128)(2,1)S(1)} %get-tuple-element.69) | copy-start | bytes 4718596
  330.3 9.4 %slice-start.3 = ((s8[4718592]{0:T(1024)(128)(4,1)}), s8[524288]{0:T(1024)(128)(4,1)S(1)}, s32[]{:S(2)}) async-start(s8[4718592]{0:T(1024)(128)(4,1)} %bitcast.93), calls=%async_computation.7 | async-start | bytes 1048576
  330.3 9.4 %copy-start.46 = (bf16[3072,768]{1,0:T(8,128)(2,1)S(1)}, bf16[3072,768]{1,0:T(8,128)(2,1)}, u32[]{:S(2)}) copy-start(bf16[3072,768]{1,0:T(8,128)(2,1)} %get-tuple-element.67) | copy-start | bytes 14155780
  371.0 173.1 %copy-start.19 = (bf16[1024,768]{1,0:T(8,128)(2,1)S(1)}, bf16[1024,768]{1,0:T(8,128)(2,1)}, u32[]{:S(2)}) copy-start(bf16[1024,768]{1,0:T(8,128)(2,1)} %param.13) | copy-start | bytes 4718596
  550.8 33.8 %copy-start.28 = (f32[96,768]{1,0:T(8,128)S(1)}, f32[96,768]{1,0:T(8,128)}, u32[]{:S(2)}) copy-start(f32[96,768]{1,0:T(8,128)} %get-tuple-element.71) | copy-start | bytes 884740
  (42 other events, 191.9 us)
Sparse Core Ops, SparseCore 0:
  266.5 92.3 reduce-scatter.6
  361.2 128.6 reduce-scatter.4

commit v5 on v4

--- a/solution.py
+++ b/solution.py
@@ -33,7 +33,7 @@
 def fwd_kernel(meta_ref, q_ref, k_ref, v_ref, o_ref, lse_ref, vt_ref):
     block = pl.program_id(1)
     place = meta_ref[0]
-    parent_row = pl.multiple_of(TRUNK + meta_ref[1 + block] * BRANCH, BRANCH)
+    parent_row = pl.multiple_of(TRUNK + block * BRANCH, BRANCH)
     own_row = pl.multiple_of(2 * TRUNK + block * BRANCH, BRANCH)
     width = k_ref.shape[1]
 
@@ -129,128 +129,6 @@
     )(meta, q, k, v)
 
 
-def bwd_kernel(meta_ref, q_ref, k_ref, v_ref, o_ref, g_ref, lse_ref,
-               dq_ref, dk_ref, dv_ref, kt_ref, qm_ref, gm_ref, delta_ref, dqt_ref, dkp_ref, dvp_ref):
-    place = meta_ref[0]
-    scale = HEAD_DIM ** (-0.5)
-    rows = q_ref.shape[0]
-    blocks = rows // BRANCH
-    kt_ref[...] = k_ref[...].T
-    queries, grads = q_ref[...], g_ref[...]
-    for head in range(2):
-        lanes = head_lanes(queries.shape, 1, head)
-        qm_ref[head] = jnp.where(lanes, queries, jnp.zeros_like(queries))
-        gm_ref[head] = jnp.where(lanes, grads, jnp.zeros_like(grads))
-    product = (grads.astype(jnp.float32) * o_ref[...].astype(jnp.float32)).T
-    for head in range(2):
-        delta_ref[head : head + 1, :] = jnp.sum(
-            product[head * HEAD_DIM : (head + 1) * HEAD_DIM], axis=0, keepdims=True
-        )
-    dqt_ref[...] = jnp.zeros_like(dqt_ref)
-
-    def step(key_row, query_row, count, mask_of=None):
-        kb = k_ref[pl.ds(key_row, BRANCH)]
-        vb = v_ref[pl.ds(key_row, BRANCH)]
-        dk = dv = None
-        for head in range(2):
-            at = pl.ds(query_row, count)
-            qm, gm = qm_ref[head, at], gm_ref[head, at]
-            scores = dot_nt(kb, qm)
-            probs = jnp.exp2(scores * EXP_SCALE - lse_ref[0, head : head + 1, at])
-            if mask_of is not None:
-                probs = mask_of(probs)
-            prob_grad = dot_nt(vb, gm)
-            score_grad = (probs * (prob_grad - delta_ref[head : head + 1, at])).astype(jnp.bfloat16)
-            dv_part = dot_nn(probs.astype(jnp.bfloat16), gm)
-            dk_part = dot_nn(score_grad, qm)
-            dv = dv_part if dv is None else dv + dv_part
-            dk = dk_part if dk is None else dk + dk_part
-            mine = slice(head * HEAD_DIM, (head + 1) * HEAD_DIM)
-            dqt_ref[mine, at] += dot_nn(kt_ref[mine, pl.ds(key_row, BRANCH)], score_grad)
-        return dk * scale, dv
-
-    def causal(offset):
-        def mask_of(probs):
-            keys = lax.broadcasted_iota(jnp.int32, probs.shape, 0) + offset
-            at = lax.broadcasted_iota(jnp.int32, probs.shape, 1)
-            return jnp.where(keys <= at, probs, 0.0)
-        return mask_of
-
-    @pl.when(place == 0)
-    def _():
-        @pl.loop(0, TRUNK // BRANCH)
-        def _(b):
-            row = pl.multiple_of(b * BRANCH, BRANCH)
-            dk, dv = step(row, 0, rows, causal(row))
-            dk_ref[pl.ds(row, BRANCH)] = dk.astype(dk_ref.dtype)
-            dv_ref[pl.ds(row, BRANCH)] = dv.astype(dv_ref.dtype)
-        rest = (dk_ref.shape[0] - TRUNK, dk_ref.shape[1])
-        dk_ref[TRUNK:] = jnp.zeros(rest, dk_ref.dtype)
-        dv_ref[TRUNK:] = jnp.zeros(rest, dv_ref.dtype)
-
-    @pl.when(place > 0)
-    def _():
-        @pl.loop(0, TRUNK // BRANCH)
-        def _(b):
-            row = pl.multiple_of(b * BRANCH, BRANCH)
-            dk, dv = step(row, 0, rows)
-            dk_ref[pl.ds(row, BRANCH)] = dk.astype(dk_ref.dtype)
-            dv_ref[pl.ds(row, BRANCH)] = dv.astype(dv_ref.dtype)
-
-        dkp_ref[...] = jnp.zeros_like(dkp_ref)
-        dvp_ref[...] = jnp.zeros_like(dvp_ref)
-
-        @pl.loop(0, blocks)
-        def _(b):
-            at = pl.multiple_of(b * BRANCH, BRANCH)
-            parent = pl.multiple_of(meta_ref[1 + b] * BRANCH, BRANCH)
-            dk, dv = step(TRUNK + parent, at, BRANCH, lambda probs: jnp.where(place > 1, probs, 0.0))
-            dkp_ref[pl.ds(parent, BRANCH)] += dk
-            dvp_ref[pl.ds(parent, BRANCH)] += dv
-            own = pl.multiple_of(2 * TRUNK + at, BRANCH)
-            dk, dv = step(own, at, BRANCH, causal(0))
-            dk_ref[pl.ds(own, BRANCH)] = dk.astype(dk_ref.dtype)
-            dv_ref[pl.ds(own, BRANCH)] = dv.astype(dv_ref.dtype)
-
-        dk_ref[TRUNK : 2 * TRUNK] = dkp_ref[...].astype(dk_ref.dtype)
-        dv_ref[TRUNK : 2 * TRUNK] = dvp_ref[...].astype(dv_ref.dtype)
-
-    dq_ref[...] = (dqt_ref[...] * scale).T.astype(dq_ref.dtype)
-
-
-def attend_back(meta, q, k, v, o, grad, lse):
-    rows, width = q.shape
-    keys = k.shape[0]
-    pairs = width // 128
-    here = pl.BlockSpec((rows, 128), lambda p, m: (0, p))
-    wide = pl.BlockSpec((keys, 128), lambda p, m: (0, p))
-    return pl.pallas_call(
-        bwd_kernel,
-        out_shape=(
-            jax.ShapeDtypeStruct((rows, width), jnp.bfloat16),
-            jax.ShapeDtypeStruct((keys, width), jnp.bfloat16),
-            jax.ShapeDtypeStruct((keys, width), jnp.bfloat16),
-        ),
-        grid_spec=pltpu.PrefetchScalarGridSpec(
-            num_scalar_prefetch=1,
-            grid=(pairs,),
-            in_specs=[here, wide, wide, here, here, pl.BlockSpec((1, 2, rows), lambda p, m: (p, 0, 0))],
-            out_specs=[here, wide, wide],
-            scratch_shapes=[
-                pltpu.VMEM((128, keys), jnp.bfloat16),
-                pltpu.VMEM((2, rows, 128), jnp.bfloat16),
-                pltpu.VMEM((2, rows, 128), jnp.bfloat16),
-                pltpu.VMEM((2, rows), jnp.float32),
-                pltpu.VMEM((128, rows), jnp.float32),
-                pltpu.VMEM((TRUNK, 128), jnp.float32),
-                pltpu.VMEM((TRUNK, 128), jnp.float32),
-            ],
-        ),
-        compiler_params=pltpu.CompilerParams(vmem_limit_bytes=48 << 20),
-        name="attend_backward",
-    )(meta, q, k, v, o, grad, lse)
-
-
 ROWS = 256
 HALF_ROOT = math.sqrt(0.5)
 PDF_SCALE = 1.0 / math.sqrt(2.0 * math.pi)
@@ -364,99 +242,6 @@
 MESH = pl.DeviceIdType.MESH
 
 
-def total_kernel(ways, tensor, part_ref, out_ref, land_ref, send1, recv1, send2, recv2):
-    me = lax.axis_index("dp") * tensor + lax.axis_index("tensor")
-
-    def other(step):
-        peer = lax.rem(me + step, ways)
-        return peer, (peer // tensor, lax.rem(peer, tensor))
-
-    barrier = pltpu.get_barrier_semaphore()
-
-    @pl.loop(1, ways)
-    def _(step):
-        pl.semaphore_signal(barrier, inc=1, device_id=other(step)[1], device_id_type=MESH)
-
-    pl.semaphore_wait(barrier, ways - 1)
-
-    def scatter(step):
-        peer, where = other(step)
-        return pltpu.make_async_remote_copy(
-            src_ref=part_ref.at[peer], dst_ref=land_ref.at[me],
-            send_sem=send1.at[step], recv_sem=recv1.at[me],
-            device_id=where, device_id_type=MESH,
-        )
-
-    def arrival(step):
-        source = lax.rem(me - step + ways, ways)
-        return pltpu.make_async_remote_copy(
-            src_ref=part_ref.at[source], dst_ref=land_ref.at[source],
-            send_sem=send1.at[step], recv_sem=recv1.at[source],
-            device_id=other(step)[1], device_id_type=MESH,
-        )
-
-    def spread(step):
-        return pltpu.make_async_remote_copy(
-            src_ref=out_ref.at[me], dst_ref=out_ref.at[me],
-            send_sem=send2.at[step], recv_sem=recv2.at[me],
-            device_id=other(step)[1], device_id_type=MESH,
-        )
-
-    def landing(step):
-        source = lax.rem(me - step + ways, ways)
-        return pltpu.make_async_remote_copy(
-            src_ref=out_ref.at[source], dst_ref=out_ref.at[source],
-            send_sem=send2.at[step], recv_sem=recv2.at[source],
-            device_id=other(step)[1], device_id_type=MESH,
-        )
-
-    @pl.loop(1, ways)
-    def _(step):
-        scatter(step).start()
-
-    def add(step, total):
-        arrival(step).wait_recv()
-        return total + land_ref[lax.rem(me - step + ways, ways)]
-
-    out_ref[me] = lax.fori_loop(1, ways, add, part_ref[me])
-
-    @pl.loop(1, ways)
-    def _(step):
-        spread(step).start()
-
-    @pl.loop(1, ways)
-    def _(step):
-        landing(step).wait_recv()
-
-    @pl.loop(1, ways)
-    def _(step):
-        scatter(step).wait_send()
-        spread(step).wait_send()
-
-
-def total_over_devices(parts):
-    tensor = lax.axis_size("tensor")
-    ways = lax.axis_size("dp") * tensor
-    flat = jnp.concatenate([part.reshape(-1) for part in parts])
-    lanes = -(-flat.shape[0] // (ways * 8 * 128)) * 128
-    padded = jnp.pad(flat, (0, ways * 8 * lanes - flat.shape[0])).reshape(ways, 8, lanes)
-    summed = pl.pallas_call(
-        lambda *refs: total_kernel(ways, tensor, *refs),
-        out_shape=jax.ShapeDtypeStruct(padded.shape, jnp.float32),
-        in_specs=[pl.BlockSpec(memory_space=pltpu.VMEM)],
-        out_specs=pl.BlockSpec(memory_space=pltpu.VMEM),
-        scratch_shapes=[pltpu.VMEM(padded.shape, jnp.float32)]
-        + [pltpu.SemaphoreType.DMA((ways,))] * 4,
-        compiler_params=pltpu.CompilerParams(collective_id=1, has_side_effects=True),
-        name="total_over_devices",
-    )(padded).reshape(-1)
-    results, first = [], 0
-    for part in parts:
-        results.append(summed[first : first + part.size].reshape(part.shape))
-        first += part.size
-    return results
-
-
 PIECE = 64
 
 
@@ -467,8 +252,8 @@
     pl.semaphore_wait(barrier, len(peers))
 
 
-def share_kernel(dp, tensor, own_ref, block_ref, seen_ref, out_ref, weights_ref,
-                 row_send, row_recv,
+def share_kernel(dp, tensor, own_ref, block_ref, parent_ref, seen_ref, out_ref, weights_ref,
+                 ordered_ref, row_send, row_recv,
                  line_send, line_recv, chip_send, chip_recv, pair_send, pair_recv):
     spot, place = lax.axis_index("dp"), lax.axis_index("tensor")
     chip, core = spot // 2, lax.rem(spot, 2)
@@ -626,6 +411,22 @@
         @pl.loop(0, pieces)
         def _(piece):
             pass_on(1, piece, False).wait_send()
+
+    @pl.when(place > 1)
+    def _():
+        blocks = rows // BRANCH
+        branches = [
+            seen_ref[rows + branch * BRANCH : rows + (branch + 1) * BRANCH]
+            for branch in range(blocks)
+        ]
+        for leaf in range(blocks):
+            chosen = None
+            for branch in range(blocks):
+                at = leaf * blocks + branch
+                part = branches[branch] * parent_ref[at : at + 1].astype(own_ref.dtype)
+                chosen = part if chosen is None else chosen + part
+            ordered_ref[leaf * BRANCH : (leaf + 1) * BRANCH] = chosen
+        seen_ref[rows : 2 * rows] = ordered_ref[...]
 
     @pl.loop(0, dp)
     def _(source):
@@ -638,7 +439,7 @@
             )
 
 
-def share_rows_and_weights(own, block):
+def share_rows_and_weights(own, block, parents):
     dp, tensor = lax.axis_size("dp"), lax.axis_size("tensor")
     rows, width = own.shape
     depth, cols = block.shape
@@ -654,10 +455,11 @@
             jax.ShapeDtypeStruct((3 * rows, width), own.dtype),
             jax.ShapeDtypeStruct((kinds, dp * padded, width), block.dtype),
         ),
-        in_specs=[here, here],
+        in_specs=[here, here, here],
         out_specs=[here, here],
         scratch_shapes=[
             pltpu.VMEM((tensor, dp, padded, cols), block.dtype),
+            pltpu.VMEM(own.shape, own.dtype),
             dma((2, pieces)), dma((2, pieces)),
             dma((tensor,)), dma((tensor,)),
             dma((tensor, chips)), dma((tensor, chips)),
@@ -667,19 +469,42 @@
             collective_id=2, has_side_effects=True, vmem_limit_bytes=48 << 20
         ),
         name="share_rows_and_weights",
-    )(own, block)
+    )(own, block, parents)
     weights = weights.reshape(kinds, dp, padded, width)[:, :, :depth]
     return seen, weights.reshape(kinds, dp * depth, width)
 
 
-def gather_grads_kernel(dp, tensor, rows_ref, grads_ref, out_ref, sum_ref,
-                        land_ref, pass_ref, grad_land, grad_sum, line_out, line_land,
-                        row_send, row_recv, grad_send, grad_recv, line_send, line_recv):
+TN = (((0,), (0,)), ((), ()))
+GROUP = 256
+
+
+def dot_tn(a, b):
+    return lax.dot_general(a, b, TN, preferred_element_type=jnp.float32)
+
+
+def back_kernel(
+    dp, tensor, depth,
+    parent_ref, q_in, k_in, v_in, o_in, grad_in, seen_in, weight_in, lse_ref, small_ref,
+    out_ref, sum_ref, total_ref,
+    q_ref, k_ref, v_ref, o_ref, bg_ref, g_ref, seen_ref, weight_ref,
+    kt_ref, qm_ref, gm_ref, delta_ref, dqt_ref,
+    rows_ref, land_ref, acc_ref, gain_ref, slab_ref, slab_land, slab_sum,
+    line_out, line_land, part_ref, part_land,
+    load_sem, pair_sem, row_send, row_recv, slab_send, slab_recv, line_send, line_recv,
+    small_send, small_recv, spread_send, spread_recv,
+):
     spot, place = lax.axis_index("dp"), lax.axis_index("tensor")
-    rows = out_ref.shape[0]
+    ways = dp * tensor
+    me = spot * tensor + place
+    scale = HEAD_DIM ** (-0.5)
+    rows, width = q_ref.shape
+    pairs = width // 128
+    groups = width // GROUP
+    blocks = rows // BRANCH
     pieces = rows // PIECE
-    parts = grads_ref.shape[2] // (tensor * sum_ref.shape[1] // 4)
-    share = sum_ref.shape[1] // parts
+
+    def device(index):
+        return (index // tensor, lax.rem(index, tensor))
 
     def along(step):
         return lax.rem(place + step, tensor)
@@ -687,34 +512,369 @@
     def peer(step):
         return lax.rem(spot + step, dp)
 
-    greet(
-        [(spot, along(step)) for step in range(1, tensor)]
-        + [(peer(step), place) for step in range(1, dp)]
-    )
-
-    def pass_down(piece, fresh):
-        at = pl.ds(piece * PIECE, PIECE)
-        source = rows_ref if fresh else pass_ref
-        return pltpu.make_async_remote_copy(
-            src_ref=source.at[at], dst_ref=land_ref.at[at],
+    barrier = pltpu.get_barrier_semaphore()
+
+    @pl.loop(1, ways)
+    def _(step):
+        pl.semaphore_signal(
+            barrier, inc=1, device_id=device(lax.rem(me + step, ways)), device_id_type=MESH
+        )
+
+    def lanes(pair):
+        return pl.ds(pl.multiple_of(pair * 128, 128), 128)
+
+    plain_loads = [
+        pltpu.make_async_copy(grad_in, bg_ref, load_sem.at[0]),
+        pltpu.make_async_copy(weight_in, weight_ref, load_sem.at[1]),
+        pltpu.make_async_copy(seen_in, seen_ref, load_sem.at[2]),
+    ]
+
+    def pair_loads(pair):
+        return [
+            pltpu.make_async_copy(
+                source.at[:, lanes(pair)], held.at[:, lanes(pair)], pair_sem.at[which, pair]
+            )
+            for which, (source, held) in enumerate(
+                ((q_in, q_ref), (k_in, k_ref), (v_in, v_ref), (o_in, o_ref))
+            )
+        ]
+
+    plain_loads[0].start()
+    plain_loads[1].start()
+
+    @pl.loop(0, pairs)
+    def _(pair):
+        for load in pair_loads(pair):
+            load.start()
+
+    plain_loads[2].start()
+    plain_loads[0].wait()
+    plain_loads[1].wait()
+
+    @pl.loop(0, blocks)
+    def _(b):
+        at = pl.ds(pl.multiple_of(b * BRANCH, BRANCH), BRANCH)
+        g_ref[at] = dot_nn(bg_ref[at], weight_ref[3]).astype(g_ref.dtype)
+
+    def mask_heads(pair):
+        queries, grads = q_ref[:, lanes(pair)], g_ref[:, lanes(pair)]
+        for head in range(2):
+            mine = head_lanes(queries.shape, 1, head)
+            qm_ref[head] = jnp.where(mine, queries, jnp.zeros_like(queries))
+            gm_ref[head] = jnp.where(mine, grads, jnp.zeros_like(grads))
+        return grads
+
+    def step(pair, key_row, query_row, count, mask_of=None):
+        kb = k_ref[pl.ds(key_row, BRANCH), lanes(pair)]
+        vb = v_ref[pl.ds(key_row, BRANCH), lanes(pair)]
+        dk = dv = None
+        at = pl.ds(query_row, count)
+        for head in range(2):
+            qm, gm = qm_ref[head, at], gm_ref[head, at]
+            probs = jnp.exp2(dot_nt(kb, qm) * EXP_SCALE - lse_ref[pair, head : head + 1, at])
+            if mask_of is not None:
+                probs = mask_of(probs)
+            prob_grad = dot_nt(vb, gm) - delta_ref[pair, head : head + 1, at]
+            score_grad = (probs * prob_grad).astype(jnp.bfloat16)
+            dv_part = dot_nn(probs.astype(jnp.bfloat16), gm)
+            dk_part = dot_nn(score_grad, qm)
+            dv = dv_part if dv is None else dv + dv_part
+            dk = dk_part if dk is None else dk + dk_part
+            mine = slice(head * HEAD_DIM, (head + 1) * HEAD_DIM)
+            dqt_ref[pair, mine, at] += dot_nn(kt_ref[mine, pl.ds(key_row, BRANCH)], score_grad)
+        return dk * scale, dv
+
+    def causal(offset):
+        def mask_of(probs):
+            keys = lax.broadcasted_iota(jnp.int32, probs.shape, 0) + offset
+            at = lax.broadcasted_iota(jnp.int32, probs.shape, 1)
+            return jnp.where(keys <= at, probs, 0.0)
+
+        return mask_of
+
+    def put(pair, row, dk, dv):
+        at = pl.ds(row, BRANCH)
+        k_ref[at, lanes(pair)] = dk.astype(k_ref.dtype)
+        v_ref[at, lanes(pair)] = dv.astype(v_ref.dtype)
+
+    @pl.loop(0, pairs)
+    def _(pair):
+        for load in pair_loads(pair):
+            load.wait()
+        kt_ref[:, 0:rows] = k_ref[0:rows, lanes(pair)].T
+        grads = mask_heads(pair)
+        product = (grads.astype(jnp.float32) * o_ref[:, lanes(pair)].astype(jnp.float32)).T
+        for head in range(2):
+            delta_ref[pair, head : head + 1, :] = jnp.sum(
+                product[head * HEAD_DIM : (head + 1) * HEAD_DIM], axis=0, keepdims=True
+            )
+        dqt_ref[pair] = jnp.zeros(dqt_ref.shape[1:], dqt_ref.dtype)
+
+        @pl.when(place == 0)
+        def _():
+            @pl.loop(0, blocks)
+            def _(b):
+                row = pl.multiple_of(b * BRANCH, BRANCH)
+                put(pair, row, *step(pair, row, 0, rows, causal(row)))
+
+        @pl.when(place > 0)
+        def _():
+            @pl.loop(0, blocks)
+            def _(b):
+                row = pl.multiple_of(b * BRANCH, BRANCH)
+                put(pair, row, *step(pair, row, 0, rows))
+
+    pl.semaphore_wait(barrier, ways - 1)
+
+    def pass_down(piece):
+        at = pl.ds(pl.multiple_of(piece * PIECE, PIECE), PIECE)
+        return pltpu.make_async_remote_copy(
+            src_ref=rows_ref.at[at], dst_ref=land_ref.at[at],
             send_sem=row_send.at[piece], recv_sem=row_recv.at[piece],
             device_id=(spot, lax.rem(place + tensor - 1, tensor)), device_id_type=MESH,
         )
 
-    def give(step):
-        return pltpu.make_async_remote_copy(
-            src_ref=grads_ref.at[peer(step)], dst_ref=grad_land.at[spot],
-            send_sem=grad_send.at[step], recv_sem=grad_recv.at[spot],
+    def row_grad(b):
+        at = pl.ds(pl.multiple_of(b * BRANCH, BRANCH), BRANCH)
+        return dot_nt(k_ref[at], weight_ref[1]) + dot_nt(v_ref[at], weight_ref[2])
+
+    def hand_down(b, total):
+        rows_ref[pl.ds(pl.multiple_of(b * BRANCH, BRANCH), BRANCH)] = total.astype(rows_ref.dtype)
+
+        @pl.when(place == tensor - 1)
+        def _():
+            for piece in range(BRANCH // PIECE):
+                pass_down(b * (BRANCH // PIECE) + piece).start()
+
+    def joined(piece):
+        at = pl.ds(pl.multiple_of(piece * PIECE, PIECE), PIECE)
+        return rows_ref[at].astype(jnp.float32) + land_ref[at].astype(jnp.float32)
+
+    middle = (place > 0) & (place < tensor - 1)
+    late = 3 * jnp.maximum(tensor - 2 - place, 0)
+    relayed = jnp.where(middle, jnp.where(place > 1, 2 * pieces, pieces), 0)
+
+    def serve(first, last):
+        def one(piece, carry):
+            pass_down(piece).wait_recv()
+            at = pl.ds(pl.multiple_of(piece * PIECE, PIECE), PIECE)
+            rows_ref[at] = joined(piece).astype(rows_ref.dtype)
+            pass_down(piece).start()
+            return carry
+
+        low = jnp.clip(first - late, 0, relayed)
+        lax.fori_loop(low, jnp.clip(last - late, low, relayed), one, 0)
+
+    @pl.loop(0, blocks)
+    def _(b):
+        hand_down(b, row_grad(b))
+
+    @pl.loop(0, pairs)
+    def _(pair):
+        @pl.when(place == 0)
+        def _():
+            for ref in (k_ref, v_ref):
+                ref[rows : 3 * rows, lanes(pair)] = jnp.zeros((2 * rows, 128), ref.dtype)
+
+        @pl.when(place > 0)
+        def _():
+            kt_ref[:, rows : 2 * rows] = k_ref[rows : 2 * rows, lanes(pair)].T
+            mask_heads(pair)
+
+            @pl.loop(0, blocks)
+            def _(b):
+                at = pl.multiple_of(b * BRANCH, BRANCH)
+                parent = pl.multiple_of(rows + at, BRANCH)
+                put(
+                    pair, parent,
+                    *step(
+                        pair, parent, at, BRANCH, lambda probs: jnp.where(place > 1, probs, 0.0)
+                    ),
+                )
+
+        serve(pair, pair + 1)
+
+    @pl.loop(0, blocks)
+    def _(leaf):
+        out_ref[pl.ds(pl.multiple_of(leaf * BRANCH, BRANCH), BRANCH)] = row_grad(blocks + leaf)
+
+    for branch in range(blocks):
+        total = None
+        for leaf in range(blocks):
+            at = leaf * blocks + branch
+            part = out_ref[leaf * BRANCH : (leaf + 1) * BRANCH] * parent_ref[at : at + 1]
+            total = part if total is None else total + part
+        hand_down(blocks + branch, total)
+
+    served = pairs
+    serve(served, served + 1)
+    served += 1
+    plain_loads[2].wait()
+    gain_ref[...] = jnp.zeros_like(gain_ref)
+
+    def give(group, step):
+        return pltpu.make_async_remote_copy(
+            src_ref=slab_ref.at[group, peer(step)], dst_ref=slab_land.at[group, spot],
+            send_sem=slab_send.at[group, step], recv_sem=slab_recv.at[group, spot],
             device_id=(peer(step), place), device_id_type=MESH,
         )
 
-    def take(step):
+    def take(group, step):
         source = peer(dp - step)
         return pltpu.make_async_remote_copy(
-            src_ref=grads_ref.at[source], dst_ref=grad_land.at[source],
-            send_sem=grad_send.at[step], recv_sem=grad_recv.at[source],
+            src_ref=slab_ref.at[group, source], dst_ref=slab_land.at[group, source],
+            send_sem=slab_send.at[group, step], recv_sem=slab_recv.at[group, source],
             device_id=(peer(step), place), device_id_type=MESH,
         )
+
+    @pl.loop(0, groups)
+    def _(group):
+        base = served + group * 4
+
+        @pl.loop(0, 2)
+        def _(half):
+            pair = group * 2 + half
+
+            @pl.when(place > 0)
+            def _():
+                kt_ref[:, 2 * rows : 3 * rows] = k_ref[2 * rows : 3 * rows, lanes(pair)].T
+                mask_heads(pair)
+
+                @pl.loop(0, blocks)
+                def _(b):
+                    at = pl.multiple_of(b * BRANCH, BRANCH)
+                    own = pl.multiple_of(2 * rows + at, BRANCH)
+                    put(pair, own, *step(pair, own, at, BRANCH, causal(0)))
+
+            q_ref[:, lanes(pair)] = (dqt_ref[pair] * scale).T.astype(q_ref.dtype)
+            serve(base + half, base + half + 1)
+
+        cols = pl.ds(pl.multiple_of(group * GROUP, GROUP), GROUP)
+
+        def keep(kind, value, weighted):
+            if weighted:
+                weight = weight_ref[kind, :, cols].astype(jnp.float32)
+                scaled = value * weight
+                gain_ref[...] += scaled[:, 0:128] + scaled[:, 128:256]
+            acc_ref[...] = value
+
+            def put_block(target, at):
+                slab_ref[group, target, 0:depth, kind * GROUP : (kind + 1) * GROUP] = acc_ref[
+                    at
+                ].astype(slab_ref.dtype)
+
+            if depth % 16:
+                for target in range(dp):
+                    put_block(target, slice(target * depth, (target + 1) * depth))
+            else:
+
+                @pl.loop(0, dp)
+                def _(target):
+                    put_block(target, pl.ds(pl.multiple_of(target * depth, depth), depth))
+
+        keep(0, dot_tn(seen_ref[2 * rows : 3 * rows], q_ref[:, cols]), True)
+        keep(3, dot_tn(bg_ref[...], o_ref[:, cols]), False)
+        serve(base + 2, base + 3)
+        for kind, ref in ((1, k_ref), (2, v_ref)):
+            value = dot_tn(seen_ref[0:rows], ref[0:rows, cols])
+            value = value + dot_tn(seen_ref[rows : 2 * rows], ref[rows : 2 * rows, cols])
+            value = value + dot_tn(seen_ref[2 * rows : 3 * rows], ref[2 * rows : 3 * rows, cols])
+            keep(kind, value, True)
+        serve(base + 3, base + 4)
+
+        @pl.loop(1, dp)
+        def _(step_):
+            give(group, step_).start()
+
+    served += groups * 4
+
+    part_ref[...] = small_ref[...]
+    gains = jnp.sum(gain_ref[...].T, axis=0, keepdims=True)
+    for row in range(width // 128):
+        part_ref[0, row : row + 1, :] = gains[:, row * 128 : (row + 1) * 128]
+
+    def scatter(step):
+        to = lax.rem(me + step, ways)
+        return pltpu.make_async_remote_copy(
+            src_ref=part_ref.at[to], dst_ref=part_land.at[me],
+            send_sem=small_send.at[step], recv_sem=small_recv.at[me],
+            device_id=device(to), device_id_type=MESH,
+        )
+
+    def arrival(step):
+        source = lax.rem(me - step + ways, ways)
+        return pltpu.make_async_remote_copy(
+            src_ref=part_ref.at[source], dst_ref=part_land.at[source],
+            send_sem=small_send.at[step], recv_sem=small_recv.at[source],
+            device_id=device(lax.rem(me + step, ways)), device_id_type=MESH,
+        )
+
+    def spread(step):
+        return pltpu.make_async_remote_copy(
+            src_ref=total_ref.at[me], dst_ref=total_ref.at[me],
+            send_sem=spread_send.at[step], recv_sem=spread_recv.at[me],
+            device_id=device(lax.rem(me + step, ways)), device_id_type=MESH,
+        )
+
+    def landing(step):
+        source = lax.rem(me - step + ways, ways)
+        return pltpu.make_async_remote_copy(
+            src_ref=total_ref.at[source], dst_ref=total_ref.at[source],
+            send_sem=spread_send.at[step], recv_sem=spread_recv.at[source],
+            device_id=device(lax.rem(me + step, ways)), device_id_type=MESH,
+        )
+
+    @pl.loop(1, ways)
+    def _(step_):
+        scatter(step_).start()
+
+    @pl.loop(0, blocks)
+    def _(b):
+        at = pl.ds(pl.multiple_of(b * BRANCH, BRANCH), BRANCH)
+        out_ref[at] = row_grad(2 * blocks + b) + dot_nt(q_ref[at], weight_ref[0])
+        serve(served + b, served + b + 1)
+
+    served += blocks
+
+    def add(step_, total):
+        arrival(step_).wait_recv()
+        return total + part_land[lax.rem(me - step_ + ways, ways)]
+
+    total_ref[me] = lax.fori_loop(1, ways, add, part_ref[me])
+
+    @pl.loop(1, ways)
+    def _(step_):
+        spread(step_).start()
+
+    serve(served, 2 * pieces)
+
+    @pl.loop(0, groups)
+    def _(group):
+        slab_sum[group] = slab_ref[group, spot].astype(jnp.float32)
+
+        @pl.loop(1, dp)
+        def _(step_):
+            take(group, step_).wait_recv()
+            slab_sum[group] += slab_land[group, peer(dp - step_)].astype(jnp.float32)
+
+    serve(2 * pieces, 2 * pieces + late)
+    share = width // tensor
+    kinds = [
+        jnp.concatenate(
+            [slab_sum[group][:, kind * GROUP : (kind + 1) * GROUP] for group in range(groups)],
+            axis=1,
+        )
+        for kind in range(4)
+    ]
+    for target in range(tensor):
+        mine = jnp.concatenate(
+            [kind[:, target * share : (target + 1) * share] for kind in kinds], axis=1
+        )
+        line_out[target] = mine.astype(line_out.dtype)
+
+        @pl.when(place == target)
+        def _():
+            sum_ref[...] = mine
 
     def line(step):
         return pltpu.make_async_remote_copy(
@@ -731,120 +891,108 @@
             device_id=(spot, along(step)), device_id_type=MESH,
         )
 
-    @pl.when(place == tensor - 1)
+    for step_ in range(1, tensor):
+        line(step_).start()
+
+    @pl.when(place < 2)
     def _():
-        @pl.loop(0, 2 * pieces)
+        @pl.loop(0, pieces)
         def _(piece):
-            pass_down(piece, True).start()
-
-    @pl.loop(1, dp)
-    def _(step):
-        give(step).start()
-
-    @pl.when(place > 1)
-    def _():
-        out_ref[...] = jnp.zeros_like(out_ref)
-
-    def row_steps(first, last):
-        @pl.loop(first, last)
-        def _(piece):
-            trunk = piece < pieces
+            source = place * pieces + piece
+            pass_down(source).wait_recv()
             at = pl.ds(pl.multiple_of(piece * PIECE, PIECE), PIECE)
-            takes = (place < tensor - 1) & ((place > 0) | trunk)
-            sends = takes & (place > 0) & ((place > 1) | trunk)
-
-            @pl.when(takes)
-            def _():
-                pass_down(piece, False).wait_recv()
-
-            @pl.when(sends)
-            def _():
-                total = rows_ref[at].astype(jnp.float32) + land_ref[at].astype(jnp.float32)
-                pass_ref[at] = total.astype(pass_ref.dtype)
-                pass_down(piece, False).start()
-
-            @pl.when(takes & jnp.logical_not(sends))
-            def _():
-                total = rows_ref[at].astype(jnp.float32) + land_ref[at].astype(jnp.float32)
-                here = lax.rem(piece, pieces) * PIECE
-                out_ref[pl.ds(pl.multiple_of(here, PIECE), PIECE)] = total
-
-    row_steps(0, pieces + pieces // 2)
-    grad_sum[...] = grads_ref[spot].astype(jnp.float32)
-
-    @pl.loop(1, dp)
-    def _(step):
-        take(step).wait_recv()
-        grad_sum[...] += grad_land[peer(dp - step)].astype(jnp.float32)
-
-    for target in range(tensor):
-        mine = jnp.concatenate(
-            [
-                grad_sum[:, (part * tensor + target) * share : (part * tensor + target + 1) * share]
-                for part in range(parts)
-            ],
-            axis=1,
-        )
-        line_out[target] = mine.astype(line_out.dtype)
-
-        @pl.when(place == target)
-        def _():
-            sum_ref[...] = mine
-
-    for step in range(1, tensor):
-        line(step).start()
-    row_steps(pieces + pieces // 2, 2 * pieces)
-    for step in range(1, tensor):
-        line_in(step).wait_recv()
-        sum_ref[...] += line_land[along(tensor - step)].astype(jnp.float32)
-    for step in range(1, tensor):
-        line(step).wait_send()
-
-    @pl.loop(1, dp)
-    def _(step):
-        give(step).wait_send()
-
-    @pl.loop(0, 2 * pieces)
-    def _(piece):
-        sends = (place > 0) & ((place > 1) | (piece < pieces))
-
-        @pl.when(sends)
-        def _():
-            pass_down(piece, True).wait_send()
-
-
-def collect_grads(rows, grads):
+            out_ref[at] += joined(source)
+
+    for step_ in range(1, tensor):
+        line_in(step_).wait_recv()
+        sum_ref[...] += line_land[along(tensor - step_)].astype(jnp.float32)
+
+    @pl.loop(1, ways)
+    def _(step_):
+        landing(step_).wait_recv()
+
+    for step_ in range(1, tensor):
+        line(step_).wait_send()
+
+    @pl.loop(1, ways)
+    def _(step_):
+        scatter(step_).wait_send()
+        spread(step_).wait_send()
+
+    @pl.loop(0, groups)
+    def _(group):
+        @pl.loop(1, dp)
+        def _(step_):
+            give(group, step_).wait_send()
+
+    sent = jnp.where(place == tensor - 1, 2 * pieces, relayed)
+
+    def sent_one(piece, carry):
+        pass_down(piece).wait_send()
+        return carry
+
+    lax.fori_loop(0, sent, sent_one, 0)
+
+
+def backward(parents, q, k, v, o, branch_grad, seen, weights, lse, small):
     dp, tensor = lax.axis_size("dp"), lax.axis_size("tensor")
-    count, width = rows.shape[0] // 2, rows.shape[1]
-    depth = grads.shape[0] // dp
-    grads = grads.reshape(dp, depth, grads.shape[1])
-    slab = grads.shape[2] // tensor
-    pieces = count // PIECE
+    ways = dp * tensor
+    rows, width = q.shape
+    seen_rows = k.shape[0]
+    depth = width // dp
+    padded = -(-depth // 16) * 16
+    pairs, groups, pieces = width // 128, width // GROUP, rows // PIECE
+    slab = (groups, dp, padded, 4 * GROUP)
+    low, full = jnp.bfloat16, jnp.float32
     dma = pltpu.SemaphoreType.DMA
+    anywhere = pl.BlockSpec(memory_space=pl.ANY)
     here = pl.BlockSpec(memory_space=pltpu.VMEM)
-    return pl.pallas_call(
-        lambda *refs: gather_grads_kernel(dp, tensor, *refs),
+    out, block, total = pl.pallas_call(
+        lambda *refs: back_kernel(dp, tensor, depth, *refs),
         out_shape=(
-            jax.ShapeDtypeStruct((count, width), jnp.float32),
-            jax.ShapeDtypeStruct((depth, slab), jnp.float32),
+            jax.ShapeDtypeStruct((rows, width), full),
+            jax.ShapeDtypeStruct((padded, width), full),
+            jax.ShapeDtypeStruct(small.shape, full),
         ),
-        in_specs=[here, here],
-        out_specs=[here, here],
+        in_specs=[here] + [anywhere] * 7 + [here] * 2,
+        out_specs=[here, here, here],
         scratch_shapes=[
-            pltpu.VMEM(rows.shape, rows.dtype),
-            pltpu.VMEM(rows.shape, rows.dtype),
-            pltpu.VMEM(grads.shape, grads.dtype),
-            pltpu.VMEM(grads.shape[1:], jnp.float32),
-            pltpu.VMEM((tensor, depth, slab), grads.dtype),
-            pltpu.VMEM((tensor, depth, slab), grads.dtype),
+            pltpu.VMEM((rows, width), low),
+            pltpu.VMEM((seen_rows, width), low),
+            pltpu.VMEM((seen_rows, width), low),
+            pltpu.VMEM((rows, width), low),
+            pltpu.VMEM((rows, width), low),
+            pltpu.VMEM((rows, width), low),
+            pltpu.VMEM((seen_rows, width), low),
+            pltpu.VMEM(weights.shape, low),
+            pltpu.VMEM((128, seen_rows), low),
+            pltpu.VMEM((2, rows, 128), low),
+            pltpu.VMEM((2, rows, 128), low),
+            pltpu.VMEM((pairs, 2, rows), full),
+            pltpu.VMEM((pairs, 128, rows), full),
+            pltpu.VMEM((2 * rows, width), low),
+            pltpu.VMEM((2 * rows, width), low),
+            pltpu.VMEM((width, GROUP), full),
+            pltpu.VMEM((width, 128), full),
+            pltpu.VMEM(slab, low),
+            pltpu.VMEM(slab, low),
+            pltpu.VMEM((groups, padded, 4 * GROUP), full),
+            pltpu.VMEM((tensor, padded, width), low),
+            pltpu.VMEM((tensor, padded, width), low),
+            pltpu.VMEM(small.shape, full),
+            pltpu.VMEM(small.shape, full),
+            dma((3,)), dma((4, pairs)),
             dma((2 * pieces,)), dma((2 * pieces,)),
-            dma((dp,)), dma((dp,)), dma((tensor,)), dma((tensor,)),
+            dma((groups, dp)), dma((groups, dp)),
+            dma((tensor,)), dma((tensor,)),
+            dma((ways,)), dma((ways,)), dma((ways,)), dma((ways,)),
         ],
         compiler_params=pltpu.CompilerParams(
-            collective_id=3, has_side_effects=True, vmem_limit_bytes=56 << 20
+            collective_id=3, has_side_effects=True, vmem_limit_bytes=62 << 20
         ),
-        name="collect_grads",
-    )(rows, grads)
+        name="attend_backward",
+    )(parents, q, k, v, o, branch_grad, seen, weights, lse, small)
+    return out, block[:depth], total
 
 
 norm_eps = 1e-05
@@ -906,7 +1054,6 @@
     experts = expert_embed.shape[0]
     capacity = rows_here // experts
     dp_size, tensor_size = lax.axis_size("dp"), lax.axis_size("tensor")
-    leaf_parents = leaf_parent[0]
 
     def hop(rows, chip_step, core_step):
         route = []
@@ -933,19 +1080,20 @@
     normed_in, norm1_back = jax.vjp(layer_norm, hidden, norm1_gain)
     own_in = normed_in.astype(jnp.bfloat16)
     flat_qkv = qkv_weight.reshape(qkv_weight.shape[0], -1)
+    place = lax.axis_index("tensor")
+    leaf_blocks = rows_here // BRANCH
+    first_leaf = jnp.maximum(place - 2, 0) * leaf_blocks
+    leaf_parents = lax.dynamic_slice_in_dim(leaf_parent[0], first_leaf, leaf_blocks, 0) - 1
+    parents = (leaf_parents[:, None] == jnp.arange(leaf_blocks)[None, :]).astype(jnp.float32)
+    parents = jnp.broadcast_to(parents.reshape(-1, 1), (leaf_blocks * leaf_blocks, model_width))
     seen_in, weights = share_rows_and_weights(
-        own_in, jnp.concatenate([flat_qkv, attn_proj.T], axis=1)
+        own_in, jnp.concatenate([flat_qkv, attn_proj.T], axis=1), parents
     )
     query_weight, key_weight, value_weight, proj_back = weights
     query_rows = low_dot(own_in, query_weight)
     key_rows = low_dot(seen_in, key_weight)
     value_rows = low_dot(seen_in, value_weight)
-    place = lax.axis_index("tensor")
-    leaf_blocks = rows_here // BRANCH
-    first_leaf = jnp.maximum(place - 2, 0) * leaf_blocks
-    parents = lax.dynamic_slice_in_dim(leaf_parents, first_leaf, leaf_blocks, 0) - 1
-    meta = jnp.concatenate([place[None], parents]).astype(jnp.int32)
-    attended, log_totals = attend(meta, query_rows, key_rows, value_rows)
+    attended, log_totals = attend(place[None].astype(jnp.int32), query_rows, key_rows, value_rows)
     branch_out = jnp.einsum(
         "sc,dc->sd", attended, proj_back, preferred_element_type=jnp.float32
     )
@@ -997,60 +1145,49 @@
     ).astype(jnp.bfloat16)
     up_grad, kept_grad, sent_grad = expert_back(late_grad, slope, expert_in, expert_out)
     in_weight_grad = jnp.einsum(
-        "rd,rf->df", expert_rows, up_grad, preferred_element_type=jnp.float32
+        "rf,rd->fd", up_grad, expert_rows, preferred_element_type=jnp.float32
     ).astype(jnp.bfloat16)
     moe_grad = from_slots(across_chips(pair_sum(kept_grad, sent_grad)))
     gate_grad = jnp.sum(upstream * expert_result, axis=-1)
     router_part, proj_grad, embed_grad = gate_back(gate_grad)
     mid_part, gain2_grad = norm2_back(moe_grad + router_part)
     mid_grad = upstream + mid_part
-    mid_grad, in_weight_grad, out_weight_grad = lax.optimization_barrier(
-        (mid_grad, in_weight_grad, out_weight_grad)
-    )
-    expert_in_grad, expert_out_grad = (
-        lax.psum_scatter(in_weight_grad, "tensor", scatter_dimension=1, tiled=True).astype(
-            jnp.float32
-        ),
-        lax.psum_scatter(out_weight_grad, "tensor", scatter_dimension=0, tiled=True).astype(
-            jnp.float32
-        ),
-    )
-    branch_grad = mid_grad.astype(jnp.bfloat16)
-    attended_grad = jnp.einsum(
-        "sd,dc->sc", branch_grad, proj_back, preferred_element_type=jnp.float32
-    ).astype(jnp.bfloat16)
-    query_grad, key_grad, value_grad = attend_back(
-        meta, query_rows, key_rows, value_rows, attended, attended_grad, log_totals
-    )
-
-    def weight_grad(rows, row_grads):
-        return jnp.einsum("sd,sc->dc", rows, row_grads, preferred_element_type=jnp.float32)
-
-    def row_grad(row_grads, weight):
-        return jnp.einsum("sc,dc->sd", row_grads, weight, preferred_element_type=jnp.float32)
-
-    weight_grads = jnp.concatenate(
+    expert_grads = jnp.stack(
         [
-            weight_grad(own_in, query_grad),
-            weight_grad(seen_in, key_grad),
-            weight_grad(seen_in, value_grad),
-            weight_grad(branch_grad, attended),
+            part.reshape(tensor_size, -1, model_width)
+            for part in (in_weight_grad, out_weight_grad)
         ],
         axis=1,
-    ).astype(jnp.bfloat16)
-    seen_grad = row_grad(key_grad, key_weight) + row_grad(value_grad, value_weight)
-    own_grad = seen_grad[2 * TRUNK :] + row_grad(query_grad, query_weight)
-    arrived_rows, grad_block = collect_grads(
-        seen_grad[: 2 * TRUNK].astype(jnp.bfloat16), weight_grads
     )
-    input_grad = own_grad + arrived_rows
+    mid_grad, expert_grads = lax.optimization_barrier((mid_grad, expert_grads))
+    expert_grad_block = lax.psum_scatter(
+        expert_grads.reshape(-1, model_width), "tensor", scatter_dimension=0, tiled=True
+    ).astype(jnp.float32)
+    half_block = expert_grad_block.shape[0] // 2
+    expert_in_grad = expert_grad_block[:half_block].T
+    expert_out_grad = expert_grad_block[half_block:]
+    branch_grad = mid_grad.astype(jnp.bfloat16)
+    later = [gain2_grad, proj_grad, embed_grad]
+    flat = jnp.concatenate([jnp.zeros_like(norm1_gain)] + [part.reshape(-1) for part in later])
+    ways = dp_size * tensor_size
+    lanes = -(-flat.shape[0] // (ways * 8 * 128)) * 128
+    small = jnp.pad(flat, (0, ways * 8 * lanes - flat.shape[0])).reshape(ways, 8, lanes)
+    input_grad, grad_block, totals = backward(
+        parents, query_rows, key_rows, value_rows, attended, branch_grad, seen_in, weights,
+        log_totals, small,
+    )
     qkv_grad = grad_block[:, : flat_qkv.shape[1]].reshape(qkv_weight.shape)
     attn_proj_grad = grad_block[:, flat_qkv.shape[1] :].T
-    token_part, gain1_grad = norm1_back(input_grad)
+    totals = totals.reshape(-1)
+    gain1_sum = totals[:model_width] / norm1_gain
+    gain2_sum, router_sum, embed_sum = (
+        totals[first : first + part.size].reshape(part.shape)
+        for first, part in zip(
+            (model_width, 2 * model_width, 2 * model_width + proj_grad.size), later
+        )
+    )
+    token_part, _ = norm1_back(input_grad)
     token_grad = mid_grad + token_part
-    gain1_sum, gain2_sum, router_sum, embed_sum = total_over_devices(
-        (gain1_grad, gain2_grad, proj_grad, embed_grad)
-    )
     return (
         output,
         token_grad,

time: 607 us -> 513 us (0.85)
  matrix products: 97.9 us -> 45.9 us
  Pallas kernels: 385 us -> 360 us
  local copies, waits for them, and re-layouts: 34.8 us -> 18 us
    dot_general x9 -> x1, matrix products: 52.1 us -> 7.66 us  [shards(): jnp.einsum('rf,rd->fd', up_grad, expert_rows, preferred_element_type=jnp....]
    pallas_call x3 -> x1, Pallas kernels: 254 us -> 231 us  [backward(): pl.pallas_call(lambda *refs: back_kernel(dp, tensor, depth, *refs), out_s...]
    unnamed x127 -> x70, local copies, waits for them, and re-layouts: 22.3 us -> 7.98 us
  transfers between devices with their start and end apart: 18 -> 17, of which waited for: 7 -> 6; matrix products, arithmetic and copies ran while one was open for 16% -> 9% of each run, Pallas kernels for 47% -> 51%
where the time goes in v5:
time: 513 us; the launch traced here: 509 us
  Pallas kernels  360 us (70%)
  matrix products  45.9 us (9%)
  waiting for transfers between devices  28.9 us (6%)
  other arithmetic  25.9 us (5%)
  local copies, waits for them, and re-layouts  18 us (4%)
  between operations  15.2 us (3%)
  starting transfers between devices  14.9 us (3%)
    pallas_call x1, Pallas kernels, backward(): pl.pallas_call(lambda *refs: back_kernel(dp, tensor, depth, *refs), out_s...  231 us
    pallas_call x1, Pallas kernels, share_rows_and_weights(): pl.pallas_call(lambda *refs: share_kernel(dp, tensor, *refs), out_shape=(...  54.7 us
    pallas_call x1, Pallas kernels, attend(): pl.pallas_call(fwd_kernel, out_shape=(jax.ShapeDtypeStruct((rows, width),...  43.7 us
    ppermute x16, waiting for transfers between devices, hop(): return lax.ppermute(rows, 'dp', route)  28.9 us
    pallas_call x1, Pallas kernels, expert_forward(): pl.pallas_call(expert_fwd_kernel, grid=(count,), in_specs=[wide(width), w...  15.7 us
    pallas_call x1, Pallas kernels, expert_back(): pl.pallas_call(expert_bwd_kernel, grid=(count,), in_specs=[wide(width), w...  15.3 us
    ppermute x16, starting transfers between devices, hop(): return lax.ppermute(rows, 'dp', route)  14.8 us
    dot_general x3, matrix products, low_dot(): jnp.dot(rows, weight, preferred_element_type=jnp.float32)  11 us
  transfers between devices with their start and end apart: 17, of which 6 were waited for; matrix products, arithmetic and copies ran while one was open for 9% of the time, Pallas kernels for 51%

profile of v5, /device:TPU:0, one launch (start us, length us, event | category | flops | bytes accessed | tf_op | source)
XLA Modules:
  0.0 508.7 jit_solution(12145758363249021721)
XLA Ops:
  8.8 2.0 select_reduce_fusion
  11.7 1.7 convert_reduce_fusion
  13.4 2.0 fusion.13
  16.6 54.7 %share_rows_and_weights.1 = (bf16[3072,768]{1,0:T(8,128)(2,1)}, bf16[4,768,768]{2,1,0:T(8,128)(2,1)}) custom-call(bf16[1024,768]{1,0:T(8,128)(2,1)S(1)} %fusion.15.refs_0_, bf16[96,768]{1,0:T(8,128)(2,1)S(1)} %pad_maximum_fusion.3.refs_1_, f32[16,768]{1,0:T(8,128)S(1)} %broadcast_in_dim.31.refs_2_.refs_0_), custom_call_target="tpu_custom_call" | custom-call | tf_op jit(solution)/shard_map/share_rows_and_weights/pallas_call | solution.py:452
  71.4 2.8 convolution_convert_fusion.4.q_ref.refs_1_
  74.2 1.8 copy-done.18
  76.0 4.1 convolution_convert_fusion.v_ref.refs_3_
  80.2 4.1 convolution_convert_fusion.1.k_ref.refs_2_
  84.3 43.7 %attend_forward.1 = (bf16[1024,768]{1,0:T(8,128)(2,1)S(1)}, f32[6,2,1024]{2,1,0:T(2,128)S(1)}) custom-call(s32[1]{0:T(128)} %bitcast.meta_ref, bf16[1024,768]{1,0:T(8,128)(2,1)S(1)} %convolution_convert_fusion.4.q_ref.refs_1_, bf16[3072,768]{1,0:T(8,128)(2,1)S(1)} %convolution_convert_fusion.1.k_ref.refs_2_, ...), custom_call_target="tpu_custom_call" | custom-call | tf_op jit(solution)/shard_map/attend_forward/pallas_call | solution.py:107
  128.1 1.6 fusion.94
  130.8 2.5 fusion.30
  133.4 2.5 collective-permute-start.2
  138.8 2.6 fusion.33
  141.4 5.1 %collective-permute-done.2 = bf16[256,768]{1,0:T(8,128)(2,1)S(1)} collective-permute-done((bf16[256,768]{1,0:T(8,128)(2,1)S(1)}, bf16[256,768]{1,0:T(8,128)(2,1)S(1)}, u32[]{:S(2)}, u32[]{:S(2)}) %collective-permute-start.2) | collective-permute-done | bytes 393248 | tf_op jit(solution)/shard_map/ppermute | solution.py:1063
  146.5 6.3 %collective-permute-done.1 = bf16[256,768]{1,0:T(8,128)(2,1)S(1)} collective-permute-done((bf16[256,768]{1,0:T(8,128)(2,1)S(1)}, bf16[256,768]{1,0:T(8,128)(2,1)S(1)}, u32[]{:S(2)}, u32[]{:S(2)}) %collective-permute-start.1) | collective-permute-done | bytes 393248 | tf_op jit(solution)/shard_map/ppermute | solution.py:1063
  153.2 1.7 collective-permute-start.5
  158.6 15.7 %expert_forward.1 = (bf16[2048,1536]{1,0:T(8,128)(2,1)}, bf16[2048,1536]{1,0:T(8,128)(2,1)}, f32[1024,768]{1,0:T(8,128)S(1)}, bf16[1024,768]{1,0:T(8,128)(2,1)S(1)}) custom-call(bf16[2048,768]{1,0:T(8,128)(2,1)S(1)} %constant_dynamic-update-slice_fusion.x_ref, bf16[768,1536]{1,0:T(8,128)(2,1)S(1)} %copy-done.7, bf16[1536,768]{1,0:T(8,128)(2,1)S(1)} %copy-done.8), custom_call_target="tpu_custom_call" | custom-call | flops 9663676416 | bytes 25165824 | tf_op jit(solution)/shard_map/expert_forward/pallas_call | solution.py:201
  175.1 2.8 collective-permute-done.8
  178.0 5.6 %convolution_convert_fusion.2 = bf16[1536,768]{1,0:T(8,128)(2,1)S(1)} fusion(bf16[2048,1536]{1,0:T(8,128)(2,1)S(1)} %copy-done.27, bf16[2048,768]{1,0:T(8,128)(2,1)S(1)} %constant_dynamic-update-slice_fusion.5.grad_ref), kind=kOutput, calls=%fused_computation.22 | convolution fusion | flops 4833017856 | bytes 11796480 | tf_op jit(solution)/shard_map/rf,rd->fd/dot_general | solution.py:1143
  187.7 15.3 %expert_backward.1 = (bf16[2048,1536]{1,0:T(8,128)(2,1)}, f32[1024,768]{1,0:T(8,128)S(1)}, bf16[1024,768]{1,0:T(8,128)(2,1)S(1)}) custom-call(bf16[2048,768]{1,0:T(8,128)(2,1)S(1)} %constant_dynamic-update-slice_fusion.5.grad_ref, bf16[2048,1536]{1,0:T(8,128)(2,1)} %get-tuple-element.57.slope_ref, bf16[768,1536]{1,0:T(8,128)(2,1)S(1)} %copy-done.7, ...), custom_call_target="tpu_custom_call" | custom-call | flops 9663676416 | bytes 25165824 | tf_op jit(solution)/shard_map/expert_backward/pallas_call | solution.py:226
  203.1 7.7 %convolution_convert_fusion.3 = bf16[1536,768]{1,0:T(8,128)(2,1)S(1)} fusion(bf16[2048,1536]{1,0:T(8,128)(2,1)} %get-tuple-element.60, bf16[2048,768]{1,0:T(8,128)(2,1)S(1)} %constant_dynamic-update-slice_fusion.x_ref), kind=kOutput, calls=%fused_computation.23 | convolution fusion | flops 4833017856 | bytes 11796480 | tf_op jit(solution)/shard_map/rf,rd->fd/dot_general | solution.py:1147
  211.2 3.4 fusion.18
  219.1 2.8 fusion.73
  221.8 6.6 %collective-permute-done.15 = bf16[256,768]{1,0:T(8,128)(2,1)S(1)} collective-permute-done((bf16[256,768]{1,0:T(8,128)(2,1)S(1)}, bf16[256,768]{1,0:T(8,128)(2,1)S(1)}, u32[]{:S(2)}, u32[]{:S(2)}) %collective-permute-start.15) | collective-permute-done | bytes 393248 | tf_op jit(solution)/shard_map/ppermute | solution.py:1063
  228.4 8.0 %collective-permute-done.14 = bf16[256,768]{1,0:T(8,128)(2,1)S(1)} collective-permute-done((bf16[256,768]{1,0:T(8,128)(2,1)S(1)}, bf16[256,768]{1,0:T(8,128)(2,1)S(1)}, u32[]{:S(2)}, u32[]{:S(2)}) %collective-permute-start.14) | collective-permute-done | bytes 393248 | tf_op jit(solution)/shard_map/ppermute | solution.py:1063
  236.4 2.7 multiply_reduce_fusion
  239.2 2.8 fusion.88
  242.4 2.6 copy.60
  245.5 3.9 fusion.72
  252.7 230.5 %attend_backward.1 = (f32[1024,768]{1,0:T(8,128)}, f32[96,768]{1,0:T(8,128)}, f32[32,8,128]{2,1,0:T(8,128)}) custom-call(f32[16,768]{1,0:T(8,128)} %copy-done.5, bf16[1024,768]{1,0:T(8,128)(2,1)} %copy-done.3, bf16[3072,768]{1,0:T(8,128)(2,1)} %copy-done.2, bf16[3072,768]{1,0:T(8,128)(2,1)} %copy-done.1, bf16[1024,768]{1,0:T(8,128)(2,1)} %copy-done.4, ...), custom_call_target="tpu_custom_call" | custom-call | tf_op jit(solution)/shard_map/attend_backward/pallas_call | solution.py:950
  489.7 2.8 fusion.16
  495.2 2.4 add_add_fusion.2
  (162 shorter events, 38.7 us)
Async XLA Ops:
  7.2 129.9 %copy-start = (f32[768,16]{0,1:T(8,128)S(1)}, f32[768,16]{0,1:T(8,128)}, u32[]{:S(2)}) copy-start(f32[768,16]{0,1:T(8,128)} %param.18) | copy-start | bytes 147460
  7.2 8.8 %copy-start.9 = (bf16[1024,768]{1,0:T(8,128)(2,1)S(1)}, bf16[1024,768]{1,0:T(8,128)(2,1)}, u32[]{:S(2)}) copy-start(bf16[1024,768]{1,0:T(8,128)(2,1)} %param.13) | copy-start | bytes 4718596
  7.2 8.3 %copy-start.24 = (bf16[192,96]{1,0:T(8,128)(2,1)S(1)}, bf16[192,96]{1,0:T(8,128)(2,1)}, u32[]{:S(2)}) copy-start(bf16[192,96]{1,0:T(8,128)(2,1)} %param.16) | copy-start | bytes 110596
  7.2 8.4 %copy-start.21 = (bf16[96,3,192]{2,0,1:T(8,128)(2,1)S(1)}, bf16[96,3,192]{2,0,1:T(8,128)(2,1)}, u32[]{:S(2)}) copy-start(bf16[96,3,192]{2,0,1:T(8,128)(2,1)} %param.15) | copy-start | bytes 331780
  7.2 8.8 %copy-start.22 = (f32[768]{0:T(1024)S(1)}, f32[768]{0:T(1024)}, u32[]{:S(2)}) copy-start(f32[768]{0:T(1024)} %param.14) | copy-start | bytes 9220
  7.2 490.4 %reduce-scatter.2.cloned.1.call-start = ((), (), s32[]{:S(2)}) async-start(), calls=%async_computation.1 | async-start | bytes 5898240 | tf_op jit(solution)/shard_map/reduce_scatter | solution.py:1163
  16.6 57.5 %copy-start.5 = (f32[16,768]{1,0:T(8,128)}, f32[16,768]{1,0:T(8,128)S(1)}, u32[]{:S(2)}) copy-start(f32[16,768]{1,0:T(8,128)S(1)} %broadcast_in_dim.31.refs_2_.refs_0_) | copy-start | bytes 147460
  71.3 4.7 copy-start.18
  74.2 10.1 %copy-start.3 = (bf16[1024,768]{1,0:T(8,128)(2,1)}, bf16[1024,768]{1,0:T(8,128)(2,1)S(1)}, u32[]{:S(2)}) copy-start(bf16[1024,768]{1,0:T(8,128)(2,1)S(1)} %convolution_convert_fusion.4.q_ref.refs_1_) | copy-start | bytes 4718596
  80.1 4.2 copy-start.1
  84.3 43.8 %copy-start.2 = (bf16[3072,768]{1,0:T(8,128)(2,1)}, bf16[3072,768]{1,0:T(8,128)(2,1)S(1)}, u32[]{:S(2)}) copy-start(bf16[3072,768]{1,0:T(8,128)(2,1)S(1)} %convolution_convert_fusion.1.k_ref.refs_2_) | copy-start | bytes 14155780
  84.3 43.7 %copy-start.10 = (bf16[1024,768]{1,0:T(8,128)(2,1)S(1)}, bf16[1024,768]{1,0:T(8,128)(2,1)}, u32[]{:S(2)}) copy-start(bf16[1024,768]{1,0:T(8,128)(2,1)} %param.13) | copy-start | bytes 4718596
  130.8 6.3 %copy-start.15 = (bf16[1024,768]{1,0:T(8,128)(2,1)}, bf16[1024,768]{1,0:T(8,128)(2,1)S(1)}, u32[]{:S(2)}) copy-start(bf16[1024,768]{1,0:T(8,128)(2,1)S(1)} %multiply_convert_fusion) | copy-start | bytes 4718596
  133.3 5.5 %copy-start.19 = (bf16[1024,768]{1,0:T(8,128)(2,1)S(1)}, bf16[1024,768]{1,0:T(8,128)(2,1)}, u32[]{:S(2)}) copy-start(bf16[1024,768]{1,0:T(8,128)(2,1)} %param.25) | copy-start | bytes 4718596
  133.4 13.1 %collective-permute-start.2 = (bf16[256,768]{1,0:T(8,128)(2,1)S(1)}, bf16[256,768]{1,0:T(8,128)(2,1)S(1)}, u32[]{:S(2)}, u32[]{:S(2)}) collective-permute-start(bf16[256,768]{1,0:T(8,128)(2,1)S(1)} %get-tuple-element.115), channel_id=1, source_target_pairs={{0,24},{4,28},{8,16},{12,20},{16,8},{20,12},{24,0},{28,4},{1,25},{... | collective-permute-start | bytes 1179656 | tf_op jit(solution)/shard_map/ppermute | solution.py:1063
  135.9 16.9 %collective-permute-start.1 = (bf16[256,768]{1,0:T(8,128)(2,1)S(1)}, bf16[256,768]{1,0:T(8,128)(2,1)S(1)}, u32[]{:S(2)}, u32[]{:S(2)}) collective-permute-start(bf16[256,768]{1,0:T(8,128)(2,1)S(1)} %get-tuple-element.116), channel_id=1, source_target_pairs={{0,16},{4,20},{8,24},{12,28},{16,0},{20,4},{24,8},{28,12},{1,17},{... | collective-permute-start | bytes 1179656 | tf_op jit(solution)/shard_map/ppermute | solution.py:1063
  136.4 16.5 %collective-permute-start = (bf16[256,768]{1,0:T(8,128)(2,1)S(1)}, bf16[256,768]{1,0:T(8,128)(2,1)S(1)}, u32[]{:S(2)}, u32[]{:S(2)}) collective-permute-start(bf16[256,768]{1,0:T(8,128)(2,1)S(1)} %get-tuple-element.117), channel_id=1, source_target_pairs={{0,8},{4,12},{8,0},{12,4},{16,24},{20,28},{24,16},{28,20},{1,9},{5... | collective-permute-start | bytes 1179656 | tf_op jit(solution)/shard_map/ppermute | solution.py:1063
  153.0 3.9 collective-permute-start.6
  153.2 21.1 %collective-permute-start.5 = (bf16[256,768]{1,0:T(8,128)(2,1)S(1)}, bf16[256,768]{1,0:T(8,128)(2,1)S(1)}, u32[]{:S(2)}, u32[]{:S(2)}) collective-permute-start(bf16[256,768]{1,0:T(8,128)(2,1)S(1)} %get-tuple-element.111), channel_id=1, source_target_pairs={{0,24},{4,28},{8,16},{12,20},{16,8},{20,12},{24,0},{28,4},{1,25},{... | collective-permute-start | bytes 1179656 | tf_op jit(solution)/shard_map/ppermute | solution.py:1063
  154.9 19.4 %collective-permute-start.4 = (bf16[256,768]{1,0:T(8,128)(2,1)S(1)}, bf16[256,768]{1,0:T(8,128)(2,1)S(1)}, u32[]{:S(2)}, u32[]{:S(2)}) collective-permute-start(bf16[256,768]{1,0:T(8,128)(2,1)S(1)} %get-tuple-element.112), channel_id=1, source_target_pairs={{0,16},{4,20},{8,24},{12,28},{16,0},{20,4},{24,8},{28,12},{1,17},{... | collective-permute-start | bytes 1179656 | tf_op jit(solution)/shard_map/ppermute | solution.py:1063
  156.2 18.1 %collective-permute-start.3 = (bf16[256,768]{1,0:T(8,128)(2,1)S(1)}, bf16[256,768]{1,0:T(8,128)(2,1)S(1)}, u32[]{:S(2)}, u32[]{:S(2)}) collective-permute-start(bf16[256,768]{1,0:T(8,128)(2,1)S(1)} %get-tuple-element.113), channel_id=1, source_target_pairs={{0,8},{4,12},{8,0},{12,4},{16,24},{20,28},{24,16},{28,20},{1,9},{5... | collective-permute-start | bytes 1179656 | tf_op jit(solution)/shard_map/ppermute | solution.py:1063
  174.4 3.5 collective-permute-start.8
  174.5 9.1 %collective-permute-start.7 = (bf16[1024,768]{1,0:T(8,128)(2,1)S(1)}, bf16[1024,768]{1,0:T(8,128)(2,1)S(1)}, u32[]{:S(2)}, u32[]{:S(2)}) collective-permute-start(bf16[1024,768]{1,0:T(8,128)(2,1)S(1)} %get-tuple-element.50), channel_id=1, source_target_pairs={{0,4},{4,0},{8,12},{12,8},{16,20},{20,16},{24,28},{28,24},{1,5},{5... | collective-permute-start | bytes 4718600 | tf_op jit(solution)/shard_map/ppermute | solution.py:1063
  184.2 27.0 %collective-permute-start.11 = (bf16[256,768]{1,0:T(8,128)(2,1)S(1)}, bf16[256,768]{1,0:T(8,128)(2,1)}, u32[]{:S(2)}, u32[]{:S(2)}) collective-permute-start(bf16[256,768]{1,0:T(8,128)(2,1)S(1)} %get-tuple-element.108), channel_id=1, source_target_pairs={{0,24},{4,28},{8,16},{12,20},{16,8},{20,12},{24,0},{28,4},{1,25},{... | collective-permute-start | bytes 1179656 | tf_op jit(solution)/shard_map/ppermute | solution.py:1063
  185.7 25.5 %collective-permute-start.10 = (bf16[256,768]{1,0:T(8,128)(2,1)S(1)}, bf16[256,768]{1,0:T(8,128)(2,1)}, u32[]{:S(2)}, u32[]{:S(2)}) collective-permute-start(bf16[256,768]{1,0:T(8,128)(2,1)S(1)} %get-tuple-element.109), channel_id=1, source_target_pairs={{0,16},{4,20},{8,24},{12,28},{16,0},{20,4},{24,8},{28,12},{1,17},{... | collective-permute-start | bytes 1179656 | tf_op jit(solution)/shard_map/ppermute | solution.py:1063
  187.0 24.2 %collective-permute-start.9 = (bf16[256,768]{1,0:T(8,128)(2,1)S(1)}, bf16[256,768]{1,0:T(8,128)(2,1)}, u32[]{:S(2)}, u32[]{:S(2)}) collective-permute-start(bf16[256,768]{1,0:T(8,128)(2,1)S(1)} %get-tuple-element.110), channel_id=1, source_target_pairs={{0,8},{4,12},{8,0},{12,4},{16,24},{20,28},{24,16},{28,20},{1,9},{5... | collective-permute-start | bytes 1179656 | tf_op jit(solution)/shard_map/ppermute | solution.py:1063
  203.1 12.0 %collective-permute-start.12 = (bf16[1024,768]{1,0:T(8,128)(2,1)S(1)}, bf16[1024,768]{1,0:T(8,128)(2,1)S(1)}, u32[]{:S(2)}, u32[]{:S(2)}) collective-permute-start(bf16[1024,768]{1,0:T(8,128)(2,1)S(1)} %get-tuple-element.59), channel_id=1, source_target_pairs={{0,4},{4,0},{8,12},{12,8},{16,20},{20,16},{24,28},{28,24},{1,5},{5... | collective-permute-start | bytes 4718600 | tf_op jit(solution)/shard_map/ppermute | solution.py:1063
  215.5 12.9 %collective-permute-start.15 = (bf16[256,768]{1,0:T(8,128)(2,1)S(1)}, bf16[256,768]{1,0:T(8,128)(2,1)S(1)}, u32[]{:S(2)}, u32[]{:S(2)}) collective-permute-start(bf16[256,768]{1,0:T(8,128)(2,1)S(1)} %get-tuple-element.104), channel_id=1, source_target_pairs={{0,24},{4,28},{8,16},{12,20},{16,8},{20,12},{24,0},{28,4},{1,25},{... | collective-permute-start | bytes 1179656 | tf_op jit(solution)/shard_map/ppermute | solution.py:1063
  217.0 19.4 %collective-permute-start.14 = (bf16[256,768]{1,0:T(8,128)(2,1)S(1)}, bf16[256,768]{1,0:T(8,128)(2,1)S(1)}, u32[]{:S(2)}, u32[]{:S(2)}) collective-permute-start(bf16[256,768]{1,0:T(8,128)(2,1)S(1)} %get-tuple-element.105), channel_id=1, source_target_pairs={{0,16},{4,20},{8,24},{12,28},{16,0},{20,4},{24,8},{28,12},{1,17},{... | collective-permute-start | bytes 1179656 | tf_op jit(solution)/shard_map/ppermute | solution.py:1063
  218.3 18.1 %collective-permute-start.13 = (bf16[256,768]{1,0:T(8,128)(2,1)S(1)}, bf16[256,768]{1,0:T(8,128)(2,1)S(1)}, u32[]{:S(2)}, u32[]{:S(2)}) collective-permute-start(bf16[256,768]{1,0:T(8,128)(2,1)S(1)} %get-tuple-element.106), channel_id=1, source_target_pairs={{0,8},{4,12},{8,0},{12,4},{16,24},{20,28},{24,16},{28,20},{1,9},{5... | collective-permute-start | bytes 1179656 | tf_op jit(solution)/shard_map/ppermute | solution.py:1063
  242.4 8.2 %copy-start.12 = (f32[1024,768]{1,0:T(8,128)}, f32[1024,768]{1,0:T(8,128)S(1)}, u32[]{:S(2)}) copy-start(f32[1024,768]{1,0:T(8,128)S(1)} %convert_add_fusion) | copy-start | bytes 9437188
  483.2 6.4 %copy-start.11 = (bf16[1024,768]{1,0:T(8,128)(2,1)S(1)}, bf16[1024,768]{1,0:T(8,128)(2,1)}, u32[]{:S(2)}) copy-start(bf16[1024,768]{1,0:T(8,128)(2,1)} %param.13) | copy-start | bytes 4718596
  (13 other events, 32.0 us)
Sparse Core Ops, SparseCore 0:
  245.2 154.9 reduce-scatter.1

commit v6 on v5

--- a/solution.py
+++ b/solution.py
@@ -1,3 +1,4 @@
+import functools
 import math
 
 import jax
@@ -30,80 +31,85 @@
     return lax.broadcasted_iota(jnp.int32, shape, dim) // HEAD_DIM == head
 
 
-def fwd_kernel(meta_ref, q_ref, k_ref, v_ref, o_ref, lse_ref, vt_ref):
-    block = pl.program_id(1)
-    place = meta_ref[0]
-    parent_row = pl.multiple_of(TRUNK + block * BRANCH, BRANCH)
-    own_row = pl.multiple_of(2 * TRUNK + block * BRANCH, BRANCH)
-    width = k_ref.shape[1]
-
-    @pl.when(block == 0)
-    def _():
-        flipped = v_ref[...].T
-        for head in range(2):
-            vt_ref[head] = jnp.where(
-                head_lanes(flipped.shape, 0, head), flipped, jnp.ones_like(flipped)
-            )
-
-    queries = q_ref[...]
-
-    def finish(outs):
-        rows = []
-        for head, (acc, top) in enumerate(outs):
-            mine, other = head * HEAD_DIM, (1 - head) * HEAD_DIM
-            total = acc[other : other + 1]
-            rows.append(acc[mine : mine + HEAD_DIM] / total)
-            lse_ref[0, head : head + 1, :] = top * EXP_SCALE + jnp.log2(total)
-        o_ref[...] = jnp.concatenate(rows, axis=0).T.astype(o_ref.dtype)
-
-    def probs(scores, top):
-        return jnp.exp2(scores * EXP_SCALE - top * EXP_SCALE).astype(jnp.bfloat16)
-
-    def masked_queries(head):
-        return jnp.where(head_lanes(queries.shape, 1, head), queries, jnp.zeros_like(queries))
+def fwd_kernel(place_ref, q_ref, k_ref, v_ref, o_ref, lse_ref, vt_ref, acc_ref):
+    place = place_ref[0]
+    rows = q_ref.shape[0]
+    blocks = rows // BRANCH
+    flipped = v_ref[...].T
+    for head in range(2):
+        vt_ref[head] = jnp.where(
+            head_lanes(flipped.shape, 0, head), flipped, jnp.ones_like(flipped)
+        )
+
+    def start(block, head, in_trunk):
+        queries = q_ref[block * BRANCH : (block + 1) * BRANCH]
+        queries = jnp.where(head_lanes(queries.shape, 1, head), queries, jnp.zeros_like(queries))
+        firsts = list(range(0, TRUNK, BRANCH))
+        if not in_trunk:
+            firsts += [rows + block * BRANCH, 2 * rows + block * BRANCH]
+        scores = [dot_nt(k_ref[first : first + BRANCH], queries) for first in firsts]
+
+        def causal(tile, offset):
+            keys = lax.broadcasted_iota(jnp.int32, tile.shape, 0) + offset
+            at = lax.broadcasted_iota(jnp.int32, tile.shape, 1)
+            return jnp.where(keys <= at, tile, MASKED)
+
+        if in_trunk:
+            scores = [
+                causal(tile, first - block * BRANCH) for tile, first in zip(scores, firsts)
+            ]
+        else:
+            scores[-2] = jnp.where(place > 1, scores[-2], MASKED)
+            scores[-1] = causal(scores[-1], 0)
+        top = jnp.max(functools.reduce(jnp.maximum, scores), axis=0, keepdims=True)
+        return firsts, scores, top
+
+    def middle(firsts, scores, top):
+        shift = top * EXP_SCALE
+        probs = [jnp.exp2(tile * EXP_SCALE - shift).astype(jnp.bfloat16) for tile in scores]
+        return firsts, probs, top
+
+    def finish(block, head, firsts, probs, top):
+        acc = None
+        for first, tile in zip(firsts, probs):
+            part = dot_nn(vt_ref[head, :, first : first + BRANCH], tile)
+            acc = part if acc is None else acc + part
+        mine, other = head * HEAD_DIM, (1 - head) * HEAD_DIM
+        total = acc[other : other + 1]
+        cols = slice(block * BRANCH, (block + 1) * BRANCH)
+        acc_ref[mine : mine + HEAD_DIM, cols] = acc[mine : mine + HEAD_DIM] / total
+        lse_ref[0, head : head + 1, cols] = top * EXP_SCALE + jnp.log2(total)
+
+    def run(in_trunk):
+        work = [(block, head) for block in range(blocks) for head in range(2)]
+        ready, held = start(*work[0], in_trunk), None
+        for at, item in enumerate(work):
+            now = ready
+            if at + 1 < len(work):
+                ready = start(*work[at + 1], in_trunk)
+            done = middle(*now)
+            if held is not None:
+                finish(*held)
+            held = (*item, *done)
+        finish(*held)
 
     @pl.when(place == 0)
     def _():
-        outs = []
-        for head in range(2):
-            scores = dot_nt(k_ref[0:TRUNK], masked_queries(head))
-            keys = lax.broadcasted_iota(jnp.int32, scores.shape, 0)
-            rows = lax.broadcasted_iota(jnp.int32, scores.shape, 1) + block * BRANCH
-            scores = jnp.where(keys <= rows, scores, MASKED)
-            top = jnp.max(scores, axis=0, keepdims=True)
-            outs.append((dot_nn(vt_ref[head, :, 0:TRUNK], probs(scores, top)), top))
-        finish(outs)
+        run(True)
 
     @pl.when(place > 0)
     def _():
-        outs = []
-        for head in range(2):
-            qm = masked_queries(head)
-            trunk = dot_nt(k_ref[0:TRUNK], qm)
-            parent = dot_nt(k_ref[pl.ds(parent_row, BRANCH)], qm)
-            parent = jnp.where(place > 1, parent, MASKED)
-            own = dot_nt(k_ref[pl.ds(own_row, BRANCH)], qm)
-            keys = lax.broadcasted_iota(jnp.int32, own.shape, 0)
-            rows = lax.broadcasted_iota(jnp.int32, own.shape, 1)
-            own = jnp.where(keys <= rows, own, MASKED)
-            top = jnp.maximum(
-                jnp.maximum(
-                    jnp.max(trunk, axis=0, keepdims=True), jnp.max(parent, axis=0, keepdims=True)
-                ),
-                jnp.max(own, axis=0, keepdims=True),
-            )
-            acc = dot_nn(vt_ref[head, :, 0:TRUNK], probs(trunk, top))
-            acc = acc + dot_nn(vt_ref[head, :, pl.ds(parent_row, BRANCH)], probs(parent, top))
-            acc = acc + dot_nn(vt_ref[head, :, pl.ds(own_row, BRANCH)], probs(own, top))
-            outs.append((acc, top))
-        finish(outs)
-
-
-def attend(meta, q, k, v):
+        run(False)
+
+    o_ref[...] = acc_ref[...].T.astype(o_ref.dtype)
+
+
+def attend(place, q, k, v):
     rows, width = q.shape
     keys = k.shape[0]
     pairs = width // 128
-    blocks = rows // BRANCH
+    few = pl.BlockSpec((rows, 128), lambda p, m: (0, p))
+    many = pl.BlockSpec((keys, 128), lambda p, m: (0, p))
     return pl.pallas_call(
         fwd_kernel,
         out_shape=(
@@ -112,21 +118,17 @@
         ),
         grid_spec=pltpu.PrefetchScalarGridSpec(
             num_scalar_prefetch=1,
-            grid=(pairs, blocks),
-            in_specs=[
-                pl.BlockSpec((BRANCH, 128), lambda p, i, m: (i, p)),
-                pl.BlockSpec((keys, 128), lambda p, i, m: (0, p)),
-                pl.BlockSpec((keys, 128), lambda p, i, m: (0, p)),
+            grid=(pairs,),
+            in_specs=[few, many, many],
+            out_specs=[few, pl.BlockSpec((1, 2, rows), lambda p, m: (p, 0, 0))],
+            scratch_shapes=[
+                pltpu.VMEM((2, 128, keys), jnp.bfloat16),
+                pltpu.VMEM((128, rows), jnp.float32),
             ],
-            out_specs=[
-                pl.BlockSpec((BRANCH, 128), lambda p, i, m: (i, p)),
-                pl.BlockSpec((1, 2, BRANCH), lambda p, i, m: (p, 0, i)),
-            ],
-            scratch_shapes=[pltpu.VMEM((2, 128, keys), jnp.bfloat16)],
         ),
-        compiler_params=pltpu.CompilerParams(vmem_limit_bytes=40 << 20),
+        compiler_params=pltpu.CompilerParams(vmem_limit_bytes=48 << 20),
         name="attend_forward",
-    )(meta, q, k, v)
+    )(place, q, k, v)
 
 
 ROWS = 256
@@ -486,12 +488,11 @@
     dp, tensor, depth,
     parent_ref, q_in, k_in, v_in, o_in, grad_in, seen_in, weight_in, lse_ref, small_ref,
     out_ref, sum_ref, total_ref,
-    q_ref, k_ref, v_ref, o_ref, bg_ref, g_ref, seen_ref, weight_ref,
-    kt_ref, qm_ref, gm_ref, delta_ref, dqt_ref,
-    rows_ref, land_ref, acc_ref, gain_ref, slab_ref, slab_land, slab_sum,
-    line_out, line_land, part_ref, part_land,
-    load_sem, pair_sem, row_send, row_recv, slab_send, slab_recv, line_send, line_recv,
-    small_send, small_recv, spread_send, spread_recv,
+    q_ref, k_ref, v_ref, o_ref, bg_ref, g_ref, stage_ref, seen_ref, weight_ref,
+    delta_ref, dqt_ref, rows_ref, land_ref, gain_ref,
+    slab_ref, slab_land, proj_ref, proj_land, line_out, line_land, part_ref, part_land,
+    load_sem, pair_sem, stage_sem, row_send, row_recv, slab_send, slab_recv,
+    line_send, line_recv, small_send, small_recv, spread_send, spread_recv,
 ):
     spot, place = lax.axis_index("dp"), lax.axis_index("tensor")
     ways = dp * tensor
@@ -502,6 +503,7 @@
     groups = width // GROUP
     blocks = rows // BRANCH
     pieces = rows // PIECE
+    stage_rows = stage_ref.shape[1]
 
     def device(index):
         return (index // tensor, lax.rem(index, tensor))
@@ -511,6 +513,9 @@
 
     def peer(step):
         return lax.rem(spot + step, dp)
+
+    def block_at(b):
+        return pl.ds(pl.multiple_of(b * BRANCH, BRANCH), BRANCH)
 
     barrier = pltpu.get_barrier_semaphore()
 
@@ -523,108 +528,172 @@
     def lanes(pair):
         return pl.ds(pl.multiple_of(pair * 128, 128), 128)
 
-    plain_loads = [
-        pltpu.make_async_copy(grad_in, bg_ref, load_sem.at[0]),
-        pltpu.make_async_copy(weight_in, weight_ref, load_sem.at[1]),
-        pltpu.make_async_copy(seen_in, seen_ref, load_sem.at[2]),
-    ]
+    grad_load = pltpu.make_async_copy(grad_in, bg_ref, load_sem.at[0])
+    weight_load = pltpu.make_async_copy(weight_in, weight_ref, load_sem.at[1])
+    value_load = pltpu.make_async_copy(o_in, o_ref, load_sem.at[2])
 
     def pair_loads(pair):
         return [
             pltpu.make_async_copy(
                 source.at[:, lanes(pair)], held.at[:, lanes(pair)], pair_sem.at[which, pair]
             )
-            for which, (source, held) in enumerate(
-                ((q_in, q_ref), (k_in, k_ref), (v_in, v_ref), (o_in, o_ref))
-            )
+            for which, (source, held) in enumerate(((q_in, q_ref), (k_in, k_ref), (v_in, v_ref)))
         ]
 
-    plain_loads[0].start()
-    plain_loads[1].start()
+    def stage(part):
+        slot = lax.rem(part, 2)
+        at = pl.ds(pl.multiple_of(part * stage_rows, stage_rows), stage_rows)
+        return pltpu.make_async_copy(seen_in.at[at], stage_ref.at[slot], stage_sem.at[slot])
+
+    grad_load.start()
+    weight_load.start()
+    value_load.start()
 
     @pl.loop(0, pairs)
     def _(pair):
         for load in pair_loads(pair):
             load.start()
 
-    plain_loads[2].start()
-    plain_loads[0].wait()
-    plain_loads[1].wait()
+    grad_load.wait()
+    weight_load.wait()
+    value_load.wait()
+
+    def keep(held, value, kind):
+        cols = slice(kind * GROUP, (kind + 1) * GROUP)
+        if depth % 16:
+            for target in range(dp):
+                held[target, 0:depth, cols] = value[target * depth : (target + 1) * depth].astype(
+                    slab_ref.dtype
+                )
+        else:
+            held[:, :, cols] = value.reshape(dp, depth, GROUP).astype(slab_ref.dtype)
+
+    for group in range(groups):
+        cols = slice(group * GROUP, (group + 1) * GROUP)
+        keep(proj_ref, dot_tn(bg_ref[...], o_ref[:, cols]), group)
 
     @pl.loop(0, blocks)
     def _(b):
-        at = pl.ds(pl.multiple_of(b * BRANCH, BRANCH), BRANCH)
+        at = block_at(b)
         g_ref[at] = dot_nn(bg_ref[at], weight_ref[3]).astype(g_ref.dtype)
 
-    def mask_heads(pair):
-        queries, grads = q_ref[:, lanes(pair)], g_ref[:, lanes(pair)]
-        for head in range(2):
-            mine = head_lanes(queries.shape, 1, head)
-            qm_ref[head] = jnp.where(mine, queries, jnp.zeros_like(queries))
-            gm_ref[head] = jnp.where(mine, grads, jnp.zeros_like(grads))
-        return grads
-
-    def step(pair, key_row, query_row, count, mask_of=None):
-        kb = k_ref[pl.ds(key_row, BRANCH), lanes(pair)]
-        vb = v_ref[pl.ds(key_row, BRANCH), lanes(pair)]
-        dk = dv = None
-        at = pl.ds(query_row, count)
-        for head in range(2):
-            qm, gm = qm_ref[head, at], gm_ref[head, at]
-            probs = jnp.exp2(dot_nt(kb, qm) * EXP_SCALE - lse_ref[pair, head : head + 1, at])
-            if mask_of is not None:
-                probs = mask_of(probs)
-            prob_grad = dot_nt(vb, gm) - delta_ref[pair, head : head + 1, at]
-            score_grad = (probs * prob_grad).astype(jnp.bfloat16)
-            dv_part = dot_nn(probs.astype(jnp.bfloat16), gm)
-            dk_part = dot_nn(score_grad, qm)
-            dv = dv_part if dv is None else dv + dv_part
-            dk = dk_part if dk is None else dk + dk_part
-            mine = slice(head * HEAD_DIM, (head + 1) * HEAD_DIM)
-            dqt_ref[pair, mine, at] += dot_nn(kt_ref[mine, pl.ds(key_row, BRANCH)], score_grad)
-        return dk * scale, dv
-
-    def causal(offset):
-        def mask_of(probs):
-            keys = lax.broadcasted_iota(jnp.int32, probs.shape, 0) + offset
-            at = lax.broadcasted_iota(jnp.int32, probs.shape, 1)
-            return jnp.where(keys <= at, probs, 0.0)
-
-        return mask_of
-
-    def put(pair, row, dk, dv):
-        at = pl.ds(row, BRANCH)
-        k_ref[at, lanes(pair)] = dk.astype(k_ref.dtype)
-        v_ref[at, lanes(pair)] = dv.astype(v_ref.dtype)
+    pl.semaphore_wait(barrier, ways - 1)
+
+    def slabs(group):
+        if isinstance(group, int) and group == groups:
+            return proj_ref, proj_land
+        return slab_ref.at[group], slab_land.at[group]
+
+    def give(group, step):
+        source, target = slabs(group)
+        return pltpu.make_async_remote_copy(
+            src_ref=source.at[peer(step)], dst_ref=target.at[spot],
+            send_sem=slab_send.at[group, step], recv_sem=slab_recv.at[group, spot],
+            device_id=(peer(step), place), device_id_type=MESH,
+        )
+
+    def take(group, step):
+        owner = peer(dp - step)
+        source, target = slabs(group)
+        return pltpu.make_async_remote_copy(
+            src_ref=source.at[owner], dst_ref=target.at[owner],
+            send_sem=slab_send.at[group, step], recv_sem=slab_recv.at[group, owner],
+            device_id=(peer(step), place), device_id_type=MESH,
+        )
+
+    @pl.loop(1, dp)
+    def _(step):
+        give(groups, step).start()
 
     @pl.loop(0, pairs)
     def _(pair):
         for load in pair_loads(pair):
             load.wait()
-        kt_ref[:, 0:rows] = k_ref[0:rows, lanes(pair)].T
-        grads = mask_heads(pair)
-        product = (grads.astype(jnp.float32) * o_ref[:, lanes(pair)].astype(jnp.float32)).T
+        product = g_ref[:, lanes(pair)].astype(jnp.float32)
+        product = (product * o_ref[:, lanes(pair)].astype(jnp.float32)).T
         for head in range(2):
             delta_ref[pair, head : head + 1, :] = jnp.sum(
                 product[head * HEAD_DIM : (head + 1) * HEAD_DIM], axis=0, keepdims=True
             )
         dqt_ref[pair] = jnp.zeros(dqt_ref.shape[1:], dqt_ref.dtype)
 
-        @pl.when(place == 0)
-        def _():
-            @pl.loop(0, blocks)
-            def _(b):
-                row = pl.multiple_of(b * BRANCH, BRANCH)
-                put(pair, row, *step(pair, row, 0, rows, causal(row)))
-
-        @pl.when(place > 0)
-        def _():
-            @pl.loop(0, blocks)
-            def _(b):
-                row = pl.multiple_of(b * BRANCH, BRANCH)
-                put(pair, row, *step(pair, row, 0, rows))
-
-    pl.semaphore_wait(barrier, ways - 1)
+    def sweep(pair, tiles):
+        work = [(tile, head) for tile in range(len(tiles)) for head in range(2)]
+        sums = [[None, None] for _ in tiles]
+        keys, flipped = {}, {}
+
+        def key_block(tile):
+            row = tiles[tile][0]
+            if id(row) not in keys:
+                kb = k_ref[pl.ds(row, BRANCH), lanes(pair)]
+                vb = v_ref[pl.ds(row, BRANCH), lanes(pair)]
+                masked = []
+                for head in range(2):
+                    mine = head_lanes(kb.shape, 1, head)
+                    masked.append(
+                        (
+                            jnp.where(mine, kb, jnp.zeros_like(kb)),
+                            jnp.where(mine, vb, jnp.zeros_like(vb)),
+                        )
+                    )
+                keys[id(row)] = masked
+                flipped[id(row)] = kb.T
+            return keys[id(row)], flipped[id(row)]
+
+        def start(tile, head):
+            at = pl.ds(tiles[tile][1], BRANCH)
+            kb, vb = key_block(tile)[0][head]
+            return dot_nt(kb, q_ref[at, lanes(pair)]), dot_nt(vb, g_ref[at, lanes(pair)])
+
+        def middle(tile, head, scores, prob_grad):
+            at = pl.ds(tiles[tile][1], BRANCH)
+            probs = jnp.exp2(scores * EXP_SCALE - lse_ref[pair, head : head + 1, at])
+            if tiles[tile][2] is not None:
+                probs = tiles[tile][2](probs)
+            score_grad = probs * (prob_grad - delta_ref[pair, head : head + 1, at])
+            return probs.astype(jnp.bfloat16), score_grad.astype(jnp.bfloat16)
+
+        def finish(tile, head, probs, score_grad):
+            at = pl.ds(tiles[tile][1], BRANCH)
+            parts = (
+                dot_nn(score_grad, q_ref[at, lanes(pair)]),
+                dot_nn(probs, g_ref[at, lanes(pair)]),
+            )
+            for which in range(2):
+                held = sums[tile][which]
+                if head == 0:
+                    sums[tile][which] = parts[which]
+                else:
+                    first = head_lanes(held.shape, 1, 0)
+                    sums[tile][which] = jnp.where(first, held, parts[which])
+            mine = slice(head * HEAD_DIM, (head + 1) * HEAD_DIM)
+            dqt_ref[pair, mine, at] += dot_nn(key_block(tile)[1][mine], score_grad)
+
+        ready = start(*work[0])
+        held = None
+        for at, item in enumerate(work):
+            now = ready
+            if at + 1 < len(work):
+                ready = start(*work[at + 1])
+            done = middle(*item, *now)
+            if held is not None:
+                finish(*held)
+            held = (*item, *done)
+        finish(*held)
+        return sums
+
+    def causal(key_row, query_row):
+        def mask_of(probs):
+            keys = lax.broadcasted_iota(jnp.int32, probs.shape, 0) + key_row
+            at = lax.broadcasted_iota(jnp.int32, probs.shape, 1) + query_row
+            return jnp.where(keys <= at, probs, 0.0)
+
+        return mask_of
+
+    def put(pair, row, dk, dv):
+        at = pl.ds(row, BRANCH)
+        k_ref[at, lanes(pair)] = (dk * scale).astype(k_ref.dtype)
+        v_ref[at, lanes(pair)] = dv.astype(v_ref.dtype)
 
     def pass_down(piece):
         at = pl.ds(pl.multiple_of(piece * PIECE, PIECE), PIECE)
@@ -635,11 +704,11 @@
         )
 
     def row_grad(b):
-        at = pl.ds(pl.multiple_of(b * BRANCH, BRANCH), BRANCH)
+        at = block_at(b)
         return dot_nt(k_ref[at], weight_ref[1]) + dot_nt(v_ref[at], weight_ref[2])
 
     def hand_down(b, total):
-        rows_ref[pl.ds(pl.multiple_of(b * BRANCH, BRANCH), BRANCH)] = total.astype(rows_ref.dtype)
+        rows_ref[block_at(b)] = total.astype(rows_ref.dtype)
 
         @pl.when(place == tensor - 1)
         def _():
@@ -650,9 +719,9 @@
         at = pl.ds(pl.multiple_of(piece * PIECE, PIECE), PIECE)
         return rows_ref[at].astype(jnp.float32) + land_ref[at].astype(jnp.float32)
 
-    middle = (place > 0) & (place < tensor - 1)
+    middle_place = (place > 0) & (place < tensor - 1)
     late = 3 * jnp.maximum(tensor - 2 - place, 0)
-    relayed = jnp.where(middle, jnp.where(place > 1, 2 * pieces, pieces), 0)
+    relayed = jnp.where(middle_place, jnp.where(place > 1, 2 * pieces, pieces), 0)
 
     def serve(first, last):
         def one(piece, carry):
@@ -665,9 +734,52 @@
         low = jnp.clip(first - late, 0, relayed)
         lax.fori_loop(low, jnp.clip(last - late, low, relayed), one, 0)
 
+    stage(0).start()
+
     @pl.loop(0, blocks)
     def _(b):
+        row = pl.multiple_of(b * BRANCH, BRANCH)
+
+        @pl.loop(0, pairs)
+        def _(pair):
+            def finish_block(masked):
+                tiles = [
+                    (row, first, causal(row, first) if masked else None)
+                    for first in range(0, rows, BRANCH)
+                ]
+                sums = sweep(pair, tiles)
+                put(pair, row, sum(part[0] for part in sums), sum(part[1] for part in sums))
+
+            @pl.when(place == 0)
+            def _():
+                finish_block(True)
+
+            @pl.when(place > 0)
+            def _():
+                finish_block(False)
+
+            @pl.when((pair > 1) & (b > 0))
+            def _():
+                piece = (b - 1) * (BRANCH // PIECE) + pair - 2
+                serve(piece, piece + 1)
+
+        for _half in range(2):
+            part = b * 2 + _half
+
+            @pl.when(part < 3 * rows // stage_rows)
+            def _():
+                stage(part).wait()
+
+                @pl.when(part + 1 < 3 * rows // stage_rows)
+                def _():
+                    stage(part + 1).start()
+
+                at = pl.ds(pl.multiple_of(part * stage_rows, stage_rows), stage_rows)
+                seen_ref[:, at] = stage_ref[lax.rem(part, 2)].T
+
         hand_down(b, row_grad(b))
+
+    served = (blocks - 1) * (BRANCH // PIECE)
 
     @pl.loop(0, pairs)
     def _(pair):
@@ -678,25 +790,21 @@
 
         @pl.when(place > 0)
         def _():
-            kt_ref[:, rows : 2 * rows] = k_ref[rows : 2 * rows, lanes(pair)].T
-            mask_heads(pair)
-
-            @pl.loop(0, blocks)
-            def _(b):
-                at = pl.multiple_of(b * BRANCH, BRANCH)
-                parent = pl.multiple_of(rows + at, BRANCH)
-                put(
-                    pair, parent,
-                    *step(
-                        pair, parent, at, BRANCH, lambda probs: jnp.where(place > 1, probs, 0.0)
-                    ),
-                )
-
-        serve(pair, pair + 1)
+            def seen_parent(probs):
+                return jnp.where(place > 1, probs, 0.0)
+
+            spots = range(0, rows, BRANCH)
+            sums = sweep(pair, [(rows + at, at, seen_parent) for at in spots])
+            for at, part in zip(spots, sums):
+                put(pair, rows + at, *part)
+
+        serve(jnp.minimum(served + pair, pieces), jnp.minimum(served + pair + 1, pieces))
+
+    served = pieces
 
     @pl.loop(0, blocks)
     def _(leaf):
-        out_ref[pl.ds(pl.multiple_of(leaf * BRANCH, BRANCH), BRANCH)] = row_grad(blocks + leaf)
+        out_ref[block_at(leaf)] = row_grad(blocks + leaf)
 
     for branch in range(blocks):
         total = None
@@ -706,26 +814,7 @@
             total = part if total is None else total + part
         hand_down(blocks + branch, total)
 
-    served = pairs
-    serve(served, served + 1)
-    served += 1
-    plain_loads[2].wait()
     gain_ref[...] = jnp.zeros_like(gain_ref)
-
-    def give(group, step):
-        return pltpu.make_async_remote_copy(
-            src_ref=slab_ref.at[group, peer(step)], dst_ref=slab_land.at[group, spot],
-            send_sem=slab_send.at[group, step], recv_sem=slab_recv.at[group, spot],
-            device_id=(peer(step), place), device_id_type=MESH,
-        )
-
-    def take(group, step):
-        source = peer(dp - step)
-        return pltpu.make_async_remote_copy(
-            src_ref=slab_ref.at[group, source], dst_ref=slab_land.at[group, source],
-            send_sem=slab_send.at[group, step], recv_sem=slab_recv.at[group, source],
-            device_id=(peer(step), place), device_id_type=MESH,
-        )
 
     @pl.loop(0, groups)
     def _(group):
@@ -737,54 +826,30 @@
 
             @pl.when(place > 0)
             def _():
-                kt_ref[:, 2 * rows : 3 * rows] = k_ref[2 * rows : 3 * rows, lanes(pair)].T
-                mask_heads(pair)
-
-                @pl.loop(0, blocks)
-                def _(b):
-                    at = pl.multiple_of(b * BRANCH, BRANCH)
-                    own = pl.multiple_of(2 * rows + at, BRANCH)
-                    put(pair, own, *step(pair, own, at, BRANCH, causal(0)))
+                spots = range(0, rows, BRANCH)
+                sums = sweep(pair, [(2 * rows + at, at, causal(0, 0)) for at in spots])
+                for at, part in zip(spots, sums):
+                    put(pair, 2 * rows + at, *part)
 
             q_ref[:, lanes(pair)] = (dqt_ref[pair] * scale).T.astype(q_ref.dtype)
             serve(base + half, base + half + 1)
 
         cols = pl.ds(pl.multiple_of(group * GROUP, GROUP), GROUP)
-
-        def keep(kind, value, weighted):
-            if weighted:
-                weight = weight_ref[kind, :, cols].astype(jnp.float32)
-                scaled = value * weight
-                gain_ref[...] += scaled[:, 0:128] + scaled[:, 128:256]
-            acc_ref[...] = value
-
-            def put_block(target, at):
-                slab_ref[group, target, 0:depth, kind * GROUP : (kind + 1) * GROUP] = acc_ref[
-                    at
-                ].astype(slab_ref.dtype)
-
-            if depth % 16:
-                for target in range(dp):
-                    put_block(target, slice(target * depth, (target + 1) * depth))
-            else:
-
-                @pl.loop(0, dp)
-                def _(target):
-                    put_block(target, pl.ds(pl.multiple_of(target * depth, depth), depth))
-
-        keep(0, dot_tn(seen_ref[2 * rows : 3 * rows], q_ref[:, cols]), True)
-        keep(3, dot_tn(bg_ref[...], o_ref[:, cols]), False)
-        serve(base + 2, base + 3)
-        for kind, ref in ((1, k_ref), (2, v_ref)):
-            value = dot_tn(seen_ref[0:rows], ref[0:rows, cols])
-            value = value + dot_tn(seen_ref[rows : 2 * rows], ref[rows : 2 * rows, cols])
-            value = value + dot_tn(seen_ref[2 * rows : 3 * rows], ref[2 * rows : 3 * rows, cols])
-            keep(kind, value, True)
-        serve(base + 3, base + 4)
+        for kind, value in (
+            (0, lambda: dot_nn(seen_ref[:, 2 * rows : 3 * rows], q_ref[:, cols])),
+            (1, lambda: dot_nn(seen_ref[...], k_ref[:, cols])),
+            (2, lambda: dot_nn(seen_ref[...], v_ref[:, cols])),
+        ):
+            product = value()
+            scaled = product * weight_ref[kind, :, cols].astype(jnp.float32)
+            gain_ref[...] += scaled[:, 0:128] + scaled[:, 128:256]
+            keep(slab_ref.at[group], product, kind)
+            if kind:
+                serve(base + 1 + kind, base + 2 + kind)
 
         @pl.loop(1, dp)
-        def _(step_):
-            give(group, step_).start()
+        def _(step):
+            give(group, step).start()
 
     served += groups * 4
 
@@ -825,47 +890,50 @@
         )
 
     @pl.loop(1, ways)
-    def _(step_):
-        scatter(step_).start()
+    def _(step):
+        scatter(step).start()
 
     @pl.loop(0, blocks)
     def _(b):
-        at = pl.ds(pl.multiple_of(b * BRANCH, BRANCH), BRANCH)
+        at = block_at(b)
         out_ref[at] = row_grad(2 * blocks + b) + dot_nt(q_ref[at], weight_ref[0])
-        serve(served + b, served + b + 1)
-
-    served += blocks
-
-    def add(step_, total):
-        arrival(step_).wait_recv()
-        return total + part_land[lax.rem(me - step_ + ways, ways)]
+        serve(served + 2 * b, served + 2 * b + 2)
+
+    served += 2 * blocks
+
+    def add(step, total):
+        arrival(step).wait_recv()
+        return total + part_land[lax.rem(me - step + ways, ways)]
 
     total_ref[me] = lax.fori_loop(1, ways, add, part_ref[me])
 
     @pl.loop(1, ways)
-    def _(step_):
-        spread(step_).start()
+    def _(step):
+        spread(step).start()
 
     serve(served, 2 * pieces)
-
-    @pl.loop(0, groups)
-    def _(group):
-        slab_sum[group] = slab_ref[group, spot].astype(jnp.float32)
+    serve(2 * pieces, 2 * pieces + late)
+
+    kinds = [[], [], [], []]
+    for group in range(groups + 1):
 
         @pl.loop(1, dp)
-        def _(step_):
-            take(group, step_).wait_recv()
-            slab_sum[group] += slab_land[group, peer(dp - step_)].astype(jnp.float32)
-
-    serve(2 * pieces, 2 * pieces + late)
+        def _(step):
+            take(group, step).wait_recv()
+
+        own, landed = slabs(group)
+
+        def add_slab(step, total):
+            return total + landed[peer(dp - step)].astype(jnp.float32)
+
+        total = lax.fori_loop(1, dp, add_slab, own[spot].astype(jnp.float32))
+        for part in range(total.shape[1] // GROUP):
+            kinds[3 if group == groups else part].append(
+                total[:, part * GROUP : (part + 1) * GROUP]
+            )
+
     share = width // tensor
-    kinds = [
-        jnp.concatenate(
-            [slab_sum[group][:, kind * GROUP : (kind + 1) * GROUP] for group in range(groups)],
-            axis=1,
-        )
-        for kind in range(4)
-    ]
+    kinds = [jnp.concatenate(parts, axis=1) for parts in kinds]
     for target in range(tensor):
         mine = jnp.concatenate(
             [kind[:, target * share : (target + 1) * share] for kind in kinds], axis=1
@@ -891,8 +959,8 @@
             device_id=(spot, along(step)), device_id_type=MESH,
         )
 
-    for step_ in range(1, tensor):
-        line(step_).start()
+    for step in range(1, tensor):
+        line(step).start()
 
     @pl.when(place < 2)
     def _():
@@ -903,27 +971,27 @@
             at = pl.ds(pl.multiple_of(piece * PIECE, PIECE), PIECE)
             out_ref[at] += joined(source)
 
-    for step_ in range(1, tensor):
-        line_in(step_).wait_recv()
-        sum_ref[...] += line_land[along(tensor - step_)].astype(jnp.float32)
+    for step in range(1, tensor):
+        line_in(step).wait_recv()
+        sum_ref[...] += line_land[along(tensor - step)].astype(jnp.float32)
 
     @pl.loop(1, ways)
-    def _(step_):
-        landing(step_).wait_recv()
-
-    for step_ in range(1, tensor):
-        line(step_).wait_send()
+    def _(step):
+        landing(step).wait_recv()
+
+    for step in range(1, tensor):
+        line(step).wait_send()
 
     @pl.loop(1, ways)
-    def _(step_):
-        scatter(step_).wait_send()
-        spread(step_).wait_send()
-
-    @pl.loop(0, groups)
-    def _(group):
+    def _(step):
+        scatter(step).wait_send()
+        spread(step).wait_send()
+
+    for group in range(groups + 1):
+
         @pl.loop(1, dp)
-        def _(step_):
-            give(group, step_).wait_send()
+        def _(step):
+            give(group, step).wait_send()
 
     sent = jnp.where(place == tensor - 1, 2 * pieces, relayed)
 
@@ -942,7 +1010,8 @@
     depth = width // dp
     padded = -(-depth // 16) * 16
     pairs, groups, pieces = width // 128, width // GROUP, rows // PIECE
-    slab = (groups, dp, padded, 4 * GROUP)
+    slab = (groups, dp, padded, 3 * GROUP)
+    proj = (dp, padded, width)
     low, full = jnp.bfloat16, jnp.float32
     dma = pltpu.SemaphoreType.DMA
     anywhere = pl.BlockSpec(memory_space=pl.ANY)
@@ -963,27 +1032,25 @@
             pltpu.VMEM((rows, width), low),
             pltpu.VMEM((rows, width), low),
             pltpu.VMEM((rows, width), low),
-            pltpu.VMEM((seen_rows, width), low),
+            pltpu.VMEM((2, rows // 2, width), low),
+            pltpu.VMEM((width, seen_rows), low),
             pltpu.VMEM(weights.shape, low),
-            pltpu.VMEM((128, seen_rows), low),
-            pltpu.VMEM((2, rows, 128), low),
-            pltpu.VMEM((2, rows, 128), low),
             pltpu.VMEM((pairs, 2, rows), full),
             pltpu.VMEM((pairs, 128, rows), full),
             pltpu.VMEM((2 * rows, width), low),
             pltpu.VMEM((2 * rows, width), low),
-            pltpu.VMEM((width, GROUP), full),
             pltpu.VMEM((width, 128), full),
             pltpu.VMEM(slab, low),
             pltpu.VMEM(slab, low),
-            pltpu.VMEM((groups, padded, 4 * GROUP), full),
+            pltpu.VMEM(proj, low),
+            pltpu.VMEM(proj, low),
             pltpu.VMEM((tensor, padded, width), low),
             pltpu.VMEM((tensor, padded, width), low),
             pltpu.VMEM(small.shape, full),
             pltpu.VMEM(small.shape, full),
-            dma((3,)), dma((4, pairs)),
+            dma((3,)), dma((3, pairs)), dma((2,)),
             dma((2 * pieces,)), dma((2 * pieces,)),
-            dma((groups, dp)), dma((groups, dp)),
+            dma((groups + 1, dp)), dma((groups + 1, dp)),
             dma((tensor,)), dma((tensor,)),
             dma((ways,)), dma((ways,)), dma((ways,)), dma((ways,)),
         ],
@@ -1152,20 +1219,14 @@
     router_part, proj_grad, embed_grad = gate_back(gate_grad)
     mid_part, gain2_grad = norm2_back(moe_grad + router_part)
     mid_grad = upstream + mid_part
-    expert_grads = jnp.stack(
-        [
-            part.reshape(tensor_size, -1, model_width)
-            for part in (in_weight_grad, out_weight_grad)
-        ],
-        axis=1,
+    expert_in_grad = (
+        lax.psum_scatter(in_weight_grad, "tensor", scatter_dimension=0, tiled=True)
+        .astype(jnp.float32)
+        .T
     )
-    mid_grad, expert_grads = lax.optimization_barrier((mid_grad, expert_grads))
-    expert_grad_block = lax.psum_scatter(
-        expert_grads.reshape(-1, model_width), "tensor", scatter_dimension=0, tiled=True
+    expert_out_grad = lax.psum_scatter(
+        out_weight_grad, "tensor", scatter_dimension=0, tiled=True
     ).astype(jnp.float32)
-    half_block = expert_grad_block.shape[0] // 2
-    expert_in_grad = expert_grad_block[:half_block].T
-    expert_out_grad = expert_grad_block[half_block:]
     branch_grad = mid_grad.astype(jnp.bfloat16)
     later = [gain2_grad, proj_grad, embed_grad]
     flat = jnp.concatenate([jnp.zeros_like(norm1_gain)] + [part.reshape(-1) for part in later])

time: 513 us -> 477 us (0.930)
  Pallas kernels: 360 us -> 301 us
  matrix products: 45.9 us -> 56.6 us
  waiting for transfers between devices: 28.9 us -> 35.7 us
    pallas_call x1, Pallas kernels: 231 us -> 196 us  [backward(): pl.pallas_call(lambda *refs: back_kernel(dp, tensor, depth, *refs), out_s...]
    pallas_call x1, Pallas kernels: 43.7 us -> 18.5 us  [attend(): pl.pallas_call(fwd_kernel, out_shape=(jax.ShapeDtypeStruct((rows, width),...]
    ppermute x16, waiting for transfers between devices: 28.9 us -> 35.7 us  [hop(): return lax.ppermute(rows, 'dp', route)]
    unnamed x70 -> x78, local copies, waits for them, and re-layouts: 7.98 us -> 11.5 us
  transfers between devices with their start and end apart: 17 -> 18, of which waited for: 6 -> 9; matrix products, arithmetic and copies ran while one was open for 9% -> 13% of each run, Pallas kernels for 51% -> 45%
where the time goes in v6:
time: 477 us; the launch traced here: 473 us
  Pallas kernels  301 us (63%)
  matrix products  56.6 us (12%)
  waiting for transfers between devices  35.7 us (7%)
  other arithmetic  28.8 us (6%)
  local copies, waits for them, and re-layouts  21.2 us (4%)
  between operations  15.1 us (3%)
  starting transfers between devices  14.9 us (3%)
    pallas_call x1, Pallas kernels, backward(): pl.pallas_call(lambda *refs: back_kernel(dp, tensor, depth, *refs), out_s...  196 us
    pallas_call x1, Pallas kernels, share_rows_and_weights(): pl.pallas_call(lambda *refs: share_kernel(dp, tensor, *refs), out_shape=(...  54.5 us
    ppermute x16, waiting for transfers between devices, hop(): return lax.ppermute(rows, 'dp', route)  35.7 us
    pallas_call x1, Pallas kernels, attend(): pl.pallas_call(fwd_kernel, out_shape=(jax.ShapeDtypeStruct((rows, width),...  18.5 us
    pallas_call x1, Pallas kernels, expert_forward(): pl.pallas_call(expert_fwd_kernel, grid=(count,), in_specs=[wide(width), w...  15.6 us
    pallas_call x1, Pallas kernels, expert_back(): pl.pallas_call(expert_bwd_kernel, grid=(count,), in_specs=[wide(width), w...  15.4 us
    ppermute x16, starting transfers between devices, hop(): return lax.ppermute(rows, 'dp', route)  14.9 us
    dot_general x3, matrix products, low_dot(): jnp.dot(rows, weight, preferred_element_type=jnp.float32)  13.7 us
  transfers between devices with their start and end apart: 18, of which 9 were waited for; matrix products, arithmetic and copies ran while one was open for 13% of the time, Pallas kernels for 45%

profile of v6, /device:TPU:0, one launch (start us, length us, event | category | flops | bytes accessed | tf_op | source)
XLA Modules:
  0.0 472.7 jit_solution(15456092625051929976)
XLA Ops:
  8.8 2.0 select_reduce_fusion
  13.4 2.0 fusion.13
  16.6 54.5 %share_rows_and_weights.1 = (bf16[3072,768]{1,0:T(8,128)(2,1)}, bf16[4,768,768]{2,1,0:T(8,128)(2,1)}) custom-call(bf16[1024,768]{1,0:T(8,128)(2,1)S(1)} %fusion.15.refs_0_, bf16[96,768]{1,0:T(8,128)(2,1)S(1)} %pad_maximum_fusion.2.refs_1_, f32[16,768]{1,0:T(8,128)S(1)} %broadcast_in_dim.31.refs_2_.refs_0_), custom_call_target="tpu_custom_call" | custom-call | tf_op jit(solution)/shard_map/share_rows_and_weights/pallas_call | solution.py:454
  71.2 2.8 convolution_convert_fusion.4.q_ref.refs_1_
  74.0 1.8 copy-done.23
  75.9 5.5 %convolution_convert_fusion.v_ref.refs_3_ = bf16[3072,768]{1,0:T(8,128)(2,1)} fusion(bf16[3072,768]{1,0:T(8,128)(2,1)S(1)} %copy-done.22, bf16[4,768,768]{2,1,0:T(8,128)(2,1)S(1)} %copy-done.23), kind=kOutput, calls=%fused_computation | convolution fusion | flops 3626237952 | bytes 10616832 | tf_op jit(solution)/shard_map/dot_general | solution.py:1101
  81.3 5.4 %convolution_convert_fusion.1.k_ref.refs_2_ = bf16[3072,768]{1,0:T(8,128)(2,1)} fusion(bf16[3072,768]{1,0:T(8,128)(2,1)S(1)} %copy-done.22, bf16[4,768,768]{2,1,0:T(8,128)(2,1)S(1)} %copy-done.23), kind=kOutput, calls=%fused_computation.1 | convolution fusion | flops 3626237952 | bytes 10616832 | tf_op jit(solution)/shard_map/dot_general | solution.py:1101
  86.8 18.5 %attend_forward.1 = (bf16[1024,768]{1,0:T(8,128)(2,1)S(1)}, f32[6,2,1024]{2,1,0:T(2,128)S(1)}) custom-call(s32[1]{0:T(128)} %bitcast.place_ref, bf16[1024,768]{1,0:T(8,128)(2,1)S(1)} %convolution_convert_fusion.4.q_ref.refs_1_, bf16[3072,768]{1,0:T(8,128)(2,1)} %convolution_convert_fusion.1.k_ref.refs_2_, bf16[3072,768]{1,0:T(8,128)(2,1)} %convolution_convert_fusion.v_ref.refs_3_), custom_call_target="tpu_custom_call" | custom-call | tf_op jit(solution)/shard_map/attend_forward/pallas_call | solution.py:113
  108.6 2.5 fusion.31
  111.2 2.5 collective-permute-start.2
  116.6 2.6 fusion.34
  119.2 5.1 %collective-permute-done.2 = bf16[256,768]{1,0:T(8,128)(2,1)S(1)} collective-permute-done((bf16[256,768]{1,0:T(8,128)(2,1)S(1)}, bf16[256,768]{1,0:T(8,128)(2,1)S(1)}, u32[]{:S(2)}, u32[]{:S(2)}) %collective-permute-start.2) | collective-permute-done | bytes 393248 | tf_op jit(solution)/shard_map/ppermute | solution.py:1130
  124.3 6.3 %collective-permute-done.1 = bf16[256,768]{1,0:T(8,128)(2,1)S(1)} collective-permute-done((bf16[256,768]{1,0:T(8,128)(2,1)S(1)}, bf16[256,768]{1,0:T(8,128)(2,1)S(1)}, u32[]{:S(2)}, u32[]{:S(2)}) %collective-permute-start.1) | collective-permute-done | bytes 393248 | tf_op jit(solution)/shard_map/ppermute | solution.py:1130
  136.4 15.6 %expert_forward.1 = (bf16[2048,1536]{1,0:T(8,128)(2,1)}, bf16[2048,1536]{1,0:T(8,128)(2,1)}, f32[1024,768]{1,0:T(8,128)S(1)}, bf16[1024,768]{1,0:T(8,128)(2,1)S(1)}) custom-call(bf16[2048,768]{1,0:T(8,128)(2,1)S(1)} %constant_dynamic-update-slice_fusion.x_ref, bf16[768,1536]{1,0:T(8,128)(2,1)S(1)} %copy-done.7, bf16[1536,768]{1,0:T(8,128)(2,1)S(1)} %copy-done.8), custom_call_target="tpu_custom_call" | custom-call | flops 9663676416 | bytes 25165824 | tf_op jit(solution)/shard_map/expert_forward/pallas_call | solution.py:203
  152.9 2.6 collective-permute-done.7
  157.9 15.4 %expert_backward.1 = (bf16[2048,1536]{1,0:T(8,128)(2,1)}, f32[1024,768]{1,0:T(8,128)S(1)}, bf16[1024,768]{1,0:T(8,128)(2,1)S(1)}) custom-call(bf16[2048,768]{1,0:T(8,128)(2,1)S(1)} %constant_dynamic-update-slice_fusion.5.grad_ref, bf16[2048,1536]{1,0:T(8,128)(2,1)} %get-tuple-element.55.slope_ref, bf16[768,1536]{1,0:T(8,128)(2,1)S(1)} %copy-done.7, ...), custom_call_target="tpu_custom_call" | custom-call | flops 9663676416 | bytes 25165824 | tf_op jit(solution)/shard_map/expert_backward/pallas_call | solution.py:228
  176.0 9.3 %convolution_convert_fusion.3 = bf16[1536,768]{1,0:T(8,128)(2,1)} fusion(bf16[2048,1536]{1,0:T(8,128)(2,1)} %get-tuple-element.62, bf16[2048,768]{1,0:T(8,128)(2,1)S(1)} %constant_dynamic-update-slice_fusion.x_ref), kind=kOutput, calls=%fused_computation.22 | convolution fusion | flops 4833017856 | bytes 11796480 | tf_op jit(solution)/shard_map/rf,rd->fd/dot_general | solution.py:1214
  185.4 2.5 fusion.91
  191.4 9.4 %convolution_convert_fusion.2 = bf16[1536,768]{1,0:T(8,128)(2,1)} fusion(bf16[2048,1536]{1,0:T(8,128)(2,1)} %get-tuple-element.63, bf16[2048,768]{1,0:T(8,128)(2,1)S(1)} %constant_dynamic-update-slice_fusion.5.grad_ref), kind=kOutput, calls=%fused_computation.21 | convolution fusion | flops 4833017856 | bytes 11796480 | tf_op jit(solution)/shard_map/rf,rd->fd/dot_general | solution.py:1210
  201.2 7.6 %collective-permute-done.10 = bf16[256,768]{1,0:T(8,128)(2,1)} collective-permute-done((bf16[256,768]{1,0:T(8,128)(2,1)}, bf16[256,768]{1,0:T(8,128)(2,1)}, u32[]{:S(2)}, u32[]{:S(2)}) %collective-permute-start.10) | collective-permute-done | bytes 393248 | tf_op jit(solution)/shard_map/ppermute | solution.py:1130
  208.8 5.8 %fusion.18 = (f32[1024]{0:T(1024)S(1)}, f32[1024,768]{1,0:T(8,128)}) fusion(bf16[1024,768]{1,0:T(8,128)(2,1)} %param.25, bf16[256,768]{1,0:T(8,128)(2,1)} %collective-permute-done.11, bf16[256,768]{1,0:T(8,128)(2,1)} %collective-permute-done.10, bf16[256,768]{1,0:T(8,128)(2,1)} %collective-permute-done.9, bf16[256,768]{1,0:T(8,128)(2,1)} %get-tuple-element.103, ...), kind=kOutput, calls=%fused_computation.28 | convolution fusion | flops 1621359616 | bytes 6300672 | tf_op jit(solution)/shard_map/dot_general | solution.py:1191
  215.3 2.5 fusion.73
  224.1 2.8 fusion.74
  226.9 5.6 %collective-permute-done.15 = bf16[256,768]{1,0:T(8,128)(2,1)} collective-permute-done((bf16[256,768]{1,0:T(8,128)(2,1)}, bf16[256,768]{1,0:T(8,128)(2,1)}, u32[]{:S(2)}, u32[]{:S(2)}) %collective-permute-start.15) | collective-permute-done | bytes 393248 | tf_op jit(solution)/shard_map/ppermute | solution.py:1130
  232.6 7.4 %collective-permute-done.14 = bf16[256,768]{1,0:T(8,128)(2,1)} collective-permute-done((bf16[256,768]{1,0:T(8,128)(2,1)}, bf16[256,768]{1,0:T(8,128)(2,1)}, u32[]{:S(2)}, u32[]{:S(2)}) %collective-permute-start.14) | collective-permute-done | bytes 393248 | tf_op jit(solution)/shard_map/ppermute | solution.py:1130
  240.0 4.1 multiply_reduce_fusion
  244.9 2.7 fusion.89
  247.5 1.9 fusion.27.refs_5_
  249.7 196.5 %attend_backward.1 = (f32[1024,768]{1,0:T(8,128)}, f32[96,768]{1,0:T(8,128)}, f32[32,8,128]{2,1,0:T(8,128)}) custom-call(f32[16,768]{1,0:T(8,128)} %copy-done.5, bf16[1024,768]{1,0:T(8,128)(2,1)} %copy-done.1, bf16[3072,768]{1,0:T(8,128)(2,1)} %convolution_convert_fusion.1.k_ref.refs_2_, bf16[3072,768]{1,0:T(8,128)(2,1)} %convolution_convert_fusion.v_ref.refs_3_, ...), custom_call_target="tpu_custom_call" | custom-call | tf_op jit(solution)/shard_map/attend_backward/pallas_call | solution.py:1019
  452.7 2.8 fusion.16
  458.3 2.7 add_add_fusion.2
  463.5 2.2 convert_element_type.93
  (169 shorter events, 46.6 us)
Async XLA Ops:
  7.2 107.7 %copy-start = (f32[768,16]{0,1:T(8,128)S(1)}, f32[768,16]{0,1:T(8,128)}, u32[]{:S(2)}) copy-start(f32[768,16]{0,1:T(8,128)} %param.18) | copy-start | bytes 147460
  7.2 8.8 %copy-start.10 = (bf16[1024,768]{1,0:T(8,128)(2,1)S(1)}, bf16[1024,768]{1,0:T(8,128)(2,1)}, u32[]{:S(2)}) copy-start(bf16[1024,768]{1,0:T(8,128)(2,1)} %param.13) | copy-start | bytes 4718596
  7.2 8.3 %copy-start.29 = (bf16[192,96]{1,0:T(8,128)(2,1)S(1)}, bf16[192,96]{1,0:T(8,128)(2,1)}, u32[]{:S(2)}) copy-start(bf16[192,96]{1,0:T(8,128)(2,1)} %param.16) | copy-start | bytes 110596
  7.2 8.4 %copy-start.26 = (bf16[96,3,192]{2,0,1:T(8,128)(2,1)S(1)}, bf16[96,3,192]{2,0,1:T(8,128)(2,1)}, u32[]{:S(2)}) copy-start(bf16[96,3,192]{2,0,1:T(8,128)(2,1)} %param.15) | copy-start | bytes 331780
  7.2 8.8 %copy-start.28 = (f32[768]{0:T(1024)S(1)}, f32[768]{0:T(1024)}, u32[]{:S(2)}) copy-start(f32[768]{0:T(1024)} %param.14) | copy-start | bytes 9220
  7.2 453.7 %reduce-scatter.3.cloned.1.call-start = ((), (), s32[]{:S(2)}) async-start(), calls=%async_computation.2 | async-start | bytes 2949120 | tf_op jit(solution)/shard_map/reduce_scatter | solution.py:1223
  16.6 57.4 %copy-start.5 = (f32[16,768]{1,0:T(8,128)}, f32[16,768]{1,0:T(8,128)S(1)}, u32[]{:S(2)}) copy-start(f32[16,768]{1,0:T(8,128)S(1)} %broadcast_in_dim.31.refs_2_.refs_0_) | copy-start | bytes 147460
  74.0 12.8 %copy-start.1 = (bf16[1024,768]{1,0:T(8,128)(2,1)}, bf16[1024,768]{1,0:T(8,128)(2,1)S(1)}, u32[]{:S(2)}) copy-start(bf16[1024,768]{1,0:T(8,128)(2,1)S(1)} %convolution_convert_fusion.4.q_ref.refs_1_) | copy-start | bytes 4718596
  108.6 6.3 %copy-start.17 = (bf16[1024,768]{1,0:T(8,128)(2,1)}, bf16[1024,768]{1,0:T(8,128)(2,1)S(1)}, u32[]{:S(2)}) copy-start(bf16[1024,768]{1,0:T(8,128)(2,1)S(1)} %multiply_convert_fusion) | copy-start | bytes 4718596
  111.1 5.5 %copy-start.19 = (bf16[1024,768]{1,0:T(8,128)(2,1)S(1)}, bf16[1024,768]{1,0:T(8,128)(2,1)}, u32[]{:S(2)}) copy-start(bf16[1024,768]{1,0:T(8,128)(2,1)} %param.25) | copy-start | bytes 4718596
  111.2 13.1 %collective-permute-start.2 = (bf16[256,768]{1,0:T(8,128)(2,1)S(1)}, bf16[256,768]{1,0:T(8,128)(2,1)S(1)}, u32[]{:S(2)}, u32[]{:S(2)}) collective-permute-start(bf16[256,768]{1,0:T(8,128)(2,1)S(1)} %get-tuple-element.111), channel_id=1, source_target_pairs={{0,24},{4,28},{8,16},{12,20},{16,8},{20,12},{24,0},{28,4},{1,25},{... | collective-permute-start | bytes 1179656 | tf_op jit(solution)/shard_map/ppermute | solution.py:1130
  113.7 16.9 %collective-permute-start.1 = (bf16[256,768]{1,0:T(8,128)(2,1)S(1)}, bf16[256,768]{1,0:T(8,128)(2,1)S(1)}, u32[]{:S(2)}, u32[]{:S(2)}) collective-permute-start(bf16[256,768]{1,0:T(8,128)(2,1)S(1)} %get-tuple-element.112), channel_id=1, source_target_pairs={{0,16},{4,20},{8,24},{12,28},{16,0},{20,4},{24,8},{28,12},{1,17},{... | collective-permute-start | bytes 1179656 | tf_op jit(solution)/shard_map/ppermute | solution.py:1130
  114.2 16.5 %collective-permute-start = (bf16[256,768]{1,0:T(8,128)(2,1)S(1)}, bf16[256,768]{1,0:T(8,128)(2,1)S(1)}, u32[]{:S(2)}, u32[]{:S(2)}) collective-permute-start(bf16[256,768]{1,0:T(8,128)(2,1)S(1)} %get-tuple-element.113), channel_id=1, source_target_pairs={{0,8},{4,12},{8,0},{12,4},{16,24},{20,28},{24,16},{28,20},{1,9},{5... | collective-permute-start | bytes 1179656 | tf_op jit(solution)/shard_map/ppermute | solution.py:1130
  130.8 3.9 collective-permute-start.6
  131.0 21.0 %collective-permute-start.5 = (bf16[256,768]{1,0:T(8,128)(2,1)S(1)}, bf16[256,768]{1,0:T(8,128)(2,1)S(1)}, u32[]{:S(2)}, u32[]{:S(2)}) collective-permute-start(bf16[256,768]{1,0:T(8,128)(2,1)S(1)} %get-tuple-element.107), channel_id=1, source_target_pairs={{0,24},{4,28},{8,16},{12,20},{16,8},{20,12},{24,0},{28,4},{1,25},{... | collective-permute-start | bytes 1179656 | tf_op jit(solution)/shard_map/ppermute | solution.py:1130
  132.7 19.3 %collective-permute-start.4 = (bf16[256,768]{1,0:T(8,128)(2,1)S(1)}, bf16[256,768]{1,0:T(8,128)(2,1)S(1)}, u32[]{:S(2)}, u32[]{:S(2)}) collective-permute-start(bf16[256,768]{1,0:T(8,128)(2,1)S(1)} %get-tuple-element.108), channel_id=1, source_target_pairs={{0,16},{4,20},{8,24},{12,28},{16,0},{20,4},{24,8},{28,12},{1,17},{... | collective-permute-start | bytes 1179656 | tf_op jit(solution)/shard_map/ppermute | solution.py:1130
  134.0 18.0 %collective-permute-start.3 = (bf16[256,768]{1,0:T(8,128)(2,1)S(1)}, bf16[256,768]{1,0:T(8,128)(2,1)S(1)}, u32[]{:S(2)}, u32[]{:S(2)}) collective-permute-start(bf16[256,768]{1,0:T(8,128)(2,1)S(1)} %get-tuple-element.109), channel_id=1, source_target_pairs={{0,8},{4,12},{8,0},{12,4},{16,24},{20,28},{24,16},{28,20},{1,9},{5... | collective-permute-start | bytes 1179656 | tf_op jit(solution)/shard_map/ppermute | solution.py:1130
  152.0 3.5 collective-permute-start.7
  152.2 5.5 %collective-permute-start.8 = (bf16[1024,768]{1,0:T(8,128)(2,1)S(1)}, bf16[1024,768]{1,0:T(8,128)(2,1)S(1)}, u32[]{:S(2)}, u32[]{:S(2)}) collective-permute-start(bf16[1024,768]{1,0:T(8,128)(2,1)S(1)} %pad_maximum_fusion.1), channel_id=1, source_target_pairs={{0,4},{4,0},{8,12},{12,8},{16,20},{20,16},{24,28},{28,24},{1,5},{5... | collective-permute-start | bytes 4718600 | tf_op jit(solution)/shard_map/ppermute | solution.py:1130
  185.4 278.1 %reduce-scatter.5.cloned.1.call-start = ((), (), s32[]{:S(2)}) async-start(), calls=%async_computation.3 | async-start | bytes 2949120 | tf_op jit(solution)/shard_map/reduce_scatter | solution.py:1227
  188.0 13.2 %collective-permute-start.11 = (bf16[256,768]{1,0:T(8,128)(2,1)}, bf16[256,768]{1,0:T(8,128)(2,1)}, u32[]{:S(2)}, u32[]{:S(2)}) collective-permute-start(bf16[256,768]{1,0:T(8,128)(2,1)} %get-tuple-element.104), channel_id=1, source_target_pairs={{0,24},{4,28},{8,16},{12,20},{16,8},{20,12},{24,0},{28,4},{1,25},{... | collective-permute-start | bytes 1179656 | tf_op jit(solution)/shard_map/ppermute | solution.py:1130
  189.4 19.4 %collective-permute-start.10 = (bf16[256,768]{1,0:T(8,128)(2,1)}, bf16[256,768]{1,0:T(8,128)(2,1)}, u32[]{:S(2)}, u32[]{:S(2)}) collective-permute-start(bf16[256,768]{1,0:T(8,128)(2,1)} %get-tuple-element.105), channel_id=1, source_target_pairs={{0,16},{4,20},{8,24},{12,28},{16,0},{20,4},{24,8},{28,12},{1,17},{... | collective-permute-start | bytes 1179656 | tf_op jit(solution)/shard_map/ppermute | solution.py:1130
  190.7 18.0 %collective-permute-start.9 = (bf16[256,768]{1,0:T(8,128)(2,1)}, bf16[256,768]{1,0:T(8,128)(2,1)}, u32[]{:S(2)}, u32[]{:S(2)}) collective-permute-start(bf16[256,768]{1,0:T(8,128)(2,1)} %get-tuple-element.106), channel_id=1, source_target_pairs={{0,8},{4,12},{8,0},{12,4},{16,24},{20,28},{24,16},{28,20},{1,9},{5... | collective-permute-start | bytes 1179656 | tf_op jit(solution)/shard_map/ppermute | solution.py:1130
  200.9 16.9 %collective-permute-start.12 = (bf16[1024,768]{1,0:T(8,128)(2,1)}, bf16[1024,768]{1,0:T(8,128)(2,1)S(1)}, u32[]{:S(2)}, u32[]{:S(2)}) collective-permute-start(bf16[1024,768]{1,0:T(8,128)(2,1)} %copy-done.9), channel_id=1, source_target_pairs={{0,4},{4,0},{8,12},{12,8},{16,20},{20,16},{24,28},{28,24},{1,5},{5... | collective-permute-start | bytes 4718600 | tf_op jit(solution)/shard_map/ppermute | solution.py:1130
  208.8 6.5 %copy-start.18 = (bf16[1024,768]{1,0:T(8,128)(2,1)S(1)}, bf16[1024,768]{1,0:T(8,128)(2,1)}, u32[]{:S(2)}) copy-start(bf16[1024,768]{1,0:T(8,128)(2,1)} %copy-done.17) | copy-start | bytes 4718596
  208.8 9.0 %copy-start.3 = (f32[1024,768]{1,0:T(8,128)S(1)}, f32[1024,768]{1,0:T(8,128)}, u32[]{:S(2)}) copy-start(f32[1024,768]{1,0:T(8,128)} %copy-done.2) | copy-start | bytes 9437188
  218.1 21.9 %copy-start.14 = (f32[1024,768]{1,0:T(8,128)S(1)}, f32[1024,768]{1,0:T(8,128)}, u32[]{:S(2)}) copy-start(f32[1024,768]{1,0:T(8,128)} %copy-done.13) | copy-start | bytes 9437188
  219.3 13.2 %collective-permute-start.15 = (bf16[256,768]{1,0:T(8,128)(2,1)}, bf16[256,768]{1,0:T(8,128)(2,1)}, u32[]{:S(2)}, u32[]{:S(2)}) collective-permute-start(bf16[256,768]{1,0:T(8,128)(2,1)} %get-tuple-element.100), channel_id=1, source_target_pairs={{0,24},{4,28},{8,16},{12,20},{16,8},{20,12},{24,0},{28,4},{1,25},{... | collective-permute-start | bytes 1179656 | tf_op jit(solution)/shard_map/ppermute | solution.py:1130
  220.8 19.2 %collective-permute-start.14 = (bf16[256,768]{1,0:T(8,128)(2,1)}, bf16[256,768]{1,0:T(8,128)(2,1)}, u32[]{:S(2)}, u32[]{:S(2)}) collective-permute-start(bf16[256,768]{1,0:T(8,128)(2,1)} %get-tuple-element.101), channel_id=1, source_target_pairs={{0,16},{4,20},{8,24},{12,28},{16,0},{20,4},{24,8},{28,12},{1,17},{... | collective-permute-start | bytes 1179656 | tf_op jit(solution)/shard_map/ppermute | solution.py:1130
  222.1 17.9 %collective-permute-start.13 = (bf16[256,768]{1,0:T(8,128)(2,1)}, bf16[256,768]{1,0:T(8,128)(2,1)}, u32[]{:S(2)}, u32[]{:S(2)}) collective-permute-start(bf16[256,768]{1,0:T(8,128)(2,1)} %get-tuple-element.102), channel_id=1, source_target_pairs={{0,8},{4,12},{8,0},{12,4},{16,24},{20,28},{24,16},{28,20},{1,9},{5... | collective-permute-start | bytes 1179656 | tf_op jit(solution)/shard_map/ppermute | solution.py:1130
  224.1 15.9 %copy-start.25 = (bf16[256,768]{1,0:T(8,128)(2,1)S(1)}, bf16[256,768]{1,0:T(8,128)(2,1)}, u32[]{:S(2)}) copy-start(bf16[256,768]{1,0:T(8,128)(2,1)} %get-tuple-element.99) | copy-start | bytes 1179652
  446.2 6.4 %copy-start.11 = (bf16[1024,768]{1,0:T(8,128)(2,1)S(1)}, bf16[1024,768]{1,0:T(8,128)(2,1)}, u32[]{:S(2)}) copy-start(bf16[1024,768]{1,0:T(8,128)(2,1)} %param.13) | copy-start | bytes 4718596
  (18 other events, 47.2 us)
Sparse Core Ops, SparseCore 0:
  185.5 99.7 reduce-scatter.2
  287.5 55.2 reduce-scatter.4

commit v7 on v6

--- a/solution.py
+++ b/solution.py
@@ -490,8 +490,9 @@
     out_ref, sum_ref, total_ref,
     q_ref, k_ref, v_ref, o_ref, bg_ref, g_ref, stage_ref, seen_ref, weight_ref,
     delta_ref, dqt_ref, rows_ref, land_ref, gain_ref,
-    slab_ref, slab_land, proj_ref, proj_land, line_out, line_land, part_ref, part_land,
-    load_sem, pair_sem, stage_sem, row_send, row_recv, slab_send, slab_recv,
+    slab_ref, pair_land, chip_land, line_out, line_land, part_ref, part_land,
+    load_sem, pair_sem, stage_sem, row_send, row_recv,
+    pair_send, pair_recv, chip_send, chip_recv,
     line_send, line_recv, small_send, small_recv, spread_send, spread_recv,
 ):
     spot, place = lax.axis_index("dp"), lax.axis_index("tensor")
@@ -511,8 +512,11 @@
     def along(step):
         return lax.rem(place + step, tensor)
 
-    def peer(step):
-        return lax.rem(spot + step, dp)
+    chips = dp // 2
+    chip, core = spot // 2, lax.rem(spot, 2)
+
+    def chip_at(step):
+        return lax.rem(chip + step, chips)
 
     def block_at(b):
         return pl.ds(pl.multiple_of(b * BRANCH, BRANCH), BRANCH)
@@ -570,7 +574,7 @@
 
     for group in range(groups):
         cols = slice(group * GROUP, (group + 1) * GROUP)
-        keep(proj_ref, dot_tn(bg_ref[...], o_ref[:, cols]), group)
+        keep(slab_ref.at[groups], dot_tn(bg_ref[...], o_ref[:, cols]), group)
 
     @pl.loop(0, blocks)
     def _(b):
@@ -579,31 +583,49 @@
 
     pl.semaphore_wait(barrier, ways - 1)
 
-    def slabs(group):
-        if isinstance(group, int) and group == groups:
-            return proj_ref, proj_land
-        return slab_ref.at[group], slab_land.at[group]
+    def halve(group, source):
+        return pltpu.make_async_remote_copy(
+            src_ref=slab_ref.at[group, source * 2 + 1 - core],
+            dst_ref=pair_land.at[group, source],
+            send_sem=pair_send.at[group, source], recv_sem=pair_recv.at[group, source],
+            device_id=(chip * 2 + 1 - core, place), device_id_type=MESH,
+        )
 
     def give(group, step):
-        source, target = slabs(group)
-        return pltpu.make_async_remote_copy(
-            src_ref=source.at[peer(step)], dst_ref=target.at[spot],
-            send_sem=slab_send.at[group, step], recv_sem=slab_recv.at[group, spot],
-            device_id=(peer(step), place), device_id_type=MESH,
+        to = chip_at(step) * 2 + core
+        return pltpu.make_async_remote_copy(
+            src_ref=slab_ref.at[group, to], dst_ref=chip_land.at[group, chip],
+            send_sem=chip_send.at[group, step], recv_sem=chip_recv.at[group, chip],
+            device_id=(to, place), device_id_type=MESH,
         )
 
     def take(group, step):
-        owner = peer(dp - step)
-        source, target = slabs(group)
-        return pltpu.make_async_remote_copy(
-            src_ref=source.at[owner], dst_ref=target.at[owner],
-            send_sem=slab_send.at[group, step], recv_sem=slab_recv.at[group, owner],
-            device_id=(peer(step), place), device_id_type=MESH,
-        )
-
-    @pl.loop(1, dp)
-    def _(step):
-        give(groups, step).start()
+        source = chip_at(chips - step)
+        return pltpu.make_async_remote_copy(
+            src_ref=slab_ref.at[group, source * 2 + core], dst_ref=chip_land.at[group, source],
+            send_sem=chip_send.at[group, step], recv_sem=chip_recv.at[group, source],
+            device_id=(chip_at(step) * 2 + core, place), device_id_type=MESH,
+        )
+
+    def share_slabs(group):
+        @pl.loop(0, chips)
+        def _(source):
+            halve(group, source).start()
+
+    def send_slabs(group):
+        @pl.loop(0, chips)
+        def _(step):
+            to = chip_at(step)
+            halve(group, to).wait_recv()
+            mine = slab_ref[group, to * 2 + core].astype(jnp.float32)
+            mine = mine + pair_land[group, to].astype(jnp.float32)
+            slab_ref[group, to * 2 + core] = mine.astype(slab_ref.dtype)
+
+            @pl.when(step > 0)
+            def _():
+                give(group, step).start()
+
+    share_slabs(groups)
 
     @pl.loop(0, pairs)
     def _(pair):
@@ -721,18 +743,54 @@
 
     middle_place = (place > 0) & (place < tensor - 1)
     late = 3 * jnp.maximum(tensor - 2 - place, 0)
-    relayed = jnp.where(middle_place, jnp.where(place > 1, 2 * pieces, pieces), 0)
+    first_relay = jnp.where(place > 1, 0, pieces)
+    last_relay = jnp.where(middle_place, 2 * pieces, first_relay)
+
+    def piece_of(order):
+        return lax.rem(order + pieces, 2 * pieces)
 
     def serve(first, last):
-        def one(piece, carry):
+        def one(order, carry):
+            piece = piece_of(order)
             pass_down(piece).wait_recv()
             at = pl.ds(pl.multiple_of(piece * PIECE, PIECE), PIECE)
             rows_ref[at] = joined(piece).astype(rows_ref.dtype)
             pass_down(piece).start()
             return carry
 
-        low = jnp.clip(first - late, 0, relayed)
-        lax.fori_loop(low, jnp.clip(last - late, low, relayed), one, 0)
+        low = jnp.clip(first - late, first_relay, last_relay)
+        lax.fori_loop(low, jnp.clip(last - late, low, last_relay), one, 0)
+
+    @pl.loop(0, pairs)
+    def _(pair):
+        @pl.when(place == 0)
+        def _():
+            for ref in (k_ref, v_ref):
+                ref[rows : 3 * rows, lanes(pair)] = jnp.zeros((2 * rows, 128), ref.dtype)
+
+        @pl.when(place > 0)
+        def _():
+            def seen_parent(probs):
+                return jnp.where(place > 1, probs, 0.0)
+
+            spots = range(0, rows, BRANCH)
+            sums = sweep(pair, [(rows + at, at, seen_parent) for at in spots])
+            for at, part in zip(spots, sums):
+                put(pair, rows + at, *part)
+
+    send_slabs(groups)
+
+    @pl.loop(0, blocks)
+    def _(leaf):
+        out_ref[block_at(leaf)] = row_grad(blocks + leaf)
+
+    for branch in range(blocks):
+        total = None
+        for leaf in range(blocks):
+            at = leaf * blocks + branch
+            part = out_ref[leaf * BRANCH : (leaf + 1) * BRANCH] * parent_ref[at : at + 1]
+            total = part if total is None else total + part
+        hand_down(blocks + branch, total)
 
     stage(0).start()
 
@@ -758,10 +816,8 @@
             def _():
                 finish_block(False)
 
-            @pl.when((pair > 1) & (b > 0))
-            def _():
-                piece = (b - 1) * (BRANCH // PIECE) + pair - 2
-                serve(piece, piece + 1)
+            slot = b * pairs + pair
+            serve(slot - 1, slot)
 
         for _half in range(2):
             part = b * 2 + _half
@@ -779,40 +835,7 @@
 
         hand_down(b, row_grad(b))
 
-    served = (blocks - 1) * (BRANCH // PIECE)
-
-    @pl.loop(0, pairs)
-    def _(pair):
-        @pl.when(place == 0)
-        def _():
-            for ref in (k_ref, v_ref):
-                ref[rows : 3 * rows, lanes(pair)] = jnp.zeros((2 * rows, 128), ref.dtype)
-
-        @pl.when(place > 0)
-        def _():
-            def seen_parent(probs):
-                return jnp.where(place > 1, probs, 0.0)
-
-            spots = range(0, rows, BRANCH)
-            sums = sweep(pair, [(rows + at, at, seen_parent) for at in spots])
-            for at, part in zip(spots, sums):
-                put(pair, rows + at, *part)
-
-        serve(jnp.minimum(served + pair, pieces), jnp.minimum(served + pair + 1, pieces))
-
-    served = pieces
-
-    @pl.loop(0, blocks)
-    def _(leaf):
-        out_ref[block_at(leaf)] = row_grad(blocks + leaf)
-
-    for branch in range(blocks):
-        total = None
-        for leaf in range(blocks):
-            at = leaf * blocks + branch
-            part = out_ref[leaf * BRANCH : (leaf + 1) * BRANCH] * parent_ref[at : at + 1]
-            total = part if total is None else total + part
-        hand_down(blocks + branch, total)
+    served = blocks * pairs - 1
 
     gain_ref[...] = jnp.zeros_like(gain_ref)
 
@@ -847,9 +870,11 @@
             if kind:
                 serve(base + 1 + kind, base + 2 + kind)
 
-        @pl.loop(1, dp)
-        def _(step):
-            give(group, step).start()
+        share_slabs(group)
+
+        @pl.when(group > 0)
+        def _():
+            send_slabs(group - 1)
 
     served += groups * 4
 
@@ -892,6 +917,8 @@
     @pl.loop(1, ways)
     def _(step):
         scatter(step).start()
+
+    send_slabs(groups - 1)
 
     @pl.loop(0, blocks)
     def _(b):
@@ -911,22 +938,16 @@
     def _(step):
         spread(step).start()
 
-    serve(served, 2 * pieces)
-    serve(2 * pieces, 2 * pieces + late)
+    serve(served, jnp.maximum(served, 2 * pieces) + late)
 
     kinds = [[], [], [], []]
     for group in range(groups + 1):
 
-        @pl.loop(1, dp)
-        def _(step):
+        def add_slab(step, total):
             take(group, step).wait_recv()
-
-        own, landed = slabs(group)
-
-        def add_slab(step, total):
-            return total + landed[peer(dp - step)].astype(jnp.float32)
-
-        total = lax.fori_loop(1, dp, add_slab, own[spot].astype(jnp.float32))
+            return total + chip_land[group, chip_at(chips - step)].astype(jnp.float32)
+
+        total = lax.fori_loop(1, chips, add_slab, slab_ref[group, spot].astype(jnp.float32))
         for part in range(total.shape[1] // GROUP):
             kinds[3 if group == groups else part].append(
                 total[:, part * GROUP : (part + 1) * GROUP]
@@ -989,17 +1010,22 @@
 
     for group in range(groups + 1):
 
-        @pl.loop(1, dp)
+        @pl.loop(0, chips)
         def _(step):
-            give(group, step).wait_send()
-
-    sent = jnp.where(place == tensor - 1, 2 * pieces, relayed)
-
-    def sent_one(piece, carry):
-        pass_down(piece).wait_send()
+            halve(group, step).wait_send()
+
+            @pl.when(step > 0)
+            def _():
+                give(group, step).wait_send()
+
+    sent = jnp.where(place == tensor - 1, 2 * pieces, last_relay)
+    first_sent = jnp.where(place == tensor - 1, 0, first_relay)
+
+    def sent_one(order, carry):
+        pass_down(piece_of(order)).wait_send()
         return carry
 
-    lax.fori_loop(0, sent, sent_one, 0)
+    lax.fori_loop(first_sent, sent, sent_one, 0)
 
 
 def backward(parents, q, k, v, o, branch_grad, seen, weights, lse, small):
@@ -1010,8 +1036,7 @@
     depth = width // dp
     padded = -(-depth // 16) * 16
     pairs, groups, pieces = width // 128, width // GROUP, rows // PIECE
-    slab = (groups, dp, padded, 3 * GROUP)
-    proj = (dp, padded, width)
+    slab = (padded, width)
     low, full = jnp.bfloat16, jnp.float32
     dma = pltpu.SemaphoreType.DMA
     anywhere = pl.BlockSpec(memory_space=pl.ANY)
@@ -1040,17 +1065,17 @@
             pltpu.VMEM((2 * rows, width), low),
             pltpu.VMEM((2 * rows, width), low),
             pltpu.VMEM((width, 128), full),
-            pltpu.VMEM(slab, low),
-            pltpu.VMEM(slab, low),
-            pltpu.VMEM(proj, low),
-            pltpu.VMEM(proj, low),
+            pltpu.VMEM((groups + 1, dp) + slab, low),
+            pltpu.VMEM((groups + 1, dp // 2) + slab, low),
+            pltpu.VMEM((groups + 1, dp // 2) + slab, low),
             pltpu.VMEM((tensor, padded, width), low),
             pltpu.VMEM((tensor, padded, width), low),
             pltpu.VMEM(small.shape, full),
             pltpu.VMEM(small.shape, full),
             dma((3,)), dma((3, pairs)), dma((2,)),
             dma((2 * pieces,)), dma((2 * pieces,)),
-            dma((groups + 1, dp)), dma((groups + 1, dp)),
+            dma((groups + 1, dp // 2)), dma((groups + 1, dp // 2)),
+            dma((groups + 1, dp // 2)), dma((groups + 1, dp // 2)),
             dma((tensor,)), dma((tensor,)),
             dma((ways,)), dma((ways,)), dma((ways,)), dma((ways,)),
         ],

time: 477 us -> 472 us (0.990)
  Pallas kernels: 301 us -> 294 us
    pallas_call x1, Pallas kernels: 196 us -> 190 us  [backward(): pl.pallas_call(lambda *refs: back_kernel(dp, tensor, depth, *refs), out_s...]
  transfers between devices with their start and end apart: 18 -> 18, of which waited for: 9 -> 9; matrix products, arithmetic and copies ran while one was open for 13% -> 13% of each run, Pallas kernels for 45% -> 44%
where the time goes in v7:
time: 472 us; the launch traced here: 466 us
  Pallas kernels  294 us (62%)
  matrix products  56.6 us (12%)
  waiting for transfers between devices  35.7 us (8%)
  other arithmetic  28.8 us (6%)
  local copies, waits for them, and re-layouts  21.2 us (4%)
  between operations  15.1 us (3%)
  starting transfers between devices  14.9 us (3%)
    pallas_call x1, Pallas kernels, backward(): pl.pallas_call(lambda *refs: back_kernel(dp, tensor, depth, *refs), out_s...  190 us
    pallas_call x1, Pallas kernels, share_rows_and_weights(): pl.pallas_call(lambda *refs: share_kernel(dp, tensor, *refs), out_shape=(...  54.5 us
    ppermute x16, waiting for transfers between devices, hop(): return lax.ppermute(rows, 'dp', route)  35.7 us
    pallas_call x1, Pallas kernels, attend(): pl.pallas_call(fwd_kernel, out_shape=(jax.ShapeDtypeStruct((rows, width),...  18.5 us
    pallas_call x1, Pallas kernels, expert_forward(): pl.pallas_call(expert_fwd_kernel, grid=(count,), in_specs=[wide(width), w...  15.6 us
    pallas_call x1, Pallas kernels, expert_back(): pl.pallas_call(expert_bwd_kernel, grid=(count,), in_specs=[wide(width), w...  15.4 us
    ppermute x16, starting transfers between devices, hop(): return lax.ppermute(rows, 'dp', route)  14.9 us
    dot_general x3, matrix products, low_dot(): jnp.dot(rows, weight, preferred_element_type=jnp.float32)  13.7 us
  transfers between devices with their start and end apart: 18, of which 9 were waited for; matrix products, arithmetic and copies ran while one was open for 13% of the time, Pallas kernels for 44%

profile of v7, /device:TPU:0, one launch (start us, length us, event | category | flops | bytes accessed | tf_op | source)
XLA Modules:
  0.0 466.3 jit_solution(17284407701908496080)
XLA Ops:
  8.8 2.0 select_reduce_fusion
  13.4 2.0 fusion.13
  16.6 54.5 %share_rows_and_weights.1 = (bf16[3072,768]{1,0:T(8,128)(2,1)}, bf16[4,768,768]{2,1,0:T(8,128)(2,1)}) custom-call(bf16[1024,768]{1,0:T(8,128)(2,1)S(1)} %fusion.15.refs_0_, bf16[96,768]{1,0:T(8,128)(2,1)S(1)} %pad_maximum_fusion.2.refs_1_, f32[16,768]{1,0:T(8,128)S(1)} %broadcast_in_dim.31.refs_2_.refs_0_), custom_call_target="tpu_custom_call" | custom-call | tf_op jit(solution)/shard_map/share_rows_and_weights/pallas_call | solution.py:454
  71.2 2.8 convolution_convert_fusion.4.q_ref.refs_1_
  74.0 1.8 copy-done.23
  75.9 5.5 %convolution_convert_fusion.v_ref.refs_3_ = bf16[3072,768]{1,0:T(8,128)(2,1)} fusion(bf16[3072,768]{1,0:T(8,128)(2,1)S(1)} %copy-done.22, bf16[4,768,768]{2,1,0:T(8,128)(2,1)S(1)} %copy-done.23), kind=kOutput, calls=%fused_computation | convolution fusion | flops 3626237952 | bytes 10616832 | tf_op jit(solution)/shard_map/dot_general | solution.py:1126
  81.3 5.4 %convolution_convert_fusion.1.k_ref.refs_2_ = bf16[3072,768]{1,0:T(8,128)(2,1)} fusion(bf16[3072,768]{1,0:T(8,128)(2,1)S(1)} %copy-done.22, bf16[4,768,768]{2,1,0:T(8,128)(2,1)S(1)} %copy-done.23), kind=kOutput, calls=%fused_computation.1 | convolution fusion | flops 3626237952 | bytes 10616832 | tf_op jit(solution)/shard_map/dot_general | solution.py:1126
  86.8 18.5 %attend_forward.1 = (bf16[1024,768]{1,0:T(8,128)(2,1)S(1)}, f32[6,2,1024]{2,1,0:T(2,128)S(1)}) custom-call(s32[1]{0:T(128)} %bitcast.place_ref, bf16[1024,768]{1,0:T(8,128)(2,1)S(1)} %convolution_convert_fusion.4.q_ref.refs_1_, bf16[3072,768]{1,0:T(8,128)(2,1)} %convolution_convert_fusion.1.k_ref.refs_2_, bf16[3072,768]{1,0:T(8,128)(2,1)} %convolution_convert_fusion.v_ref.refs_3_), custom_call_target="tpu_custom_call" | custom-call | tf_op jit(solution)/shard_map/attend_forward/pallas_call | solution.py:113
  108.6 2.5 fusion.31
  111.2 2.5 collective-permute-start.2
  116.6 2.6 fusion.34
  119.2 5.1 %collective-permute-done.2 = bf16[256,768]{1,0:T(8,128)(2,1)S(1)} collective-permute-done((bf16[256,768]{1,0:T(8,128)(2,1)S(1)}, bf16[256,768]{1,0:T(8,128)(2,1)S(1)}, u32[]{:S(2)}, u32[]{:S(2)}) %collective-permute-start.2) | collective-permute-done | bytes 393248 | tf_op jit(solution)/shard_map/ppermute | solution.py:1155
  124.3 6.3 %collective-permute-done.1 = bf16[256,768]{1,0:T(8,128)(2,1)S(1)} collective-permute-done((bf16[256,768]{1,0:T(8,128)(2,1)S(1)}, bf16[256,768]{1,0:T(8,128)(2,1)S(1)}, u32[]{:S(2)}, u32[]{:S(2)}) %collective-permute-start.1) | collective-permute-done | bytes 393248 | tf_op jit(solution)/shard_map/ppermute | solution.py:1155
  136.4 15.6 %expert_forward.1 = (bf16[2048,1536]{1,0:T(8,128)(2,1)}, bf16[2048,1536]{1,0:T(8,128)(2,1)}, f32[1024,768]{1,0:T(8,128)S(1)}, bf16[1024,768]{1,0:T(8,128)(2,1)S(1)}) custom-call(bf16[2048,768]{1,0:T(8,128)(2,1)S(1)} %constant_dynamic-update-slice_fusion.x_ref, bf16[768,1536]{1,0:T(8,128)(2,1)S(1)} %copy-done.7, bf16[1536,768]{1,0:T(8,128)(2,1)S(1)} %copy-done.8), custom_call_target="tpu_custom_call" | custom-call | flops 9663676416 | bytes 25165824 | tf_op jit(solution)/shard_map/expert_forward/pallas_call | solution.py:203
  152.9 2.6 collective-permute-done.7
  157.9 15.4 %expert_backward.1 = (bf16[2048,1536]{1,0:T(8,128)(2,1)}, f32[1024,768]{1,0:T(8,128)S(1)}, bf16[1024,768]{1,0:T(8,128)(2,1)S(1)}) custom-call(bf16[2048,768]{1,0:T(8,128)(2,1)S(1)} %constant_dynamic-update-slice_fusion.5.grad_ref, bf16[2048,1536]{1,0:T(8,128)(2,1)} %get-tuple-element.55.slope_ref, bf16[768,1536]{1,0:T(8,128)(2,1)S(1)} %copy-done.7, ...), custom_call_target="tpu_custom_call" | custom-call | flops 9663676416 | bytes 25165824 | tf_op jit(solution)/shard_map/expert_backward/pallas_call | solution.py:228
  176.0 9.3 %convolution_convert_fusion.3 = bf16[1536,768]{1,0:T(8,128)(2,1)} fusion(bf16[2048,1536]{1,0:T(8,128)(2,1)} %get-tuple-element.62, bf16[2048,768]{1,0:T(8,128)(2,1)S(1)} %constant_dynamic-update-slice_fusion.x_ref), kind=kOutput, calls=%fused_computation.22 | convolution fusion | flops 4833017856 | bytes 11796480 | tf_op jit(solution)/shard_map/rf,rd->fd/dot_general | solution.py:1239
  185.4 2.5 fusion.91
  191.4 9.4 %convolution_convert_fusion.2 = bf16[1536,768]{1,0:T(8,128)(2,1)} fusion(bf16[2048,1536]{1,0:T(8,128)(2,1)} %get-tuple-element.63, bf16[2048,768]{1,0:T(8,128)(2,1)S(1)} %constant_dynamic-update-slice_fusion.5.grad_ref), kind=kOutput, calls=%fused_computation.21 | convolution fusion | flops 4833017856 | bytes 11796480 | tf_op jit(solution)/shard_map/rf,rd->fd/dot_general | solution.py:1235
  201.2 7.6 %collective-permute-done.10 = bf16[256,768]{1,0:T(8,128)(2,1)} collective-permute-done((bf16[256,768]{1,0:T(8,128)(2,1)}, bf16[256,768]{1,0:T(8,128)(2,1)}, u32[]{:S(2)}, u32[]{:S(2)}) %collective-permute-start.10) | collective-permute-done | bytes 393248 | tf_op jit(solution)/shard_map/ppermute | solution.py:1155
  208.8 5.8 %fusion.18 = (f32[1024]{0:T(1024)S(1)}, f32[1024,768]{1,0:T(8,128)}) fusion(bf16[1024,768]{1,0:T(8,128)(2,1)} %param.25, bf16[256,768]{1,0:T(8,128)(2,1)} %collective-permute-done.11, bf16[256,768]{1,0:T(8,128)(2,1)} %collective-permute-done.10, bf16[256,768]{1,0:T(8,128)(2,1)} %collective-permute-done.9, bf16[256,768]{1,0:T(8,128)(2,1)} %get-tuple-element.103, ...), kind=kOutput, calls=%fused_computation.28 | convolution fusion | flops 1621359616 | bytes 6300672 | tf_op jit(solution)/shard_map/dot_general | solution.py:1216
  215.3 2.5 fusion.73
  224.1 2.8 fusion.74
  226.9 5.6 %collective-permute-done.15 = bf16[256,768]{1,0:T(8,128)(2,1)} collective-permute-done((bf16[256,768]{1,0:T(8,128)(2,1)}, bf16[256,768]{1,0:T(8,128)(2,1)}, u32[]{:S(2)}, u32[]{:S(2)}) %collective-permute-start.15) | collective-permute-done | bytes 393248 | tf_op jit(solution)/shard_map/ppermute | solution.py:1155
  232.6 7.4 %collective-permute-done.14 = bf16[256,768]{1,0:T(8,128)(2,1)} collective-permute-done((bf16[256,768]{1,0:T(8,128)(2,1)}, bf16[256,768]{1,0:T(8,128)(2,1)}, u32[]{:S(2)}, u32[]{:S(2)}) %collective-permute-start.14) | collective-permute-done | bytes 393248 | tf_op jit(solution)/shard_map/ppermute | solution.py:1155
  240.0 4.1 multiply_reduce_fusion
  244.9 2.7 fusion.89
  247.5 1.9 fusion.27.refs_5_
  249.7 190.0 %attend_backward.1 = (f32[1024,768]{1,0:T(8,128)}, f32[96,768]{1,0:T(8,128)}, f32[32,8,128]{2,1,0:T(8,128)}) custom-call(f32[16,768]{1,0:T(8,128)} %copy-done.5, bf16[1024,768]{1,0:T(8,128)(2,1)} %copy-done.1, bf16[3072,768]{1,0:T(8,128)(2,1)} %convolution_convert_fusion.1.k_ref.refs_2_, bf16[3072,768]{1,0:T(8,128)(2,1)} %convolution_convert_fusion.v_ref.refs_3_, ...), custom_call_target="tpu_custom_call" | custom-call | tf_op jit(solution)/shard_map/attend_backward/pallas_call | solution.py:1044
  446.2 2.8 fusion.16
  451.8 2.7 add_add_fusion.2
  457.0 2.2 convert_element_type.93
  (169 shorter events, 46.6 us)
Async XLA Ops:
  7.2 107.7 %copy-start = (f32[768,16]{0,1:T(8,128)S(1)}, f32[768,16]{0,1:T(8,128)}, u32[]{:S(2)}) copy-start(f32[768,16]{0,1:T(8,128)} %param.18) | copy-start | bytes 147460
  7.2 8.8 %copy-start.10 = (bf16[1024,768]{1,0:T(8,128)(2,1)S(1)}, bf16[1024,768]{1,0:T(8,128)(2,1)}, u32[]{:S(2)}) copy-start(bf16[1024,768]{1,0:T(8,128)(2,1)} %param.13) | copy-start | bytes 4718596
  7.2 8.3 %copy-start.29 = (bf16[192,96]{1,0:T(8,128)(2,1)S(1)}, bf16[192,96]{1,0:T(8,128)(2,1)}, u32[]{:S(2)}) copy-start(bf16[192,96]{1,0:T(8,128)(2,1)} %param.16) | copy-start | bytes 110596
  7.2 8.4 %copy-start.26 = (bf16[96,3,192]{2,0,1:T(8,128)(2,1)S(1)}, bf16[96,3,192]{2,0,1:T(8,128)(2,1)}, u32[]{:S(2)}) copy-start(bf16[96,3,192]{2,0,1:T(8,128)(2,1)} %param.15) | copy-start | bytes 331780
  7.2 8.8 %copy-start.28 = (f32[768]{0:T(1024)S(1)}, f32[768]{0:T(1024)}, u32[]{:S(2)}) copy-start(f32[768]{0:T(1024)} %param.14) | copy-start | bytes 9220
  7.2 447.2 %reduce-scatter.3.cloned.1.call-start = ((), (), s32[]{:S(2)}) async-start(), calls=%async_computation.2 | async-start | bytes 2949120 | tf_op jit(solution)/shard_map/reduce_scatter | solution.py:1248
  16.6 57.4 %copy-start.5 = (f32[16,768]{1,0:T(8,128)}, f32[16,768]{1,0:T(8,128)S(1)}, u32[]{:S(2)}) copy-start(f32[16,768]{1,0:T(8,128)S(1)} %broadcast_in_dim.31.refs_2_.refs_0_) | copy-start | bytes 147460
  74.0 12.8 %copy-start.1 = (bf16[1024,768]{1,0:T(8,128)(2,1)}, bf16[1024,768]{1,0:T(8,128)(2,1)S(1)}, u32[]{:S(2)}) copy-start(bf16[1024,768]{1,0:T(8,128)(2,1)S(1)} %convolution_convert_fusion.4.q_ref.refs_1_) | copy-start | bytes 4718596
  108.6 6.3 %copy-start.17 = (bf16[1024,768]{1,0:T(8,128)(2,1)}, bf16[1024,768]{1,0:T(8,128)(2,1)S(1)}, u32[]{:S(2)}) copy-start(bf16[1024,768]{1,0:T(8,128)(2,1)S(1)} %multiply_convert_fusion) | copy-start | bytes 4718596
  111.1 5.5 %copy-start.19 = (bf16[1024,768]{1,0:T(8,128)(2,1)S(1)}, bf16[1024,768]{1,0:T(8,128)(2,1)}, u32[]{:S(2)}) copy-start(bf16[1024,768]{1,0:T(8,128)(2,1)} %param.25) | copy-start | bytes 4718596
  111.2 13.1 %collective-permute-start.2 = (bf16[256,768]{1,0:T(8,128)(2,1)S(1)}, bf16[256,768]{1,0:T(8,128)(2,1)S(1)}, u32[]{:S(2)}, u32[]{:S(2)}) collective-permute-start(bf16[256,768]{1,0:T(8,128)(2,1)S(1)} %get-tuple-element.111), channel_id=1, source_target_pairs={{0,24},{4,28},{8,16},{12,20},{16,8},{20,12},{24,0},{28,4},{1,25},{... | collective-permute-start | bytes 1179656 | tf_op jit(solution)/shard_map/ppermute | solution.py:1155
  113.7 16.9 %collective-permute-start.1 = (bf16[256,768]{1,0:T(8,128)(2,1)S(1)}, bf16[256,768]{1,0:T(8,128)(2,1)S(1)}, u32[]{:S(2)}, u32[]{:S(2)}) collective-permute-start(bf16[256,768]{1,0:T(8,128)(2,1)S(1)} %get-tuple-element.112), channel_id=1, source_target_pairs={{0,16},{4,20},{8,24},{12,28},{16,0},{20,4},{24,8},{28,12},{1,17},{... | collective-permute-start | bytes 1179656 | tf_op jit(solution)/shard_map/ppermute | solution.py:1155
  114.2 16.5 %collective-permute-start = (bf16[256,768]{1,0:T(8,128)(2,1)S(1)}, bf16[256,768]{1,0:T(8,128)(2,1)S(1)}, u32[]{:S(2)}, u32[]{:S(2)}) collective-permute-start(bf16[256,768]{1,0:T(8,128)(2,1)S(1)} %get-tuple-element.113), channel_id=1, source_target_pairs={{0,8},{4,12},{8,0},{12,4},{16,24},{20,28},{24,16},{28,20},{1,9},{5... | collective-permute-start | bytes 1179656 | tf_op jit(solution)/shard_map/ppermute | solution.py:1155
  130.8 3.9 collective-permute-start.6
  131.0 21.0 %collective-permute-start.5 = (bf16[256,768]{1,0:T(8,128)(2,1)S(1)}, bf16[256,768]{1,0:T(8,128)(2,1)S(1)}, u32[]{:S(2)}, u32[]{:S(2)}) collective-permute-start(bf16[256,768]{1,0:T(8,128)(2,1)S(1)} %get-tuple-element.107), channel_id=1, source_target_pairs={{0,24},{4,28},{8,16},{12,20},{16,8},{20,12},{24,0},{28,4},{1,25},{... | collective-permute-start | bytes 1179656 | tf_op jit(solution)/shard_map/ppermute | solution.py:1155
  132.7 19.3 %collective-permute-start.4 = (bf16[256,768]{1,0:T(8,128)(2,1)S(1)}, bf16[256,768]{1,0:T(8,128)(2,1)S(1)}, u32[]{:S(2)}, u32[]{:S(2)}) collective-permute-start(bf16[256,768]{1,0:T(8,128)(2,1)S(1)} %get-tuple-element.108), channel_id=1, source_target_pairs={{0,16},{4,20},{8,24},{12,28},{16,0},{20,4},{24,8},{28,12},{1,17},{... | collective-permute-start | bytes 1179656 | tf_op jit(solution)/shard_map/ppermute | solution.py:1155
  134.0 18.0 %collective-permute-start.3 = (bf16[256,768]{1,0:T(8,128)(2,1)S(1)}, bf16[256,768]{1,0:T(8,128)(2,1)S(1)}, u32[]{:S(2)}, u32[]{:S(2)}) collective-permute-start(bf16[256,768]{1,0:T(8,128)(2,1)S(1)} %get-tuple-element.109), channel_id=1, source_target_pairs={{0,8},{4,12},{8,0},{12,4},{16,24},{20,28},{24,16},{28,20},{1,9},{5... | collective-permute-start | bytes 1179656 | tf_op jit(solution)/shard_map/ppermute | solution.py:1155
  152.0 3.5 collective-permute-start.7
  152.2 5.5 %collective-permute-start.8 = (bf16[1024,768]{1,0:T(8,128)(2,1)S(1)}, bf16[1024,768]{1,0:T(8,128)(2,1)S(1)}, u32[]{:S(2)}, u32[]{:S(2)}) collective-permute-start(bf16[1024,768]{1,0:T(8,128)(2,1)S(1)} %pad_maximum_fusion.1), channel_id=1, source_target_pairs={{0,4},{4,0},{8,12},{12,8},{16,20},{20,16},{24,28},{28,24},{1,5},{5... | collective-permute-start | bytes 4718600 | tf_op jit(solution)/shard_map/ppermute | solution.py:1155
  185.4 271.6 %reduce-scatter.5.cloned.1.call-start = ((), (), s32[]{:S(2)}) async-start(), calls=%async_computation.3 | async-start | bytes 2949120 | tf_op jit(solution)/shard_map/reduce_scatter | solution.py:1252
  188.0 13.2 %collective-permute-start.11 = (bf16[256,768]{1,0:T(8,128)(2,1)}, bf16[256,768]{1,0:T(8,128)(2,1)}, u32[]{:S(2)}, u32[]{:S(2)}) collective-permute-start(bf16[256,768]{1,0:T(8,128)(2,1)} %get-tuple-element.104), channel_id=1, source_target_pairs={{0,24},{4,28},{8,16},{12,20},{16,8},{20,12},{24,0},{28,4},{1,25},{... | collective-permute-start | bytes 1179656 | tf_op jit(solution)/shard_map/ppermute | solution.py:1155
  189.4 19.4 %collective-permute-start.10 = (bf16[256,768]{1,0:T(8,128)(2,1)}, bf16[256,768]{1,0:T(8,128)(2,1)}, u32[]{:S(2)}, u32[]{:S(2)}) collective-permute-start(bf16[256,768]{1,0:T(8,128)(2,1)} %get-tuple-element.105), channel_id=1, source_target_pairs={{0,16},{4,20},{8,24},{12,28},{16,0},{20,4},{24,8},{28,12},{1,17},{... | collective-permute-start | bytes 1179656 | tf_op jit(solution)/shard_map/ppermute | solution.py:1155
  190.7 18.0 %collective-permute-start.9 = (bf16[256,768]{1,0:T(8,128)(2,1)}, bf16[256,768]{1,0:T(8,128)(2,1)}, u32[]{:S(2)}, u32[]{:S(2)}) collective-permute-start(bf16[256,768]{1,0:T(8,128)(2,1)} %get-tuple-element.106), channel_id=1, source_target_pairs={{0,8},{4,12},{8,0},{12,4},{16,24},{20,28},{24,16},{28,20},{1,9},{5... | collective-permute-start | bytes 1179656 | tf_op jit(solution)/shard_map/ppermute | solution.py:1155
  200.9 16.9 %collective-permute-start.12 = (bf16[1024,768]{1,0:T(8,128)(2,1)}, bf16[1024,768]{1,0:T(8,128)(2,1)S(1)}, u32[]{:S(2)}, u32[]{:S(2)}) collective-permute-start(bf16[1024,768]{1,0:T(8,128)(2,1)} %copy-done.9), channel_id=1, source_target_pairs={{0,4},{4,0},{8,12},{12,8},{16,20},{20,16},{24,28},{28,24},{1,5},{5... | collective-permute-start | bytes 4718600 | tf_op jit(solution)/shard_map/ppermute | solution.py:1155
  208.8 6.5 %copy-start.18 = (bf16[1024,768]{1,0:T(8,128)(2,1)S(1)}, bf16[1024,768]{1,0:T(8,128)(2,1)}, u32[]{:S(2)}) copy-start(bf16[1024,768]{1,0:T(8,128)(2,1)} %copy-done.17) | copy-start | bytes 4718596
  208.8 9.0 %copy-start.3 = (f32[1024,768]{1,0:T(8,128)S(1)}, f32[1024,768]{1,0:T(8,128)}, u32[]{:S(2)}) copy-start(f32[1024,768]{1,0:T(8,128)} %copy-done.2) | copy-start | bytes 9437188
  218.1 21.9 %copy-start.14 = (f32[1024,768]{1,0:T(8,128)S(1)}, f32[1024,768]{1,0:T(8,128)}, u32[]{:S(2)}) copy-start(f32[1024,768]{1,0:T(8,128)} %copy-done.13) | copy-start | bytes 9437188
  219.3 13.2 %collective-permute-start.15 = (bf16[256,768]{1,0:T(8,128)(2,1)}, bf16[256,768]{1,0:T(8,128)(2,1)}, u32[]{:S(2)}, u32[]{:S(2)}) collective-permute-start(bf16[256,768]{1,0:T(8,128)(2,1)} %get-tuple-element.100), channel_id=1, source_target_pairs={{0,24},{4,28},{8,16},{12,20},{16,8},{20,12},{24,0},{28,4},{1,25},{... | collective-permute-start | bytes 1179656 | tf_op jit(solution)/shard_map/ppermute | solution.py:1155
  220.8 19.2 %collective-permute-start.14 = (bf16[256,768]{1,0:T(8,128)(2,1)}, bf16[256,768]{1,0:T(8,128)(2,1)}, u32[]{:S(2)}, u32[]{:S(2)}) collective-permute-start(bf16[256,768]{1,0:T(8,128)(2,1)} %get-tuple-element.101), channel_id=1, source_target_pairs={{0,16},{4,20},{8,24},{12,28},{16,0},{20,4},{24,8},{28,12},{1,17},{... | collective-permute-start | bytes 1179656 | tf_op jit(solution)/shard_map/ppermute | solution.py:1155
  222.1 17.9 %collective-permute-start.13 = (bf16[256,768]{1,0:T(8,128)(2,1)}, bf16[256,768]{1,0:T(8,128)(2,1)}, u32[]{:S(2)}, u32[]{:S(2)}) collective-permute-start(bf16[256,768]{1,0:T(8,128)(2,1)} %get-tuple-element.102), channel_id=1, source_target_pairs={{0,8},{4,12},{8,0},{12,4},{16,24},{20,28},{24,16},{28,20},{1,9},{5... | collective-permute-start | bytes 1179656 | tf_op jit(solution)/shard_map/ppermute | solution.py:1155
  224.1 15.9 %copy-start.25 = (bf16[256,768]{1,0:T(8,128)(2,1)S(1)}, bf16[256,768]{1,0:T(8,128)(2,1)}, u32[]{:S(2)}) copy-start(bf16[256,768]{1,0:T(8,128)(2,1)} %get-tuple-element.99) | copy-start | bytes 1179652
  439.7 6.4 %copy-start.11 = (bf16[1024,768]{1,0:T(8,128)(2,1)S(1)}, bf16[1024,768]{1,0:T(8,128)(2,1)}, u32[]{:S(2)}) copy-start(bf16[1024,768]{1,0:T(8,128)(2,1)} %param.13) | copy-start | bytes 4718596
  (18 other events, 47.2 us)
Sparse Core Ops, SparseCore 0:
  185.5 99.7 reduce-scatter.2
  287.5 53.9 reduce-scatter.4

commit v8 on v7

--- a/solution.py
+++ b/solution.py
@@ -131,119 +131,7 @@
     )(place, q, k, v)
 
 
-ROWS = 256
-HALF_ROOT = math.sqrt(0.5)
-PDF_SCALE = 1.0 / math.sqrt(2.0 * math.pi)
-CHUNK = 512
-
-
-def expert_fwd_kernel(x_ref, in_ref, out_ref, active_ref, slope_ref, keep_ref, send_ref):
-    step = pl.program_id(0)
-    half = pl.num_programs(0) // 2
-    rows = x_ref[...]
-    total = None
-    for first in range(0, in_ref.shape[1], CHUNK):
-        cols = slice(first, first + CHUNK)
-        up = dot_nn(rows, in_ref[:, cols])
-        below = 0.5 * (1.0 + lax.erf(up * HALF_ROOT))
-        active = (up * below).astype(jnp.bfloat16)
-        slope = below + up * (jnp.exp(-0.5 * up * up) * PDF_SCALE)
-        active_ref[:, cols] = active
-        slope_ref[:, cols] = slope.astype(jnp.bfloat16)
-        part = dot_nn(active, out_ref[cols])
-        total = part if total is None else total + part
-
-    @pl.when(step < half)
-    def _():
-        keep_ref[...] = total
-
-    @pl.when(step >= half)
-    def _():
-        send_ref[...] = total.astype(send_ref.dtype)
-
-
-def expert_bwd_kernel(grad_ref, slope_ref, in_ref, out_ref, upgrad_ref, keep_ref, send_ref):
-    step = pl.program_id(0)
-    half = pl.num_programs(0) // 2
-    grads = grad_ref[...]
-    total = None
-    for first in range(0, in_ref.shape[1], CHUNK):
-        cols = slice(first, first + CHUNK)
-        active_grad = dot_nt(grads, out_ref[cols])
-        up_grad = (active_grad * slope_ref[:, cols].astype(jnp.float32)).astype(jnp.bfloat16)
-        upgrad_ref[:, cols] = up_grad
-        part = dot_nt(up_grad, in_ref[:, cols])
-        total = part if total is None else total + part
-
-    @pl.when(step < half)
-    def _():
-        keep_ref[...] = total
-
-    @pl.when(step >= half)
-    def _():
-        send_ref[...] = total.astype(send_ref.dtype)
-
-
-def split_specs(count, width):
-    half = count // 2
-    return [
-        pl.BlockSpec((ROWS, width), lambda i: (jnp.minimum(i, half - 1), 0)),
-        pl.BlockSpec((ROWS, width), lambda i: (jnp.maximum(i - half, 0), 0)),
-    ]
-
-
-def expert_forward(x, w_in, w_out):
-    rows, width = x.shape
-    hidden = w_in.shape[1]
-    count = rows // ROWS
-    def wide(cols):
-        return pl.BlockSpec((ROWS, cols), lambda i: (i, 0))
-    def whole(shape):
-        return pl.BlockSpec(shape, lambda i: (0, 0), pipeline_mode=pl.Buffered(1))
-    return pl.pallas_call(
-        expert_fwd_kernel,
-        grid=(count,),
-        in_specs=[wide(width), whole(w_in.shape), whole(w_out.shape)],
-        out_specs=[wide(hidden), wide(hidden)] + split_specs(count, width),
-        out_shape=(
-            jax.ShapeDtypeStruct((rows, hidden), jnp.bfloat16),
-            jax.ShapeDtypeStruct((rows, hidden), jnp.bfloat16),
-            jax.ShapeDtypeStruct((rows // 2, width), jnp.float32),
-            jax.ShapeDtypeStruct((rows // 2, width), jnp.bfloat16),
-        ),
-        cost_estimate=pl.CostEstimate(flops=4 * rows * width * hidden, bytes_accessed=24 << 20, transcendentals=2 * rows * hidden),
-        compiler_params=pltpu.CompilerParams(vmem_limit_bytes=40 << 20),
-        name="expert_forward",
-    )(x, w_in, w_out)
-
-
-def expert_back(grads, slope, w_in, w_out):
-    rows, width = grads.shape
-    hidden = w_in.shape[1]
-    count = rows // ROWS
-    def wide(cols):
-        return pl.BlockSpec((ROWS, cols), lambda i: (i, 0))
-    def whole(shape):
-        return pl.BlockSpec(shape, lambda i: (0, 0), pipeline_mode=pl.Buffered(1))
-    return pl.pallas_call(
-        expert_bwd_kernel,
-        grid=(count,),
-        in_specs=[wide(width), wide(hidden), whole(w_in.shape), whole(w_out.shape)],
-        out_specs=[wide(hidden)] + split_specs(count, width),
-        out_shape=(
-            jax.ShapeDtypeStruct((rows, hidden), jnp.bfloat16),
-            jax.ShapeDtypeStruct((rows // 2, width), jnp.float32),
-            jax.ShapeDtypeStruct((rows // 2, width), jnp.bfloat16),
-        ),
-        cost_estimate=pl.CostEstimate(flops=4 * rows * width * hidden, bytes_accessed=24 << 20, transcendentals=0),
-        compiler_params=pltpu.CompilerParams(vmem_limit_bytes=40 << 20),
-        name="expert_backward",
-    )(grads, slope, w_in, w_out)
-
-
 MESH = pl.DeviceIdType.MESH
-
-
 PIECE = 64
 
 
@@ -1087,6 +975,231 @@
     return out, block[:depth], total
 
 
+HALF_ROOT = math.sqrt(0.5)
+PDF_SCALE = 1.0 / math.sqrt(2.0 * math.pi)
+CHUNK = 512
+BAND = 256
+
+
+def expert_kernel(
+    dp, x_in, g_in, w_in, w_out, result_ref, back_ref, in_grad_ref, out_grad_ref,
+    x_ref, g_ref, active_ref, slope_ref, keep_ref, part_ref, land_ref, home_ref,
+    back_part, back_land, back_home,
+    x_send, x_recv, x_pair_send, x_pair_recv, g_send, g_recv, g_pair_send, g_pair_recv,
+    y_pair_send, y_pair_recv, y_send, y_recv, d_pair_send, d_pair_recv, d_send, d_recv,
+):
+    spot, place = lax.axis_index("dp"), lax.axis_index("tensor")
+    chips = dp // 2
+    chip, core = spot // 2, lax.rem(spot, 2)
+    partner = (chip * 2 + 1 - core, place)
+    capacity = x_in.shape[0] // chips
+
+    def ahead(step):
+        return (lax.rem(chip + step, chips) * 2 + core, place)
+
+    def behind(step):
+        return (lax.rem(chip - step + chips, chips) * 2 + core, place)
+
+    def at(side, step):
+        return pl.ds(pl.multiple_of((side * chips + step) * capacity, capacity), capacity)
+
+    greet([ahead(step) for step in range(1, chips)] + [partner])
+
+    def copy(source, target, send, recv, step, where):
+        return pltpu.make_async_remote_copy(
+            src_ref=source, dst_ref=target, send_sem=send.at[step], recv_sem=recv.at[step],
+            device_id=where, device_id_type=MESH,
+        )
+
+    def go_x(step):
+        return copy(x_in.at[at(0, step)], x_ref.at[at(0, step)], x_send, x_recv, step, ahead(step))
+
+    def go_g(step):
+        return copy(g_in.at[at(0, step)], g_ref.at[at(0, step)], g_send, g_recv, step, ahead(step))
+
+    def pair_x(step):
+        return copy(
+            x_ref.at[at(0, step)], x_ref.at[at(1, step)], x_pair_send, x_pair_recv, step, partner
+        )
+
+    def pair_g(step):
+        return copy(
+            g_ref.at[at(0, step)], g_ref.at[at(1, step)], g_pair_send, g_pair_recv, step, partner
+        )
+
+    def pair_y(step):
+        here = at(0, step)
+        return copy(part_ref.at[here], land_ref.at[here], y_pair_send, y_pair_recv, step, partner)
+
+    def pair_d(step):
+        here = at(0, step)
+        return copy(back_part.at[here], back_land.at[here], d_pair_send, d_pair_recv, step, partner)
+
+    def home_y(step):
+        here = at(0, step)
+        return copy(home_ref.at[here], result_ref.at[here], y_send, y_recv, step, behind(step))
+
+    def home_d(step):
+        here = at(0, step)
+        return copy(back_home.at[here], back_ref.at[here], d_send, d_recv, step, behind(step))
+
+    @pl.loop(1, chips)
+    def _(step):
+        go_x(step).start()
+
+    x_ref[at(0, 0)] = x_in[at(0, 0)]
+    pair_x(0).start()
+
+    @pl.loop(1, chips)
+    def _(step):
+        go_g(step).start()
+
+    g_ref[at(0, 0)] = g_in[at(0, 0)]
+
+    def ahead_pass(side, step):
+        rows = x_ref[at(side, step)]
+        total = None
+        for first in range(0, w_in.shape[1], CHUNK):
+            cols = slice(first, first + CHUNK)
+            up = dot_nn(rows, w_in[:, cols])
+            below = 0.5 * (1.0 + lax.erf(up * HALF_ROOT))
+            active = (up * below).astype(jnp.bfloat16)
+            slope = below + up * (jnp.exp(-0.5 * up * up) * PDF_SCALE)
+            active_ref[at(side, step), cols] = active
+            slope_ref[at(side, step), cols] = slope.astype(jnp.bfloat16)
+            part = dot_nn(active, w_out[cols])
+            total = part if total is None else total + part
+        return total
+
+    def back_pass(side, step):
+        grads = g_ref[at(side, step)]
+        total = None
+        for first in range(0, w_in.shape[1], CHUNK):
+            cols = slice(first, first + CHUNK)
+            active_grad = dot_nt(grads, w_out[cols])
+            up_grad = active_grad * slope_ref[at(side, step), cols].astype(jnp.float32)
+            up_grad = up_grad.astype(jnp.bfloat16)
+            slope_ref[at(side, step), cols] = up_grad
+            part = dot_nt(up_grad, w_in[:, cols])
+            total = part if total is None else total + part
+        return total
+
+    keep_ref[at(0, 0)] = ahead_pass(0, 0)
+
+    @pl.loop(1, chips)
+    def _(step):
+        go_x(step).wait_recv()
+        pair_x(step).start()
+        keep_ref[at(0, step)] = ahead_pass(0, step)
+
+    pair_g(0).start()
+
+    @pl.loop(0, chips)
+    def _(step):
+        pair_x(step).wait_recv()
+        part_ref[at(0, step)] = ahead_pass(1, step).astype(part_ref.dtype)
+        pair_y(step).start()
+
+    @pl.loop(1, chips)
+    def _(step):
+        go_g(step).wait_recv()
+        pair_g(step).start()
+
+    @pl.loop(0, chips)
+    def _(step):
+        pair_y(step).wait_recv()
+        here = at(0, step)
+        total = keep_ref[here] + land_ref[here].astype(jnp.float32)
+        home_ref[here] = total.astype(home_ref.dtype)
+
+        @pl.when(step > 0)
+        def _():
+            home_y(step).start()
+
+        @pl.when(step == 0)
+        def _():
+            result_ref[here] = total.astype(result_ref.dtype)
+
+    @pl.loop(0, chips)
+    def _(step):
+        pair_g(step).wait_recv()
+        back_part[at(0, step)] = back_pass(1, step).astype(back_part.dtype)
+        pair_d(step).start()
+
+    @pl.loop(0, chips)
+    def _(turn):
+        step = chips - 1 - turn
+        here = at(0, step)
+        total = back_pass(0, step)
+        pair_d(step).wait_recv()
+        total = (total + back_land[here].astype(jnp.float32)).astype(back_home.dtype)
+        back_home[here] = total
+
+        @pl.when(step > 0)
+        def _():
+            home_d(step).start()
+
+        @pl.when(step == 0)
+        def _():
+            back_ref[here] = total
+
+    @pl.loop(0, w_in.shape[1] // BAND)
+    def _(band):
+        cols = pl.ds(pl.multiple_of(band * BAND, BAND), BAND)
+        out_grad_ref[cols] = dot_tn(active_ref[:, cols], g_ref[...]).astype(out_grad_ref.dtype)
+        in_grad_ref[cols] = dot_tn(slope_ref[:, cols], x_ref[...]).astype(in_grad_ref.dtype)
+
+    @pl.loop(1, chips)
+    def _(step):
+        home_y(step).wait_recv()
+        home_d(step).wait_recv()
+
+    @pl.loop(0, chips)
+    def _(step):
+        pair_x(step).wait_send()
+        pair_g(step).wait_send()
+        pair_y(step).wait_send()
+        pair_d(step).wait_send()
+
+    @pl.loop(1, chips)
+    def _(step):
+        go_x(step).wait_send()
+        go_g(step).wait_send()
+        home_y(step).wait_send()
+        home_d(step).wait_send()
+
+
+def run_experts(slot_rows, slot_grads, w_in, w_out):
+    dp = lax.axis_size("dp")
+    rows, width = slot_rows.shape
+    hidden = w_in.shape[1]
+    low = jnp.bfloat16
+    here = pl.BlockSpec(memory_space=pltpu.VMEM)
+    near = pltpu.VMEM((rows, width), low)
+    both = pltpu.VMEM((2 * rows, width), low)
+    middle = pltpu.VMEM((2 * rows, hidden), low)
+    return pl.pallas_call(
+        lambda *refs: expert_kernel(dp, *refs),
+        out_shape=(
+            jax.ShapeDtypeStruct((rows, width), low),
+            jax.ShapeDtypeStruct((rows, width), low),
+            jax.ShapeDtypeStruct((hidden, width), low),
+            jax.ShapeDtypeStruct((hidden, width), low),
+        ),
+        in_specs=[here] * 4,
+        out_specs=[here] * 4,
+        scratch_shapes=[
+            both, both, middle, middle, pltpu.VMEM((rows, width), jnp.float32),
+            near, near, near, near, near, near,
+        ]
+        + [pltpu.SemaphoreType.DMA((dp // 2,))] * 16,
+        compiler_params=pltpu.CompilerParams(
+            collective_id=4, has_side_effects=True, vmem_limit_bytes=60 << 20
+        ),
+        name="run_experts",
+    )(slot_rows, slot_grads, w_in, w_out)
+
+
 norm_eps = 1e-05
 route_scale = 3.0
 masked_score = -1e30
@@ -1146,27 +1259,6 @@
     experts = expert_embed.shape[0]
     capacity = rows_here // experts
     dp_size, tensor_size = lax.axis_size("dp"), lax.axis_size("tensor")
-
-    def hop(rows, chip_step, core_step):
-        route = []
-        for source in range(dp_size):
-            chip, core = source // 2, source % 2
-            route.append((source, (chip ^ chip_step) * 2 + (core ^ core_step)))
-        return lax.ppermute(rows, "dp", route)
-
-    def chip_blocks(rows):
-        blocks = rows.reshape(experts, capacity, model_width)
-        return [blocks[0]] + [hop(blocks[step], step, 0) for step in range(1, experts)]
-
-    def across_chips(rows):
-        return jnp.concatenate(chip_blocks(rows), axis=0)
-
-    def with_partner(blocks):
-        arrived = jnp.concatenate(blocks, axis=0)
-        return jnp.concatenate([arrived, hop(arrived, 0, 1)], axis=0)
-
-    def pair_sum(kept_rows, sent_rows):
-        return (kept_rows + hop(sent_rows, 0, 1).astype(jnp.float32)).astype(jnp.bfloat16)
 
     hidden = tokens.astype(jnp.float32)
     normed_in, norm1_back = jax.vjp(layer_norm, hidden, norm1_gain)
@@ -1193,7 +1285,7 @@
     normed_mid, norm2_back = jax.vjp(layer_norm, mid_stream, norm2_gain)
     moe_in = normed_mid.astype(jnp.bfloat16)
     route_ids = routes[:, 0]
-    near_route = route_ids ^ (lax.axis_index("dp") // 2)
+    near_route = (route_ids - lax.axis_index("dp") // 2) % experts
     column, kept_mask = slot_table(near_route, orders[0], capacity)
     picked = (route_ids[:, None] == jnp.arange(experts)[None, :]).astype(jnp.float32)
     gate_value, gate_back = jax.vjp(
@@ -1217,29 +1309,12 @@
 
     upstream = cotangent.astype(jnp.float32)
     slot_grads = to_slots((gate_value[:, None] * upstream).astype(jnp.bfloat16))
-    row_blocks, slot_grads = lax.optimization_barrier(
-        (chip_blocks(to_slots(moe_in)), slot_grads)
+    result_rows, grad_rows, in_weight_grad, out_weight_grad = run_experts(
+        to_slots(moe_in), slot_grads, expert_in, expert_out
     )
-    grad_blocks = chip_blocks(slot_grads)
-    expert_rows = with_partner(row_blocks)
-    active, slope, kept_result, sent_result = expert_forward(expert_rows, expert_in, expert_out)
-    grad_blocks, kept_result, sent_result = lax.optimization_barrier(
-        (grad_blocks, kept_result, sent_result)
-    )
-    arrived_grad = with_partner(grad_blocks)
-    result_rows, late_grad = lax.optimization_barrier(
-        (pair_sum(kept_result, sent_result), arrived_grad)
-    )
-    expert_result = from_slots(across_chips(result_rows))
+    expert_result = from_slots(result_rows)
     output = (mid_stream + gate_value[:, None] * expert_result).astype(jnp.bfloat16)
-    out_weight_grad = jnp.einsum(
-        "rf,rd->fd", active, arrived_grad, preferred_element_type=jnp.float32
-    ).astype(jnp.bfloat16)
-    up_grad, kept_grad, sent_grad = expert_back(late_grad, slope, expert_in, expert_out)
-    in_weight_grad = jnp.einsum(
-        "rf,rd->fd", up_grad, expert_rows, preferred_element_type=jnp.float32
-    ).astype(jnp.bfloat16)
-    moe_grad = from_slots(across_chips(pair_sum(kept_grad, sent_grad)))
+    moe_grad = from_slots(grad_rows)
     gate_grad = jnp.sum(upstream * expert_result, axis=-1)
     router_part, proj_grad, embed_grad = gate_back(gate_grad)
     mid_part, gain2_grad = norm2_back(moe_grad + router_part)

time: 472 us -> 483 us (1.023)
  Pallas kernels: 294 us -> 375 us
  waiting for transfers between devices: 35.7 us -> 0.71 us
  matrix products: 56.6 us -> 40.1 us
  starting transfers between devices: 14.9 us -> 0.08 us
    pallas_call x2 -> x1, Pallas kernels: 31 us -> 80.4 us  [run_experts(): pl.pallas_call(lambda *refs: expert_kernel(dp, *refs), out_shape=(jax.Sha...]
    ppermute x16 -> x0, waiting for transfers between devices: 35.7 us -> none  [hop(): return lax.ppermute(rows, 'dp', route)]
    pallas_call x1, Pallas kernels: 190 us -> 222 us  [backward(): pl.pallas_call(lambda *refs: back_kernel(dp, tensor, depth, *refs), out_s...]
    dot_general x2 -> x0, matrix products: 18.8 us -> none  [the longest x1 9.45 us: shards(): jnp.einsum('rf,rd->fd', active, arrived_grad, preferred_element_type=jnp....]
    ppermute x16 -> x0, starting transfers between devices: 14.9 us -> none  [hop(): return lax.ppermute(rows, 'dp', route)]
    unnamed x78 -> x52, local copies, waits for them, and re-layouts: 11.5 us -> 7.82 us
  transfers between devices with their start and end apart: 18 -> 2, of which waited for: 9 -> 0; matrix products, arithmetic and copies ran while one was open for 13% -> 10% of each run, Pallas kernels for 44% -> 47%
where the time goes in v8:
time: 483 us; the launch traced here: 476 us
  Pallas kernels  375 us (78%)
  matrix products  40.1 us (8%)
  other arithmetic  26.8 us (6%)
  local copies, waits for them, and re-layouts  18.4 us (4%)
  between operations  15 us (3%)
    pallas_call x1, Pallas kernels, backward(): pl.pallas_call(lambda *refs: back_kernel(dp, tensor, depth, *refs), out_s...  222 us
    pallas_call x1, Pallas kernels, run_experts(): pl.pallas_call(lambda *refs: expert_kernel(dp, *refs), out_shape=(jax.Sha...  80.4 us
    pallas_call x1, Pallas kernels, share_rows_and_weights(): pl.pallas_call(lambda *refs: share_kernel(dp, tensor, *refs), out_shape=(...  54.5 us
    pallas_call x1, Pallas kernels, attend(): pl.pallas_call(fwd_kernel, out_shape=(jax.ShapeDtypeStruct((rows, width),...  18.7 us
    dot_general x3, matrix products, low_dot(): jnp.dot(rows, weight, preferred_element_type=jnp.float32)  13.9 us
  transfers between devices with their start and end apart: 2, of which 0 were waited for; matrix products, arithmetic and copies ran while one was open for 10% of the time, Pallas kernels for 47%

profile of v8, /device:TPU:0, one launch (start us, length us, event | category | flops | bytes accessed | tf_op | source)
XLA Modules:
  0.0 476.3 jit_solution(8696890098354599089)
XLA Ops:
  8.8 2.0 select_reduce_fusion
  11.8 1.7 convert_reduce_fusion
  13.5 2.0 fusion.13
  16.7 54.5 %share_rows_and_weights.1 = (bf16[3072,768]{1,0:T(8,128)(2,1)}, bf16[4,768,768]{2,1,0:T(8,128)(2,1)}) custom-call(bf16[1024,768]{1,0:T(8,128)(2,1)S(1)} %fusion.15.refs_0_, bf16[96,768]{1,0:T(8,128)(2,1)S(1)} %pad_maximum_fusion.refs_1_, f32[16,768]{1,0:T(8,128)S(1)} %broadcast_in_dim.31.refs_2_.refs_0_), custom_call_target="tpu_custom_call" | custom-call | tf_op jit(solution)/shard_map/share_rows_and_weights/pallas_call | solution.py:342
  71.2 2.8 convolution_convert_fusion.2.q_ref.refs_1_
  74.0 1.8 copy-done.15
  75.8 5.5 %convolution_convert_fusion.v_ref.refs_3_ = bf16[3072,768]{1,0:T(8,128)(2,1)} fusion(bf16[3072,768]{1,0:T(8,128)(2,1)S(1)} %copy-done.14, bf16[4,768,768]{2,1,0:T(8,128)(2,1)S(1)} %copy-done.15), kind=kOutput, calls=%fused_computation | convolution fusion | flops 3626237952 | bytes 10616832 | tf_op jit(solution)/shard_map/dot_general | solution.py:1239
  81.4 5.6 %convolution_convert_fusion.1.k_ref.refs_2_ = bf16[3072,768]{1,0:T(8,128)(2,1)} fusion(bf16[3072,768]{1,0:T(8,128)(2,1)S(1)} %copy-done.14, bf16[4,768,768]{2,1,0:T(8,128)(2,1)S(1)} %copy-done.15), kind=kOutput, calls=%fused_computation.1 | convolution fusion | flops 3626237952 | bytes 10616832 | tf_op jit(solution)/shard_map/dot_general | solution.py:1239
  87.1 18.7 %attend_forward.1 = (bf16[1024,768]{1,0:T(8,128)(2,1)S(1)}, f32[6,2,1024]{2,1,0:T(2,128)S(1)}) custom-call(s32[1]{0:T(128)} %bitcast.place_ref, bf16[1024,768]{1,0:T(8,128)(2,1)S(1)} %convolution_convert_fusion.2.q_ref.refs_1_, bf16[3072,768]{1,0:T(8,128)(2,1)} %convolution_convert_fusion.1.k_ref.refs_2_, bf16[3072,768]{1,0:T(8,128)(2,1)} %convolution_convert_fusion.v_ref.refs_3_), custom_call_target="tpu_custom_call" | custom-call | tf_op jit(solution)/shard_map/attend_forward/pallas_call | solution.py:113
  105.9 1.6 fusion.73
  109.1 1.3 multiply_reduce_fusion.4
  110.8 3.6 fusion.28.refs_0_
  114.4 3.7 fusion.31.refs_1_
  118.1 80.4 %run_experts.1 = (bf16[1024,768]{1,0:T(8,128)(2,1)}, bf16[1024,768]{1,0:T(8,128)(2,1)}, bf16[1536,768]{1,0:T(8,128)(2,1)}, bf16[1536,768]{1,0:T(8,128)(2,1)}) custom-call(bf16[1024,768]{1,0:T(8,128)(2,1)} %fusion.28.refs_0_, bf16[1024,768]{1,0:T(8,128)(2,1)} %fusion.31.refs_1_, bf16[768,1536]{1,0:T(8,128)(2,1)} %refs_2_.1, bf16[1536,768]{1,0:T(8,128)(2,1)} %refs_3_.1), custom_call_target="tpu_custom_call" | custom-call | tf_op jit(solution)/shard_map/run_experts/pallas_call | solution.py:1181
  199.3 5.1 %fusion.18 = (f32[1024]{0:T(1024)S(1)}, f32[1024,768]{1,0:T(8,128)}) fusion(bf16[1024,768]{1,0:T(8,128)(2,1)S(1)} %copy-done.13, bf16[1024,768]{1,0:T(8,128)(2,1)} %get-tuple-element.24, s32[1024]{0:T(1024)S(1)} %bitcast.57, pred[1024]{0:T(1024)(128)(4,1)S(1)} %broadcast_compare_fusion), kind=kOutput, calls=%fused_computation.26 | convolution fusion | flops 1615068160 | bytes 6300672 | tf_op jit(solution)/shard_map/dot_general | solution.py:1308
  205.3 2.5 fusion.56
  209.0 3.7 fusion.5
  212.7 3.8 multiply_reduce_fusion
  217.2 2.7 fusion.71
  219.9 2.0 fusion.27.refs_5_
  222.1 221.6 %attend_backward.1 = (f32[1024,768]{1,0:T(8,128)}, f32[96,768]{1,0:T(8,128)}, f32[32,8,128]{2,1,0:T(8,128)}) custom-call(f32[16,768]{1,0:T(8,128)} %copy-done.3, bf16[1024,768]{1,0:T(8,128)(2,1)} %copy-done.1, bf16[3072,768]{1,0:T(8,128)(2,1)} %convolution_convert_fusion.1.k_ref.refs_2_, bf16[3072,768]{1,0:T(8,128)(2,1)} %convolution_convert_fusion.v_ref.refs_3_, ...), custom_call_target="tpu_custom_call" | custom-call | tf_op jit(solution)/shard_map/attend_backward/pallas_call | solution.py:932
  443.7 2.3 slice.26
  446.0 1.3 slice.32
  447.3 1.8 slice.31
  449.0 1.7 slice.23
  454.4 1.8 copy.60
  456.1 2.8 fusion.16
  459.0 1.4 fusion.70
  460.4 1.4 fusion.72
  461.7 2.6 add_add_fusion.2
  465.5 1.4 copy.61
  466.9 2.2 convert_element_type.69
  (98 shorter events, 14.2 us)
Async XLA Ops:
  7.2 102.0 %copy-start = (f32[768,16]{0,1:T(8,128)S(1)}, f32[768,16]{0,1:T(8,128)}, u32[]{:S(2)}) copy-start(f32[768,16]{0,1:T(8,128)} %param.18) | copy-start | bytes 147460
  7.2 8.8 %copy-start.5 = (bf16[1024,768]{1,0:T(8,128)(2,1)S(1)}, bf16[1024,768]{1,0:T(8,128)(2,1)}, u32[]{:S(2)}) copy-start(bf16[1024,768]{1,0:T(8,128)(2,1)} %param.13) | copy-start | bytes 4718596
  7.2 8.3 %copy-start.20 = (bf16[192,96]{1,0:T(8,128)(2,1)S(1)}, bf16[192,96]{1,0:T(8,128)(2,1)}, u32[]{:S(2)}) copy-start(bf16[192,96]{1,0:T(8,128)(2,1)} %param.16) | copy-start | bytes 110596
  7.2 8.4 %copy-start.17 = (bf16[96,3,192]{2,0,1:T(8,128)(2,1)S(1)}, bf16[96,3,192]{2,0,1:T(8,128)(2,1)}, u32[]{:S(2)}) copy-start(bf16[96,3,192]{2,0,1:T(8,128)(2,1)} %param.15) | copy-start | bytes 331780
  7.2 8.8 %copy-start.19 = (f32[768]{0:T(1024)S(1)}, f32[768]{0:T(1024)}, u32[]{:S(2)}) copy-start(f32[768]{0:T(1024)} %param.14) | copy-start | bytes 9220
  7.2 457.1 %reduce-scatter.3.cloned.1.call-start = ((), (), s32[]{:S(2)}) async-start(), calls=%async_computation.2 | async-start | bytes 2949120 | tf_op jit(solution)/shard_map/reduce_scatter | solution.py:1323
  16.7 57.3 %copy-start.3 = (f32[16,768]{1,0:T(8,128)}, f32[16,768]{1,0:T(8,128)S(1)}, u32[]{:S(2)}) copy-start(f32[16,768]{1,0:T(8,128)S(1)} %broadcast_in_dim.31.refs_2_.refs_0_) | copy-start | bytes 147460
  71.1 2.9 copy-start.14
  71.1 4.7 copy-start.15
  74.0 13.1 %copy-start.1 = (bf16[1024,768]{1,0:T(8,128)(2,1)}, bf16[1024,768]{1,0:T(8,128)(2,1)S(1)}, u32[]{:S(2)}) copy-start(bf16[1024,768]{1,0:T(8,128)(2,1)S(1)} %convolution_convert_fusion.2.q_ref.refs_1_) | copy-start | bytes 4718596
  81.4 5.6 %copy-start.22 = (f32[4,16]{1,0:T(4,128)S(1)}, f32[4,16]{1,0:T(4,128)}, u32[]{:S(2)}) copy-start(f32[4,16]{1,0:T(4,128)} %param.19) | copy-start | bytes 772
  81.4 5.7 %copy-start.18 = (s32[1024,1]{0,1:T(1,128)S(1)}, s32[1024,1]{0,1:T(1,128)}, u32[]{:S(2)}) copy-start(s32[1024,1]{0,1:T(1,128)} %param.22) | copy-start | bytes 12292
  87.1 18.7 %copy-start.6 = (bf16[1024,768]{1,0:T(8,128)(2,1)S(1)}, bf16[1024,768]{1,0:T(8,128)(2,1)}, u32[]{:S(2)}) copy-start(bf16[1024,768]{1,0:T(8,128)(2,1)} %param.13) | copy-start | bytes 4718596
  105.8 1.6 copy-start.2
  105.8 1.6 copy-start.4
  107.5 1.7 copy-start.8
  107.5 0.7 copy-start.21
  110.8 3.6 copy-start.13
  198.6 268.3 %reduce-scatter.5.cloned.1.call-start = ((), (), s32[]{:S(2)}) async-start(), calls=%async_computation.3 | async-start | bytes 2949120 | tf_op jit(solution)/shard_map/reduce_scatter | solution.py:1327
  209.0 3.7 copy-start.9
  212.7 4.5 copy-start.16
  219.9 2.2 copy-start.11
  443.7 12.5 %copy-start.7 = (bf16[1024,768]{1,0:T(8,128)(2,1)S(1)}, bf16[1024,768]{1,0:T(8,128)(2,1)}, u32[]{:S(2)}) copy-start(bf16[1024,768]{1,0:T(8,128)(2,1)} %param.13) | copy-start | bytes 4718596
  456.1 2.8 copy-start.10
  458.9 2.8 copy-start.12
Sparse Core Ops, SparseCore 0:
  198.7 102.6 reduce-scatter.2
  303.7 85.2 reduce-scatter.4

commit v9 on v8

--- a/solution.py
+++ b/solution.py
@@ -982,11 +982,12 @@
 
 
 def expert_kernel(
-    dp, x_in, g_in, w_in, w_out, result_ref, back_ref, in_grad_ref, out_grad_ref,
+    dp, tensor, x_in, g_in, w_in, w_out, result_ref, back_ref, in_grad_ref, out_grad_ref,
     x_ref, g_ref, active_ref, slope_ref, keep_ref, part_ref, land_ref, home_ref,
-    back_part, back_land, back_home,
+    back_part, back_land, back_home, grad_ref, grad_land,
     x_send, x_recv, x_pair_send, x_pair_recv, g_send, g_recv, g_pair_send, g_pair_recv,
     y_pair_send, y_pair_recv, y_send, y_recv, d_pair_send, d_pair_recv, d_send, d_recv,
+    line_send, line_recv,
 ):
     spot, place = lax.axis_index("dp"), lax.axis_index("tensor")
     chips = dp // 2
@@ -1003,7 +1004,30 @@
     def at(side, step):
         return pl.ds(pl.multiple_of((side * chips + step) * capacity, capacity), capacity)
 
-    greet([ahead(step) for step in range(1, chips)] + [partner])
+    def along(step):
+        return lax.rem(place + step, tensor)
+
+    greet(
+        [ahead(step) for step in range(1, chips)]
+        + [partner]
+        + [(spot, along(step)) for step in range(1, tensor)]
+    )
+    share = out_grad_ref.shape[0]
+
+    def line(step):
+        return pltpu.make_async_remote_copy(
+            src_ref=grad_ref.at[along(step)], dst_ref=grad_land.at[place],
+            send_sem=line_send.at[step], recv_sem=line_recv.at[place],
+            device_id=(spot, along(step)), device_id_type=MESH,
+        )
+
+    def line_in(step):
+        source = along(tensor - step)
+        return pltpu.make_async_remote_copy(
+            src_ref=grad_ref.at[source], dst_ref=grad_land.at[source],
+            send_sem=line_send.at[step], recv_sem=line_recv.at[source],
+            device_id=(spot, along(step)), device_id_type=MESH,
+        )
 
     def copy(source, target, send, recv, step, where):
         return pltpu.make_async_remote_copy(
@@ -1123,6 +1147,20 @@
     @pl.loop(0, chips)
     def _(step):
         pair_g(step).wait_recv()
+
+    @pl.loop(0, tensor)
+    def _(part):
+        for first in range(0, share, 128):
+            cols = pl.ds(pl.multiple_of(part * share + first, 128), 128)
+            grad_ref[part, first : first + 128] = dot_tn(active_ref[:, cols], g_ref[...]).astype(
+                grad_ref.dtype
+            )
+
+    for step in range(1, tensor):
+        line(step).start()
+
+    @pl.loop(0, chips)
+    def _(step):
         back_part[at(0, step)] = back_pass(1, step).astype(back_part.dtype)
         pair_d(step).start()
 
@@ -1146,8 +1184,14 @@
     @pl.loop(0, w_in.shape[1] // BAND)
     def _(band):
         cols = pl.ds(pl.multiple_of(band * BAND, BAND), BAND)
-        out_grad_ref[cols] = dot_tn(active_ref[:, cols], g_ref[...]).astype(out_grad_ref.dtype)
         in_grad_ref[cols] = dot_tn(slope_ref[:, cols], x_ref[...]).astype(in_grad_ref.dtype)
+
+    out_grad_ref[...] = grad_ref[place].astype(jnp.float32)
+    for step in range(1, tensor):
+        line_in(step).wait_recv()
+        out_grad_ref[...] += grad_land[along(tensor - step)].astype(jnp.float32)
+    for step in range(1, tensor):
+        line(step).wait_send()
 
     @pl.loop(1, chips)
     def _(step):
@@ -1170,7 +1214,7 @@
 
 
 def run_experts(slot_rows, slot_grads, w_in, w_out):
-    dp = lax.axis_size("dp")
+    dp, tensor = lax.axis_size("dp"), lax.axis_size("tensor")
     rows, width = slot_rows.shape
     hidden = w_in.shape[1]
     low = jnp.bfloat16
@@ -1179,20 +1223,23 @@
     both = pltpu.VMEM((2 * rows, width), low)
     middle = pltpu.VMEM((2 * rows, hidden), low)
     return pl.pallas_call(
-        lambda *refs: expert_kernel(dp, *refs),
+        lambda *refs: expert_kernel(dp, tensor, *refs),
         out_shape=(
             jax.ShapeDtypeStruct((rows, width), low),
             jax.ShapeDtypeStruct((rows, width), low),
             jax.ShapeDtypeStruct((hidden, width), low),
-            jax.ShapeDtypeStruct((hidden, width), low),
+            jax.ShapeDtypeStruct((hidden // tensor, width), jnp.float32),
         ),
         in_specs=[here] * 4,
         out_specs=[here] * 4,
         scratch_shapes=[
             both, both, middle, middle, pltpu.VMEM((rows, width), jnp.float32),
             near, near, near, near, near, near,
+            pltpu.VMEM((tensor, hidden // tensor, width), low),
+            pltpu.VMEM((tensor, hidden // tensor, width), low),
         ]
-        + [pltpu.SemaphoreType.DMA((dp // 2,))] * 16,
+        + [pltpu.SemaphoreType.DMA((dp // 2,))] * 16
+        + [pltpu.SemaphoreType.DMA((tensor,))] * 2,
         compiler_params=pltpu.CompilerParams(
             collective_id=4, has_side_effects=True, vmem_limit_bytes=60 << 20
         ),
@@ -1309,7 +1356,7 @@
 
     upstream = cotangent.astype(jnp.float32)
     slot_grads = to_slots((gate_value[:, None] * upstream).astype(jnp.bfloat16))
-    result_rows, grad_rows, in_weight_grad, out_weight_grad = run_experts(
+    result_rows, grad_rows, in_weight_grad, expert_out_grad = run_experts(
         to_slots(moe_in), slot_grads, expert_in, expert_out
     )
     expert_result = from_slots(result_rows)
@@ -1324,9 +1371,6 @@
         .astype(jnp.float32)
         .T
     )
-    expert_out_grad = lax.psum_scatter(
-        out_weight_grad, "tensor", scatter_dimension=0, tiled=True
-    ).astype(jnp.float32)
     branch_grad = mid_grad.astype(jnp.bfloat16)
     later = [gain2_grad, proj_grad, embed_grad]
     flat = jnp.concatenate([jnp.zeros_like(norm1_gain)] + [part.reshape(-1) for part in later])

time: 483 us -> 465 us (0.963)
  Pallas kernels: 375 us -> 360 us
    pallas_call x1, Pallas kernels: 222 us -> 144 us  [backward(): pl.pallas_call(lambda *refs: back_kernel(dp, tensor, depth, *refs), out_s...]
    pallas_call x1, Pallas kernels: 80.4 us -> 143 us  [run_experts(): pl.pallas_call(lambda *refs: expert_kernel(dp, tensor, *refs), out_shape=...]
  transfers between devices with their start and end apart: 2 -> 1, of which waited for: 0 -> 0; matrix products, arithmetic and copies ran while one was open for 10% -> 9% of each run, Pallas kernels for 47% -> 31%
where the time goes in v9:
time: 465 us; the launch traced here: 460 us
  Pallas kernels  360 us (77%)
  matrix products  40.1 us (9%)
  other arithmetic  24.7 us (5%)
  local copies, waits for them, and re-layouts  19.5 us (4%)
  between operations  15 us (3%)
    pallas_call x1, Pallas kernels, backward(): pl.pallas_call(lambda *refs: back_kernel(dp, tensor, depth, *refs), out_s...  144 us
    pallas_call x1, Pallas kernels, run_experts(): pl.pallas_call(lambda *refs: expert_kernel(dp, tensor, *refs), out_shape=...  143 us
    pallas_call x1, Pallas kernels, share_rows_and_weights(): pl.pallas_call(lambda *refs: share_kernel(dp, tensor, *refs), out_shape=(...  54.5 us
    pallas_call x1, Pallas kernels, attend(): pl.pallas_call(fwd_kernel, out_shape=(jax.ShapeDtypeStruct((rows, width),...  18.7 us
    dot_general x3, matrix products, low_dot(): jnp.dot(rows, weight, preferred_element_type=jnp.float32)  13.9 us
  transfers between devices with their start and end apart: 1, of which 0 were waited for; matrix products, arithmetic and copies ran while one was open for 9% of the time, Pallas kernels for 31%

profile of v9, /device:TPU:0, one launch (start us, length us, event | category | flops | bytes accessed | tf_op | source)
XLA Modules:
  0.0 459.6 jit_solution(12353864510152363457)
XLA Ops:
  8.8 2.0 select_reduce_fusion
  11.8 1.7 convert_reduce_fusion
  13.5 2.0 fusion.13
  16.7 54.5 %share_rows_and_weights.1 = (bf16[3072,768]{1,0:T(8,128)(2,1)}, bf16[4,768,768]{2,1,0:T(8,128)(2,1)}) custom-call(bf16[1024,768]{1,0:T(8,128)(2,1)S(1)} %fusion.15.refs_0_, bf16[96,768]{1,0:T(8,128)(2,1)S(1)} %pad_maximum_fusion.refs_1_, f32[16,768]{1,0:T(8,128)S(1)} %broadcast_in_dim.31.refs_2_.refs_0_), custom_call_target="tpu_custom_call" | custom-call | tf_op jit(solution)/shard_map/share_rows_and_weights/pallas_call | solution.py:342
  71.2 2.8 convolution_convert_fusion.2.q_ref.refs_1_
  74.0 1.8 copy-done.15
  75.8 5.5 %convolution_convert_fusion.v_ref.refs_3_ = bf16[3072,768]{1,0:T(8,128)(2,1)} fusion(bf16[3072,768]{1,0:T(8,128)(2,1)S(1)} %copy-done.14, bf16[4,768,768]{2,1,0:T(8,128)(2,1)S(1)} %copy-done.15), kind=kOutput, calls=%fused_computation | convolution fusion | flops 3626237952 | bytes 10616832 | tf_op jit(solution)/shard_map/dot_general | solution.py:1286
  81.4 5.6 %convolution_convert_fusion.1.k_ref.refs_2_ = bf16[3072,768]{1,0:T(8,128)(2,1)} fusion(bf16[3072,768]{1,0:T(8,128)(2,1)S(1)} %copy-done.14, bf16[4,768,768]{2,1,0:T(8,128)(2,1)S(1)} %copy-done.15), kind=kOutput, calls=%fused_computation.1 | convolution fusion | flops 3626237952 | bytes 10616832 | tf_op jit(solution)/shard_map/dot_general | solution.py:1286
  87.1 18.7 %attend_forward.1 = (bf16[1024,768]{1,0:T(8,128)(2,1)S(1)}, f32[6,2,1024]{2,1,0:T(2,128)S(1)}) custom-call(s32[1]{0:T(128)} %bitcast.place_ref, bf16[1024,768]{1,0:T(8,128)(2,1)S(1)} %convolution_convert_fusion.2.q_ref.refs_1_, bf16[3072,768]{1,0:T(8,128)(2,1)} %convolution_convert_fusion.1.k_ref.refs_2_, bf16[3072,768]{1,0:T(8,128)(2,1)} %convolution_convert_fusion.v_ref.refs_3_), custom_call_target="tpu_custom_call" | custom-call | tf_op jit(solution)/shard_map/attend_forward/pallas_call | solution.py:113
  105.9 1.6 fusion.73
  109.1 1.3 multiply_reduce_fusion.4
  110.8 3.6 fusion.28.refs_0_
  114.4 3.7 fusion.31.refs_1_
  118.1 142.7 %run_experts.1 = (bf16[1024,768]{1,0:T(8,128)(2,1)}, bf16[1024,768]{1,0:T(8,128)(2,1)}, bf16[1536,768]{1,0:T(8,128)(2,1)}, f32[384,768]{1,0:T(8,128)}) custom-call(bf16[1024,768]{1,0:T(8,128)(2,1)} %fusion.28.refs_0_, bf16[1024,768]{1,0:T(8,128)(2,1)} %fusion.31.refs_1_, bf16[768,1536]{1,0:T(8,128)(2,1)} %refs_2_.1, bf16[1536,768]{1,0:T(8,128)(2,1)} %refs_3_.1), custom_call_target="tpu_custom_call" | custom-call | tf_op jit(solution)/shard_map/run_experts/pallas_call | solution.py:1225
  260.9 5.1 %fusion.18 = (f32[1024]{0:T(1024)S(1)}, f32[1024,768]{1,0:T(8,128)}) fusion(bf16[1024,768]{1,0:T(8,128)(2,1)S(1)} %copy-done.13, bf16[1024,768]{1,0:T(8,128)(2,1)} %get-tuple-element.24, s32[1024]{0:T(1024)S(1)} %bitcast.57, pred[1024]{0:T(1024)(128)(4,1)S(1)} %broadcast_compare_fusion), kind=kOutput, calls=%fused_computation.26 | convolution fusion | flops 1615068160 | bytes 6300672 | tf_op jit(solution)/shard_map/dot_general | solution.py:1355
  266.8 2.5 fusion.56
  270.6 3.7 fusion.5
  274.3 3.8 multiply_reduce_fusion
  278.8 2.7 fusion.71
  281.5 2.0 fusion.27.refs_5_
  283.6 144.4 %attend_backward.1 = (f32[1024,768]{1,0:T(8,128)}, f32[96,768]{1,0:T(8,128)}, f32[32,8,128]{2,1,0:T(8,128)}) custom-call(f32[16,768]{1,0:T(8,128)} %copy-done.3, bf16[1024,768]{1,0:T(8,128)(2,1)} %copy-done.1, bf16[3072,768]{1,0:T(8,128)(2,1)} %convolution_convert_fusion.1.k_ref.refs_2_, bf16[3072,768]{1,0:T(8,128)(2,1)} %convolution_convert_fusion.v_ref.refs_3_, ...), custom_call_target="tpu_custom_call" | custom-call | tf_op jit(solution)/shard_map/attend_backward/pallas_call | solution.py:932
  428.0 2.3 slice.26
  430.3 1.3 slice.32
  431.6 1.8 slice.31
  433.4 1.7 slice.23
  438.7 1.8 copy.60
  440.5 2.8 fusion.16
  443.3 1.4 fusion.70
  444.7 1.4 fusion.72
  446.1 2.6 add_add_fusion.2
  448.7 1.2 convert_bitcast_fusion
  449.9 1.4 copy.61
  (97 shorter events, 13.4 us)
Async XLA Ops:
  7.2 102.0 %copy-start = (f32[768,16]{0,1:T(8,128)S(1)}, f32[768,16]{0,1:T(8,128)}, u32[]{:S(2)}) copy-start(f32[768,16]{0,1:T(8,128)} %param.18) | copy-start | bytes 147460
  7.2 8.8 %copy-start.5 = (bf16[1024,768]{1,0:T(8,128)(2,1)S(1)}, bf16[1024,768]{1,0:T(8,128)(2,1)}, u32[]{:S(2)}) copy-start(bf16[1024,768]{1,0:T(8,128)(2,1)} %param.13) | copy-start | bytes 4718596
  7.2 8.3 %copy-start.21 = (bf16[192,96]{1,0:T(8,128)(2,1)S(1)}, bf16[192,96]{1,0:T(8,128)(2,1)}, u32[]{:S(2)}) copy-start(bf16[192,96]{1,0:T(8,128)(2,1)} %param.16) | copy-start | bytes 110596
  7.2 8.4 %copy-start.18 = (bf16[96,3,192]{2,0,1:T(8,128)(2,1)S(1)}, bf16[96,3,192]{2,0,1:T(8,128)(2,1)}, u32[]{:S(2)}) copy-start(bf16[96,3,192]{2,0,1:T(8,128)(2,1)} %param.15) | copy-start | bytes 331780
  7.2 8.8 %copy-start.20 = (f32[768]{0:T(1024)S(1)}, f32[768]{0:T(1024)}, u32[]{:S(2)}) copy-start(f32[768]{0:T(1024)} %param.14) | copy-start | bytes 9220
  7.2 441.5 %reduce-scatter.2.cloned.1.call-start = ((), (), s32[]{:S(2)}) async-start(), calls=%async_computation.1 | async-start | bytes 2949120 | tf_op jit(solution)/shard_map/reduce_scatter | solution.py:1370
  16.7 57.3 %copy-start.3 = (f32[16,768]{1,0:T(8,128)}, f32[16,768]{1,0:T(8,128)S(1)}, u32[]{:S(2)}) copy-start(f32[16,768]{1,0:T(8,128)S(1)} %broadcast_in_dim.31.refs_2_.refs_0_) | copy-start | bytes 147460
  71.1 2.9 copy-start.14
  71.1 4.7 %copy-start.15 = (bf16[4,768,768]{2,1,0:T(8,128)(2,1)S(1)}, bf16[4,768,768]{2,1,0:T(8,128)(2,1)}, u32[]{:S(2)}) copy-start(bf16[4,768,768]{2,1,0:T(8,128)(2,1)} %get-tuple-element.21.refs_7_) | copy-start | bytes 14155780
  74.0 13.1 %copy-start.1 = (bf16[1024,768]{1,0:T(8,128)(2,1)}, bf16[1024,768]{1,0:T(8,128)(2,1)S(1)}, u32[]{:S(2)}) copy-start(bf16[1024,768]{1,0:T(8,128)(2,1)S(1)} %convolution_convert_fusion.2.q_ref.refs_1_) | copy-start | bytes 4718596
  81.4 5.6 %copy-start.23 = (f32[4,16]{1,0:T(4,128)S(1)}, f32[4,16]{1,0:T(4,128)}, u32[]{:S(2)}) copy-start(f32[4,16]{1,0:T(4,128)} %param.19) | copy-start | bytes 772
  81.4 5.7 %copy-start.19 = (s32[1024,1]{0,1:T(1,128)S(1)}, s32[1024,1]{0,1:T(1,128)}, u32[]{:S(2)}) copy-start(s32[1024,1]{0,1:T(1,128)} %param.22) | copy-start | bytes 12292
  87.1 18.7 %copy-start.6 = (bf16[1024,768]{1,0:T(8,128)(2,1)S(1)}, bf16[1024,768]{1,0:T(8,128)(2,1)}, u32[]{:S(2)}) copy-start(bf16[1024,768]{1,0:T(8,128)(2,1)} %param.13) | copy-start | bytes 4718596
  105.8 1.6 copy-start.2
  105.8 1.6 copy-start.4
  107.5 1.7 copy-start.8
  107.5 0.7 copy-start.22
  110.8 3.6 copy-start.13
  270.6 3.7 copy-start.9
  274.3 4.5 copy-start.16
  281.5 2.2 copy-start.11
  428.0 12.5 %copy-start.7 = (bf16[1024,768]{1,0:T(8,128)(2,1)S(1)}, bf16[1024,768]{1,0:T(8,128)(2,1)}, u32[]{:S(2)}) copy-start(bf16[1024,768]{1,0:T(8,128)(2,1)} %param.13) | copy-start | bytes 4718596
  440.5 2.8 copy-start.10
  443.3 2.8 copy-start.12
  448.7 2.6 copy-start.17
Sparse Core Ops, SparseCore 0:
  261.0 61.6 reduce-scatter.1

commit v10 on v9

--- a/solution.py
+++ b/solution.py
@@ -31,106 +31,6 @@
     return lax.broadcasted_iota(jnp.int32, shape, dim) // HEAD_DIM == head
 
 
-def fwd_kernel(place_ref, q_ref, k_ref, v_ref, o_ref, lse_ref, vt_ref, acc_ref):
-    place = place_ref[0]
-    rows = q_ref.shape[0]
-    blocks = rows // BRANCH
-    flipped = v_ref[...].T
-    for head in range(2):
-        vt_ref[head] = jnp.where(
-            head_lanes(flipped.shape, 0, head), flipped, jnp.ones_like(flipped)
-        )
-
-    def start(block, head, in_trunk):
-        queries = q_ref[block * BRANCH : (block + 1) * BRANCH]
-        queries = jnp.where(head_lanes(queries.shape, 1, head), queries, jnp.zeros_like(queries))
-        firsts = list(range(0, TRUNK, BRANCH))
-        if not in_trunk:
-            firsts += [rows + block * BRANCH, 2 * rows + block * BRANCH]
-        scores = [dot_nt(k_ref[first : first + BRANCH], queries) for first in firsts]
-
-        def causal(tile, offset):
-            keys = lax.broadcasted_iota(jnp.int32, tile.shape, 0) + offset
-            at = lax.broadcasted_iota(jnp.int32, tile.shape, 1)
-            return jnp.where(keys <= at, tile, MASKED)
-
-        if in_trunk:
-            scores = [
-                causal(tile, first - block * BRANCH) for tile, first in zip(scores, firsts)
-            ]
-        else:
-            scores[-2] = jnp.where(place > 1, scores[-2], MASKED)
-            scores[-1] = causal(scores[-1], 0)
-        top = jnp.max(functools.reduce(jnp.maximum, scores), axis=0, keepdims=True)
-        return firsts, scores, top
-
-    def middle(firsts, scores, top):
-        shift = top * EXP_SCALE
-        probs = [jnp.exp2(tile * EXP_SCALE - shift).astype(jnp.bfloat16) for tile in scores]
-        return firsts, probs, top
-
-    def finish(block, head, firsts, probs, top):
-        acc = None
-        for first, tile in zip(firsts, probs):
-            part = dot_nn(vt_ref[head, :, first : first + BRANCH], tile)
-            acc = part if acc is None else acc + part
-        mine, other = head * HEAD_DIM, (1 - head) * HEAD_DIM
-        total = acc[other : other + 1]
-        cols = slice(block * BRANCH, (block + 1) * BRANCH)
-        acc_ref[mine : mine + HEAD_DIM, cols] = acc[mine : mine + HEAD_DIM] / total
-        lse_ref[0, head : head + 1, cols] = top * EXP_SCALE + jnp.log2(total)
-
-    def run(in_trunk):
-        work = [(block, head) for block in range(blocks) for head in range(2)]
-        ready, held = start(*work[0], in_trunk), None
-        for at, item in enumerate(work):
-            now = ready
-            if at + 1 < len(work):
-                ready = start(*work[at + 1], in_trunk)
-            done = middle(*now)
-            if held is not None:
-                finish(*held)
-            held = (*item, *done)
-        finish(*held)
-
-    @pl.when(place == 0)
-    def _():
-        run(True)
-
-    @pl.when(place > 0)
-    def _():
-        run(False)
-
-    o_ref[...] = acc_ref[...].T.astype(o_ref.dtype)
-
-
-def attend(place, q, k, v):
-    rows, width = q.shape
-    keys = k.shape[0]
-    pairs = width // 128
-    few = pl.BlockSpec((rows, 128), lambda p, m: (0, p))
-    many = pl.BlockSpec((keys, 128), lambda p, m: (0, p))
-    return pl.pallas_call(
-        fwd_kernel,
-        out_shape=(
-            jax.ShapeDtypeStruct((rows, width), jnp.bfloat16),
-            jax.ShapeDtypeStruct((pairs, 2, rows), jnp.float32),
-        ),
-        grid_spec=pltpu.PrefetchScalarGridSpec(
-            num_scalar_prefetch=1,
-            grid=(pairs,),
-            in_specs=[few, many, many],
-            out_specs=[few, pl.BlockSpec((1, 2, rows), lambda p, m: (p, 0, 0))],
-            scratch_shapes=[
-                pltpu.VMEM((2, 128, keys), jnp.bfloat16),
-                pltpu.VMEM((128, rows), jnp.float32),
-            ],
-        ),
-        compiler_params=pltpu.CompilerParams(vmem_limit_bytes=48 << 20),
-        name="attend_forward",
-    )(place, q, k, v)
-
-
 MESH = pl.DeviceIdType.MESH
 PIECE = 64
 
@@ -142,15 +42,20 @@
     pl.semaphore_wait(barrier, len(peers))
 
 
-def share_kernel(dp, tensor, own_ref, block_ref, parent_ref, seen_ref, out_ref, weights_ref,
-                 ordered_ref, row_send, row_recv,
-                 line_send, line_recv, chip_send, chip_recv, pair_send, pair_recv):
+def front_kernel(
+    dp, tensor, depth, own_ref, block_ref, parent_ref,
+    seen_out, weight_out, q_out, k_out, v_out, o_out, lse_ref,
+    seen_ref, land_ref, weight_ref, q_ref, k_ref, v_ref, o_ref, acc_ref, top_ref, spare_ref,
+    row_send, row_recv, line_send, line_recv, chip_send, chip_recv, pair_send, pair_recv, save_sem,
+):
     spot, place = lax.axis_index("dp"), lax.axis_index("tensor")
     chip, core = spot // 2, lax.rem(spot, 2)
     chips = dp // 2
-    rows = own_ref.shape[0]
+    rows, width = own_ref.shape
     pieces = rows // PIECE
-    part_width = out_ref.shape[2] // tensor
+    pairs = width // 128
+    blocks = rows // BRANCH
+    share = width // tensor
     partner = (chip * 2 + 1 - core, place)
 
     def along(step):
@@ -165,18 +70,21 @@
         + [partner]
     )
 
-    def pass_on(part, piece, fresh):
-        at = pl.ds(part * rows + piece * PIECE, PIECE)
-        source = own_ref.at[pl.ds(piece * PIECE, PIECE)] if fresh else seen_ref.at[at]
+    def pass_on(piece, fresh):
+        at = pl.ds(pl.multiple_of(piece * PIECE, PIECE), PIECE)
+        source = seen_ref.at[at]
+        if fresh:
+            here = lax.rem(piece, pieces) * PIECE
+            source = own_ref.at[pl.ds(pl.multiple_of(here, PIECE), PIECE)]
         return pltpu.make_async_remote_copy(
             src_ref=source, dst_ref=seen_ref.at[at],
-            send_sem=row_send.at[part, piece], recv_sem=row_recv.at[part, piece],
+            send_sem=row_send.at[piece], recv_sem=row_recv.at[piece],
             device_id=(spot, lax.rem(place + 1, tensor)), device_id_type=MESH,
         )
 
     def line(step):
         return pltpu.make_async_remote_copy(
-            src_ref=block_ref, dst_ref=weights_ref.at[place, spot],
+            src_ref=block_ref, dst_ref=land_ref.at[place, spot],
             send_sem=line_send.at[step], recv_sem=line_recv.at[place],
             device_id=(spot, along(step)), device_id_type=MESH,
         )
@@ -184,13 +92,13 @@
     def line_in(step):
         source = along(tensor - step)
         return pltpu.make_async_remote_copy(
-            src_ref=block_ref, dst_ref=weights_ref.at[source, spot],
+            src_ref=block_ref, dst_ref=land_ref.at[source, spot],
             send_sem=line_send.at[step], recv_sem=line_recv.at[source],
             device_id=(spot, along(step)), device_id_type=MESH,
         )
 
     def plane(part, step):
-        block = weights_ref.at[part, spot]
+        block = land_ref.at[part, spot]
         return pltpu.make_async_remote_copy(
             src_ref=block, dst_ref=block,
             send_sem=chip_send.at[part, step], recv_sem=chip_recv.at[part, chip],
@@ -199,7 +107,7 @@
 
     def plane_in(part, step):
         source = chip_at(chips - step)
-        block = weights_ref.at[part, source * 2 + core]
+        block = land_ref.at[part, source * 2 + core]
         return pltpu.make_async_remote_copy(
             src_ref=block, dst_ref=block,
             send_sem=chip_send.at[part, step], recv_sem=chip_recv.at[part, source],
@@ -207,7 +115,7 @@
         )
 
     def across(part, source, source_core):
-        block = weights_ref.at[part, source * 2 + source_core]
+        block = land_ref.at[part, source * 2 + source_core]
         return pltpu.make_async_remote_copy(
             src_ref=block, dst_ref=block,
             send_sem=pair_send.at[part, source], recv_sem=pair_recv.at[part, source],
@@ -217,34 +125,13 @@
     for step in range(1, tensor):
         line(step).start()
 
-    def row_steps(first, last):
-        @pl.loop(first, last)
+    @pl.when(place == 0)
+    def _():
+        @pl.loop(0, pieces)
         def _(piece):
-            @pl.when(place == 0)
-            def _():
-                pass_on(0, piece, True).start()
-
-            @pl.when(place > 0)
-            def _():
-                pass_on(0, piece, False).wait_recv()
-
-            @pl.when((place > 0) & (place < tensor - 1))
-            def _():
-                pass_on(0, piece, False).start()
-
-            @pl.when(place == 1)
-            def _():
-                pass_on(1, piece, True).start()
-
-            @pl.when(place > 1)
-            def _():
-                pass_on(1, piece, False).wait_recv()
-
-            @pl.when((place > 1) & (place < tensor - 1))
-            def _():
-                pass_on(1, piece, False).start()
-
-    weights_ref[place, spot] = block_ref[...]
+            pass_on(piece, True).start()
+
+    land_ref[place, spot] = block_ref[...]
     seen_ref[2 * rows :] = own_ref[...]
 
     @pl.when(place < 2)
@@ -255,7 +142,40 @@
     def _():
         seen_ref[0:rows] = own_ref[...]
 
-    row_steps(0, pieces // 4)
+    def serve(first, last):
+        @pl.loop(first, last)
+        def _(piece):
+            trunk = piece < pieces
+            takes = (place > 1) | ((place > 0) & trunk)
+
+            @pl.when(takes)
+            def _():
+                pass_on(piece, False).wait_recv()
+
+                @pl.when(place < tensor - 1)
+                def _():
+                    pass_on(piece, False).start()
+
+            @pl.when((place == 1) & jnp.logical_not(trunk))
+            def _():
+                pass_on(piece, True).start()
+
+    def part_of(index):
+        return pl.ds(index * rows, rows)
+
+    saves = [
+        pltpu.make_async_copy(source, target, save_sem.at[index])
+        for index, (source, target) in enumerate(
+            [(weight_ref, weight_out), (q_ref, q_out), (o_ref, o_out)]
+            + [
+                (held.at[part_of(part)], target.at[part_of(part)])
+                for part in (2, 0, 1)
+                for held, target in ((seen_ref, seen_out), (k_ref, k_out), (v_ref, v_out))
+            ]
+        )
+    ]
+
+    serve(0, pieces // 4)
     for step in range(tensor):
         part = along(tensor - step)
         if step:
@@ -266,7 +186,7 @@
             plane(part, hop).start()
 
         across(part, chip, core).start()
-    row_steps(pieces // 4, (pieces * 5) // 8)
+    serve(pieces // 4, pieces // 2)
     for step in range(tensor):
         part = along(tensor - step)
 
@@ -275,36 +195,153 @@
             plane_in(part, hop).wait_recv()
             across(part, chip_at(chips - hop), core).start()
 
-    row_steps((pieces * 5) // 8, pieces)
     for part in range(tensor):
 
         @pl.loop(0, chips)
         def _(source):
             across(part, source, 1 - core).wait_recv()
-            across(part, source, core).wait_send()
-
-        @pl.loop(1, chips)
-        def _(hop):
-            plane(part, hop).wait_send()
-
-    for step in range(1, tensor):
-        line(step).wait_send()
-
-    @pl.when(place < tensor - 1)
-    def _():
-        @pl.loop(0, pieces)
-        def _(piece):
-            pass_on(0, piece, False).wait_send()
+
+    def ordered(source, kind):
+        cols = slice(kind * share, (kind + 1) * share)
+        return jnp.concatenate(
+            [land_ref[part, source][:, cols] for part in range(tensor)], axis=1
+        )
+
+    if depth % 16:
+        for kind in range(4):
+            for source in range(dp):
+                spare_ref[source * depth : (source + 1) * depth] = ordered(source, kind)[
+                    0:depth
+                ].astype(jnp.float32)
+            weight_ref[kind] = spare_ref[...].astype(weight_ref.dtype)
+    else:
+
+        @pl.loop(0, dp)
+        def _(source):
+            at = pl.ds(pl.multiple_of(source * depth, depth), depth)
+            for kind in range(4):
+                weight_ref[kind, at] = ordered(source, kind)
+
+    saves[0].start()
+
+    def lanes(pair):
+        return pl.ds(pl.multiple_of(pair * 128, 128), 128)
+
+    def project(first, also_queries=False):
+        @pl.loop(0, blocks)
+        def _(b):
+            at = pl.ds(pl.multiple_of(first + b * BRANCH, BRANCH), BRANCH)
+            normed = seen_ref[at]
+            k_ref[at] = dot_nn(normed, weight_ref[1]).astype(k_ref.dtype)
+            v_ref[at] = dot_nn(normed, weight_ref[2]).astype(v_ref.dtype)
+            if also_queries:
+                here = pl.ds(pl.multiple_of(b * BRANCH, BRANCH), BRANCH)
+                q_ref[here] = dot_nn(normed, weight_ref[0]).astype(q_ref.dtype)
+
+    def attend_tiles(pair, tiles_of, opening):
+        values, work = {}, [(block, head) for block in range(blocks) for head in range(2)]
+
+        def value_tile(first, head):
+            if (first, head) not in values:
+                flipped = v_ref[first : first + BRANCH, lanes(pair)].T
+                for side in range(2):
+                    values[first, side] = jnp.where(
+                        head_lanes(flipped.shape, 0, side), flipped, jnp.ones_like(flipped)
+                    )
+            return values[first, head]
+
+        def start(block, head):
+            queries = q_ref[block * BRANCH : (block + 1) * BRANCH, lanes(pair)]
+            queries = jnp.where(
+                head_lanes(queries.shape, 1, head), queries, jnp.zeros_like(queries)
+            )
+            scores = []
+            for first, masked in tiles_of(block):
+                tile = dot_nt(k_ref[first : first + BRANCH, lanes(pair)], queries)
+                if masked:
+                    keys = lax.broadcasted_iota(jnp.int32, tile.shape, 0)
+                    at = lax.broadcasted_iota(jnp.int32, tile.shape, 1)
+                    tile = jnp.where(keys <= at, tile, MASKED)
+                scores.append(tile)
+            top = jnp.max(functools.reduce(jnp.maximum, scores), axis=0, keepdims=True)
+            return scores, top
+
+        def middle(block, head, scores, top):
+            cols = slice(block * BRANCH, (block + 1) * BRANCH)
+            fade = None
+            if not opening:
+                before = top_ref[pair, head : head + 1, cols]
+                top = jnp.maximum(before, top)
+                fade = jnp.exp2((before - top) * EXP_SCALE)
+            top_ref[pair, head : head + 1, cols] = top
+            shift = top * EXP_SCALE
+            return [
+                jnp.exp2(tile * EXP_SCALE - shift).astype(jnp.bfloat16) for tile in scores
+            ], fade
+
+        def finish(block, head, probs, fade):
+            cols = slice(block * BRANCH, (block + 1) * BRANCH)
+            acc = None if opening else acc_ref[pair, head, :, cols] * fade
+            for (first, _), tile in zip(tiles_of(block), probs):
+                part = dot_nn(value_tile(first, head), tile)
+                acc = part if acc is None else acc + part
+            acc_ref[pair, head, :, cols] = acc
+
+        ready, held = start(*work[0]), None
+        for at, item in enumerate(work):
+            now = ready
+            if at + 1 < len(work):
+                ready = start(*work[at + 1])
+            done = middle(*item, *now)
+            if held is not None:
+                finish(*held)
+            held = (*item, *done)
+        finish(*held)
+
+    project(2 * rows, True)
+    for index in (1, 3, 4, 5):
+        saves[index].start()
+    serve(pieces // 2, (3 * pieces) // 4)
+
+    @pl.loop(0, pairs)
+    def _(pair):
+        @pl.when(place == 0)
+        def _():
+            attend_tiles(
+                pair,
+                lambda block: [
+                    (2 * rows + j * BRANCH, j == block) for j in range(block + 1)
+                ],
+                True,
+            )
+
+        @pl.when(place > 0)
+        def _():
+            attend_tiles(pair, lambda block: [(2 * rows + block * BRANCH, True)], True)
+
+    serve((3 * pieces) // 4, pieces)
+    project(0)
+    for index in (6, 7, 8):
+        saves[index].start()
+    per_pair = -(-pieces // pairs)
+
+    @pl.loop(0, pairs)
+    def _(pair):
+        @pl.when(place > 0)
+        def _():
+            attend_tiles(pair, lambda block: [(j * BRANCH, False) for j in range(blocks)], False)
+
+        first = pieces + pair * per_pair
+        serve(jnp.minimum(first, 2 * pieces), jnp.minimum(first + per_pair, 2 * pieces))
 
     @pl.when((place > 0) & (place < tensor - 1))
     def _():
-        @pl.loop(0, pieces)
+        @pl.loop(0, 2 * pieces)
         def _(piece):
-            pass_on(1, piece, False).wait_send()
+            pass_on(piece, False).wait_send()
 
     @pl.when(place > 1)
     def _():
-        blocks = rows // BRANCH
         branches = [
             seen_ref[rows + branch * BRANCH : rows + (branch + 1) * BRANCH]
             for branch in range(blocks)
@@ -315,53 +352,96 @@
                 at = leaf * blocks + branch
                 part = branches[branch] * parent_ref[at : at + 1].astype(own_ref.dtype)
                 chosen = part if chosen is None else chosen + part
-            ordered_ref[leaf * BRANCH : (leaf + 1) * BRANCH] = chosen
-        seen_ref[rows : 2 * rows] = ordered_ref[...]
-
-    @pl.loop(0, dp)
-    def _(source):
-        depth = block_ref.shape[0]
-        at = pl.ds(pl.multiple_of(source * depth, depth), depth)
-        for kind in range(out_ref.shape[0]):
-            cols = slice(kind * part_width, (kind + 1) * part_width)
-            out_ref[kind, at] = jnp.concatenate(
-                [weights_ref[part, source][:, cols] for part in range(tensor)], axis=1
+            o_ref[leaf * BRANCH : (leaf + 1) * BRANCH] = chosen
+        seen_ref[rows : 2 * rows] = o_ref[...]
+
+    project(rows)
+    for index in (9, 10, 11):
+        saves[index].start()
+
+    @pl.loop(0, pairs)
+    def _(pair):
+        @pl.when(place > 1)
+        def _():
+            attend_tiles(pair, lambda block: [(rows + block * BRANCH, False)], False)
+
+        outs = []
+        for head in range(2):
+            mine, other = head * HEAD_DIM, (1 - head) * HEAD_DIM
+            total = acc_ref[pair, head, other : other + 1]
+            outs.append(acc_ref[pair, head, mine : mine + HEAD_DIM] / total)
+            lse_ref[pair, head : head + 1] = (
+                top_ref[pair, head : head + 1] * EXP_SCALE + jnp.log2(total)
             )
-
-
-def share_rows_and_weights(own, block, parents):
+        o_ref[:, lanes(pair)] = jnp.concatenate(outs, axis=0).T.astype(o_ref.dtype)
+
+    saves[2].start()
+    for part in range(tensor):
+
+        @pl.loop(0, chips)
+        def _(source):
+            across(part, source, core).wait_send()
+
+        @pl.loop(1, chips)
+        def _(hop):
+            plane(part, hop).wait_send()
+
+    for step in range(1, tensor):
+        line(step).wait_send()
+
+    @pl.when(place == 0)
+    def _():
+        @pl.loop(0, pieces)
+        def _(piece):
+            pass_on(piece, True).wait_send()
+
+    for save in saves:
+        save.wait()
+
+
+def front(own, block, parents):
     dp, tensor = lax.axis_size("dp"), lax.axis_size("tensor")
     rows, width = own.shape
     depth, cols = block.shape
-    pieces, chips = rows // PIECE, dp // 2
-    kinds = cols * tensor // width
+    pieces, chips, pairs = rows // PIECE, dp // 2, width // 128
     padded = -(-depth // 16) * 16
     block = jnp.pad(block, ((0, padded - depth), (0, 0)))
+    low, full = jnp.bfloat16, jnp.float32
+    few, many = (rows, width), (3 * rows, width)
+    weights = (4, width, width)
     dma = pltpu.SemaphoreType.DMA
     here = pl.BlockSpec(memory_space=pltpu.VMEM)
-    seen, weights = pl.pallas_call(
-        lambda *refs: share_kernel(dp, tensor, *refs),
-        out_shape=(
-            jax.ShapeDtypeStruct((3 * rows, width), own.dtype),
-            jax.ShapeDtypeStruct((kinds, dp * padded, width), block.dtype),
-        ),
+    anywhere = pl.BlockSpec(memory_space=pl.ANY)
+    return pl.pallas_call(
+        lambda *refs: front_kernel(dp, tensor, depth, *refs),
+        out_shape=tuple(
+            jax.ShapeDtypeStruct(shape, low) for shape in (many, weights, few, many, many, few)
+        )
+        + (jax.ShapeDtypeStruct((pairs, 2, rows), full),),
         in_specs=[here, here, here],
-        out_specs=[here, here],
+        out_specs=[anywhere] * 6 + [here],
         scratch_shapes=[
-            pltpu.VMEM((tensor, dp, padded, cols), block.dtype),
-            pltpu.VMEM(own.shape, own.dtype),
-            dma((2, pieces)), dma((2, pieces)),
+            pltpu.VMEM(many, low),
+            pltpu.VMEM((tensor, dp, padded, cols), low),
+            pltpu.VMEM(weights, low),
+            pltpu.VMEM(few, low),
+            pltpu.VMEM(many, low),
+            pltpu.VMEM(many, low),
+            pltpu.VMEM(few, low),
+            pltpu.VMEM((pairs, 2, 128, rows), full),
+            pltpu.VMEM((pairs, 2, rows), full),
+            pltpu.VMEM((width, width) if depth % 16 else (8, 128), full),
+            dma((2 * pieces,)), dma((2 * pieces,)),
             dma((tensor,)), dma((tensor,)),
             dma((tensor, chips)), dma((tensor, chips)),
             dma((tensor, chips)), dma((tensor, chips)),
+            dma((12,)),
         ],
         compiler_params=pltpu.CompilerParams(
-            collective_id=2, has_side_effects=True, vmem_limit_bytes=48 << 20
+            collective_id=2, has_side_effects=True, vmem_limit_bytes=58 << 20
         ),
-        name="share_rows_and_weights",
+        name="front",
     )(own, block, parents)
-    weights = weights.reshape(kinds, dp, padded, width)[:, :, :depth]
-    return seen, weights.reshape(kinds, dp * depth, width)
 
 
 TN = (((0,), (0,)), ((), ()))
@@ -1317,14 +1397,10 @@
     leaf_parents = lax.dynamic_slice_in_dim(leaf_parent[0], first_leaf, leaf_blocks, 0) - 1
     parents = (leaf_parents[:, None] == jnp.arange(leaf_blocks)[None, :]).astype(jnp.float32)
     parents = jnp.broadcast_to(parents.reshape(-1, 1), (leaf_blocks * leaf_blocks, model_width))
-    seen_in, weights = share_rows_and_weights(
+    seen_in, weights, query_rows, key_rows, value_rows, attended, log_totals = front(
         own_in, jnp.concatenate([flat_qkv, attn_proj.T], axis=1), parents
     )
-    query_weight, key_weight, value_weight, proj_back = weights
-    query_rows = low_dot(own_in, query_weight)
-    key_rows = low_dot(seen_in, key_weight)
-    value_rows = low_dot(seen_in, value_weight)
-    attended, log_totals = attend(place[None].astype(jnp.int32), query_rows, key_rows, value_rows)
+    proj_back = weights[3]
     branch_out = jnp.einsum(
         "sc,dc->sd", attended, proj_back, preferred_element_type=jnp.float32
     )

time: 465 us -> 465 us (level)
  the two profiles are of different devices: /device:TPU:0 before, /device:TPU:25 now
where the time goes in v10:
time: 465 us; the launch traced here: 456 us
  Pallas kernels  372 us (80%)
  matrix products  28.5 us (6%)
  other arithmetic  27.9 us (6%)
  between operations  14.9 us (3%)
  local copies, waits for them, and re-layouts  12.1 us (3%)
    pallas_call x1, Pallas kernels, front(): pl.pallas_call(lambda *refs: front_kernel(dp, tensor, depth, *refs), out_...  134 us
    pallas_call x1, Pallas kernels, backward(): pl.pallas_call(lambda *refs: back_kernel(dp, tensor, depth, *refs), out_s...  133 us
    pallas_call x1, Pallas kernels, run_experts(): pl.pallas_call(lambda *refs: expert_kernel(dp, tensor, *refs), out_shape=...  105 us
  transfers between devices with their start and end apart: 1, of which 0 were waited for; matrix products, arithmetic and copies ran while one was open for 8% of the time, Pallas kernels for 29%

profile of v10, /device:TPU:25, one launch (start us, length us, event | category | flops | bytes accessed | tf_op | source)
XLA Modules:
  0.0 455.8 jit_solution(13021324474397652441)
XLA Ops:
  7.3 0.8 and_select_fusion
  8.8 2.0 select_reduce_fusion
  10.9 0.8 multiply_reduce_fusion.6
  13.3 1.7 convert_reduce_fusion
  15.0 2.0 fusion.13
  18.2 1.7 fusion.15.refs_0_
  20.6 134.2 %front.1 = (bf16[3072,768]{1,0:T(8,128)(2,1)}, bf16[4,768,768]{2,1,0:T(8,128)(2,1)}, bf16[1024,768]{1,0:T(8,128)(2,1)}, bf16[3072,768]{1,0:T(8,128)(2,1)}, bf16[...) custom-call(bf16[1024,768]{1,0:T(8,128)(2,1)} %fusion.15.refs_0_, ...), custom_call_target="tpu_custom_call" | custom-call | tf_op jit(solution)/shard_map/front/pallas_call | solution.py:415
  154.8 3.3 fusion.67
  159.8 1.3 multiply_reduce_fusion.4
  161.5 3.6 fusion.28.refs_0_
  165.1 3.8 fusion.31.refs_1_
  168.8 105.5 %run_experts.1 = (bf16[1024,768]{1,0:T(8,128)(2,1)}, bf16[1024,768]{1,0:T(8,128)(2,1)}, bf16[1536,768]{1,0:T(8,128)(2,1)}, f32[384,768]{1,0:T(8,128)}) custom-call(bf16[1024,768]{1,0:T(8,128)(2,1)} %fusion.28.refs_0_, bf16[1024,768]{1,0:T(8,128)(2,1)} %fusion.31.refs_1_, bf16[768,1536]{1,0:T(8,128)(2,1)} %refs_2_.1, bf16[1536,768]{1,0:T(8,128)(2,1)} %refs_3_.1), custom_call_target="tpu_custom_call" | custom-call | tf_op jit(solution)/shard_map/run_experts/pallas_call | solution.py:1305
  274.4 5.5 %fusion.18 = (f32[1024]{0:T(1024)S(1)}, f32[1024,768]{1,0:T(8,128)}) fusion(bf16[1024,768]{1,0:T(8,128)(2,1)} %param.25, bf16[1024,768]{1,0:T(8,128)(2,1)} %get-tuple-element.26, s32[1024]{0:T(1024)S(1)} %bitcast.44, pred[1024]{0:T(1024)(128)(4,1)S(1)} %broadcast_compare_fusion), kind=kOutput, calls=%fused_computation.24 | convolution fusion | flops 1615068160 | bytes 6300672 | tf_op jit(solution)/shard_map/dot_general | solution.py:1431
  280.6 2.5 fusion.50
  283.3 1.1 reshape.192
  284.5 3.7 fusion.5
  288.2 3.9 multiply_reduce_fusion
  292.8 2.7 fusion.65
  295.4 1.9 fusion.27.refs_5_
  297.6 132.7 %attend_backward.1 = (f32[1024,768]{1,0:T(8,128)}, f32[96,768]{1,0:T(8,128)}, f32[32,8,128]{2,1,0:T(8,128)}) custom-call(f32[16,768]{1,0:T(8,128)} %broadcast_in_dim.28.refs_2_.refs_0_, bf16[1024,768]{1,0:T(8,128)(2,1)} %get-tuple-element.28.refs_1_, bf16[3072,768]{1,0:T(8,128)(2,1)} %get-tuple-element.29.refs_2_, ...), custom_call_target="tpu_custom_call" | custom-call | tf_op jit(solution)/shard_map/attend_backward/pallas_call | solution.py:1012
  430.3 1.2 slice.30
  432.2 1.0 slice.27
  433.1 1.0 slice_bitcast_fusion
  435.0 0.9 copy.58
  435.9 0.8 copy.60
  436.6 2.8 fusion.16
  439.5 1.4 fusion.64
  440.9 1.4 fusion.66
  442.2 2.7 add_add_fusion.2
  444.9 1.2 convert_bitcast_fusion
  446.1 1.4 copy.61
  447.5 1.0 copy.68
  (83 shorter events, 9.6 us)
Async XLA Ops:
  7.2 152.6 %copy-start = (f32[768,16]{0,1:T(8,128)S(1)}, f32[768,16]{0,1:T(8,128)}, u32[]{:S(2)}) copy-start(f32[768,16]{0,1:T(8,128)} %param.18) | copy-start | bytes 147460
  7.2 11.0 %copy-start.2 = (bf16[1024,768]{1,0:T(8,128)(2,1)S(1)}, bf16[1024,768]{1,0:T(8,128)(2,1)}, u32[]{:S(2)}) copy-start(bf16[1024,768]{1,0:T(8,128)(2,1)} %param.13) | copy-start | bytes 4718596
  7.2 9.8 %copy-start.16 = (bf16[192,96]{1,0:T(8,128)(2,1)S(1)}, bf16[192,96]{1,0:T(8,128)(2,1)}, u32[]{:S(2)}) copy-start(bf16[192,96]{1,0:T(8,128)(2,1)} %param.16) | copy-start | bytes 110596
  7.2 9.9 %copy-start.13 = (bf16[96,3,192]{2,0,1:T(8,128)(2,1)S(1)}, bf16[96,3,192]{2,0,1:T(8,128)(2,1)}, u32[]{:S(2)}) copy-start(bf16[96,3,192]{2,0,1:T(8,128)(2,1)} %param.15) | copy-start | bytes 331780
  7.2 11.0 %copy-start.15 = (f32[768]{0:T(1024)S(1)}, f32[768]{0:T(1024)}, u32[]{:S(2)}) copy-start(f32[768]{0:T(1024)} %param.14) | copy-start | bytes 9220
  7.2 437.7 %reduce-scatter.2.cloned.1.call-start = ((), (), s32[]{:S(2)}) async-start(), calls=%async_computation.1 | async-start | bytes 2949120 | tf_op jit(solution)/shard_map/reduce_scatter | solution.py:1446
  158.1 1.7 copy-start.3
  158.1 0.7 copy-start.17
  158.8 2.3 copy-start.18
  158.8 2.6 copy-start.14
  161.5 3.6 copy-start.8
  284.5 3.7 copy-start.4
  288.2 4.6 %copy-start.11 = (f32[1024,768]{1,0:T(8,128)S(1)}, f32[1024,768]{1,0:T(8,128)}, u32[]{:S(2)}) copy-start(f32[1024,768]{1,0:T(8,128)} %get-tuple-element.82) | copy-start | bytes 9437188
  292.7 2.7 copy-start.9
  295.4 2.2 copy-start.6
  436.6 2.8 copy-start.5
  439.4 2.8 copy-start.7
  439.4 2.8 copy-start.10
  442.2 6.3 %copy-start.1 = (f32[768,16]{0,1:T(8,128)S(1)}, f32[768,16]{0,1:T(8,128)}, u32[]{:S(2)}) copy-start(f32[768,16]{0,1:T(8,128)} %param.18) | copy-start | bytes 147460
  444.9 2.6 copy-start.12
Sparse Core Ops, SparseCore 0:
  274.5 46.0 reduce-scatter.1

commit v11 on v10

--- a/solution.py
+++ b/solution.py
@@ -145,8 +145,7 @@
     def serve(first, last):
         @pl.loop(first, last)
         def _(piece):
-            trunk = piece < pieces
-            takes = (place > 1) | ((place > 0) & trunk)
+            takes = (place > 1) | ((place > 0) & (piece < pieces))
 
             @pl.when(takes)
             def _():
@@ -155,10 +154,6 @@
                 @pl.when(place < tensor - 1)
                 def _():
                     pass_on(piece, False).start()
-
-            @pl.when((place == 1) & jnp.logical_not(trunk))
-            def _():
-                pass_on(piece, True).start()
 
     def part_of(index):
         return pl.ds(index * rows, rows)
@@ -175,7 +170,7 @@
         )
     ]
 
-    serve(0, pieces // 4)
+    serve(0, pieces // 8)
     for step in range(tensor):
         part = along(tensor - step)
         if step:
@@ -186,7 +181,7 @@
             plane(part, hop).start()
 
         across(part, chip, core).start()
-    serve(pieces // 4, pieces // 2)
+    serve(pieces // 8, (5 * pieces) // 8)
     for step in range(tensor):
         part = along(tensor - step)
 
@@ -194,6 +189,14 @@
         def _(hop):
             plane_in(part, hop).wait_recv()
             across(part, chip_at(chips - hop), core).start()
+
+    serve((5 * pieces) // 8, pieces)
+
+    @pl.when(place == 1)
+    def _():
+        @pl.loop(pieces, 2 * pieces)
+        def _(piece):
+            pass_on(piece, True).start()
 
     for part in range(tensor):
 
@@ -301,7 +304,7 @@
     project(2 * rows, True)
     for index in (1, 3, 4, 5):
         saves[index].start()
-    serve(pieces // 2, (3 * pieces) // 4)
+    serve(pieces, pieces + 2)
 
     @pl.loop(0, pairs)
     def _(pair):
@@ -319,11 +322,16 @@
         def _():
             attend_tiles(pair, lambda block: [(2 * rows + block * BRANCH, True)], True)
 
-    serve((3 * pieces) // 4, pieces)
+        @pl.when(lax.rem(pair, 2) == 1)
+        def _():
+            piece = pieces + 2 + pair // 2
+            serve(piece, piece + 1)
+
     project(0)
     for index in (6, 7, 8):
         saves[index].start()
-    per_pair = -(-pieces // pairs)
+    served = pieces + 2 + pairs // 2
+    per_pair = -(-(2 * pieces - served) // pairs)
 
     @pl.loop(0, pairs)
     def _(pair):
@@ -331,7 +339,7 @@
         def _():
             attend_tiles(pair, lambda block: [(j * BRANCH, False) for j in range(blocks)], False)
 
-        first = pieces + pair * per_pair
+        first = served + pair * per_pair
         serve(jnp.minimum(first, 2 * pieces), jnp.minimum(first + per_pair, 2 * pieces))
 
     @pl.when((place > 0) & (place < tensor - 1))
@@ -1153,11 +1161,6 @@
 
     x_ref[at(0, 0)] = x_in[at(0, 0)]
     pair_x(0).start()
-
-    @pl.loop(1, chips)
-    def _(step):
-        go_g(step).start()
-
     g_ref[at(0, 0)] = g_in[at(0, 0)]
 
     def ahead_pass(side, step):
@@ -1194,6 +1197,7 @@
     def _(step):
         go_x(step).wait_recv()
         pair_x(step).start()
+        go_g(step).start()
         keep_ref[at(0, step)] = ahead_pass(0, step)
 
     pair_g(0).start()
@@ -1228,16 +1232,19 @@
     def _(step):
         pair_g(step).wait_recv()
 
-    @pl.loop(0, tensor)
-    def _(part):
+    @pl.loop(1, tensor + 1)
+    def _(turn):
+        step = lax.rem(turn, tensor)
+        part = along(step)
         for first in range(0, share, 128):
             cols = pl.ds(pl.multiple_of(part * share + first, 128), 128)
             grad_ref[part, first : first + 128] = dot_tn(active_ref[:, cols], g_ref[...]).astype(
                 grad_ref.dtype
             )
 
-    for step in range(1, tensor):
-        line(step).start()
+        @pl.when(step > 0)
+        def _():
+            line(step).start()
 
     @pl.loop(0, chips)
     def _(step):

time: 465 us -> 439 us (0.944)
  the two profiles are of different devices: /device:TPU:25 before, /device:TPU:0 now
where the time goes in v11:
time: 439 us; the launch traced here: 430 us
  Pallas kernels  347 us (79%)
  matrix products  28.4 us (6%)
  other arithmetic  27.9 us (6%)
  between operations  14.9 us (3%)
  local copies, waits for them, and re-layouts  12.1 us (3%)
    pallas_call x1, Pallas kernels, run_experts(): pl.pallas_call(lambda *refs: expert_kernel(dp, tensor, *refs), out_shape=...  144 us
    pallas_call x1, Pallas kernels, backward(): pl.pallas_call(lambda *refs: back_kernel(dp, tensor, depth, *refs), out_s...  141 us
    pallas_call x1, Pallas kernels, front(): pl.pallas_call(lambda *refs: front_kernel(dp, tensor, depth, *refs), out_...  62.8 us
    dot_general x2, matrix products, from_slots(): return jnp.dot(select, slot_rows, preferred_element_type=jnp.float32)  9.18 us
  transfers between devices with their start and end apart: 1, of which 0 were waited for; matrix products, arithmetic and copies ran while one was open for 9% of the time, Pallas kernels for 33%

profile of v11, /device:TPU:0, one launch (start us, length us, event | category | flops | bytes accessed | tf_op | source)
XLA Modules:
  0.0 430.3 jit_solution(17308422139603396881)
XLA Ops:
  7.3 0.8 and_select_fusion
  8.8 2.0 select_reduce_fusion
  10.9 0.8 multiply_reduce_fusion.6
  13.3 1.7 convert_reduce_fusion
  15.0 2.0 fusion.13
  18.2 1.7 fusion.15.refs_0_
  20.6 62.8 %front.1 = (bf16[3072,768]{1,0:T(8,128)(2,1)}, bf16[4,768,768]{2,1,0:T(8,128)(2,1)}, bf16[1024,768]{1,0:T(8,128)(2,1)}, bf16[3072,768]{1,0:T(8,128)(2,1)}, bf16[...) custom-call(bf16[1024,768]{1,0:T(8,128)(2,1)} %fusion.15.refs_0_, ...), custom_call_target="tpu_custom_call" | custom-call | tf_op jit(solution)/shard_map/front/pallas_call | solution.py:423
  83.4 3.3 fusion.67
  88.3 1.3 multiply_reduce_fusion.4
  90.0 3.6 fusion.28.refs_0_
  93.6 3.8 fusion.31.refs_1_
  97.4 143.6 %run_experts.1 = (bf16[1024,768]{1,0:T(8,128)(2,1)}, bf16[1024,768]{1,0:T(8,128)(2,1)}, bf16[1536,768]{1,0:T(8,128)(2,1)}, f32[384,768]{1,0:T(8,128)}) custom-call(bf16[1024,768]{1,0:T(8,128)(2,1)} %fusion.28.refs_0_, bf16[1024,768]{1,0:T(8,128)(2,1)} %fusion.31.refs_1_, bf16[768,1536]{1,0:T(8,128)(2,1)} %refs_2_.1, bf16[1536,768]{1,0:T(8,128)(2,1)} %refs_3_.1), custom_call_target="tpu_custom_call" | custom-call | tf_op jit(solution)/shard_map/run_experts/pallas_call | solution.py:1312
  241.0 5.5 %fusion.18 = (f32[1024]{0:T(1024)S(1)}, f32[1024,768]{1,0:T(8,128)}) fusion(bf16[1024,768]{1,0:T(8,128)(2,1)} %param.25, bf16[1024,768]{1,0:T(8,128)(2,1)} %get-tuple-element.26, s32[1024]{0:T(1024)S(1)} %bitcast.44, pred[1024]{0:T(1024)(128)(4,1)S(1)} %broadcast_compare_fusion), kind=kOutput, calls=%fused_computation.24 | convolution fusion | flops 1615068160 | bytes 6300672 | tf_op jit(solution)/shard_map/dot_general | solution.py:1438
  247.3 2.5 fusion.50
  250.0 1.1 reshape.192
  251.1 3.7 fusion.5
  254.8 3.9 multiply_reduce_fusion
  259.4 2.7 fusion.65
  262.1 1.9 fusion.27.refs_5_
  264.2 140.6 %attend_backward.1 = (f32[1024,768]{1,0:T(8,128)}, f32[96,768]{1,0:T(8,128)}, f32[32,8,128]{2,1,0:T(8,128)}) custom-call(f32[16,768]{1,0:T(8,128)} %broadcast_in_dim.28.refs_2_.refs_0_, bf16[1024,768]{1,0:T(8,128)(2,1)} %get-tuple-element.28.refs_1_, bf16[3072,768]{1,0:T(8,128)(2,1)} %get-tuple-element.29.refs_2_, ...), custom_call_target="tpu_custom_call" | custom-call | tf_op jit(solution)/shard_map/attend_backward/pallas_call | solution.py:1020
  404.8 1.2 slice.30
  406.7 1.0 slice.27
  407.6 1.0 slice_bitcast_fusion
  409.5 0.9 copy.58
  410.4 0.8 copy.60
  411.2 2.8 fusion.16
  414.0 1.4 fusion.64
  415.4 1.4 fusion.66
  416.8 2.7 add_add_fusion.2
  419.4 1.2 convert_bitcast_fusion
  420.7 1.4 copy.61
  422.0 1.0 copy.68
  (83 shorter events, 9.6 us)
Async XLA Ops:
  7.2 81.2 %copy-start = (f32[768,16]{0,1:T(8,128)S(1)}, f32[768,16]{0,1:T(8,128)}, u32[]{:S(2)}) copy-start(f32[768,16]{0,1:T(8,128)} %param.18) | copy-start | bytes 147460
  7.2 11.0 %copy-start.2 = (bf16[1024,768]{1,0:T(8,128)(2,1)S(1)}, bf16[1024,768]{1,0:T(8,128)(2,1)}, u32[]{:S(2)}) copy-start(bf16[1024,768]{1,0:T(8,128)(2,1)} %param.13) | copy-start | bytes 4718596
  7.2 9.8 %copy-start.16 = (bf16[192,96]{1,0:T(8,128)(2,1)S(1)}, bf16[192,96]{1,0:T(8,128)(2,1)}, u32[]{:S(2)}) copy-start(bf16[192,96]{1,0:T(8,128)(2,1)} %param.16) | copy-start | bytes 110596
  7.2 9.9 %copy-start.13 = (bf16[96,3,192]{2,0,1:T(8,128)(2,1)S(1)}, bf16[96,3,192]{2,0,1:T(8,128)(2,1)}, u32[]{:S(2)}) copy-start(bf16[96,3,192]{2,0,1:T(8,128)(2,1)} %param.15) | copy-start | bytes 331780
  7.2 11.0 %copy-start.15 = (f32[768]{0:T(1024)S(1)}, f32[768]{0:T(1024)}, u32[]{:S(2)}) copy-start(f32[768]{0:T(1024)} %param.14) | copy-start | bytes 9220
  7.2 412.2 %reduce-scatter.2.cloned.1.call-start = ((), (), s32[]{:S(2)}) async-start(), calls=%async_computation.1 | async-start | bytes 2949120 | tf_op jit(solution)/shard_map/reduce_scatter | solution.py:1453
  86.7 1.7 copy-start.3
  86.7 0.7 copy-start.17
  87.4 2.3 copy-start.18
  87.4 2.6 copy-start.14
  90.0 3.6 copy-start.8
  251.1 3.7 copy-start.4
  254.8 4.6 %copy-start.11 = (f32[1024,768]{1,0:T(8,128)S(1)}, f32[1024,768]{1,0:T(8,128)}, u32[]{:S(2)}) copy-start(f32[1024,768]{1,0:T(8,128)} %get-tuple-element.82) | copy-start | bytes 9437188
  259.4 2.7 copy-start.9
  262.1 2.2 copy-start.6
  411.2 2.8 copy-start.5
  413.9 2.8 copy-start.7
  414.0 2.8 copy-start.10
  416.7 6.3 %copy-start.1 = (f32[768,16]{0,1:T(8,128)S(1)}, f32[768,16]{0,1:T(8,128)}, u32[]{:S(2)}) copy-start(f32[768,16]{0,1:T(8,128)} %param.18) | copy-start | bytes 147460
  419.4 2.6 copy-start.12
Sparse Core Ops, SparseCore 0:
  241.2 57.1 reduce-scatter.1
